TPU v7x, 32 devices: a whole 2x2x4 slice. The times are simulated.
32 devices in a mesh: seq: 2 (over z_hi), fsdp: 8 (over y, x, core), dp: 2 (over z_lo).
Axes of the slice: x: 2, y: 2, z: 4 (z_hi: 2, z_lo: 2; z = z_hi * 2 + z_lo), core: 2. Of those that a mesh axis runs over, the one named last changes fastest.
Arguments:
- images: bfloat16 [48, 584, 1024], P(('fsdp', 'dp'), 'seq'), may hold values from -6 to 6
- key_mask: int32 [48, 584], P(('fsdp', 'dp')), may hold values from 0 to 1, as said below
- out_grad: bfloat16 [48, 584, 1024], P(('fsdp', 'dp'), 'seq'), may hold values from -6 to 6
- step_count: int32 [], replicated, may hold values from 2 to 20
- in_weights: float32 [1024, 3072], P(('seq', 'fsdp')), may hold values from -0.25 to 0.25
- out_weights: float32 [1024, 1024], P(('seq', 'fsdp')), may hold values from -0.375 to 0.375
- up_weights: float32 [4096, 1024], P(('seq', 'fsdp')), may hold values from -0.1875 to 0.1875
- down_weights: float32 [4096, 1024], P(('seq', 'fsdp')), may hold values from -0.09375 to 0.09375
- vectors: float32 [12288], P(('seq', 'fsdp')), may hold values from -0.4 to 1.4
- first_in: float32 [1024, 3072], P(('seq', 'fsdp')), may hold values from -1.5 to 1.5
- first_out: float32 [1024, 1024], P(('seq', 'fsdp')), may hold values from -0.9 to 0.9
- first_up: float32 [4096, 1024], P(('seq', 'fsdp')), may hold values from -2.2 to 2.2
- first_down: float32 [4096, 1024], P(('seq', 'fsdp')), may hold values from -4.5 to 4.5
- first_vectors: float32 [12288], P(('seq', 'fsdp')), may hold values from -4.5 to 4.5
- second_in: float32 [1024, 3072], P(('seq', 'fsdp')), may hold values from 0.03 to 0.25
- second_out: float32 [1024, 1024], P(('seq', 'fsdp')), may hold values from 0.012 to 0.09
- second_up: float32 [4096, 1024], P(('seq', 'fsdp')), may hold values from 0.07 to 0.55
- second_down: float32 [4096, 1024], P(('seq', 'fsdp')), may hold values from 0.28 to 2.2
- second_vectors: float32 [12288], P(('seq', 'fsdp')), may hold values from 0.28 to 2.2
Outputs:
- grad_norm: float32 [], replicated
- new_in: float32 [1024, 3072], P(('seq', 'fsdp'))
- new_out: float32 [1024, 1024], P(('seq', 'fsdp'))
- new_up: float32 [4096, 1024], P(('seq', 'fsdp'))
- new_down: float32 [4096, 1024], P(('seq', 'fsdp'))
- new_vectors: float32 [12288], P(('seq', 'fsdp'))
- first_in_new: float32 [1024, 3072], P(('seq', 'fsdp'))
- first_out_new: float32 [1024, 1024], P(('seq', 'fsdp'))
- first_up_new: float32 [4096, 1024], P(('seq', 'fsdp'))
- first_down_new: float32 [4096, 1024], P(('seq', 'fsdp'))
- first_vectors_new: float32 [12288], P(('seq', 'fsdp'))
- second_in_new: float32 [1024, 3072], P(('seq', 'fsdp'))
- second_out_new: float32 [1024, 1024], P(('seq', 'fsdp'))
- second_up_new: float32 [4096, 1024], P(('seq', 'fsdp'))
- second_down_new: float32 [4096, 1024], P(('seq', 'fsdp'))
- second_vectors_new: float32 [12288], P(('seq', 'fsdp'))
- copy_in: bfloat16 [1024, 3072], P(('seq', 'fsdp'))
- copy_out: bfloat16 [1024, 1024], P(('seq', 'fsdp'))
- copy_up: bfloat16 [4096, 1024], P(('seq', 'fsdp'))
- copy_down: bfloat16 [4096, 1024], P(('seq', 'fsdp'))
- copy_vectors: bfloat16 [12288], P(('seq', 'fsdp'))
- activations: float32 [48, 584, 1024], P(('fsdp', 'dp'), 'seq')
- input_grad: float32 [48, 584, 1024], P(('fsdp', 'dp'), 'seq')
Inputs may be any that keep to these rules, and one draw needn't show every extreme that they name: `key_mask`: every image has exactly 577 ones; where its 7 zeros stand is drawn afresh for each image.
All inputs are finite; a program needn't handle non-finite values.
Results may differ from a plain program's by a relative error of at most 0.02.
The roundings to bfloat16 on the way count: a program that leaves them out, or rounds other values in their place, can miss the bound.
Values may be sent and summed in bfloat16 or wider, within the bound.
A program may use at most 256 MiB of HBM per device.

v0:
```python
import math

import jax
import jax.numpy as jnp
from jax import lax
from jax.sharding import PartitionSpec as P

D = 1024
HD = 64
FF = 4096


NEG_FILL = -1000000000.0
NORM_EPS = 1e-06
ADAM_EPS = 1e-08
WEIGHT_DECAY = 0.05


def layer_norm(values, norm_gain, norm_shift):
    center = values - jnp.mean(values, axis=-1, keepdims=True)
    spread = jnp.mean(center * center, axis=-1, keepdims=True)
    return center * lax.rsqrt(spread + NORM_EPS) * norm_gain + norm_shift


def gelu_tanh(values):
    return jax.nn.gelu(values, approximate=True)


def matmul(former, latter):
    return jnp.dot(former, latter, preferred_element_type=jnp.float32)


def by_rows(former, latter):
    return lax.dot_general(
        former, latter, (((0,), (0,)), ((), ())), preferred_element_type=jnp.float32
    )


def by_columns(former, latter):
    return lax.dot_general(
        former, latter, (((1,), (1,)), ((), ())), preferred_element_type=jnp.float32
    )


def split_heads(head_block):
    token_count = head_block.shape[0]
    local_heads = head_block.shape[2] // HD
    queries = head_block[:, 0].reshape(token_count, local_heads, HD)
    key_rows = head_block[:, 1].reshape(token_count, local_heads, HD)
    value_rows = head_block[:, 2].reshape(token_count, local_heads, HD)
    return (queries, key_rows, value_rows)


def masked_scores(queries, key_rows, mask_row):
    scores = jnp.einsum(
        "qhd,khd->hqk", queries, key_rows, preferred_element_type=jnp.float32
    ) * HD ** (-0.5)
    return jnp.where((mask_row > 0)[None, None, :], scores, NEG_FILL)


def attend_image(packed_item):
    head_block, mask_row = packed_item
    queries, key_rows, value_rows = split_heads(head_block)
    scores = masked_scores(queries, key_rows, mask_row)
    row_max = jnp.max(scores, axis=-1, keepdims=True)
    exponent = jnp.exp(scores - row_max)
    row_total = jnp.sum(exponent, axis=-1, keepdims=True)
    attention = (exponent / row_total).astype(jnp.bfloat16)
    log_totals = (row_max + jnp.log(row_total))[..., 0]
    mixed = jnp.einsum("hqk,khd->qhd", attention, value_rows, preferred_element_type=jnp.float32)
    token_count = head_block.shape[0]
    return (mixed.reshape(token_count, head_block.shape[2]).astype(jnp.bfloat16), log_totals)


def attend_back(packed_item):
    head_block, log_totals, mask_row, grad_mixed = packed_item
    queries, key_rows, value_rows = split_heads(head_block)
    token_count = head_block.shape[0]
    local_heads = head_block.shape[2] // HD
    scores = masked_scores(queries, key_rows, mask_row)
    attention = jnp.exp(scores - log_totals[..., None])
    grad_view = grad_mixed.reshape(token_count, local_heads, HD)
    grad_attention = jnp.einsum(
        "qhd,khd->hqk", grad_view, value_rows, preferred_element_type=jnp.float32
    )
    row_delta = jnp.sum(attention * grad_attention, axis=-1, keepdims=True)
    grad_scores = jnp.where(
        (mask_row > 0)[None, None, :], attention * (grad_attention - row_delta), 0.0
    ).astype(jnp.bfloat16)
    grad_queries = jnp.einsum(
        "hqk,khd->qhd", grad_scores, key_rows, preferred_element_type=jnp.float32
    ) * HD ** (-0.5)
    grad_keys = jnp.einsum(
        "hqk,qhd->khd", grad_scores, queries, preferred_element_type=jnp.float32
    ) * HD ** (-0.5)
    grad_values = jnp.einsum(
        "hqk,qhd->khd",
        attention.astype(jnp.bfloat16),
        grad_view,
        preferred_element_type=jnp.float32,
    )
    stacked = jnp.stack([grad_queries, grad_keys, grad_values], axis=1)
    return stacked.reshape(token_count, 3, head_block.shape[2]).astype(jnp.bfloat16)


def adam_update(master, first_moment, second_moment, gradient, step_rate, bias_one, bias_two):
    first_new = 0.5 * first_moment + 0.5 * gradient
    second_new = 0.5 * second_moment + 0.5 * gradient * gradient
    update = first_new / bias_one / (jnp.sqrt(second_new / bias_two) + ADAM_EPS)
    master_new = master - step_rate * (update + WEIGHT_DECAY * master)
    return (master_new, first_new, second_new)


def on_device(
    images,
    key_mask,
    out_grad,
    step_count,
    in_weights,
    out_weights,
    up_weights,
    down_weights,
    vectors,
    first_in,
    first_out,
    first_up,
    first_down,
    first_vectors,
    second_in,
    second_out,
    second_up,
    second_down,
    second_vectors,
):
    full_in, full_out, full_vec = (
        lax.all_gather(in_weights.astype(jnp.bfloat16), ("seq", "fsdp"), axis=0, tiled=True),
        lax.all_gather(out_weights.astype(jnp.bfloat16), ("seq", "fsdp"), axis=0, tiled=True),
        lax.all_gather(vectors.astype(jnp.bfloat16), ("seq", "fsdp"), axis=0, tiled=True),
    )
    full_up, full_down = (
        lax.all_gather(up_weights.astype(jnp.bfloat16), ("seq", "fsdp"), axis=0, tiled=True),
        lax.all_gather(down_weights.astype(jnp.bfloat16), ("seq", "fsdp"), axis=0, tiled=True),
    )
    image_count, half_tokens, features = images.shape
    row_count = image_count * half_tokens
    vector_copy = full_vec.astype(jnp.float32)
    gain_one = vector_copy[0:features]
    shift_one = vector_copy[features : 2 * features]
    query_bias = vector_copy[2 * features : 3 * features]
    value_bias = vector_copy[3 * features : 4 * features]
    out_bias = vector_copy[4 * features : 5 * features]
    gain_two = vector_copy[5 * features : 6 * features]
    shift_two = vector_copy[6 * features : 7 * features]
    down_bias = vector_copy[7 * features : 8 * features]
    up_bias = vector_copy[8 * features :]
    in_bias = jnp.concatenate([query_bias, jnp.zeros_like(query_bias), value_bias])
    flat_input = images.reshape(row_count, features).astype(jnp.float32)
    normed_one = layer_norm(flat_input, gain_one, shift_one).astype(jnp.bfloat16)
    packed = (matmul(normed_one, full_in) + in_bias).astype(jnp.bfloat16)
    packed = packed.reshape(image_count, half_tokens, 3, features)
    head_packed = lax.all_to_all(packed, "seq", split_axis=3, concat_axis=1, tiled=True)
    mixed_heads, log_totals = lax.map(attend_image, (head_packed, key_mask))
    mixed = lax.all_to_all(mixed_heads, "seq", split_axis=1, concat_axis=2, tiled=True).reshape(
        row_count, features
    )
    middle = flat_input + matmul(mixed, full_out) + out_bias
    normed_two = layer_norm(middle, gain_two, shift_two).astype(jnp.bfloat16)
    grad_result = out_grad.reshape(row_count, features)
    grad_result_wide = grad_result.astype(jnp.float32)
    grad_down_b = jnp.sum(grad_result_wide, axis=0)
    hidden_input = by_columns(normed_two, full_up) + up_bias
    hidden = gelu_tanh(hidden_input).astype(jnp.bfloat16)
    result = middle + matmul(hidden, full_down) + down_bias
    grad_down_w = by_rows(hidden, grad_result)
    grad_hidden = by_columns(grad_result, full_down)
    unused_value, gelu_back = jax.vjp(gelu_tanh, hidden_input)
    grad_hidden_in = gelu_back(grad_hidden)[0].astype(jnp.bfloat16)
    grad_up_b = jnp.sum(grad_hidden_in.astype(jnp.float32), axis=0)
    grad_up_w = by_rows(grad_hidden_in, normed_two)
    grad_normed_two = matmul(grad_hidden_in, full_up)
    unused_two, norm_back_two = jax.vjp(layer_norm, middle, gain_two, shift_two)
    grad_middle_norm, grad_gain_two, grad_shift_two = norm_back_two(grad_normed_two)
    grad_middle = grad_result_wide + grad_middle_norm
    grad_branch = grad_middle.astype(jnp.bfloat16)
    grad_out_b = jnp.sum(grad_branch.astype(jnp.float32), axis=0)
    grad_out_w = by_rows(mixed, grad_branch)
    grad_mixed = (
        by_columns(grad_branch, full_out)
        .astype(jnp.bfloat16)
        .reshape(image_count, half_tokens, features)
    )
    grad_heads = lax.all_to_all(grad_mixed, "seq", split_axis=2, concat_axis=1, tiled=True)
    grad_packed_heads = lax.map(attend_back, (head_packed, log_totals, key_mask, grad_heads))
    grad_packed = lax.all_to_all(
        grad_packed_heads, "seq", split_axis=1, concat_axis=3, tiled=True
    ).reshape(row_count, 3 * features)
    grad_in_w = by_rows(normed_one, grad_packed)
    column_sums = jnp.sum(grad_packed.astype(jnp.float32), axis=0)
    grad_query_b = column_sums[0:features]
    grad_value_b = column_sums[2 * features :]
    grad_normed_one = by_columns(grad_packed, full_in)
    unused_one, norm_back_one = jax.vjp(layer_norm, flat_input, gain_one, shift_one)
    grad_input_norm, grad_gain_one, grad_shift_one = norm_back_one(grad_normed_one)
    input_grad = grad_middle + grad_input_norm
    grad_vec = jnp.concatenate(
        [
            grad_gain_one,
            grad_shift_one,
            grad_query_b,
            grad_value_b,
            grad_out_b,
            grad_gain_two,
            grad_shift_two,
            grad_down_b,
            grad_up_b,
        ]
    )
    share_in, share_out, share_vec = (
        lax.psum_scatter(grad_in_w, ("seq", "fsdp"), scatter_dimension=0, tiled=True),
        lax.psum_scatter(grad_out_w, ("seq", "fsdp"), scatter_dimension=0, tiled=True),
        lax.psum_scatter(grad_vec, ("seq", "fsdp"), scatter_dimension=0, tiled=True),
    )
    share_up, share_down = (
        lax.psum_scatter(grad_up_w, ("seq", "fsdp"), scatter_dimension=0, tiled=True),
        lax.psum_scatter(grad_down_w, ("seq", "fsdp"), scatter_dimension=0, tiled=True),
    )
    share_in, share_out, share_up, share_down, share_vec = (
        lax.psum(share_in.astype(jnp.bfloat16), "dp").astype(jnp.float32),
        lax.psum(share_out.astype(jnp.bfloat16), "dp").astype(jnp.float32),
        lax.psum(share_up.astype(jnp.bfloat16), "dp").astype(jnp.float32),
        lax.psum(share_down.astype(jnp.bfloat16), "dp").astype(jnp.float32),
        lax.psum(share_vec.astype(jnp.bfloat16), "dp").astype(jnp.float32),
    )
    shares = (share_in, share_out, share_up, share_down, share_vec)
    square_part = (
        jnp.sum(share_in * share_in)
        + jnp.sum(share_out * share_out)
        + jnp.sum(share_up * share_up)
        + jnp.sum(share_down * share_down)
        + jnp.sum(share_vec * share_vec)
    )
    square_total = lax.psum(square_part, ("seq", "fsdp"))
    grad_norm = jnp.sqrt(square_total)
    threshold = 0.5 * math.sqrt(4 * D * D + 2 * D * FF + 12 * D)
    clip_factor = jnp.minimum(1.0, threshold / grad_norm)
    decay_power = jnp.power(jnp.float32(0.5), step_count.astype(jnp.float32))
    bias_one = 1.0 - decay_power
    bias_two = 1.0 - decay_power
    rates = ((D // 2) ** (-0.5), (D // 4) ** (-0.5), D ** (-0.5), FF ** (-0.5), 0.2)
    masters = (in_weights, out_weights, up_weights, down_weights, vectors)
    firsts = (first_in, first_out, first_up, first_down, first_vectors)
    seconds = (second_in, second_out, second_up, second_down, second_vectors)
    results = [
        adam_update(
            masters[index],
            firsts[index],
            seconds[index],
            shares[index] * clip_factor,
            rates[index],
            bias_one,
            bias_two,
        )
        for index in range(5)
    ]
    new_masters = [entry[0] for entry in results]
    new_firsts = [entry[1] for entry in results]
    new_seconds = [entry[2] for entry in results]
    copies = [master.astype(jnp.bfloat16) for master in new_masters]
    activations = result.reshape(image_count, half_tokens, features)
    input_grad = input_grad.reshape(image_count, half_tokens, features)
    return (
        grad_norm,
        new_masters[0],
        new_masters[1],
        new_masters[2],
        new_masters[3],
        new_masters[4],
        new_firsts[0],
        new_firsts[1],
        new_firsts[2],
        new_firsts[3],
        new_firsts[4],
        new_seconds[0],
        new_seconds[1],
        new_seconds[2],
        new_seconds[3],
        new_seconds[4],
        copies[0],
        copies[1],
        copies[2],
        copies[3],
        copies[4],
        activations,
        input_grad,
    )


def solution(mesh):
    placed = (
        P(("fsdp", "dp"), "seq", None),
        P(("fsdp", "dp"), None),
        P(("fsdp", "dp"), "seq", None),
        P(),
        P(("seq", "fsdp"), None),
        P(("seq", "fsdp"), None),
        P(("seq", "fsdp"), None),
        P(("seq", "fsdp"), None),
        P(("seq", "fsdp")),
        P(("seq", "fsdp"), None),
        P(("seq", "fsdp"), None),
        P(("seq", "fsdp"), None),
        P(("seq", "fsdp"), None),
        P(("seq", "fsdp")),
        P(("seq", "fsdp"), None),
        P(("seq", "fsdp"), None),
        P(("seq", "fsdp"), None),
        P(("seq", "fsdp"), None),
        P(("seq", "fsdp")),
    )
    return jax.shard_map(
        on_device,
        mesh=mesh,
        in_specs=placed,
        out_specs=(
            P(),
            P(("seq", "fsdp"), None),
            P(("seq", "fsdp"), None),
            P(("seq", "fsdp"), None),
            P(("seq", "fsdp"), None),
            P(("seq", "fsdp")),
            P(("seq", "fsdp"), None),
            P(("seq", "fsdp"), None),
            P(("seq", "fsdp"), None),
            P(("seq", "fsdp"), None),
            P(("seq", "fsdp")),
            P(("seq", "fsdp"), None),
            P(("seq", "fsdp"), None),
            P(("seq", "fsdp"), None),
            P(("seq", "fsdp"), None),
            P(("seq", "fsdp")),
            P(("seq", "fsdp"), None),
            P(("seq", "fsdp"), None),
            P(("seq", "fsdp"), None),
            P(("seq", "fsdp"), None),
            P(("seq", "fsdp")),
            P(("fsdp", "dp"), "seq", None),
            P(("fsdp", "dp"), "seq", None),
        ),
        check_vma=False,
    )
```

profile of v0, /device:TPU:1, one launch (start us, length us, event | category | flops | bytes accessed | tf_op | source)
XLA Modules:
  0.0 1768.6 jit_solution(14183998428511871880)
XLA Ops:
  17.8 23.2 %all-gather = bf16[16,1,768]{2,1,0:T(2,128)(2,1)S(1)} all-gather(bf16[1,1,768]{2,1,0:T(2,128)(2,1)S(1)} %reshape.302), channel_id=1, replica_groups=mesh['seq'=2,'fsdp'=8,'dp'=2] {'seq','fsdp'}, dimensions={0}, use_global_device_ids=true | all-gather | bytes 26112 | tf_op jit(solution)/shard_map/all_gather | solution.py:138
  42.3 39.7 %all-gather.6.cloned.1.call-done = bf16[1024,3072]{1,0:T(8,128)(2,1)} async-done(((bf16[64,3072]{1,0:T(8,128)(2,1)}), bf16[1024,3072]{1,0:T(8,128)(2,1)}) %all-gather.6.cloned.1.call-update) | async-done | bytes 6291472 | tf_op jit(solution)/shard_map/all_gather | solution.py:136
  82.0 11.2 add_convert_fusion
  93.3 16.3 reshape.294
  109.6 17.9 %copy.98 = bf16[3,292,3,1024]{1,2,0,3:T(4,128)(2,1)} copy(bf16[3,292,3,1024]{3,2,1,0:T(4,128)(2,1)} %reshape.294) | data formatting | bytes 10764288 | tf_op jit(solution)/shard_map/reshape | solution.py:160
  127.6 7.5 all-to-all-start
  136.2 308.3 %all-to-all-done = bf16[3,292,3,1024]{1,2,0,3:T(4,128)(2,1)} async-done(((bf16[3,292,3,1024]{1,2,0,3:T(4,128)(2,1)}), bf16[3,292,3,1024]{1,2,0,3:T(4,128)(2,1)}, u32[]{:S(2)}, u32[]{:S(2)}) %all-to-all-start) | async-done | bytes 5382176 | tf_op jit(solution)/shard_map/all_to_all | solution.py:161
  444.6 14.7 copy.135
  459.3 14.5 reshape.307
  473.8 32.3 %while.22 = (s32[]{:T(128)}, bf16[3,584,512]{1,2,0:T(8,128)(2,1)S(1)}, f32[3,8,584]{2,1,0:T(8,128)S(1)}, bf16[3,584,3,512]{1,3,2,0:T(8,128)(2,1)}, s32[3,584]{1,0:T(4,128)S(1)}, /*index=5*/s32[]{:T(128)}) while((s32[]{:T(128)}, bf16[3,584,512]{1,2,0:T(8,128)(2,1)S(1)}, f32[3,8,584]{2,1,0:T(8,128)S(1)}, bf16[3,584,3,512]{1,3,2,0:T(8,128)(2,1)}, ...), condition=%wide.region_5.6_spmd, body=%wide.region_2.5_spmd.sunk | while | flops 731518976 | bytes 43779996 | solution.py:162
  481.1 3.3 fusion.172
  486.5 2.8 fusion.170
  491.9 3.3 fusion.172
  497.3 2.8 fusion.170
  502.7 3.3 fusion.172
  506.2 3.7 copy.102
  509.8 5.4 all-to-all-start.1
  517.6 43.0 %all-to-all-done.1 = bf16[3,584,512]{2,0,1:T(4,128)(2,1)} async-done(((bf16[3,584,512]{2,0,1:T(4,128)(2,1)}), bf16[3,584,512]{2,0,1:T(4,128)(2,1)}, u32[]{:S(2)}, u32[]{:S(2)}) %all-to-all-start.1) | async-done | bytes 1794080 | tf_op jit(solution)/shard_map/all_to_all | solution.py:163
  567.2 5.3 fusion.109
  575.0 15.2 fusion.90
  590.1 22.0 %convert_reduce_fusion = (f32[4096]{0:T(1024)}, bf16[876,4096]{1,0:T(8,128)(2,1)}) fusion(f32[876,4096]{1,0:T(8,128)} %fusion.90, f32[4096]{0:T(1024)S(1)} %slice.83, bf16[876,1024]{1,0:T(8,128)(2,1)S(1)} %reshape.295, bf16[4096,1024]{1,0:T(8,128)(2,1)} %all-gather.8.cloned.1.call-done), kind=kOutput, calls=%fused_computation.60 | convolution fusion | flops 7430942720 | bytes 31744000 | tf_op jit(solution)/shard_map/dot_general | solution.py:40
  612.2 13.6 multiply_reduce_fusion.3
  631.3 3.3 convolution_convert_fusion
  636.2 3.9 copy.105
  640.1 3.9 all-to-all-start.2
  644.1 6.4 fusion.113
  650.5 89.5 %all-to-all-done.2 = bf16[3,292,1024]{1,0,2:T(4,128)(2,1)S(1)} async-done(((bf16[3,292,1024]{1,0,2:T(4,128)(2,1)}), bf16[3,292,1024]{1,0,2:T(4,128)(2,1)S(1)}, u32[]{:S(2)}, u32[]{:S(2)}) %all-to-all-start.2) | async-done | bytes 1794080 | tf_op jit(solution)/shard_map/all_to_all | solution.py:192
  740.1 4.2 copy.136
  744.2 5.8 reshape.305
  750.1 183.9 %while.23 = (s32[]{:T(128)}, bf16[3,584,3,512]{1,3,2,0:T(8,128)(2,1)}, bf16[3,584,3,512]{1,3,2,0:T(8,128)(2,1)}, s32[3,584]{1,0:T(4,128)S(1)}, f32[3,8,584]{2,1,...) while((s32[]{:T(128)}, bf16[3,584,3,512]{1,3,2,0:T(8,128)(2,1)}, ...), condition=%wide.region_12.13_spmd, body=%wide.region_10.12_spmd.sunk | while | flops 1824034688 | bytes 138262480 | solution.py:193
  755.7 2.8 fusion.185
  760.0 6.4 fusion.186
  766.4 21.8 %fusion.188 = bf16[8,64,584]{2,1,0:T(8,128)(2,1)S(1)} fusion(bf16[584,8,64]{0,2,1:T(8,128)(2,1)S(1)} %bitcast.145, f32[8,584,584]{1,2,0:T(8,128)} %fusion.186, f32[8,584,584]{1,2,0:T(8,128)} %copy-done, f32[8,584]{1,0:T(8,128)S(1)} %dynamic-slice_bitcast_fusion.8, pred[584]{0:T(1024)(128)(4,1)S(1)} %compare_reduce_fusion.5), kind=kOutput, calls=%fused_computation.38.clone.1 | convolution fusion | flops 379857536 | bytes 23042888 | tf_op jit(solution)/shard_map/while/body/eval_jaxpr/hqk,khd->qhd/dot_general | solution.py:90
  788.2 21.9 %fusion.187 = bf16[8,64,584]{2,1,0:T(8,128)(2,1)S(1)} fusion(bf16[584,8,64]{0,2,1:T(8,128)(2,1)S(1)} %bitcast.143, f32[8,584,584]{1,2,0:T(8,128)} %fusion.186, f32[8,584,584]{1,2,0:T(8,128)} %copy-done, f32[8,584]{1,0:T(8,128)S(1)} %dynamic-slice_bitcast_fusion.8, pred[584]{0:T(1024)(128)(4,1)S(1)} %compare_reduce_fusion.5), kind=kOutput, calls=%fused_computation.37.clone.1 | convolution fusion | flops 379857536 | bytes 23042888 | tf_op jit(solution)/shard_map/while/body/eval_jaxpr/hqk,qhd->khd/dot_general | solution.py:93
  816.8 2.8 fusion.185
  821.2 6.4 fusion.186
  827.5 21.8 %fusion.188 = bf16[8,64,584]{2,1,0:T(8,128)(2,1)S(1)} fusion(bf16[584,8,64]{0,2,1:T(8,128)(2,1)S(1)} %bitcast.145, f32[8,584,584]{1,2,0:T(8,128)} %fusion.186, f32[8,584,584]{1,2,0:T(8,128)} %copy-done, f32[8,584]{1,0:T(8,128)S(1)} %dynamic-slice_bitcast_fusion.8, pred[584]{0:T(1024)(128)(4,1)S(1)} %compare_reduce_fusion.5), kind=kOutput, calls=%fused_computation.38.clone.1 | convolution fusion | flops 379857536 | bytes 23042888 | tf_op jit(solution)/shard_map/while/body/eval_jaxpr/hqk,khd->qhd/dot_general | solution.py:90
  849.4 21.9 %fusion.187 = bf16[8,64,584]{2,1,0:T(8,128)(2,1)S(1)} fusion(bf16[584,8,64]{0,2,1:T(8,128)(2,1)S(1)} %bitcast.143, f32[8,584,584]{1,2,0:T(8,128)} %fusion.186, f32[8,584,584]{1,2,0:T(8,128)} %copy-done, f32[8,584]{1,0:T(8,128)S(1)} %dynamic-slice_bitcast_fusion.8, pred[584]{0:T(1024)(128)(4,1)S(1)} %compare_reduce_fusion.5), kind=kOutput, calls=%fused_computation.37.clone.1 | convolution fusion | flops 379857536 | bytes 23042888 | tf_op jit(solution)/shard_map/while/body/eval_jaxpr/hqk,qhd->khd/dot_general | solution.py:93
  877.9 2.8 fusion.185
  882.3 6.4 fusion.186
  888.7 21.8 %fusion.188 = bf16[8,64,584]{2,1,0:T(8,128)(2,1)S(1)} fusion(bf16[584,8,64]{0,2,1:T(8,128)(2,1)S(1)} %bitcast.145, f32[8,584,584]{1,2,0:T(8,128)} %fusion.186, f32[8,584,584]{1,2,0:T(8,128)} %copy-done, f32[8,584]{1,0:T(8,128)S(1)} %dynamic-slice_bitcast_fusion.8, pred[584]{0:T(1024)(128)(4,1)S(1)} %compare_reduce_fusion.5), kind=kOutput, calls=%fused_computation.38.clone.1 | convolution fusion | flops 379857536 | bytes 23042888 | tf_op jit(solution)/shard_map/while/body/eval_jaxpr/hqk,khd->qhd/dot_general | solution.py:90
  910.5 21.9 %fusion.187 = bf16[8,64,584]{2,1,0:T(8,128)(2,1)S(1)} fusion(bf16[584,8,64]{0,2,1:T(8,128)(2,1)S(1)} %bitcast.143, f32[8,584,584]{1,2,0:T(8,128)} %fusion.186, f32[8,584,584]{1,2,0:T(8,128)} %copy-done, f32[8,584]{1,0:T(8,128)S(1)} %dynamic-slice_bitcast_fusion.8, pred[584]{0:T(1024)(128)(4,1)S(1)} %compare_reduce_fusion.5), kind=kOutput, calls=%fused_computation.37.clone.1 | convolution fusion | flops 379857536 | bytes 23042888 | tf_op jit(solution)/shard_map/while/body/eval_jaxpr/hqk,qhd->khd/dot_general | solution.py:93
  934.0 13.4 copy.110
  947.4 6.7 all-to-all-start.3
  957.8 143.0 %all-to-all-done.3 = bf16[3,584,3,512]{3,2,0,1:T(4,128)(2,1)} async-done(((bf16[3,584,3,512]{3,2,0,1:T(4,128)(2,1)}), bf16[3,584,3,512]{3,2,0,1:T(4,128)(2,1)}, u32[]{:S(2)}, u32[]{:S(2)}) %all-to-all-start.3) | async-done | bytes 5382176 | tf_op jit(solution)/shard_map/all_to_all | solution.py:194
  1100.8 4.6 convert_reduce_fusion.1
  1105.4 9.6 copy.112
  1115.0 12.9 reshape.298
  1128.0 12.1 fusion.112
  1141.5 18.8 %fusion.91 = f32[4096,1024]{1,0:T(8,128)} fusion(bf16[876,1024]{1,0:T(8,128)(2,1)S(1)} %copy-done.6, f32[876,4096]{1,0:T(8,128)} %fusion.90, f32[4096]{0:T(1024)S(1)} %copy-done.45), kind=kOutput, calls=%fused_computation.152 | convolution fusion | flops 7384301568 | bytes 32940032 | tf_op jit(solution)/shard_map/dot_general | solution.py:34
  1161.1 17.9 %fusion.89 = f32[4096,1024]{1,0:T(8,128)} fusion(bf16[876,4096]{1,0:T(8,128)(2,1)} %get-tuple-element.185, f32[876,1024]{1,0:T(8,128)} %copy-done.7, f32[1024]{0:T(1024)S(1)} %copy-done.51, f32[1024]{0:T(1024)S(1)} %copy-done.35, f32[876]{0:T(1024)S(1)} %copy-done.41, f32[876]{0:T(1024)S(1)} %copy-done.26), kind=kOutput, calls=%fused_computation.150 | convolution fusion | flops 7352905728 | bytes 27556704 | tf_op jit(solution)/shard_map/dot_general | solution.py:34
  1182.8 17.0 add_add_fusion.3
  1199.9 3.8 reshape.299
  1203.7 12.4 multiply_reduce_fusion.2
  1216.2 67.7 %all-reduce = bf16[12288]{0:T(1024)(128)(2,1)S(1)} all-reduce(f32[12288]{0:T(1024)S(1)} %constant_dynamic-update-slice_fusion.1), channel_id=6, replica_groups=mesh['seq'=2,'fsdp'=8,'dp'=2] {'seq','fsdp'}, use_global_device_ids=true, to_apply=%region_33.34.clone | all-reduce | flops 12288 | bytes 73728
  1284.0 4.1 psum.46
  1291.6 169.1 %reduce-scatter.11.cloned.1.call-done = f32[256,1024]{1,0:T(8,128)} async-done(((f32[4096,1024]{1,0:T(8,128)}), f32[256,1024]{1,0:T(8,128)}) %reduce-scatter.11.cloned.1.call-update) | async-done | bytes 1048592 | tf_op jit(solution)/shard_map/reduce_scatter | solution.py:225
  1462.9 183.6 %reduce-scatter.9.cloned.1.call-done = f32[256,1024]{1,0:T(8,128)} async-done(((f32[4096,1024]{1,0:T(8,128)}), f32[256,1024]{1,0:T(8,128)}) %reduce-scatter.9.cloned.1.call-update) | async-done | bytes 1048592 | tf_op jit(solution)/shard_map/reduce_scatter | solution.py:224
  1649.2 4.3 fusion.92
  1656.1 48.4 %all-reduce.4.cloned.1.call-done = (bf16[64,3072]{1,0:T(8,128)(2,1)}, bf16[64,1024]{1,0:T(8,128)(2,1)}, bf16[256,1024]{1,0:T(8,128)(2,1)}, bf16[256,1024]{1,0:T(8,128)(2,1)}) async-done(((bf16[64,3072]{1,0:T(8,128)(2,1)}, bf16[64,1024]{1,0:T(8,128)(2,1)}, bf16[256,1024]{1,0:T(8,128)(2,1)}, bf16[256,1024]{1,0:T(8,128)(2,1)}), (bf16[64,3072]{1,0:T(8,128)(2,1)}, bf16[64,1024]{1,0:T(8,128)(2,1)}, ...) | async-done | bytes 1572880 | tf_op jit(solution)/shard_map/psum | solution.py:228
  1715.0 3.7 reshape.300
  1718.8 30.4 %psum.47 = f32[]{:T(128)} all-reduce(f32[]{:T(128)S(6)} %add.246), channel_id=1, replica_groups=mesh['seq'=2,'fsdp'=8,'dp'=2] {'seq','fsdp'}, use_global_device_ids=true, to_apply=%region_36.37 | all-reduce | flops 1 | bytes 8 | tf_op jit(solution)/shard_map/psum | solution.py:242
  1753.2 3.5 fusion.101
  1756.7 3.7 fusion.95
  (251 shorter events, 102.2 us)
Async XLA Ops:
  7.2 6.7 copy-start.3
  7.2 74.8 %all-gather.6.cloned.1.call-start = ((), (), s32[]{:S(2)}) async-start(), calls=%async_computation.8 | async-start | bytes 6684672 | tf_op jit(solution)/shard_map/all_gather | solution.py:136
  9.3 557.9 %all-gather.10.cloned.1.call-start = ((), (), s32[]{:S(2)}) async-start(), calls=%async_computation.10 | async-start | bytes 2228224 | tf_op jit(solution)/shard_map/all_gather | solution.py:137
  11.0 563.9 %all-gather.12.cloned.1.call-start = ((), (), s32[]{:S(2)}) async-start(), calls=%async_computation.11 | async-start | bytes 8912896 | tf_op jit(solution)/shard_map/all_gather | solution.py:141
  16.4 76.9 %copy-start.22 = (f32[3,292]{1,0:T(4,128)}, f32[3,292]{1,0:T(4,128)S(1)}, u32[]{:S(2)}) copy-start(f32[3,292]{1,0:T(4,128)S(1)} %broadcast_multiply_fusion) | copy-start | bytes 10516
  16.4 76.8 %copy-start.36 = (f32[876]{0:T(1024)}, f32[876]{0:T(1024)S(1)}, u32[]{:S(2)}) copy-start(f32[876]{0:T(1024)S(1)} %div.108) | copy-start | bytes 10516
  17.8 23.3 %copy-start.31 = (f32[876]{0:T(1024)}, f32[876]{0:T(1024)S(1)}, u32[]{:S(2)}) copy-start(f32[876]{0:T(1024)S(1)} %add.227) | copy-start | bytes 10516
  17.8 75.5 %copy-start.38 = (f32[876]{0:T(1024)}, f32[876]{0:T(1024)S(1)}, u32[]{:S(2)}) copy-start(f32[876]{0:T(1024)S(1)} %rsqrt.26) | copy-start | bytes 10516
  42.3 51.0 %copy-start.27 = (f32[1024]{0:T(1024)}, f32[1024]{0:T(1024)S(1)}, u32[]{:S(2)}) copy-start(f32[1024]{0:T(1024)S(1)} %get-tuple-element.207) | copy-start | bytes 12292
  42.3 51.0 %copy-start.47 = (f32[1024]{0:T(1024)}, f32[1024]{0:T(1024)S(1)}, u32[]{:S(2)}) copy-start(f32[1024]{0:T(1024)S(1)} %get-tuple-element.206) | copy-start | bytes 12292
  127.6 7.7 copy-start.10
  127.6 317.0 %all-to-all-start = ((bf16[3,292,3,1024]{1,2,0,3:T(4,128)(2,1)}), bf16[3,292,3,1024]{1,2,0,3:T(4,128)(2,1)}, u32[]{:S(2)}, u32[]{:S(2)}) async-start(bf16[3,292,3,1024]{1,2,0,3:T(4,128)(2,1)} %copy.98), calls=%async_computation | async-start | bytes 18874368 | tf_op jit(solution)/shard_map/all_to_all | solution.py:161
  135.0 455.1 %all-gather.8.cloned.1.call-start = ((), (), s32[]{:S(2)}) async-start(), calls=%async_computation.9 | async-start | bytes 8912896 | tf_op jit(solution)/shard_map/all_gather | solution.py:142
  459.3 14.5 copy-start.24
  509.8 50.8 %all-to-all-start.1 = ((bf16[3,584,512]{2,0,1:T(4,128)(2,1)}), bf16[3,584,512]{2,0,1:T(4,128)(2,1)}, u32[]{:S(2)}, u32[]{:S(2)}) async-start(bf16[3,584,512]{2,0,1:T(4,128)(2,1)} %copy.102), calls=%async_computation.1 | async-start | bytes 4784128 | tf_op jit(solution)/shard_map/all_to_all | solution.py:163
  516.0 74.1 %copy-start.44 = (f32[4096]{0:T(1024)}, f32[4096]{0:T(1024)S(1)}, u32[]{:S(2)}) copy-start(f32[4096]{0:T(1024)S(1)} %slice.83) | copy-start | bytes 49156
  517.6 109.4 %copy-start.5 = (bf16[876,1024]{1,0:T(8,128)(2,1)}, bf16[876,1024]{1,0:T(8,128)(2,1)S(1)}, u32[]{:S(2)}) copy-start(bf16[876,1024]{1,0:T(8,128)(2,1)S(1)} %reshape.295) | copy-start | bytes 5382148
  562.8 4.5 copy-start.52
  567.2 7.7 copy-start.34
  567.2 7.7 copy-start.50
  572.6 53.2 %copy-start.25 = (f32[876]{0:T(1024)}, f32[876]{0:T(1024)S(1)}, u32[]{:S(2)}) copy-start(f32[876]{0:T(1024)S(1)} %broadcast_multiply_fusion.1) | copy-start | bytes 10516
  574.9 50.9 %copy-start.40 = (f32[876]{0:T(1024)}, f32[876]{0:T(1024)S(1)}, u32[]{:S(2)}) copy-start(f32[876]{0:T(1024)S(1)} %fusion.87) | copy-start | bytes 10516
  590.1 22.0 %copy-start.8 = (f32[876,1024]{1,0:T(8,128)S(1)}, f32[876,1024]{1,0:T(8,128)}, u32[]{:S(2)}) copy-start(f32[876,1024]{1,0:T(8,128)} %copy-done.7) | copy-start | bytes 10764292
  627.0 1.8 copy-start.1
  627.0 4.3 copy-start.57
  627.0 3.1 copy-start.29
  640.1 100.0 %all-to-all-start.2 = ((bf16[3,292,1024]{1,0,2:T(4,128)(2,1)}), bf16[3,292,1024]{1,0,2:T(4,128)(2,1)S(1)}, u32[]{:S(2)}, u32[]{:S(2)}) async-start(bf16[3,292,1024]{1,0,2:T(4,128)(2,1)} %copy.105), calls=%async_computation.2 | async-start | bytes 6291456 | tf_op jit(solution)/shard_map/all_to_all | solution.py:192
  644.0 644.0 %reduce-scatter.7.cloned.1.call-start = ((), (), s32[]{:S(2)}) async-start(), calls=%async_computation.13 | async-start | bytes 4456448 | tf_op jit(solution)/shard_map/reduce_scatter | solution.py:220
  755.6 4.4 copy-start
  816.8 4.4 copy-start
  877.9 4.4 copy-start
  947.4 6.8 copy-start.4
  947.4 6.8 copy-start.23
  947.4 6.8 copy-start.28
  947.4 6.8 copy-start.33
  947.4 6.8 copy-start.48
  947.4 153.4 %all-to-all-start.3 = ((bf16[3,584,3,512]{3,2,0,1:T(4,128)(2,1)}), bf16[3,584,3,512]{3,2,0,1:T(4,128)(2,1)}, u32[]{:S(2)}, u32[]{:S(2)}) async-start(bf16[3,584,3,512]{3,2,0,1:T(4,128)(2,1)} %copy.110), calls=%async_computation.3 | async-start | bytes 14352384 | tf_op jit(solution)/shard_map/all_to_all | solution.py:194
  954.1 335.6 %reduce-scatter.5.cloned.1.call-start = ((), (), s32[]{:S(2)}) async-start(), calls=%async_computation.12 | async-start | bytes 13369344 | tf_op jit(solution)/shard_map/reduce_scatter | solution.py:219
  1140.1 320.7 %reduce-scatter.11.cloned.1.call-start = ((), (), s32[]{:S(2)}) async-start(), calls=%async_computation.15 | async-start | bytes 17825792 | tf_op jit(solution)/shard_map/reduce_scatter | solution.py:225
  1160.4 486.0 %reduce-scatter.9.cloned.1.call-start = ((), (), s32[]{:S(2)}) async-start(), calls=%async_computation.14 | async-start | bytes 17825792 | tf_op jit(solution)/shard_map/reduce_scatter | solution.py:224
  1179.0 3.8 copy-start.49
  1179.0 525.5 %all-reduce.4.cloned.1.call-start = ((), (), s32[]{:S(2)}) async-start(), calls=%async_computation.16 | async-start | bytes 3145728 | tf_op jit(solution)/shard_map/psum | solution.py:228
  1199.8 3.8 copy-start.37
  1199.8 3.8 copy-start.39
  1203.6 12.5 copy-start.42
  1203.6 12.5 copy-start.54
  1203.7 12.5 copy-start.53
  1203.7 12.6 copy-start.43
  1216.1 433.1 %copy-start.32 = (f32[876]{0:T(1024)S(1)}, f32[876]{0:T(1024)}, u32[]{:S(2)}) copy-start(f32[876]{0:T(1024)} %copy-done.31) | copy-start | bytes 10516
  1649.2 4.3 copy-start.2
  1649.2 4.3 copy-start.30
  1656.1 93.9 %copy-start.46 = (f32[768]{0:T(1024)S(1)}, f32[768]{0:T(1024)}, u32[]{:S(2)}) copy-start(f32[768]{0:T(1024)} %param.31) | copy-start | bytes 9220
  1656.1 93.9 %copy-start.55 = (f32[768]{0:T(1024)S(1)}, f32[768]{0:T(1024)}, u32[]{:S(2)}) copy-start(f32[768]{0:T(1024)} %param.41) | copy-start | bytes 9220
  1656.1 93.9 %copy-start.56 = (f32[768]{0:T(1024)S(1)}, f32[768]{0:T(1024)}, u32[]{:S(2)}) copy-start(f32[768]{0:T(1024)} %param.36) | copy-start | bytes 9220
  1656.1 97.1 %copy-start.12 = (f32[64,3072]{1,0:T(8,128)S(1)}, f32[64,3072]{1,0:T(8,128)}, u32[]{:S(2)}) copy-start(f32[64,3072]{1,0:T(8,128)} %param.27) | copy-start | bytes 2359300
  1704.5 46.1 %copy-start.20 = (bf16[64,1024]{1,0:T(8,128)(2,1)S(1)}, bf16[64,1024]{1,0:T(8,128)(2,1)}, u32[]{:S(2)}) copy-start(bf16[64,1024]{1,0:T(8,128)(2,1)} %get-tuple-element.159) | copy-start | bytes 393220
  1718.8 37.9 %copy-start.9 = (f32[256,1024]{1,0:T(8,128)S(1)}, f32[256,1024]{1,0:T(8,128)}, u32[]{:S(2)}) copy-start(f32[256,1024]{1,0:T(8,128)} %param.29) | copy-start | bytes 3145732
  1718.8 37.9 %copy-start.11 = (f32[256,1024]{1,0:T(8,128)S(1)}, f32[256,1024]{1,0:T(8,128)}, u32[]{:S(2)}) copy-start(f32[256,1024]{1,0:T(8,128)} %param.30) | copy-start | bytes 3145732
  1718.8 37.9 %copy-start.13 = (bf16[256,1024]{1,0:T(8,128)(2,1)S(1)}, bf16[256,1024]{1,0:T(8,128)(2,1)}, u32[]{:S(2)}) copy-start(bf16[256,1024]{1,0:T(8,128)(2,1)} %get-tuple-element.160) | copy-start | bytes 1572868
  1750.0 6.7 copy-start.14
  1750.0 6.7 copy-start.16
  1750.0 6.7 copy-start.17
  1750.0 6.7 copy-start.18
  1750.0 6.7 copy-start.19
  (10 other events, 10.3 us)
Sparse Core Ops, SparseCore 0:
  10.9 71.0 all-gather.5
  84.9 40.6 all-gather.9
  128.6 207.7 all-gather.11
  339.1 107.4 all-gather.7
  650.7 104.8 reduce-scatter.6
  1140.2 138.1 reduce-scatter.4
  1280.8 179.9 reduce-scatter.10
  1463.2 183.2 reduce-scatter.8
  1649.8 54.7 all-reduce.3
where the time goes:
time: 1780 us; the launch traced here: 1770 us
  waiting for transfers between devices  1020 us (57%)
  matrix products  339 us (19%)
  local copies, waits for them, and re-layouts  168 us (9%)
  blocking collectives  125 us (7%)
  other arithmetic  65.3 us (4%)
  starting transfers between devices  24.1 us (1%)
  between operations  21.6 us (1%)
    all_to_all x1, waiting for transfers between devices, on_device(): lax.all_to_all(packed, 'seq', split_axis=3, concat_axis=1, tiled=True)  308 us
    reduce_scatter x1, waiting for transfers between devices, on_device(): lax.psum_scatter(grad_up_w, ('seq', 'fsdp'), scatter_dimension=0, tiled=T...  184 us
    reduce_scatter x1, waiting for transfers between devices, on_device(): lax.psum_scatter(grad_down_w, ('seq', 'fsdp'), scatter_dimension=0, tiled...  169 us
    all_to_all x1, waiting for transfers between devices, on_device(): lax.all_to_all(grad_packed_heads, 'seq', split_axis=1, concat_axis=3, til...  143 us
    all_to_all x1, waiting for transfers between devices, on_device(): lax.all_to_all(grad_mixed, 'seq', split_axis=2, concat_axis=1, tiled=True)  89.5 us
    unnamed x1, blocking collectives  67.7 us
    dot_general x3, matrix products, attend_back(): jnp.einsum('hqk,qhd->khd', grad_scores, queries, preferred_element_type=j...  65.8 us
    dot_general x3, matrix products, attend_back(): jnp.einsum('hqk,khd->qhd', grad_scores, key_rows, preferred_element_type=...  65.4 us
  transfers between devices with their start and end apart: 13, of which 8 were waited for; matrix products, arithmetic and copies ran while one was open for 28% of the time, Pallas kernels for 0%

commit v1 on v0

v1 whole, which is shorter than its diff:
```python
import functools
import math

import jax
import jax.numpy as jnp
import numpy as np
from jax import lax
from jax.experimental import pallas as pl
from jax.experimental.pallas import tpu as pltpu
from jax.sharding import Mesh
from jax.sharding import PartitionSpec as P

D = 1024
FF = 4096
PAD_ROWS = 16

NEG_FILL = -1000000000.0
ADAM_EPS = 1e-08
WEIGHT_DECAY = 0.05
AXES = ("seq", "y", "x", "core", "dp")
SHARD = ("seq", "y", "x", "core")

BF=jnp.bfloat16; F32=jnp.float32
def dot(a, b, dims=(((1,), (0,)), ((), ()))):
    return lax.dot_general(a, b, dims, preferred_element_type=F32)
NT=(((1,),(1,)),((),()))
TN=(((0,),(0,)),((),()))
ANY=pl.BlockSpec(memory_space=pl.ANY)
VM=pl.BlockSpec(memory_space=pltpu.VMEM)
SM=pl.BlockSpec(memory_space=pltpu.SMEM)

def gelu_both(u):
    c0=math.sqrt(2/math.pi)
    sq=u*u
    t=jnp.tanh(u*(c0+(c0*0.044715)*sq))
    half=0.5+0.5*t
    value=u*half
    slope=half+(0.5*u)*(1.0-t*t)*(c0+(3*c0*0.044715)*sq)
    return value,slope

def mlp_kernel(keys,*refs,gtile):
    nk=len(keys)
    at_ref,h2_ref,go_ref,gt_ref,bu_ref=refs[:5]
    pa,pb=refs[5:5+nk],refs[5+nk:5+2*nk]
    o=5+2*nk
    ga,gb=refs[o:o+nk],refs[o+nk:o+2*nk]
    yown_ref,yoth_ref,dh_ref,gbu_ref=refs[o+2*nk:o+2*nk+4]
    w,dd,a_all,du_all,y_acc,dh_acc,g_out,wsem,gsem=refs[o+2*nk+4:]
    images,half,feat=go_ref.shape
    hid=pa[0].shape[2]
    width=4*hid
    padded=h2_ref.shape[0]//(2*images)
    blocks=2*images

    def load(i,slot,go):
        for ki in range(nk):
            @pl.when(i==ki)
            def _():
                for kz in range(2):
                    for ud in range(2):
                        for ab,src in enumerate((pa[ki],pb[ki])):
                            cp=pltpu.make_async_copy(src.at[kz,ud],w.at[slot,ud,pl.ds((kz*2+ab)*hid,hid)],wsem.at[slot,kz*4+ud*2+ab])
                            cp.start() if go else cp.wait()
    def save(i,go):
        for ki in range(nk):
            @pl.when(i==ki)
            def _():
                for kz in range(2):
                    for ud in range(2):
                        for ab,dst in enumerate((ga[ki],gb[ki])):
                            cp=pltpu.make_async_copy(g_out.at[ud,pl.ds((kz*2+ab)*hid,hid)],dst.at[kz,ud],gsem.at[kz*4+ud*2+ab])
                            cp.start() if go else cp.wait()
    load(0,0,True)
    gbu_ref[...]=jnp.zeros_like(gbu_ref)
    for i in range(images):
        for s,src in enumerate((go_ref,gt_ref)):
            r=(2*i+s)*padded
            tail=padded-16
            dd[r+tail:r+padded,:]=jnp.zeros((16,feat),BF)
            dd[r:r+half,:]=src[i]
    def step(i,_):
        slot=lax.rem(i,2)
        load(i,slot,False)
        @pl.when(i+1<nk)
        def _(): load(i+1,1-slot,True)
        rows=[]
        for kz in range(2):
            for ab in range(2):
                row=jnp.int32(0)
                for ki,(ky,kx) in enumerate(keys):
                    z=lax.rem(at_ref[0]+kz,2); y=lax.rem(at_ref[1]+ky,at_ref[4]); x=lax.rem(at_ref[2]+kx,at_ref[5])
                    here=(((z*at_ref[4]+y)*at_ref[5]+x)*2+at_ref[3])*2+ab
                    row=jnp.where(i==ki,here,row)
                rows.append(row)
        bias=jnp.concatenate([bu_ref[pl.ds(r,1),:] for r in rows],axis=1)
        wu=w.at[slot,0]; wd=w.at[slot,1]
        def tokens(b,sums):
            r=pl.ds(pl.multiple_of(b*padded,16),padded)
            u=dot(h2_ref[r,:],wu[...],NT)+bias
            value,slope=gelu_both(u)
            a=value.astype(BF)
            a_all[r,:]=a
            dg=dot(dd[r,:],wd[...],NT)
            du=(dg*slope).astype(BF)
            du_all[r,:]=du
            ynew=dot(a,wd[...]); dnew=dot(du,wu[...])
            @pl.when(i==0)
            def _():
                y_acc[r,:]=ynew; dh_acc[r,:]=dnew
            @pl.when(i>0)
            def _():
                y_acc[r,:]+=ynew; dh_acc[r,:]+=dnew
            return sums+jnp.sum(du.astype(F32),axis=0,keepdims=True)
        sums=lax.fori_loop(0,blocks,tokens,jnp.zeros((1,width),F32))
        for q,row in enumerate(rows):
            gbu_ref[pl.ds(row,1),:]=sums[:,q*hid:(q+1)*hid]
        @pl.when(i>0)
        def _(): save(i-1,False)
        for t in range(0,width,gtile):
            g_out[1,t:t+gtile,:]=dot(a_all[:,t:t+gtile],dd[...],TN).astype(BF)
            g_out[0,t:t+gtile,:]=dot(du_all[:,t:t+gtile],h2_ref[...],TN).astype(BF)
        save(i,True)
        return 0
    lax.fori_loop(0,nk,step,0)
    for i in range(images):
        r=2*i*padded
        yown_ref[i]=y_acc[r:r+padded,:]
        yoth_ref[i]=y_acc[r+padded:r+2*padded,:].astype(BF)
    dh_ref[...]=dh_acc[...].astype(BF)
    save(nk-1,False)

def mlp(at,h2,g_own,g_oth,bu_rows,fa,fb,gtile=256):
    keys=sorted(fa); nk=len(keys)
    images,half,feat=g_own.shape
    tokens=h2.shape[0]; padded=tokens//(2*images)
    _,_,hid,_=fa[keys[0]].shape
    width=4*hid
    piece=jax.ShapeDtypeStruct(fa[keys[0]].shape,BF)
    out=pl.pallas_call(functools.partial(mlp_kernel,keys,gtile=min(gtile,width)),
        in_specs=[SM]+[VM]*4+[ANY]*(2*nk),
        out_specs=[ANY]*(2*nk)+[VM]*4,
        out_shape=[piece]*(2*nk)+[jax.ShapeDtypeStruct((images,padded,feat),F32),jax.ShapeDtypeStruct((images,padded,feat),BF),
            jax.ShapeDtypeStruct((tokens,feat),BF),jax.ShapeDtypeStruct(bu_rows.shape,F32)],
        scratch_shapes=[pltpu.VMEM((2,2,width,feat),BF),pltpu.VMEM((tokens,feat),BF),pltpu.VMEM((tokens,width),BF),pltpu.VMEM((tokens,width),BF),
            pltpu.VMEM((tokens,feat),F32),pltpu.VMEM((tokens,feat),F32),pltpu.VMEM((2,width,feat),BF),
            pltpu.SemaphoreType.DMA((2,8)),pltpu.SemaphoreType.DMA((8,))],
        name="feed_forward",
        compiler_params=pltpu.CompilerParams(vmem_limit_bytes=60<<20),
        cost_estimate=pl.CostEstimate(flops=nk*6*2*tokens*feat*width,bytes_accessed=40<<20,transcendentals=nk*tokens*width),
    )(at,h2,g_own,g_oth,bu_rows,*[fa[k] for k in keys],*[fb[k] for k in keys])
    return dict(zip(keys,out[:nk])),dict(zip(keys,out[nk:2*nk])),out[2*nk],out[2*nk+1],out[2*nk+2],out[2*nk+3]

HD=64; HALF_D=512

def head_operands(q_ref,k_ref,kb_ref,scale):
    q=q_ref[0].astype(F32)*scale; k=k_ref[0].astype(F32); kb=kb_ref[0].astype(F32)
    lane=lax.broadcasted_iota(jnp.int32,q.shape,1)
    low=lane<HD
    one=jnp.where((lane==0)|(lane==HD),1.0,0.0)
    qs=[jnp.where(low,q,one).astype(BF),jnp.where(low,one,q).astype(BF)]
    ks=[jnp.where(low,k,kb).astype(BF),jnp.where(low,kb,k).astype(BF)]
    return q,k,low,qs,ks

def attend_kernel(q_ref,k_ref,v_ref,kb_ref,o_ref,lse_ref):
    q,k,low,qs,ks=head_operands(q_ref,k_ref,kb_ref,HD**-0.5)
    vt=v_ref[0].astype(F32).T.astype(BF)
    outs=[]
    for j in range(2):
        s=dot(ks[j],qs[j],NT)
        m=jnp.max(s,axis=0,keepdims=True)
        e=jnp.exp(s-m)
        l=jnp.sum(e,axis=0,keepdims=True)
        o=dot(vt[j*HD:(j+1)*HD],e.astype(BF))
        outs.append(o*(1.0/l))
        lse_ref[0,0,j:j+1,:]=m+jnp.log(l)
    o_ref[0]=jnp.concatenate(outs,axis=0).T.astype(BF)

def attend(qkv,kbias):
    n,rows,w=qkv.shape; pairs=w//3//128
    blk=lambda off: pl.BlockSpec((1,rows,128),lambda i,p: (i,0,off+p))
    return pl.pallas_call(attend_kernel,grid=(n,pairs),
        in_specs=[blk(0),blk(pairs),blk(2*pairs),pl.BlockSpec((1,rows,128),lambda i,p:(i,0,0))],
        out_specs=[blk(0),pl.BlockSpec((1,1,8,rows),lambda i,p:(i,p,0,0))],
        out_shape=[jax.ShapeDtypeStruct((n,rows,w//3),BF),jax.ShapeDtypeStruct((n,pairs,8,rows),F32)],
        name="attend",
        compiler_params=pltpu.CompilerParams(vmem_limit_bytes=50<<20),
        cost_estimate=pl.CostEstimate(flops=n*pairs*8*rows*rows*128,bytes_accessed=n*rows*w*3,transcendentals=n*pairs*2*rows*rows),
    )(qkv,qkv,qkv,kbias)

def attend_back_kernel(q_ref,k_ref,v_ref,kb_ref,o_ref,g_ref,lse_ref,out_ref,sum_ref,*,pairs,chunk):
    p=pl.program_id(1)
    @pl.when((pl.program_id(0)==0)&(p==0))
    def _(): sum_ref[...]=jnp.zeros_like(sum_ref)
    scale=HD**-0.5
    q,k,low,qs,ks=head_operands(q_ref,k_ref,kb_ref,scale)
    qb=q.astype(BF)
    kt=k.T.astype(BF)
    g=g_ref[0]; gf=g.astype(F32)
    prod=(gf*o_ref[0].astype(F32)).T
    v=v_ref[0]
    rows=q.shape[0]
    dqs=[];dks=[];dvs=[]
    for j in range(2):
        gj=(jnp.where(low,gf,0.0) if j==0 else jnp.where(low,0.0,gf)).astype(BF)
        delta=jnp.sum(prod[j*HD:(j+1)*HD],axis=0,keepdims=True)
        lse=lse_ref[0,0,j:j+1,:]
        dq=None; dk=[]; dv=[]
        for r in range(0,rows,chunk):
            s=dot(ks[j][r:r+chunk],qs[j],NT)
            pr=jnp.exp(s-lse)
            dp=dot(v[r:r+chunk],gj,NT)
            ds=(pr*(dp-delta)).astype(BF)
            dv.append(dot(pr.astype(BF),g))
            dk.append(dot(ds,qb))
            t=dot(kt[j*HD:(j+1)*HD,r:r+chunk],ds) if chunk==rows else dot(k[r:r+chunk].astype(BF),ds,TN)[j*HD:(j+1)*HD]
            dq=t if dq is None else dq+t
        dqs.append(dq)
        dks.append(jnp.concatenate(dk,axis=0) if len(dk)>1 else dk[0]); dvs.append(jnp.concatenate(dv,axis=0) if len(dv)>1 else dv[0])
    parts=((jnp.concatenate(dqs,axis=0)*scale).T.astype(BF),jnp.where(low,dks[0],dks[1]).astype(BF),jnp.where(low,dvs[0],dvs[1]).astype(BF))
    for t,part in enumerate(parts):
        at=pl.ds(pl.multiple_of((t*pairs+p)*128,128),128)
        out_ref[0,:,at]=part
        sum_ref[0:1,at]+=jnp.sum(part.astype(F32),axis=0,keepdims=True)

def attend_back(qkv,kbias,mixed,grad,lse,chunk=None):
    n,rows,w=qkv.shape; pairs=w//3//128
    chunk=chunk or rows
    blk=lambda off: pl.BlockSpec((1,rows,128),lambda i,p: (i,0,off+p))
    return pl.pallas_call(functools.partial(attend_back_kernel,pairs=pairs,chunk=chunk),grid=(n,pairs),
        in_specs=[blk(0),blk(pairs),blk(2*pairs),pl.BlockSpec((1,rows,128),lambda i,p:(i,0,0)),blk(0),blk(0),pl.BlockSpec((1,1,8,rows),lambda i,p:(i,p,0,0))],
        out_specs=[pl.BlockSpec((1,rows,w),lambda i,p:(i,0,0)),pl.BlockSpec((8,w),lambda i,p:(0,0))],
        out_shape=[jax.ShapeDtypeStruct((n,rows,w),BF),jax.ShapeDtypeStruct((8,w),F32)],
        name="attend_back",
        compiler_params=pltpu.CompilerParams(vmem_limit_bytes=50<<20),
        cost_estimate=pl.CostEstimate(flops=n*pairs*20*rows*rows*128,bytes_accessed=n*rows*w*5,transcendentals=n*pairs*2*rows*rows),
    )(qkv,qkv,qkv,kbias,mixed,grad,lse)

NORM_EPS=1e-6
def norm_parts(values):
    center = values - jnp.mean(values, axis=-1, keepdims=True)
    inverse = lax.rsqrt(jnp.mean(center * center, axis=-1, keepdims=True) + NORM_EPS)
    return center * inverse, inverse

def norm_back(values, gain, grad):
    normed, inverse = norm_parts(values)
    scaled = grad * gain
    mean_one = jnp.mean(scaled, axis=-1, keepdims=True)
    mean_two = jnp.mean(scaled * normed, axis=-1, keepdims=True)
    return (scaled - mean_one - normed * mean_two) * inverse, grad * normed

def wide_rows(buf,block):
    n=block.shape[0]; total=buf.shape[0]
    buf[total-16:,:]=jnp.zeros((16,buf.shape[1]),F32)
    buf[0:n,:]=block.astype(F32)
    return buf[...]

def place(at_ref,keys,ka,size,pieces,buf,sem,gather):
    def both(go):
        n=0
        for ki,(ky,kx) in enumerate(keys):
            y=lax.rem(at_ref[1]+ky,at_ref[4]); x=lax.rem(at_ref[2]+kx,at_ref[5])
            for ab in range(2):
                for kz in range(ka):
                    z=lax.rem(at_ref[0]+kz,2) if ka==2 else 0
                    core=at_ref[3] if ab==0 else 1-at_ref[3]
                    if ka==1: core=at_ref[0] if ab==0 else 1-at_ref[0]
                    row=(((z*at_ref[4]+y)*at_ref[5]+x)*2+core)*size
                    inner=buf.at[pl.ds(pl.multiple_of(row,16),size)]
                    piece=pieces[ab*len(keys)+ki]
                    piece=piece.at[kz] if ka==2 else piece
                    cp=pltpu.make_async_copy(piece,inner,sem.at[n]) if gather else pltpu.make_async_copy(inner,piece,sem.at[n])
                    cp.start() if go else cp.wait()
                    n+=1
    both(True); both(False)

def project_kernel(keys,at_ref,own_ref,oth_ref,gain_ref,shift_ref,bias_ref,*refs):
    nk=len(keys)
    pieces=refs[:2*nk]; h_ref,qkv_ref,w,buf,sem=refs[2*nk:]
    @pl.when(pl.program_id(0)==0)
    def _(): place(at_ref,keys,2,pieces[0].shape[1],pieces,w,sem,True)
    for s,src in enumerate((own_ref,oth_ref)):
        v=wide_rows(buf.at[s],src[0])
        h=(norm_parts(v)[0]*gain_ref[...]+shift_ref[...]).astype(BF)
        h_ref[0,s]=h
        qkv_ref[0,s]=(dot(h,w[...])+bias_ref[...]).astype(BF)

def project(at,x_own,x_oth,gain,shift,bias,wa,wb,padded):
    keys=sorted(wa); nk=len(keys)
    n,half,feat=x_own.shape
    width=wa[keys[0]].shape[-1]
    tok=pl.BlockSpec((1,half,feat),lambda i:(i,0,0))
    row=lambda w: pl.BlockSpec((1,w),lambda i:(0,0))
    return pl.pallas_call(functools.partial(project_kernel,keys),grid=(n,),
        in_specs=[SM,tok,tok,row(feat),row(feat),row(width)]+[ANY]*(2*nk),
        out_specs=[pl.BlockSpec((1,2,padded,feat),lambda i:(i,0,0,0)),pl.BlockSpec((1,2,padded,width),lambda i:(i,0,0,0))],
        out_shape=[jax.ShapeDtypeStruct((n,2,padded,feat),BF),jax.ShapeDtypeStruct((n,2,padded,width),BF)],
        scratch_shapes=[pltpu.VMEM((feat,width),BF),pltpu.VMEM((2,padded,feat),F32),pltpu.SemaphoreType.DMA((4*nk,))],
        name="project",
        compiler_params=pltpu.CompilerParams(vmem_limit_bytes=50<<20),
        cost_estimate=pl.CostEstimate(flops=n*4*padded*feat*width,bytes_accessed=24<<20,transcendentals=0),
    )(at,x_own,x_oth,gain[None],shift[None],bias[None],*[wa[k] for k in keys],*[wb[k] for k in keys])

def gather_kernel(keys,at_ref,*refs):
    nk=len(keys)
    place(at_ref,keys,1,refs[0].shape[0],refs[:2*nk],refs[2*nk],refs[2*nk+1],True)

def gather_rows(at,pa,pb):
    keys=sorted(pa); nk=len(keys)
    rows,feat=pa[keys[0]].shape
    return pl.pallas_call(functools.partial(gather_kernel,keys),in_specs=[SM]+[ANY]*(2*nk),out_specs=ANY,
        out_shape=jax.ShapeDtypeStruct((2*nk*rows,feat),BF),scratch_shapes=[pltpu.SemaphoreType.DMA((2*nk,))],name="gather_rows",
    )(at,*[pa[k] for k in keys],*[pb[k] for k in keys])

def middle_kernel(own_ref,oth_ref,mo_ref,mt_ref,wo_ref,wt_ref,bias_ref,gain_ref,shift_ref,x2_ref,h2_ref,buf):
    for s,src in enumerate((own_ref,oth_ref)):
        v=wide_rows(buf.at[s],src[0])
        v=v+(dot(mo_ref[0,s],wo_ref[...])+dot(mt_ref[0,1-s],wt_ref[...]))+bias_ref[...]
        x2_ref[0,s]=v
        h2_ref[0,s]=(norm_parts(v)[0]*gain_ref[...]+shift_ref[...]).astype(BF)

def middle(x_own,x_oth,mixed,mixed_oth,w_own,w_oth,bias,gain,shift):
    n,half,feat=x_own.shape
    _,_,padded,width=mixed.shape
    tok=pl.BlockSpec((1,half,feat),lambda i:(i,0,0))
    mix=pl.BlockSpec((1,2,padded,width),lambda i:(i,0,0,0))
    swp=pl.BlockSpec((1,2,padded,width),lambda i:(i,0,0,0))
    full=pl.BlockSpec((width,feat),lambda i:(0,0))
    row=pl.BlockSpec((1,feat),lambda i:(0,0))
    out=pl.BlockSpec((1,2,padded,feat),lambda i:(i,0,0,0))
    return pl.pallas_call(middle_kernel,grid=(n,),in_specs=[tok,tok,mix,swp,full,full,row,row,row],out_specs=[out,out],
        out_shape=[jax.ShapeDtypeStruct((n,2,padded,feat),F32),jax.ShapeDtypeStruct((n,2,padded,feat),BF)],
        scratch_shapes=[pltpu.VMEM((2,padded,feat),F32)],name="middle",
        compiler_params=pltpu.CompilerParams(vmem_limit_bytes=50<<20),
        cost_estimate=pl.CostEstimate(flops=n*8*padded*feat*width,bytes_accessed=26<<20,transcendentals=0),
    )(x_own,x_oth,mixed,mixed_oth,w_own,w_oth,bias[None],gain[None],shift[None])

def middle_back_kernel(x2_ref,da_ref,db_ref,go_ref,gt_ref,mix_ref,w_ref,gain_ref,dx_ref,dat_ref,gw_ref,sum_ref,buf,acc):
    i=pl.program_id(0)
    @pl.when(i==0)
    def _():
        acc[...]=jnp.zeros_like(acc); sum_ref[...]=jnp.zeros_like(sum_ref)
    for s,src in enumerate((go_ref,gt_ref)):
        dd=wide_rows(buf.at[s],src[0])
        grad=da_ref[0,s].astype(F32)+db_ref[0,1-s].astype(F32)
        dx,gg=norm_back(x2_ref[0,s],gain_ref[...],grad)
        dx=dx+dd
        dob=dx.astype(BF)
        if s==0:
            dx_ref[0]=dx
            for r,t in enumerate((gg,grad,dob.astype(F32),dd)):
                sum_ref[r:r+1,:]+=jnp.sum(t,axis=0,keepdims=True)
        dat_ref[0,s]=dot(dob,w_ref[...],NT).astype(BF)
        acc[...]+=dot(mix_ref[0,s],dob,TN)
    @pl.when(i==pl.num_programs(0)-1)
    def _(): gw_ref[...]=acc[...].astype(BF)

def middle_back(x2,dh_own,dh_oth,g_own,g_oth,mixed,w_own,gain):
    n,half,feat=g_own.shape
    _,_,padded,width=mixed.shape
    tok=pl.BlockSpec((1,half,feat),lambda i:(i,0,0))
    mix=pl.BlockSpec((1,2,padded,width),lambda i:(i,0,0,0))
    big=pl.BlockSpec((1,2,padded,feat),lambda i:(i,0,0,0))
    full=pl.BlockSpec((width,feat),lambda i:(0,0))
    return pl.pallas_call(middle_back_kernel,grid=(n,),
        in_specs=[big,big,big,tok,tok,mix,full,pl.BlockSpec((1,feat),lambda i:(0,0))],
        out_specs=[pl.BlockSpec((1,padded,feat),lambda i:(i,0,0)),mix,full,pl.BlockSpec((8,feat),lambda i:(0,0))],
        out_shape=[jax.ShapeDtypeStruct((n,padded,feat),F32),jax.ShapeDtypeStruct(mixed.shape,BF),jax.ShapeDtypeStruct((width,feat),BF),jax.ShapeDtypeStruct((8,feat),F32)],
        scratch_shapes=[pltpu.VMEM((2,padded,feat),F32),pltpu.VMEM((width,feat),F32)],name="middle_back",
        compiler_params=pltpu.CompilerParams(vmem_limit_bytes=56<<20),
        cost_estimate=pl.CostEstimate(flops=n*8*padded*feat*width,bytes_accessed=30<<20,transcendentals=0),
    )(x2,dh_own,dh_oth,g_own,g_oth,mixed,w_own,gain[None])

def grad_in_kernel(keys,tile,at_ref,h_ref,d_ref,*refs):
    nk=len(keys)
    pieces=refs[:2*nk]; buf,sem=refs[2*nk:]
    for t in range(0,h_ref.shape[1],tile):
        buf[t:t+tile,:]=dot(h_ref[:,t:t+tile],d_ref[...],TN).astype(BF)
    place(at_ref,keys,2,pieces[0].shape[1],pieces,buf,sem,False)

def grad_in(at,h1,dqkv,keys,rows):
    tokens,feat=h1.shape; width=dqkv.shape[1]
    nk=len(keys)
    out=pl.pallas_call(functools.partial(grad_in_kernel,keys,256),in_specs=[SM,VM,VM],out_specs=[ANY]*(2*nk),
        out_shape=[jax.ShapeDtypeStruct((2,rows,width),BF)]*(2*nk),
        scratch_shapes=[pltpu.VMEM((feat,width),BF),pltpu.SemaphoreType.DMA((4*nk,))],name="grad_in",
        compiler_params=pltpu.CompilerParams(vmem_limit_bytes=50<<20),
        cost_estimate=pl.CostEstimate(flops=2*tokens*feat*width,bytes_accessed=14<<20,transcendentals=0),
    )(at,h1,dqkv)
    return dict(zip(keys,out[:nk])),dict(zip(keys,out[nk:]))

def project_back_kernel(keys,at_ref,d_ref,*refs):
    nk=len(keys)
    pieces=refs[:2*nk]; own_ref,oth_ref,w,sem=refs[2*nk:]
    @pl.when(pl.program_id(0)==0)
    def _(): place(at_ref,keys,2,pieces[0].shape[1],pieces,w,sem,True)
    own_ref[0]=dot(d_ref[0,0],w[...],NT)
    oth_ref[0]=dot(d_ref[0,1],w[...],NT).astype(BF)

def project_back(at,dqkv,wa,wb):
    keys=sorted(wa); nk=len(keys)
    n,_,padded,width=dqkv.shape
    feat=wa[keys[0]].shape[1]*4*nk
    out=pl.BlockSpec((1,padded,feat),lambda i:(i,0,0))
    return pl.pallas_call(functools.partial(project_back_kernel,keys),grid=(n,),
        in_specs=[SM,pl.BlockSpec((1,2,padded,width),lambda i:(i,0,0,0))]+[ANY]*(2*nk),out_specs=[out,out],
        out_shape=[jax.ShapeDtypeStruct((n,padded,feat),F32),jax.ShapeDtypeStruct((n,padded,feat),BF)],
        scratch_shapes=[pltpu.VMEM((feat,width),BF),pltpu.SemaphoreType.DMA((4*nk,))],name="project_back",
        compiler_params=pltpu.CompilerParams(vmem_limit_bytes=50<<20),
        cost_estimate=pl.CostEstimate(flops=n*4*padded*feat*width,bytes_accessed=18<<20,transcendentals=0),
    )(at,dqkv,*[wa[k] for k in keys],*[wb[k] for k in keys])

def input_back_kernel(x_ref,da_ref,db_ref,dx_ref,gain_ref,out_ref,sum_ref,buf):
    @pl.when(pl.program_id(0)==0)
    def _(): sum_ref[...]=jnp.zeros_like(sum_ref)
    half=x_ref.shape[1]
    v=wide_rows(buf,x_ref[0])
    grad=da_ref[0]+db_ref[0].astype(F32)
    dx,gg=norm_back(v,gain_ref[...],grad)
    out_ref[0]=(dx+dx_ref[0]).astype(BF)[:half]
    sum_ref[0:1,:]+=jnp.sum(gg,axis=0,keepdims=True)
    sum_ref[1:2,:]+=jnp.sum(grad,axis=0,keepdims=True)

def input_back(x_own,dh_own,dh_oth,dx2,gain):
    n,half,feat=x_own.shape
    padded=dx2.shape[1]
    tok=pl.BlockSpec((1,half,feat),lambda i:(i,0,0))
    big=pl.BlockSpec((1,padded,feat),lambda i:(i,0,0))
    return pl.pallas_call(input_back_kernel,grid=(n,),in_specs=[tok,big,big,big,pl.BlockSpec((1,feat),lambda i:(0,0))],
        out_specs=[tok,pl.BlockSpec((8,feat),lambda i:(0,0))],
        out_shape=[jax.ShapeDtypeStruct(x_own.shape,BF),jax.ShapeDtypeStruct((8,feat),F32)],
        scratch_shapes=[pltpu.VMEM((padded,feat),F32)],name="input_back",
        compiler_params=pltpu.CompilerParams(vmem_limit_bytes=40<<20),
        cost_estimate=pl.CostEstimate(flops=n*20*padded*feat,bytes_accessed=14<<20,transcendentals=0),
    )(x_own,dh_own,dh_oth,dx2,gain[None])


def shift(value, axis, up):
    n = lax.axis_size(axis)
    return lax.ppermute(value, axis, [(i, (i + up) % n) for i in range(n)])


def crossed(value):
    return lax.ppermute(value, ("seq", "core"), [(0, 0), (1, 2), (2, 1), (3, 3)])


def small_sum(value, axes):
    for axis in axes:
        n = lax.axis_size(axis)
        moved, total = value, value
        for _ in range(n - 1):
            moved = shift(moved, axis, 1)
            total = total + moved
        value = total
    return value


def gather_list(piece, axis):
    out = [piece]
    for _ in range(lax.axis_size(axis) - 1):
        out.append(shift(out[-1], axis, -1))
    return out


def gather_plane(piece, first, second):
    out = {}
    for i, one in enumerate(gather_list(piece, first)):
        for j, two in enumerate(gather_list(one, second)):
            out[(j, i) if first == "x" else (i, j)] = two
    return out


def reduce_list(pieces, axis):
    total = pieces[-1]
    for piece in pieces[-2::-1]:
        total = (shift(total, axis, 1).astype(F32) + piece.astype(F32)).astype(BF)
    return total


def reduce_plane(pieces, first, second):
    n_first, n_second = lax.axis_size(first), lax.axis_size(second)
    part = []
    for i in range(n_first):
        row = [pieces[(j, i) if first == "x" else (i, j)] for j in range(n_second)]
        part.append(reduce_list(row, second))
    return reduce_list(part, first)


def adam_update(master, first_moment, second_moment, gradient, step_rate, bias_one, bias_two):
    first_new = 0.5 * first_moment + 0.5 * gradient
    second_new = 0.5 * second_moment + 0.5 * gradient * gradient
    update = first_new / bias_one / (jnp.sqrt(second_new / bias_two) + ADAM_EPS)
    master_new = master - step_rate * (update + WEIGHT_DECAY * master)
    return (master_new, first_new, second_new)


def on_device(images, key_mask, out_grad, step_count, *params):
    masters, firsts, seconds = params[0:5], params[5:10], params[10:15]
    in_weights, out_weights, up_weights, down_weights, vectors = masters
    image_count, half, features = images.shape
    padded = -(-half // PAD_ROWS) * PAD_ROWS
    h, c = lax.axis_index("seq"), lax.axis_index("core")
    y, x = lax.axis_index("y"), lax.axis_index("x")
    ny, nx = lax.axis_size("y"), lax.axis_size("x")
    shards = 4 * ny * nx
    shard = ((h * ny + y) * nx + x) * 2 + c
    at = jnp.stack([h, y, x, c, jnp.int32(ny), jnp.int32(nx), jnp.int32(0), jnp.int32(0)]).astype(jnp.int32)

    placed = jnp.where(
        lax.broadcasted_iota(jnp.int32, (shards, 1), 0) == shard, vectors.astype(BF)[None, :], jnp.zeros((), BF)
    )
    full_vec = small_sum(placed, SHARD).reshape(-1).astype(F32)
    gain_one, shift_one, query_bias, value_bias, out_bias, gain_two, shift_two, down_bias = (
        full_vec[i * D : (i + 1) * D] for i in range(8)
    )
    up_bias = full_vec[8 * D :]

    rows_in = in_weights.shape[0]
    by_core = in_weights.astype(BF).reshape(rows_in, 3, 2, HALF_D)
    mine = jnp.where(c == 0, by_core[:, :, 0], by_core[:, :, 1]).reshape(rows_in, 3 * HALF_D)
    theirs = jnp.where(c == 0, by_core[:, :, 1], by_core[:, :, 0]).reshape(rows_in, 3 * HALF_D)
    in_a = jnp.stack(gather_list(mine, "seq"))
    in_b = jnp.stack(gather_list(shift(theirs, "core", 1), "seq"))
    in_a = gather_plane(in_a, "x", "y")
    in_b = gather_plane(in_b, "y", "x")
    keys = sorted(in_a)

    out_low = out_weights.astype(BF)
    rows_out = out_low.shape[0]
    out_a = gather_plane(crossed(out_low), "x", "y")
    out_b = gather_plane(crossed(shift(out_low, "core", 1)), "y", "x")
    my_out = gather_rows(at, out_a, out_b)
    other_out = shift(my_out, "core", 1)

    rows_ff = up_weights.shape[0]
    half_ff = rows_ff // 2
    updown = [jnp.stack([up_weights[r].astype(BF), down_weights[r].astype(BF)]) for r in (slice(0, half_ff), slice(half_ff, rows_ff))]
    ff_a = gather_plane(jnp.stack(gather_list(updown[0], "seq")), "x", "y")
    ff_b = gather_plane(jnp.stack(gather_list(updown[1], "seq")), "y", "x")

    x_own = crossed(images)
    x_oth = shift(x_own, "core", 1)
    g_own = crossed(out_grad)
    g_oth = shift(g_own, "core", 1)
    mask = key_mask.astype(F32)
    mask = jnp.where(h == c, mask, shift(mask, "core", 1)).reshape(image_count, 2, half)
    mask = jnp.where(c == 0, mask, mask[:, ::-1])
    mask = jnp.pad(mask, ((0, 0), (0, 0), (0, padded - half))).reshape(image_count, 2 * padded)
    key_fill = jnp.broadcast_to(jnp.where(mask > 0, 0.0, NEG_FILL)[..., None], mask.shape + (128,)).astype(BF)

    q_bias = lax.dynamic_slice(query_bias, (c * HALF_D,), (HALF_D,))
    v_bias = lax.dynamic_slice(value_bias, (c * HALF_D,), (HALF_D,))
    in_bias = jnp.concatenate([q_bias, jnp.zeros_like(q_bias), v_bias])
    h1, qkv = project(at, x_own, x_oth, gain_one, shift_one, in_bias, in_a, in_b, padded)
    tokens = image_count * 2 * padded
    qkv = qkv.reshape(image_count, 2 * padded, 3 * HALF_D)
    mixed, lse = attend(qkv, key_fill)
    halved = mixed.reshape(image_count, 2, padded, HALF_D)
    mixed_oth = shift(halved, "core", 1)
    x2, h2 = middle(x_own, x_oth, halved, mixed_oth, my_out, other_out, out_bias, gain_two, shift_two)

    grad_a, grad_b, y_own, y_oth, dh2, g_bu = mlp(
        at, h2.reshape(tokens, D), g_own, g_oth, up_bias.reshape(shards * 2, half_ff), ff_a, ff_b
    )
    share_ff = []
    for grads, order in ((grad_a, ("x", "y")), (grad_b, ("y", "x"))):
        total = reduce_plane(grads, *order)
        share_ff.append(reduce_list([total[0], total[1]], "seq"))
    share_ff = jnp.concatenate(share_ff, axis=1)
    result = y_own[:, :half] + shift(y_oth, "core", 1)[:, :half].astype(F32) + x2[:, 0, :half] + down_bias
    activations = crossed(result.astype(BF)).astype(F32)

    dh2 = dh2.reshape(image_count, 2, padded, D)
    dh2_oth = shift(dh2, "core", 1)
    dx2, dattn, g_out, sums_two = middle_back(x2, dh2, dh2_oth, g_own, g_oth, halved, my_out, gain_two)
    g_out = g_out.reshape(ny, nx, 2, rows_out, D)
    oa, ob = {}, {}
    for ky, kx in keys:
        spot = ((y + ky) % ny, (x + kx) % nx)
        oa[ky, kx] = lax.dynamic_slice(g_out, (*spot, h, 0, 0), (1, 1, 1, rows_out, D)).reshape(rows_out, D)
        ob[ky, kx] = lax.dynamic_slice(g_out, (*spot, 1 - h, 0, 0), (1, 1, 1, rows_out, D)).reshape(rows_out, D)
    keep = crossed(reduce_plane(oa, "x", "y"))
    give = crossed(reduce_plane(ob, "y", "x"))
    share_out = (keep.astype(F32) + shift(give, "core", 1).astype(F32)).astype(BF)

    dqkv, sums_qkv = attend_back(qkv, key_fill, mixed, dattn.reshape(mixed.shape), lse)
    ia, ib = grad_in(at, h1.reshape(tokens, D), dqkv.reshape(tokens, 3 * HALF_D), keys, rows_in)
    ia = reduce_plane(ia, "x", "y")
    ib = reduce_plane(ib, "y", "x")
    ia, ib = reduce_list([ia[0], ia[1]], "seq"), reduce_list([ib[0], ib[1]], "seq")
    ib = shift(ib, "core", 1)
    ia, ib = (t.reshape(rows_in, 3, 1, HALF_D) for t in (ia, ib))
    share_in = jnp.where(c == 0, jnp.concatenate([ia, ib], 2), jnp.concatenate([ib, ia], 2)).reshape(rows_in, 3 * D)

    dh_own, dh_oth = project_back(at, dqkv.reshape(image_count, 2, padded, 3 * HALF_D), in_a, in_b)
    input_grad, sums_one = input_back(x_own, dh_own, shift(dh_oth, "core", 1), dx2, gain_one)
    input_grad = crossed(input_grad).astype(F32)

    zero = jnp.zeros((D,), F32)
    grad_vec = jnp.concatenate(
        [
            sums_one[0],
            sums_one[1],
            lax.dynamic_update_slice(zero, sums_qkv[0, :HALF_D], (c * HALF_D,)),
            lax.dynamic_update_slice(zero, sums_qkv[0, 2 * HALF_D :], (c * HALF_D,)),
            sums_two[2],
            sums_two[0],
            sums_two[1],
            sums_two[3],
            g_bu.reshape(-1),
        ]
    ).reshape(shards, -1)
    grad_vec = small_sum(grad_vec, AXES)
    share_vec = lax.dynamic_slice(grad_vec, (shard, 0), (1, grad_vec.shape[1])).reshape(-1)

    def over_dp(share):
        return small_sum(share, ("dp",)).astype(F32)

    shares = (over_dp(share_in), over_dp(share_out), over_dp(share_ff[0]), over_dp(share_ff[1]), share_vec)
    square = sum(jnp.sum(s * s) for s in shares)
    square = small_sum(jnp.full((8, 128), square), SHARD)[0, 0]
    grad_norm = jnp.sqrt(square)
    threshold = 0.5 * math.sqrt(4 * D * D + 2 * D * FF + 12 * D)
    clip_factor = jnp.minimum(1.0, threshold / grad_norm)
    bias = 1.0 - jnp.power(F32(0.5), step_count.astype(F32))
    rates = ((D // 2) ** (-0.5), (D // 4) ** (-0.5), D ** (-0.5), FF ** (-0.5), 0.2)
    results = [
        adam_update(masters[i], firsts[i], seconds[i], shares[i] * clip_factor, rates[i], bias, bias) for i in range(5)
    ]
    return (
        grad_norm,
        *(r[0] for r in results),
        *(r[1] for r in results),
        *(r[2] for r in results),
        *(r[0].astype(BF) for r in results),
        activations,
        input_grad,
    )


def solution(mesh):
    seq_n, fsdp_n, dp_n = (mesh.shape[a] for a in ("seq", "fsdp", "dp"))
    nx = math.isqrt(fsdp_n // 2)
    ny = fsdp_n // 2 // nx
    grid = Mesh(np.asarray(mesh.devices).reshape(seq_n, ny, nx, 2, dp_n), AXES)
    tokens = P(("y", "x", "core", "dp"), "seq", None)
    matrix, vector = P(SHARD, None), P(SHARD)
    five = (matrix, matrix, matrix, matrix, vector)
    return jax.shard_map(
        on_device,
        mesh=grid,
        in_specs=(tokens, P(("y", "x", "core", "dp"), None), tokens, P()) + five * 3,
        out_specs=(P(),) + five * 4 + (tokens, tokens),
        check_vma=False,
    )
```

time: 1780 us -> 735 us (0.41)
  waiting for transfers between devices: 1020 us -> 248 us
  matrix products: 339 us -> 0 us
  Pallas kernels: 0 us -> 229 us
  local copies, waits for them, and re-layouts: 168 us -> 20.5 us
  starting transfers between devices: 24.1 us -> 165 us
  blocking collectives: 125 us -> 0 us
    all_to_all x4 -> x0, waiting for transfers between devices: 584 us -> none  [the longest x1 308 us: on_device(): lax.all_to_all(packed, 'seq', split_axis=3, concat_axis=1, tiled=True)]
    reduce_scatter x4 -> x0, waiting for transfers between devices: 353 us -> none  [the longest x1 184 us: on_device(): lax.psum_scatter(grad_up_w, ('seq', 'fsdp'), scatter_dimension=0, tiled=T...]
    dot_general x33 -> x0, matrix products: 339 us -> none  [the longest x3 65.8 us: attend_back(): jnp.einsum('hqk,qhd->khd', grad_scores, queries, preferred_element_type=j...]
    ppermute x0 -> x81, waiting for transfers between devices: none -> 248 us  [the longest x73 221 us: shift(): return lax.ppermute(value, axis, [(i, (i + up) % n) for i in range(n)])]
    pallas_call x0 -> x10, Pallas kernels: none -> 229 us  [the longest x1 73.8 us: mlp(): pl.pallas_call(functools.partial(mlp_kernel, keys, gtile=min(gtile, width...]
    ppermute x0 -> x81, starting transfers between devices: none -> 165 us  [the longest x73 134 us: shift(): return lax.ppermute(value, axis, [(i, (i + up) % n) for i in range(n)])]
    unnamed x1 -> x0, blocking collectives: 67.7 us -> none
    reshape x8 -> x6, local copies, waits for them, and re-layouts: 61.8 us -> 0.68 us  [the longest x1 0.28 us: on_device(): by_core = in_weights.astype(BF).reshape(rows_in, 3, 2, HALF_D)]
  transfers between devices with their start and end apart: 13 -> 81, of which waited for: 8 -> 32; matrix products, arithmetic and copies ran while one was open for 28% -> 9% of each run, Pallas kernels for 0% -> 13%
where the time goes in v1:
time: 735 us; the launch traced here: 728 us
  waiting for transfers between devices  248 us (34%)
  Pallas kernels  229 us (31%)
  starting transfers between devices  165 us (22%)
  other arithmetic  58.1 us (8%)
  local copies, waits for them, and re-layouts  20.5 us (3%)
  between operations  7.95 us (1%)
    ppermute x73, waiting for transfers between devices, shift(): return lax.ppermute(value, axis, [(i, (i + up) % n) for i in range(n)])  221 us
    ppermute x73, starting transfers between devices, shift(): return lax.ppermute(value, axis, [(i, (i + up) % n) for i in range(n)])  134 us
    pallas_call x1, Pallas kernels, mlp(): pl.pallas_call(functools.partial(mlp_kernel, keys, gtile=min(gtile, width...  73.8 us
    pallas_call x1, Pallas kernels, gather_rows(): pl.pallas_call(functools.partial(gather_kernel, keys), in_specs=[SM] + [A...  33.6 us
    ppermute x8, starting transfers between devices, crossed(): lax.ppermute(value, ('seq', 'core'), [(0, 0), (1, 2), (2, 1), (3, 3)])  30.4 us
    pallas_call x1, Pallas kernels, attend_back(): pl.pallas_call(functools.partial(attend_back_kernel, pairs=pairs, chunk=c...  30.3 us
    ppermute x8, waiting for transfers between devices, crossed(): lax.ppermute(value, ('seq', 'core'), [(0, 0), (1, 2), (2, 1), (3, 3)])  27.3 us
    pallas_call x1, Pallas kernels, attend(): pl.pallas_call(attend_kernel, grid=(n, pairs), in_specs=[blk(0), blk(pair...  20.3 us
  transfers between devices with their start and end apart: 81, of which 32 were waited for; matrix products, arithmetic and copies ran while one was open for 9% of the time, Pallas kernels for 13%

profile of v1, /device:TPU:1, one launch (start us, length us, event | category | flops | bytes accessed | tf_op | source)
XLA Modules:
  0.0 727.6 jit_solution(9494250433126759906)
XLA Ops:
  0.7 5.6 collective-permute-start
  9.8 19.6 %collective-permute-done.2 = bf16[16,768]{1,0:T(8,128)(2,1)S(1)} collective-permute-done((bf16[16,768]{1,0:T(8,128)(2,1)S(1)}, bf16[16,768]{1,0:T(8,128)(2,1)S(1)}, u32[]{:S(2)}, u32[]{:S(2)}) %collective-permute-start.2) | collective-permute-done | bytes 24608 | tf_op jit(solution)/shard_map/ppermute | solution.py:439
  33.9 23.0 %collective-permute-start.10 = (bf16[64,1536]{1,0:T(8,128)(2,1)}, bf16[64,1536]{1,0:T(8,128)(2,1)}, u32[]{:S(2)}, u32[]{:S(2)}) collective-permute-start(bf16[64,1536]{1,0:T(8,128)(2,1)} %bitcast.74), channel_id=1, source_target_pairs={{0,2},{2,0},{1,3},{3,1},{4,6},{6,4},{5,7},{7,5},{8,10},{10,8},{9,1... | collective-permute-start | bytes 589832 | tf_op jit(solution)/shard_map/ppermute | solution.py:439
  62.3 5.2 collective-permute-start.17
  68.7 11.3 %collective-permute-done.11 = bf16[64,1536]{1,0:T(8,128)(2,1)S(1)} collective-permute-done((bf16[64,1536]{1,0:T(8,128)(2,1)}, bf16[64,1536]{1,0:T(8,128)(2,1)S(1)}, u32[]{:S(2)}, u32[]{:S(2)}) %collective-permute-start.11) | collective-permute-done | bytes 196640 | tf_op jit(solution)/shard_map/ppermute | solution.py:439
  85.6 4.5 collective-permute-done.7.refs_1_
  92.6 7.8 %collective-permute-done.8.refs_2_ = bf16[2,64,1536]{2,1,0:T(8,128)(2,1)} collective-permute-done((bf16[2,64,1536]{2,1,0:T(8,128)(2,1)S(1)}, bf16[2,64,1536]{2,1,0:T(8,128)(2,1)}, u32[]{:S(2)}, u32[]{:S(2)}) %collective-permute-start.8) | collective-permute-done | bytes 393248 | tf_op jit(solution)/shard_map/ppermute | solution.py:439
  100.5 4.5 collective-permute-start.27
  105.3 3.6 collective-permute-done.9.refs_3_
  109.1 3.5 collective-permute-start.22
  112.6 13.5 %project.1 = (bf16[3,2,304,1024]{3,2,1,0:T(8,128)(2,1)}, bf16[3,2,304,1536]{3,2,1,0:T(8,128)(2,1)}) custom-call(s32[8]{0:T(128)S(1)} %stack.70.at_ref.refs_0_, bf16[3,292,1024]{2,1,0:T(8,128)(2,1)} %copy-done.5, bf16[3,292,1024]{2,1,0:T(8,128)(2,1)} %collective-permute-done.1.oth_ref, f32[1,1024]{1,0:T(1,128)S(1)} %bitcast.119, f32[1,1024]{1,0:T(1,128)S(1)} %bitcast.125, ...), custom_call_target="tpu_custom_call" | custom-call | flops 5737807872 | bytes 25165824 | tf_op jit(solution)/shard_map/project/pallas_call | solution.py:293
  126.6 20.3 %attend.1 = (bf16[3,608,512]{2,1,0:T(8,128)(2,1)S(1)}, f32[3,4,8,608]{3,2,1,0:T(8,128)S(1)}) custom-call(bf16[3,608,1536]{2,1,0:T(8,128)(2,1)} %bitcast.126, bf16[3,608,1536]{2,1,0:T(8,128)(2,1)} %bitcast.127, bf16[3,608,1536]{2,1,0:T(8,128)(2,1)} %bitcast.128, bf16[3,608,128]{2,1,0:T(8,128)(2,1)S(1)} %broadcast_in_dim.71.kb_ref), custom_call_target="tpu_custom_call" | custom-call | flops 4542431232 | bytes 8404992 | tf_op jit(solution)/shard_map/attend/pallas_call | solution.py:181
  147.6 9.2 %collective-permute-start.16 = (bf16[3,2,304,512]{3,2,1,0:T(8,128)(2,1)S(1)}, bf16[3,2,304,512]{3,2,1,0:T(8,128)(2,1)}, u32[]{:S(2)}, u32[]{:S(2)}) collective-permute-start(bf16[3,2,304,512]{3,2,1,0:T(8,128)(2,1)S(1)} %bitcast.116), channel_id=1, source_target_pairs={{0,2},{2,0},{1,3},{3,1},{4,6},{6,4},{5,7},{7,5},{8,10},{10,8},{9,1... | collective-permute-start | bytes 5603336 | tf_op jit(solution)/shard_map/ppermute | solution.py:439
  162.7 2.0 collective-permute-start.33
  166.0 2.9 collective-permute-done.24.refs_6_
  170.1 2.9 collective-permute-done.25.refs_7_
  173.0 33.6 %gather_rows.1.wo_ref.w_ref = bf16[512,1024]{1,0:T(8,128)(2,1)} custom-call(s32[8]{0:T(128)} %copy-done.13, bf16[64,1024]{1,0:T(8,128)(2,1)} %collective-permute-done.17.refs_0_, bf16[64,1024]{1,0:T(8,128)(2,1)} %copy-done.51, bf16[64,1024]{1,0:T(8,128)(2,1)} %copy-done.52, bf16[64,1024]{1,0:T(8,128)(2,1)} %copy-done.54, bf16[64,1024]{1,0:T(8,128)(2,1)} %copy-done.53, ...), custom_call_target="tpu_custom_call" | custom-call | tf_op jit(solution)/shard_map/gather_rows/pallas_call | solution.py:310
  206.6 3.4 collective-permute-start.26
  210.8 2.4 pad_maximum_fusion.refs_5_
  214.4 2.3 pad_maximum_fusion.1.refs_9_
  219.7 18.6 %collective-permute-done.30.refs_6_ = bf16[2,2,128,1024]{3,2,1,0:T(8,128)(2,1)} collective-permute-done((bf16[2,2,128,1024]{3,2,1,0:T(8,128)(2,1)}, bf16[2,2,128,1024]{3,2,1,0:T(8,128)(2,1)}, u32[]{:S(2)}, u32[]{:S(2)}) %collective-permute-start.30) | collective-permute-done | bytes 1048608 | tf_op jit(solution)/shard_map/ppermute | solution.py:439
  239.5 1.9 collective-permute-done.35.refs_11_
  246.3 9.6 %middle.1 = (f32[3,2,304,1024]{3,2,1,0:T(8,128)}, bf16[3,2,304,1024]{3,2,1,0:T(8,128)(2,1)}) custom-call(bf16[3,292,1024]{2,1,0:T(8,128)(2,1)S(1)} %copy-done.6, bf16[3,292,1024]{2,1,0:T(8,128)(2,1)} %collective-permute-done.1.oth_ref, bf16[3,2,304,512]{3,2,1,0:T(8,128)(2,1)} %bitcast.117, bf16[3,2,304,512]{3,2,1,0:T(8,128)(2,1)} %collective-permute-done.16.mt_ref, ...), custom_call_target="tpu_custom_call" | custom-call | flops 3825205248 | bytes 27262976 | tf_op jit(solution)/shard_map/middle/pallas_call | solution.py:330
  255.9 8.0 %collective-permute-done.31.refs_7_ = bf16[2,2,128,1024]{3,2,1,0:T(8,128)(2,1)} collective-permute-done((bf16[2,2,128,1024]{3,2,1,0:T(8,128)(2,1)}, bf16[2,2,128,1024]{3,2,1,0:T(8,128)(2,1)}, u32[]{:S(2)}, u32[]{:S(2)}) %collective-permute-start.31) | collective-permute-done | bytes 1048608 | tf_op jit(solution)/shard_map/ppermute | solution.py:439
  263.9 22.5 %collective-permute-done.32.refs_8_ = bf16[2,2,128,1024]{3,2,1,0:T(8,128)(2,1)} collective-permute-done((bf16[2,2,128,1024]{3,2,1,0:T(8,128)(2,1)}, bf16[2,2,128,1024]{3,2,1,0:T(8,128)(2,1)}, u32[]{:S(2)}, u32[]{:S(2)}) %collective-permute-start.32) | collective-permute-done | bytes 1048608 | tf_op jit(solution)/shard_map/ppermute | solution.py:439
  286.4 73.8 %feed_forward.1 = (bf16[2,2,128,1024]{3,2,1,0:T(8,128)(2,1)}, bf16[2,2,128,1024]{3,2,1,0:T(8,128)(2,1)}, bf16[2,2,128,1024]{3,2,1,0:T(8,128)(2,1)}, bf16[2,2,128...) custom-call(s32[8]{0:T(128)} %copy-done.13, ...), custom_call_target="tpu_custom_call" | custom-call | flops 45902462976 | bytes 41943040 | tf_op jit(solution)/shard_map/feed_forward/pallas_call | solution.py:139
  362.9 21.0 %collective-permute-done.62 = bf16[2,2,128,1024]{3,2,1,0:T(8,128)(2,1)S(1)} collective-permute-done((bf16[2,2,128,1024]{3,2,1,0:T(8,128)(2,1)}, bf16[2,2,128,1024]{3,2,1,0:T(8,128)(2,1)S(1)}, u32[]{:S(2)}, u32[]{:S(2)}) %collective-permute-start.62) | collective-permute-done | bytes 1048608 | tf_op jit(solution)/shard_map/ppermute | solution.py:439
  386.9 4.0 collective-permute-start.37
  392.0 14.5 %collective-permute-done.64 = bf16[2,2,128,1024]{3,2,1,0:T(8,128)(2,1)S(1)} collective-permute-done((bf16[2,2,128,1024]{3,2,1,0:T(8,128)(2,1)}, bf16[2,2,128,1024]{3,2,1,0:T(8,128)(2,1)S(1)}, u32[]{:S(2)}, u32[]{:S(2)}) %collective-permute-start.64) | collective-permute-done | bytes 1048608 | tf_op jit(solution)/shard_map/ppermute | solution.py:439
  406.4 3.7 collective-permute-start.78
  411.8 17.4 %collective-permute-done.60 = bf16[2,2,128,1024]{3,2,1,0:T(8,128)(2,1)S(1)} collective-permute-done((bf16[2,2,128,1024]{3,2,1,0:T(8,128)(2,1)S(1)}, bf16[2,2,128,1024]{3,2,1,0:T(8,128)(2,1)S(1)}, u32[]{:S(2)}, u32[]{:S(2)}) %collective-permute-start.60) | collective-permute-done | bytes 1048608 | tf_op jit(solution)/shard_map/ppermute | solution.py:439
  431.5 15.3 %collective-permute-done.65 = bf16[2,128,1024]{2,1,0:T(8,128)(2,1)} collective-permute-done((bf16[2,128,1024]{2,1,0:T(8,128)(2,1)S(1)}, bf16[2,128,1024]{2,1,0:T(8,128)(2,1)}, u32[]{:S(2)}, u32[]{:S(2)}) %collective-permute-start.65) | collective-permute-done | bytes 524320 | tf_op jit(solution)/shard_map/ppermute | solution.py:439
  448.2 9.8 %collective-permute-done.61 = bf16[2,128,1024]{2,1,0:T(8,128)(2,1)} collective-permute-done((bf16[2,128,1024]{2,1,0:T(8,128)(2,1)}, bf16[2,128,1024]{2,1,0:T(8,128)(2,1)}, u32[]{:S(2)}, u32[]{:S(2)}) %collective-permute-start.61) | collective-permute-done | bytes 524320 | tf_op jit(solution)/shard_map/ppermute | solution.py:439
  460.2 5.1 fusion.2
  465.3 7.7 %collective-permute-done.66 = bf16[256,1024]{1,0:T(8,128)(2,1)S(1)} collective-permute-done((bf16[256,1024]{1,0:T(8,128)(2,1)S(1)}, bf16[256,1024]{1,0:T(8,128)(2,1)S(1)}, u32[]{:S(2)}, u32[]{:S(2)}) %collective-permute-start.66) | collective-permute-done | bytes 524320 | tf_op jit(solution)/shard_map/ppermute | solution.py:439
  474.0 17.1 %middle_back.1 = (f32[3,304,1024]{2,1,0:T(8,128)}, bf16[3,2,304,512]{3,2,1,0:T(8,128)(2,1)}, bf16[512,1024]{1,0:T(8,128)(2,1)}, f32[8,1024]{1,0:T(8,128)}) custom-call(f32[3,2,304,1024]{3,2,1,0:T(8,128)} %get-tuple-element.62.x2_ref, bf16[3,2,304,1024]{3,2,1,0:T(8,128)(2,1)} %bitcast.133, bf16[3,2,304,1024]{3,2,1,0:T(8,128)(2,1)} %collective-permute-done.37.db_ref, ...), custom_call_target="tpu_custom_call" | custom-call | flops 3825205248 | bytes 31457280 | tf_op jit(solution)/shard_map/middle_back/pallas_call | solution.py:364
  491.1 30.3 %attend_back.1 = (bf16[3,608,1536]{2,1,0:T(8,128)(2,1)}, f32[8,1536]{1,0:T(8,128)S(1)}) custom-call(bf16[3,608,1536]{2,1,0:T(8,128)(2,1)} %bitcast.129, bf16[3,608,1536]{2,1,0:T(8,128)(2,1)} %bitcast.130, bf16[3,608,1536]{2,1,0:T(8,128)(2,1)} %bitcast.131, bf16[3,608,128]{2,1,0:T(8,128)(2,1)S(1)} %broadcast_in_dim.71.kb_ref, ...), custom_call_target="tpu_custom_call" | custom-call | flops 11356078080 | bytes 14008320 | tf_op jit(solution)/shard_map/attend_back/pallas_call | solution.py:229
  521.4 15.3 %grad_in.1 = (bf16[2,64,1536]{2,1,0:T(8,128)(2,1)S(1)}, bf16[2,64,1536]{2,1,0:T(8,128)(2,1)S(1)}, bf16[2,64,1536]{2,1,0:T(8,128)(2,1)S(1)}, bf16[2,64,1536]{2,1,...) custom-call(s32[8]{0:T(128)S(1)} %copy-done.14, ...), custom_call_target="tpu_custom_call" | custom-call | flops 5737807872 | bytes 14680064 | tf_op jit(solution)/shard_map/grad_in/pallas_call | solution.py:383
  540.2 12.4 %project_back.1 = (f32[3,304,1024]{2,1,0:T(8,128)}, bf16[3,304,1024]{2,1,0:T(8,128)(2,1)}) custom-call(s32[8]{0:T(128)S(1)} %copy-done.14, bf16[3,2,304,1536]{3,2,1,0:T(8,128)(2,1)} %bitcast.151, bf16[2,64,1536]{2,1,0:T(8,128)(2,1)S(1)} %copy-done.9, bf16[2,64,1536]{2,1,0:T(8,128)(2,1)S(1)} %copy-done.20, ...), custom_call_target="tpu_custom_call" | custom-call | flops 5737807872 | bytes 18874368 | tf_op jit(solution)/shard_map/project_back/pallas_call | solution.py:404
  556.7 4.5 collective-permute-start.79
  566.1 2.2 collective-permute-done.38
  568.6 16.2 %collective-permute-start.68 = (bf16[3,304,1024]{2,1,0:T(8,128)(2,1)}, bf16[3,304,1024]{2,1,0:T(8,128)(2,1)S(1)}, u32[]{:S(2)}, u32[]{:S(2)}) collective-permute-start(bf16[3,304,1024]{2,1,0:T(8,128)(2,1)} %get-tuple-element.86), channel_id=1, source_target_pairs={{0,2},{2,0},{1,3},{3,1},{4,6},{6,4},{5,7},{7,5},{8,10},{10,8},{9,1... | collective-permute-start | bytes 5603336 | tf_op jit(solution)/shard_map/ppermute | solution.py:439
  586.1 1.9 collective-permute-start.55
  588.0 3.7 collective-permute-done.39
  591.7 6.3 collective-permute-start.45
  598.1 7.2 collective-permute-done.45
  605.4 7.8 %collective-permute-done.41 = bf16[64,1536]{1,0:T(8,128)(2,1)S(1)} collective-permute-done((bf16[64,1536]{1,0:T(8,128)(2,1)S(1)}, bf16[64,1536]{1,0:T(8,128)(2,1)S(1)}, u32[]{:S(2)}, u32[]{:S(2)}) %collective-permute-start.41) | collective-permute-done | bytes 196640 | tf_op jit(solution)/shard_map/ppermute | solution.py:439
  613.2 9.3 %collective-permute-start.46 = (bf16[64,1536]{1,0:T(8,128)(2,1)S(1)}, bf16[64,1536]{1,0:T(8,128)(2,1)S(1)}, u32[]{:S(2)}, u32[]{:S(2)}) collective-permute-start(bf16[64,1536]{1,0:T(8,128)(2,1)S(1)} %fusion.14), channel_id=1, source_target_pairs={{0,2},{2,0},{1,3},{3,1},{4,6},{6,4},{5,7},{7,5},{8,10},{10,8},{9,1... | collective-permute-start | bytes 589832 | tf_op jit(solution)/shard_map/ppermute | solution.py:439
  624.9 2.0 copy-done.1
  627.0 2.1 copy-done.2
  630.5 2.9 input_back.1
  634.8 2.8 collective-permute-start.69
  639.0 2.0 collective-permute-start.47
  647.6 3.7 collective-permute-start.72
  658.2 2.0 collective-permute-start.74
  666.6 6.3 collective-permute-start.77
  673.6 3.9 convert_element_type.404
  677.5 3.3 collective-permute-start.80
  682.8 2.2 fusion.33
  685.1 4.3 fusion.31
  689.5 3.7 fusion.29
  693.2 2.0 fusion.35
  695.2 27.3 %collective-permute-done.80 = bf16[3,292,1024]{2,1,0:T(8,128)(2,1)} collective-permute-done((bf16[3,292,1024]{2,1,0:T(8,128)(2,1)S(1)}, bf16[3,292,1024]{2,1,0:T(8,128)(2,1)}, u32[]{:S(2)}, u32[]{:S(2)}) %collective-permute-start.80) | collective-permute-done | bytes 1794080 | tf_op jit(solution)/shard_map/ppermute | solution.py:443
  722.5 3.7 convert_element_type.405
  (347 shorter events, 97.3 us)
Async XLA Ops:
  0.7 57.8 %collective-permute-start = (bf16[3,292,1024]{2,1,0:T(8,128)(2,1)}, bf16[3,292,1024]{2,1,0:T(8,128)(2,1)S(1)}, u32[]{:S(2)}, u32[]{:S(2)}) collective-permute-start(bf16[3,292,1024]{2,1,0:T(8,128)(2,1)} %param.19), channel_id=1, source_target_pairs={{0,0},{2,16},{16,2},{18,18},{1,1},{3,17},{17,3},{19,19},{4,4},{6,2... | collective-permute-start | bytes 5382152 | tf_op jit(solution)/shard_map/ppermute | solution.py:443
  7.1 22.4 %collective-permute-start.2 = (bf16[16,768]{1,0:T(8,128)(2,1)S(1)}, bf16[16,768]{1,0:T(8,128)(2,1)S(1)}, u32[]{:S(2)}, u32[]{:S(2)}) collective-permute-start(bf16[16,768]{1,0:T(8,128)(2,1)S(1)} %broadcast_select_fusion.2), channel_id=1, source_target_pairs={{0,16},{16,0},{1,17},{17,1},{2,18},{18,2},{3,19},{19,3},{4,20},{20... | collective-permute-start | bytes 73736 | tf_op jit(solution)/shard_map/ppermute | solution.py:439
  29.5 29.5 %collective-permute-start.3 = (bf16[16,768]{1,0:T(8,128)(2,1)S(1)}, bf16[16,768]{1,0:T(8,128)(2,1)S(1)}, u32[]{:S(2)}, u32[]{:S(2)}) collective-permute-start(bf16[16,768]{1,0:T(8,128)(2,1)S(1)} %fusion.24), channel_id=1, source_target_pairs={{0,8},{8,0},{1,9},{9,1},{2,10},{10,2},{3,11},{11,3},{4,12},{12,4},... | collective-permute-start | bytes 73736 | tf_op jit(solution)/shard_map/ppermute | solution.py:439
  32.7 34.8 %collective-permute-start.6 = (bf16[64,1536]{1,0:T(8,128)(2,1)}, bf16[64,1536]{1,0:T(8,128)(2,1)}, u32[]{:S(2)}, u32[]{:S(2)}) collective-permute-start(bf16[64,1536]{1,0:T(8,128)(2,1)} %bitcast.70), channel_id=1, source_target_pairs={{0,16},{16,0},{1,17},{17,1},{2,18},{18,2},{3,19},{19,3},{4,20},{20... | collective-permute-start | bytes 589832 | tf_op jit(solution)/shard_map/ppermute | solution.py:439
  33.9 33.7 %collective-permute-start.10 = (bf16[64,1536]{1,0:T(8,128)(2,1)}, bf16[64,1536]{1,0:T(8,128)(2,1)}, u32[]{:S(2)}, u32[]{:S(2)}) collective-permute-start(bf16[64,1536]{1,0:T(8,128)(2,1)} %bitcast.74), channel_id=1, source_target_pairs={{0,2},{2,0},{1,3},{3,1},{4,6},{6,4},{5,7},{7,5},{8,10},{10,8},{9,1... | collective-permute-start | bytes 589832 | tf_op jit(solution)/shard_map/ppermute | solution.py:439
  58.3 23.9 %collective-permute-start.15 = (f32[3,584]{1,0:T(4,128)}, f32[3,584]{1,0:T(4,128)}, u32[]{:S(2)}, u32[]{:S(2)}) collective-permute-start(f32[3,584]{1,0:T(4,128)} %convert_element_type.310), channel_id=1, source_target_pairs={{0,2},{2,0},{1,3},{3,1},{4,6},{6,4},{5,7},{7,5},{8,10},{10,8},{9,1... | collective-permute-start | bytes 21032 | tf_op jit(solution)/shard_map/ppermute | solution.py:439
  58.5 54.1 %collective-permute-start.1 = (bf16[3,292,1024]{2,1,0:T(8,128)(2,1)S(1)}, bf16[3,292,1024]{2,1,0:T(8,128)(2,1)}, u32[]{:S(2)}, u32[]{:S(2)}) collective-permute-start(bf16[3,292,1024]{2,1,0:T(8,128)(2,1)S(1)} %collective-permute-done.own_ref.x_ref), channel_id=1, source_target_pairs={{0,2},{2,0},{1,3},{3,1},{4,6},{6,4},{5,7},{7,5},{8,10},{10,8},{9,1... | collective-permute-start | bytes 5382152 | tf_op jit(solution)/shard_map/ppermute | solution.py:439
  62.3 21.7 %collective-permute-start.17 = (bf16[64,1024]{1,0:T(8,128)(2,1)S(1)}, bf16[64,1024]{1,0:T(8,128)(2,1)}, u32[]{:S(2)}, u32[]{:S(2)}) collective-permute-start(bf16[64,1024]{1,0:T(8,128)(2,1)S(1)} %convert_element_type.313), channel_id=1, source_target_pairs={{0,0},{2,16},{16,2},{18,18},{1,1},{3,17},{17,3},{19,19},{4,4},{6,2... | collective-permute-start | bytes 393224 | tf_op jit(solution)/shard_map/ppermute | solution.py:443
  67.5 15.9 %collective-permute-start.5 = (bf16[16,768]{1,0:T(8,128)(2,1)S(1)}, bf16[16,768]{1,0:T(8,128)(2,1)S(1)}, u32[]{:S(2)}, u32[]{:S(2)}) collective-permute-start(bf16[16,768]{1,0:T(8,128)(2,1)S(1)} %add.302), channel_id=1, source_target_pairs={{0,2},{2,0},{1,3},{3,1},{4,6},{6,4},{5,7},{7,5},{8,10},{10,8},{9,1... | collective-permute-start | bytes 73736 | tf_op jit(solution)/shard_map/ppermute | solution.py:439
  67.6 12.4 %collective-permute-start.11 = (bf16[64,1536]{1,0:T(8,128)(2,1)}, bf16[64,1536]{1,0:T(8,128)(2,1)S(1)}, u32[]{:S(2)}, u32[]{:S(2)}) collective-permute-start(bf16[64,1536]{1,0:T(8,128)(2,1)} %collective-permute-done.10), channel_id=1, source_target_pairs={{0,16},{16,0},{1,17},{17,1},{2,18},{18,2},{3,19},{19,3},{4,20},{20... | collective-permute-start | bytes 589832 | tf_op jit(solution)/shard_map/ppermute | solution.py:439
  80.0 10.1 %collective-permute-start.7 = (bf16[2,64,1536]{2,1,0:T(8,128)(2,1)S(1)}, bf16[2,64,1536]{2,1,0:T(8,128)(2,1)S(1)}, u32[]{:S(2)}, u32[]{:S(2)}) collective-permute-start(bf16[2,64,1536]{2,1,0:T(8,128)(2,1)S(1)} %pad_maximum_fusion.5.refs_0_), channel_id=1, source_target_pairs={{0,4},{4,0},{1,5},{5,1},{2,6},{6,2},{3,7},{7,3},{8,12},{12,8},{9,1... | collective-permute-start | bytes 1179656 | tf_op jit(solution)/shard_map/ppermute | solution.py:439
  82.2 9.8 %collective-permute-start.13 = (bf16[2,64,1536]{2,1,0:T(8,128)(2,1)S(1)}, bf16[2,64,1536]{2,1,0:T(8,128)(2,1)}, u32[]{:S(2)}, u32[]{:S(2)}) collective-permute-start(bf16[2,64,1536]{2,1,0:T(8,128)(2,1)S(1)} %pad_maximum_fusion.6.refs_4_), channel_id=1, source_target_pairs={{0,8},{8,0},{1,9},{9,1},{2,10},{10,2},{3,11},{11,3},{4,12},{12,4},... | collective-permute-start | bytes 1179656 | tf_op jit(solution)/shard_map/ppermute | solution.py:439
  84.0 16.4 %collective-permute-start.8 = (bf16[2,64,1536]{2,1,0:T(8,128)(2,1)S(1)}, bf16[2,64,1536]{2,1,0:T(8,128)(2,1)}, u32[]{:S(2)}, u32[]{:S(2)}) collective-permute-start(bf16[2,64,1536]{2,1,0:T(8,128)(2,1)S(1)} %pad_maximum_fusion.5.refs_0_), channel_id=1, source_target_pairs={{0,8},{8,0},{1,9},{9,1},{2,10},{10,2},{3,11},{11,3},{4,12},{12,4},... | collective-permute-start | bytes 1179656 | tf_op jit(solution)/shard_map/ppermute | solution.py:439
  85.3 19.6 %collective-permute-start.12 = (bf16[2,64,1536]{2,1,0:T(8,128)(2,1)S(1)}, bf16[2,64,1536]{2,1,0:T(8,128)(2,1)}, u32[]{:S(2)}, u32[]{:S(2)}) collective-permute-start(bf16[2,64,1536]{2,1,0:T(8,128)(2,1)S(1)} %pad_maximum_fusion.6.refs_4_), channel_id=1, source_target_pairs={{0,4},{4,0},{1,5},{5,1},{2,6},{6,2},{3,7},{7,3},{8,12},{12,8},{9,1... | collective-permute-start | bytes 1179656 | tf_op jit(solution)/shard_map/ppermute | solution.py:439
  90.1 18.8 %collective-permute-start.9 = (bf16[2,64,1536]{2,1,0:T(8,128)(2,1)S(1)}, bf16[2,64,1536]{2,1,0:T(8,128)(2,1)}, u32[]{:S(2)}, u32[]{:S(2)}) collective-permute-start(bf16[2,64,1536]{2,1,0:T(8,128)(2,1)S(1)} %collective-permute-done.7.refs_1_), channel_id=1, source_target_pairs={{0,8},{8,0},{1,9},{9,1},{2,10},{10,2},{3,11},{11,3},{4,12},{12,4},... | collective-permute-start | bytes 1179656 | tf_op jit(solution)/shard_map/ppermute | solution.py:439
  92.0 17.1 %collective-permute-start.14 = (bf16[2,64,1536]{2,1,0:T(8,128)(2,1)}, bf16[2,64,1536]{2,1,0:T(8,128)(2,1)}, u32[]{:S(2)}, u32[]{:S(2)}) collective-permute-start(bf16[2,64,1536]{2,1,0:T(8,128)(2,1)} %collective-permute-done.13.refs_6_), channel_id=1, source_target_pairs={{0,4},{4,0},{1,5},{5,1},{2,6},{6,2},{3,7},{7,3},{8,12},{12,8},{9,1... | collective-permute-start | bytes 1179656 | tf_op jit(solution)/shard_map/ppermute | solution.py:439
  100.5 117.5 %collective-permute-start.27 = (bf16[3,292,1024]{2,1,0:T(8,128)(2,1)}, bf16[3,292,1024]{2,1,0:T(8,128)(2,1)}, u32[]{:S(2)}, u32[]{:S(2)}) collective-permute-start(bf16[3,292,1024]{2,1,0:T(8,128)(2,1)} %param.21), channel_id=1, source_target_pairs={{0,0},{2,16},{16,2},{18,18},{1,1},{3,17},{17,3},{19,19},{4,4},{6,2... | collective-permute-start | bytes 5382152 | tf_op jit(solution)/shard_map/ppermute | solution.py:443
  104.9 52.7 %collective-permute-start.18 = (bf16[64,1024]{1,0:T(8,128)(2,1)}, bf16[64,1024]{1,0:T(8,128)(2,1)S(1)}, u32[]{:S(2)}, u32[]{:S(2)}) collective-permute-start(bf16[64,1024]{1,0:T(8,128)(2,1)} %collective-permute-done.17.refs_0_), channel_id=1, source_target_pairs={{0,4},{4,0},{1,5},{5,1},{2,6},{6,2},{3,7},{7,3},{8,12},{12,8},{9,1... | collective-permute-start | bytes 393224 | tf_op jit(solution)/shard_map/ppermute | solution.py:439
  108.9 48.8 %collective-permute-start.19 = (bf16[64,1024]{1,0:T(8,128)(2,1)}, bf16[64,1024]{1,0:T(8,128)(2,1)S(1)}, u32[]{:S(2)}, u32[]{:S(2)}) collective-permute-start(bf16[64,1024]{1,0:T(8,128)(2,1)} %collective-permute-done.17.refs_0_), channel_id=1, source_target_pairs={{0,8},{8,0},{1,9},{9,1},{2,10},{10,2},{3,11},{11,3},{4,12},{12,4},... | collective-permute-start | bytes 393224 | tf_op jit(solution)/shard_map/ppermute | solution.py:439
  109.1 49.9 %collective-permute-start.22 = (bf16[64,1024]{1,0:T(8,128)(2,1)}, bf16[64,1024]{1,0:T(8,128)(2,1)S(1)}, u32[]{:S(2)}, u32[]{:S(2)}) collective-permute-start(bf16[64,1024]{1,0:T(8,128)(2,1)} %collective-permute-done.21), channel_id=1, source_target_pairs={{0,0},{2,16},{16,2},{18,18},{1,1},{3,17},{17,3},{19,19},{4,4},{6,2... | collective-permute-start | bytes 393224 | tf_op jit(solution)/shard_map/ppermute | solution.py:443
  147.6 95.1 %collective-permute-start.16 = (bf16[3,2,304,512]{3,2,1,0:T(8,128)(2,1)S(1)}, bf16[3,2,304,512]{3,2,1,0:T(8,128)(2,1)}, u32[]{:S(2)}, u32[]{:S(2)}) collective-permute-start(bf16[3,2,304,512]{3,2,1,0:T(8,128)(2,1)S(1)} %bitcast.116), channel_id=1, source_target_pairs={{0,2},{2,0},{1,3},{3,1},{4,6},{6,4},{5,7},{7,5},{8,10},{10,8},{9,1... | collective-permute-start | bytes 5603336 | tf_op jit(solution)/shard_map/ppermute | solution.py:439
  157.6 52.4 %collective-permute-start.29 = (bf16[2,128,1024]{2,1,0:T(8,128)(2,1)S(1)}, bf16[2,128,1024]{2,1,0:T(8,128)(2,1)S(1)}, u32[]{:S(2)}, u32[]{:S(2)}) collective-permute-start(bf16[2,128,1024]{2,1,0:T(8,128)(2,1)S(1)} %get-tuple-element.136), channel_id=1, source_target_pairs={{0,16},{16,0},{1,17},{17,1},{2,18},{18,2},{3,19},{19,3},{4,20},{20... | collective-permute-start | bytes 1572872 | tf_op jit(solution)/shard_map/ppermute | solution.py:439
  162.7 51.7 %collective-permute-start.33 = (bf16[2,128,1024]{2,1,0:T(8,128)(2,1)}, bf16[2,128,1024]{2,1,0:T(8,128)(2,1)}, u32[]{:S(2)}, u32[]{:S(2)}) collective-permute-start(bf16[2,128,1024]{2,1,0:T(8,128)(2,1)} %get-tuple-element.130), channel_id=1, source_target_pairs={{0,16},{16,0},{1,17},{17,1},{2,18},{18,2},{3,19},{19,3},{4,20},{20... | collective-permute-start | bytes 1572872 | tf_op jit(solution)/shard_map/ppermute | solution.py:439
  206.6 11.9 %collective-permute-start.26 = (bf16[512,1024]{1,0:T(8,128)(2,1)}, bf16[512,1024]{1,0:T(8,128)(2,1)S(1)}, u32[]{:S(2)}, u32[]{:S(2)}) collective-permute-start(bf16[512,1024]{1,0:T(8,128)(2,1)} %gather_rows.1.wo_ref.w_ref), channel_id=1, source_target_pairs={{0,2},{2,0},{1,3},{3,1},{4,6},{6,4},{5,7},{7,5},{8,10},{10,8},{9,1... | collective-permute-start | bytes 3145736 | tf_op jit(solution)/shard_map/ppermute | solution.py:439
  213.2 25.1 %collective-permute-start.30 = (bf16[2,2,128,1024]{3,2,1,0:T(8,128)(2,1)}, bf16[2,2,128,1024]{3,2,1,0:T(8,128)(2,1)}, u32[]{:S(2)}, u32[]{:S(2)}) collective-permute-start(bf16[2,2,128,1024]{3,2,1,0:T(8,128)(2,1)} %pad_maximum_fusion.refs_5_), channel_id=1, source_target_pairs={{0,4},{4,0},{1,5},{5,1},{2,6},{6,2},{3,7},{7,3},{8,12},{12,8},{9,1... | collective-permute-start | bytes 3145736 | tf_op jit(solution)/shard_map/ppermute | solution.py:439
  216.7 24.8 %collective-permute-start.35 = (bf16[2,2,128,1024]{3,2,1,0:T(8,128)(2,1)}, bf16[2,2,128,1024]{3,2,1,0:T(8,128)(2,1)}, u32[]{:S(2)}, u32[]{:S(2)}) collective-permute-start(bf16[2,2,128,1024]{3,2,1,0:T(8,128)(2,1)} %pad_maximum_fusion.1.refs_9_), channel_id=1, source_target_pairs={{0,8},{8,0},{1,9},{9,1},{2,10},{10,2},{3,11},{11,3},{4,12},{12,4},... | collective-permute-start | bytes 3145736 | tf_op jit(solution)/shard_map/ppermute | solution.py:439
  217.9 68.5 %collective-permute-start.28 = (bf16[3,292,1024]{2,1,0:T(8,128)(2,1)}, bf16[3,292,1024]{2,1,0:T(8,128)(2,1)}, u32[]{:S(2)}, u32[]{:S(2)}) collective-permute-start(bf16[3,292,1024]{2,1,0:T(8,128)(2,1)} %collective-permute-done.27.refs_2_.go_ref), channel_id=1, source_target_pairs={{0,2},{2,0},{1,3},{3,1},{4,6},{6,4},{5,7},{7,5},{8,10},{10,8},{9,1... | collective-permute-start | bytes 5382152 | tf_op jit(solution)/shard_map/ppermute | solution.py:439
  219.5 44.4 %collective-permute-start.31 = (bf16[2,2,128,1024]{3,2,1,0:T(8,128)(2,1)}, bf16[2,2,128,1024]{3,2,1,0:T(8,128)(2,1)}, u32[]{:S(2)}, u32[]{:S(2)}) collective-permute-start(bf16[2,2,128,1024]{3,2,1,0:T(8,128)(2,1)} %pad_maximum_fusion.refs_5_), channel_id=1, source_target_pairs={{0,8},{8,0},{1,9},{9,1},{2,10},{10,2},{3,11},{11,3},{4,12},{12,4},... | collective-permute-start | bytes 3145736 | tf_op jit(solution)/shard_map/ppermute | solution.py:439
  238.3 25.6 %collective-permute-start.34 = (bf16[2,2,128,1024]{3,2,1,0:T(8,128)(2,1)}, bf16[2,2,128,1024]{3,2,1,0:T(8,128)(2,1)}, u32[]{:S(2)}, u32[]{:S(2)}) collective-permute-start(bf16[2,2,128,1024]{3,2,1,0:T(8,128)(2,1)} %pad_maximum_fusion.1.refs_9_), channel_id=1, source_target_pairs={{0,4},{4,0},{1,5},{5,1},{2,6},{6,2},{3,7},{7,3},{8,12},{12,8},{9,1... | collective-permute-start | bytes 3145736 | tf_op jit(solution)/shard_map/ppermute | solution.py:439
  241.4 44.9 %collective-permute-start.32 = (bf16[2,2,128,1024]{3,2,1,0:T(8,128)(2,1)}, bf16[2,2,128,1024]{3,2,1,0:T(8,128)(2,1)}, u32[]{:S(2)}, u32[]{:S(2)}) collective-permute-start(bf16[2,2,128,1024]{3,2,1,0:T(8,128)(2,1)} %collective-permute-done.30.refs_6_), channel_id=1, source_target_pairs={{0,8},{8,0},{1,9},{9,1},{2,10},{10,2},{3,11},{11,3},{4,12},{12,4},... | collective-permute-start | bytes 3145736 | tf_op jit(solution)/shard_map/ppermute | solution.py:439
  242.7 43.7 %collective-permute-start.36 = (bf16[2,2,128,1024]{3,2,1,0:T(8,128)(2,1)}, bf16[2,2,128,1024]{3,2,1,0:T(8,128)(2,1)}, u32[]{:S(2)}, u32[]{:S(2)}) collective-permute-start(bf16[2,2,128,1024]{3,2,1,0:T(8,128)(2,1)} %collective-permute-done.35.refs_11_), channel_id=1, source_target_pairs={{0,4},{4,0},{1,5},{5,1},{2,6},{6,2},{3,7},{7,3},{8,12},{12,8},{9,1... | collective-permute-start | bytes 3145736 | tf_op jit(solution)/shard_map/ppermute | solution.py:439
  360.2 23.8 %collective-permute-start.62 = (bf16[2,2,128,1024]{3,2,1,0:T(8,128)(2,1)}, bf16[2,2,128,1024]{3,2,1,0:T(8,128)(2,1)S(1)}, u32[]{:S(2)}, u32[]{:S(2)}) collective-permute-start(bf16[2,2,128,1024]{3,2,1,0:T(8,128)(2,1)} %get-tuple-element.81), channel_id=1, source_target_pairs={{0,4},{4,0},{1,5},{5,1},{2,6},{6,2},{3,7},{7,3},{8,12},{12,8},{9,1... | collective-permute-start | bytes 3145736 | tf_op jit(solution)/shard_map/ppermute | solution.py:439
  360.5 30.6 %collective-permute-start.58 = (bf16[2,2,128,1024]{3,2,1,0:T(8,128)(2,1)}, bf16[2,2,128,1024]{3,2,1,0:T(8,128)(2,1)S(1)}, u32[]{:S(2)}, u32[]{:S(2)}) collective-permute-start(bf16[2,2,128,1024]{3,2,1,0:T(8,128)(2,1)} %get-tuple-element.77), channel_id=1, source_target_pairs={{0,8},{8,0},{1,9},{9,1},{2,10},{10,2},{3,11},{11,3},{4,12},{12,4},... | collective-permute-start | bytes 3145736 | tf_op jit(solution)/shard_map/ppermute | solution.py:439
  361.7 44.7 %collective-permute-start.64 = (bf16[2,2,128,1024]{3,2,1,0:T(8,128)(2,1)}, bf16[2,2,128,1024]{3,2,1,0:T(8,128)(2,1)S(1)}, u32[]{:S(2)}, u32[]{:S(2)}) collective-permute-start(bf16[2,2,128,1024]{3,2,1,0:T(8,128)(2,1)} %get-tuple-element.83), channel_id=1, source_target_pairs={{0,4},{4,0},{1,5},{5,1},{2,6},{6,2},{3,7},{7,3},{8,12},{12,8},{9,1... | collective-permute-start | bytes 3145736 | tf_op jit(solution)/shard_map/ppermute | solution.py:439
  385.6 24.5 %collective-permute-start.63 = (bf16[2,2,128,1024]{3,2,1,0:T(8,128)(2,1)S(1)}, bf16[2,2,128,1024]{3,2,1,0:T(8,128)(2,1)S(1)}, u32[]{:S(2)}, u32[]{:S(2)}) collective-permute-start(bf16[2,2,128,1024]{3,2,1,0:T(8,128)(2,1)S(1)} %add_convert_fusion.2), channel_id=1, source_target_pairs={{0,8},{8,0},{1,9},{9,1},{2,10},{10,2},{3,11},{11,3},{4,12},{12,4},... | collective-permute-start | bytes 3145736 | tf_op jit(solution)/shard_map/ppermute | solution.py:439
  386.9 87.1 %collective-permute-start.37 = (bf16[3,2,304,1024]{3,2,1,0:T(8,128)(2,1)}, bf16[3,2,304,1024]{3,2,1,0:T(8,128)(2,1)}, u32[]{:S(2)}, u32[]{:S(2)}) collective-permute-start(bf16[3,2,304,1024]{3,2,1,0:T(8,128)(2,1)} %bitcast.132), channel_id=1, source_target_pairs={{0,2},{2,0},{1,3},{3,1},{4,6},{6,4},{5,7},{7,5},{8,10},{10,8},{9,1... | collective-permute-start | bytes 11206664 | tf_op jit(solution)/shard_map/ppermute | solution.py:439
  390.9 38.3 %collective-permute-start.60 = (bf16[2,2,128,1024]{3,2,1,0:T(8,128)(2,1)S(1)}, bf16[2,2,128,1024]{3,2,1,0:T(8,128)(2,1)S(1)}, u32[]{:S(2)}, u32[]{:S(2)}) collective-permute-start(bf16[2,2,128,1024]{3,2,1,0:T(8,128)(2,1)S(1)} %copy-done.63), channel_id=1, source_target_pairs={{0,8},{8,0},{1,9},{9,1},{2,10},{10,2},{3,11},{11,3},{4,12},{12,4},... | collective-permute-start | bytes 3145736 | tf_op jit(solution)/shard_map/ppermute | solution.py:439
  391.6 37.6 %collective-permute-start.59 = (bf16[2,2,128,1024]{3,2,1,0:T(8,128)(2,1)S(1)}, bf16[2,2,128,1024]{3,2,1,0:T(8,128)(2,1)S(1)}, u32[]{:S(2)}, u32[]{:S(2)}) collective-permute-start(bf16[2,2,128,1024]{3,2,1,0:T(8,128)(2,1)S(1)} %add_convert_fusion.5), channel_id=1, source_target_pairs={{0,4},{4,0},{1,5},{5,1},{2,6},{6,2},{3,7},{7,3},{8,12},{12,8},{9,1... | collective-permute-start | bytes 3145736 | tf_op jit(solution)/shard_map/ppermute | solution.py:439
  406.4 53.7 %collective-permute-start.78 = (bf16[3,304,1024]{2,1,0:T(8,128)(2,1)}, bf16[3,304,1024]{2,1,0:T(8,128)(2,1)}, u32[]{:S(2)}, u32[]{:S(2)}) collective-permute-start(bf16[3,304,1024]{2,1,0:T(8,128)(2,1)} %get-tuple-element.93), channel_id=1, source_target_pairs={{0,2},{2,0},{1,3},{3,1},{4,6},{6,4},{5,7},{7,5},{8,10},{10,8},{9,1... | collective-permute-start | bytes 5603336 | tf_op jit(solution)/shard_map/ppermute | solution.py:439
  410.9 36.0 %collective-permute-start.65 = (bf16[2,128,1024]{2,1,0:T(8,128)(2,1)S(1)}, bf16[2,128,1024]{2,1,0:T(8,128)(2,1)}, u32[]{:S(2)}, u32[]{:S(2)}) collective-permute-start(bf16[2,128,1024]{2,1,0:T(8,128)(2,1)S(1)} %slice_bitcast_fusion.2), channel_id=1, source_target_pairs={{0,16},{16,0},{1,17},{17,1},{2,18},{18,2},{3,19},{19,3},{4,20},{20... | collective-permute-start | bytes 1572872 | tf_op jit(solution)/shard_map/ppermute | solution.py:439
  430.7 27.4 %collective-permute-start.61 = (bf16[2,128,1024]{2,1,0:T(8,128)(2,1)}, bf16[2,128,1024]{2,1,0:T(8,128)(2,1)}, u32[]{:S(2)}, u32[]{:S(2)}) collective-permute-start(bf16[2,128,1024]{2,1,0:T(8,128)(2,1)} %slice_bitcast_fusion.4), channel_id=1, source_target_pairs={{0,16},{16,0},{1,17},{17,1},{2,18},{18,2},{3,19},{19,3},{4,20},{20... | collective-permute-start | bytes 1572872 | tf_op jit(solution)/shard_map/ppermute | solution.py:439
  460.2 12.9 %collective-permute-start.66 = (bf16[256,1024]{1,0:T(8,128)(2,1)S(1)}, bf16[256,1024]{1,0:T(8,128)(2,1)S(1)}, u32[]{:S(2)}, u32[]{:S(2)}) collective-permute-start(bf16[256,1024]{1,0:T(8,128)(2,1)S(1)} %get-tuple-element.118), channel_id=1, source_target_pairs={{0,1},{1,0},{2,3},{3,2},{4,5},{5,4},{6,7},{7,6},{8,9},{9,8},{10,11... | collective-permute-start | bytes 1572872 | tf_op jit(solution)/shard_map/ppermute | solution.py:439
  536.7 27.0 %collective-permute-start.42 = (bf16[2,64,1536]{2,1,0:T(8,128)(2,1)}, bf16[2,64,1536]{2,1,0:T(8,128)(2,1)}, u32[]{:S(2)}, u32[]{:S(2)}) collective-permute-start(bf16[2,64,1536]{2,1,0:T(8,128)(2,1)} %get-tuple-element.72), channel_id=1, source_target_pairs={{0,4},{4,0},{1,5},{5,1},{2,6},{6,2},{3,7},{7,3},{8,12},{12,8},{9,1... | collective-permute-start | bytes 1179656 | tf_op jit(solution)/shard_map/ppermute | solution.py:439
  537.2 15.9 %collective-permute-start.48 = (bf16[64,1024]{1,0:T(8,128)(2,1)S(1)}, bf16[64,1024]{1,0:T(8,128)(2,1)S(1)}, u32[]{:S(2)}, u32[]{:S(2)}) collective-permute-start(bf16[64,1024]{1,0:T(8,128)(2,1)S(1)} %get-tuple-element.124), channel_id=1, source_target_pairs={{0,8},{8,0},{1,9},{9,1},{2,10},{10,2},{3,11},{11,3},{4,12},{12,4},... | collective-permute-start | bytes 393224 | tf_op jit(solution)/shard_map/ppermute | solution.py:439
  538.5 14.6 %collective-permute-start.52 = (bf16[64,1024]{1,0:T(8,128)(2,1)S(1)}, bf16[64,1024]{1,0:T(8,128)(2,1)}, u32[]{:S(2)}, u32[]{:S(2)}) collective-permute-start(bf16[64,1024]{1,0:T(8,128)(2,1)S(1)} %get-tuple-element.123), channel_id=1, source_target_pairs={{0,4},{4,0},{1,5},{5,1},{2,6},{6,2},{3,7},{7,3},{8,12},{12,8},{9,1... | collective-permute-start | bytes 393224 | tf_op jit(solution)/shard_map/ppermute | solution.py:439
  539.6 17.1 %collective-permute-start.50 = (bf16[64,1024]{1,0:T(8,128)(2,1)S(1)}, bf16[64,1024]{1,0:T(8,128)(2,1)}, u32[]{:S(2)}, u32[]{:S(2)}) collective-permute-start(bf16[64,1024]{1,0:T(8,128)(2,1)S(1)} %get-tuple-element.121), channel_id=1, source_target_pairs={{0,8},{8,0},{1,9},{9,1},{2,10},{10,2},{3,11},{11,3},{4,12},{12,4},... | collective-permute-start | bytes 393224 | tf_op jit(solution)/shard_map/ppermute | solution.py:439
  539.8 21.3 %collective-permute-start.54 = (bf16[64,1024]{1,0:T(8,128)(2,1)S(1)}, bf16[64,1024]{1,0:T(8,128)(2,1)}, u32[]{:S(2)}, u32[]{:S(2)}) collective-permute-start(bf16[64,1024]{1,0:T(8,128)(2,1)S(1)} %get-tuple-element.122), channel_id=1, source_target_pairs={{0,4},{4,0},{1,5},{5,1},{2,6},{6,2},{3,7},{7,3},{8,12},{12,8},{9,1... | collective-permute-start | bytes 393224 | tf_op jit(solution)/shard_map/ppermute | solution.py:439
  554.2 7.0 collective-permute-start.49
  556.7 116.9 %collective-permute-start.79 = (bf16[3,292,1024]{2,1,0:T(8,128)(2,1)}, bf16[3,292,1024]{2,1,0:T(8,128)(2,1)}, u32[]{:S(2)}, u32[]{:S(2)}) collective-permute-start(bf16[3,292,1024]{2,1,0:T(8,128)(2,1)} %fusion.2), channel_id=1, source_target_pairs={{0,0},{2,16},{16,2},{18,18},{1,1},{3,17},{17,3},{19,19},{4,4},{6,2... | collective-permute-start | bytes 5382152 | tf_op jit(solution)/shard_map/ppermute | solution.py:443
  561.2 84.3 %collective-permute-start.67 = (bf16[256,1024]{1,0:T(8,128)(2,1)}, bf16[256,1024]{1,0:T(8,128)(2,1)}, u32[]{:S(2)}, u32[]{:S(2)}) collective-permute-start(bf16[256,1024]{1,0:T(8,128)(2,1)} %get-tuple-element.117), channel_id=1, source_target_pairs={{0,1},{1,0},{2,3},{3,2},{4,5},{5,4},{6,7},{7,6},{8,9},{9,8},{10,11... | collective-permute-start | bytes 1572872 | tf_op jit(solution)/shard_map/ppermute | solution.py:439
  561.2 7.4 %collective-permute-start.44 = (bf16[2,64,1536]{2,1,0:T(8,128)(2,1)S(1)}, bf16[2,64,1536]{2,1,0:T(8,128)(2,1)S(1)}, u32[]{:S(2)}, u32[]{:S(2)}) collective-permute-start(bf16[2,64,1536]{2,1,0:T(8,128)(2,1)S(1)} %get-tuple-element.74), channel_id=1, source_target_pairs={{0,4},{4,0},{1,5},{5,1},{2,6},{6,2},{3,7},{7,3},{8,12},{12,8},{9,1... | collective-permute-start | bytes 1179656 | tf_op jit(solution)/shard_map/ppermute | solution.py:439
  563.8 22.3 %collective-permute-start.40 = (bf16[2,64,1536]{2,1,0:T(8,128)(2,1)S(1)}, bf16[2,64,1536]{2,1,0:T(8,128)(2,1)S(1)}, u32[]{:S(2)}, u32[]{:S(2)}) collective-permute-start(bf16[2,64,1536]{2,1,0:T(8,128)(2,1)S(1)} %get-tuple-element.70), channel_id=1, source_target_pairs={{0,8},{8,0},{1,9},{9,1},{2,10},{10,2},{3,11},{11,3},{4,12},{12,4},... | collective-permute-start | bytes 1179656 | tf_op jit(solution)/shard_map/ppermute | solution.py:439
  568.3 16.5 %collective-permute-start.43 = (bf16[2,64,1536]{2,1,0:T(8,128)(2,1)S(1)}, bf16[2,64,1536]{2,1,0:T(8,128)(2,1)S(1)}, u32[]{:S(2)}, u32[]{:S(2)}) collective-permute-start(bf16[2,64,1536]{2,1,0:T(8,128)(2,1)S(1)} %add_convert_fusion.8), channel_id=1, source_target_pairs={{0,8},{8,0},{1,9},{9,1},{2,10},{10,2},{3,11},{11,3},{4,12},{12,4},... | collective-permute-start | bytes 1179656 | tf_op jit(solution)/shard_map/ppermute | solution.py:439
  568.6 56.3 %collective-permute-start.68 = (bf16[3,304,1024]{2,1,0:T(8,128)(2,1)}, bf16[3,304,1024]{2,1,0:T(8,128)(2,1)S(1)}, u32[]{:S(2)}, u32[]{:S(2)}) collective-permute-start(bf16[3,304,1024]{2,1,0:T(8,128)(2,1)} %get-tuple-element.86), channel_id=1, source_target_pairs={{0,2},{2,0},{1,3},{3,1},{4,6},{6,4},{5,7},{7,5},{8,10},{10,8},{9,1... | collective-permute-start | bytes 5603336 | tf_op jit(solution)/shard_map/ppermute | solution.py:439
  586.1 36.6 %collective-permute-start.55 = (bf16[64,1024]{1,0:T(8,128)(2,1)S(1)}, bf16[64,1024]{1,0:T(8,128)(2,1)}, u32[]{:S(2)}, u32[]{:S(2)}) collective-permute-start(bf16[64,1024]{1,0:T(8,128)(2,1)S(1)} %get-tuple-element.120), channel_id=1, source_target_pairs={{0,0},{2,16},{16,2},{18,18},{1,1},{3,17},{17,3},{19,19},{4,4},{6,2... | collective-permute-start | bytes 393224 | tf_op jit(solution)/shard_map/ppermute | solution.py:443
  591.7 13.6 %collective-permute-start.45 = (bf16[64,1536]{1,0:T(8,128)(2,1)S(1)}, bf16[64,1536]{1,0:T(8,128)(2,1)S(1)}, u32[]{:S(2)}, u32[]{:S(2)}) collective-permute-start(bf16[64,1536]{1,0:T(8,128)(2,1)S(1)} %slice_bitcast_fusion.10), channel_id=1, source_target_pairs={{0,16},{16,0},{1,17},{17,1},{2,18},{18,2},{3,19},{19,3},{4,20},{20... | collective-permute-start | bytes 589832 | tf_op jit(solution)/shard_map/ppermute | solution.py:439
  605.3 7.9 %collective-permute-start.41 = (bf16[64,1536]{1,0:T(8,128)(2,1)S(1)}, bf16[64,1536]{1,0:T(8,128)(2,1)S(1)}, u32[]{:S(2)}, u32[]{:S(2)}) collective-permute-start(bf16[64,1536]{1,0:T(8,128)(2,1)S(1)} %slice_bitcast_fusion.12), channel_id=1, source_target_pairs={{0,16},{16,0},{1,17},{17,1},{2,18},{18,2},{3,19},{19,3},{4,20},{20... | collective-permute-start | bytes 589832 | tf_op jit(solution)/shard_map/ppermute | solution.py:439
  613.2 11.5 %collective-permute-start.46 = (bf16[64,1536]{1,0:T(8,128)(2,1)S(1)}, bf16[64,1536]{1,0:T(8,128)(2,1)S(1)}, u32[]{:S(2)}, u32[]{:S(2)}) collective-permute-start(bf16[64,1536]{1,0:T(8,128)(2,1)S(1)} %fusion.14), channel_id=1, source_target_pairs={{0,2},{2,0},{1,3},{3,1},{4,6},{6,4},{5,7},{7,5},{8,10},{10,8},{9,1... | collective-permute-start | bytes 589832 | tf_op jit(solution)/shard_map/ppermute | solution.py:439
  622.7 18.3 %collective-permute-start.51 = (bf16[64,1024]{1,0:T(8,128)(2,1)}, bf16[64,1024]{1,0:T(8,128)(2,1)S(1)}, u32[]{:S(2)}, u32[]{:S(2)}) collective-permute-start(bf16[64,1024]{1,0:T(8,128)(2,1)} %get-tuple-element.119), channel_id=1, source_target_pairs={{0,0},{2,16},{16,2},{18,18},{1,1},{3,17},{17,3},{19,19},{4,4},{6,2... | collective-permute-start | bytes 393224 | tf_op jit(solution)/shard_map/ppermute | solution.py:443
  624.7 17.3 %collective-permute-start.56 = (bf16[64,1024]{1,0:T(8,128)(2,1)}, bf16[64,1024]{1,0:T(8,128)(2,1)}, u32[]{:S(2)}, u32[]{:S(2)}) collective-permute-start(bf16[64,1024]{1,0:T(8,128)(2,1)} %collective-permute-done.55), channel_id=1, source_target_pairs={{0,2},{2,0},{1,3},{3,1},{4,6},{6,4},{5,7},{7,5},{8,10},{10,8},{9,1... | collective-permute-start | bytes 393224 | tf_op jit(solution)/shard_map/ppermute | solution.py:439
  639.0 14.5 %collective-permute-start.47 = (bf16[64,3072]{1,0:T(8,128)(2,1)S(1)}, bf16[64,3072]{1,0:T(8,128)(2,1)S(1)}, u32[]{:S(2)}, u32[]{:S(2)}) collective-permute-start(bf16[64,3072]{1,0:T(8,128)(2,1)S(1)} %select_n.158), channel_id=1, source_target_pairs={{0,1},{1,0},{2,3},{3,2},{4,5},{5,4},{6,7},{7,6},{8,9},{9,8},{10,11... | collective-permute-start | bytes 1179656 | tf_op jit(solution)/shard_map/ppermute | solution.py:439
  643.0 8.6 %collective-permute-start.57 = (bf16[64,1024]{1,0:T(8,128)(2,1)S(1)}, bf16[64,1024]{1,0:T(8,128)(2,1)S(1)}, u32[]{:S(2)}, u32[]{:S(2)}) collective-permute-start(bf16[64,1024]{1,0:T(8,128)(2,1)S(1)} %add_convert_fusion.12), channel_id=1, source_target_pairs={{0,1},{1,0},{2,3},{3,2},{4,5},{5,4},{6,7},{7,6},{8,9},{9,8},{10,11... | collective-permute-start | bytes 393224 | tf_op jit(solution)/shard_map/ppermute | solution.py:439
  666.6 14.3 %collective-permute-start.77 = (f32[8,128]{1,0:T(8,128)S(1)}, f32[8,128]{1,0:T(8,128)S(1)}, u32[]{:S(2)}, u32[]{:S(2)}) collective-permute-start(f32[8,128]{1,0:T(8,128)S(1)} %add.356), channel_id=1, source_target_pairs={{0,2},{2,0},{1,3},{3,1},{4,6},{6,4},{5,7},{7,5},{8,10},{10,8},{9,1... | collective-permute-start | bytes 12296 | tf_op jit(solution)/shard_map/ppermute | solution.py:439
  677.5 45.0 %collective-permute-start.80 = (bf16[3,292,1024]{2,1,0:T(8,128)(2,1)S(1)}, bf16[3,292,1024]{2,1,0:T(8,128)(2,1)}, u32[]{:S(2)}, u32[]{:S(2)}) collective-permute-start(bf16[3,292,1024]{2,1,0:T(8,128)(2,1)S(1)} %copy-done.16), channel_id=1, source_target_pairs={{0,0},{2,16},{16,2},{18,18},{1,1},{3,17},{17,3},{19,19},{4,4},{6,2... | collective-permute-start | bytes 5382152 | tf_op jit(solution)/shard_map/ppermute | solution.py:443
  (81 other events, 1243.2 us)

commit v2 on v1

--- a/solution.py
+++ b/solution.py
@@ -307,7 +307,7 @@
 def gather_rows(at,pa,pb):
     keys=sorted(pa); nk=len(keys)
     rows,feat=pa[keys[0]].shape
-    return pl.pallas_call(functools.partial(gather_kernel,keys),in_specs=[SM]+[ANY]*(2*nk),out_specs=ANY,
+    return pl.pallas_call(functools.partial(gather_kernel,keys),in_specs=[SM]+[ANY]*(2*nk),out_specs=VM,
         out_shape=jax.ShapeDtypeStruct((2*nk*rows,feat),BF),scratch_shapes=[pltpu.SemaphoreType.DMA((2*nk,))],name="gather_rows",
     )(at,*[pa[k] for k in keys],*[pb[k] for k in keys])
 
@@ -439,8 +439,20 @@
     return lax.ppermute(value, axis, [(i, (i + up) % n) for i in range(n)])
 
 
+def after(value, *others):
+    return lax.optimization_barrier((value, others))[0]
+
+
+def crossing(value):
+    return lax.ppermute(value, ("seq", "core"), [(1, 2), (2, 1)])
+
+
+def pick(own, received):
+    return jnp.where(lax.axis_index("seq") == lax.axis_index("core"), own, received)
+
+
 def crossed(value):
-    return lax.ppermute(value, ("seq", "core"), [(0, 0), (1, 2), (2, 1), (3, 3)])
+    return pick(value, crossing(value))
 
 
 def small_sum(value, axes):
@@ -461,28 +473,29 @@
     return out
 
 
-def gather_plane(piece, first, second):
+def gather_plane(piece, first, second, dep=()):
     out = {}
     for i, one in enumerate(gather_list(piece, first)):
+        one = after(one, dep) if i else one
         for j, two in enumerate(gather_list(one, second)):
             out[(j, i) if first == "x" else (i, j)] = two
     return out
 
 
-def reduce_list(pieces, axis):
+def reduce_list(pieces, axis, dep):
     total = pieces[-1]
     for piece in pieces[-2::-1]:
-        total = (shift(total, axis, 1).astype(F32) + piece.astype(F32)).astype(BF)
+        total = (after(shift(total, axis, 1), dep).astype(F32) + piece.astype(F32)).astype(BF)
     return total
 
 
-def reduce_plane(pieces, first, second):
+def reduce_plane(pieces, first, second, dep_one, dep_two):
     n_first, n_second = lax.axis_size(first), lax.axis_size(second)
     part = []
     for i in range(n_first):
         row = [pieces[(j, i) if first == "x" else (i, j)] for j in range(n_second)]
-        part.append(reduce_list(row, second))
-    return reduce_list(part, first)
+        part.append(reduce_list(row, second, dep_one))
+    return reduce_list(part, first, dep_two)
 
 
 def adam_update(master, first_moment, second_moment, gradient, step_rate, bias_one, bias_two):
@@ -518,13 +531,22 @@
     by_core = in_weights.astype(BF).reshape(rows_in, 3, 2, HALF_D)
     mine = jnp.where(c == 0, by_core[:, :, 0], by_core[:, :, 1]).reshape(rows_in, 3 * HALF_D)
     theirs = jnp.where(c == 0, by_core[:, :, 1], by_core[:, :, 0]).reshape(rows_in, 3 * HALF_D)
-    in_a = jnp.stack(gather_list(mine, "seq"))
-    in_b = jnp.stack(gather_list(shift(theirs, "core", 1), "seq"))
-    in_a = gather_plane(in_a, "x", "y")
-    in_b = gather_plane(in_b, "y", "x")
+    in_za = jnp.stack(gather_list(mine, "seq"))
+    in_zb = jnp.stack(gather_list(shift(theirs, "core", 1), "seq"))
+    in_a = gather_plane(in_za, "x", "y")
+    in_b = gather_plane(in_zb, "y", "x")
     keys = sorted(in_a)
 
-    out_low = out_weights.astype(BF)
+    x_got = crossing(images)
+    x_own = pick(images, after(x_got, list(in_a.values()), list(in_b.values())))
+    x_oth = shift(x_own, "core", 1)
+    mask = key_mask.astype(F32)
+    mask = jnp.where(h == c, mask, shift(mask, "core", 1)).reshape(image_count, 2, half)
+    mask = jnp.where(c == 0, mask, mask[:, ::-1])
+    mask = jnp.pad(mask, ((0, 0), (0, 0), (0, padded - half))).reshape(image_count, 2 * padded)
+    key_fill = jnp.broadcast_to(jnp.where(mask > 0, 0.0, NEG_FILL)[..., None], mask.shape + (128,)).astype(BF)
+
+    out_low = after(out_weights.astype(BF), in_za, in_zb)
     rows_out = out_low.shape[0]
     out_a = gather_plane(crossed(out_low), "x", "y")
     out_b = gather_plane(crossed(shift(out_low, "core", 1)), "y", "x")
@@ -534,40 +556,29 @@
     rows_ff = up_weights.shape[0]
     half_ff = rows_ff // 2
     updown = [jnp.stack([up_weights[r].astype(BF), down_weights[r].astype(BF)]) for r in (slice(0, half_ff), slice(half_ff, rows_ff))]
-    ff_a = gather_plane(jnp.stack(gather_list(updown[0], "seq")), "x", "y")
-    ff_b = gather_plane(jnp.stack(gather_list(updown[1], "seq")), "y", "x")
-
-    x_own = crossed(images)
-    x_oth = shift(x_own, "core", 1)
-    g_own = crossed(out_grad)
-    g_oth = shift(g_own, "core", 1)
-    mask = key_mask.astype(F32)
-    mask = jnp.where(h == c, mask, shift(mask, "core", 1)).reshape(image_count, 2, half)
-    mask = jnp.where(c == 0, mask, mask[:, ::-1])
-    mask = jnp.pad(mask, ((0, 0), (0, 0), (0, padded - half))).reshape(image_count, 2 * padded)
-    key_fill = jnp.broadcast_to(jnp.where(mask > 0, 0.0, NEG_FILL)[..., None], mask.shape + (128,)).astype(BF)
+    ff_za, ff_zb = (jnp.stack([t, after(shift(after(t, in_za, in_zb), "seq", -1), x_own)]) for t in updown)
+    g_got = crossing(after(out_grad, x_got))
 
     q_bias = lax.dynamic_slice(query_bias, (c * HALF_D,), (HALF_D,))
     v_bias = lax.dynamic_slice(value_bias, (c * HALF_D,), (HALF_D,))
     in_bias = jnp.concatenate([q_bias, jnp.zeros_like(q_bias), v_bias])
     h1, qkv = project(at, x_own, x_oth, gain_one, shift_one, in_bias, in_a, in_b, padded)
     tokens = image_count * 2 * padded
+    ff_a = gather_plane(ff_za, "x", "y", qkv)
+    ff_b = gather_plane(ff_zb, "y", "x", qkv)
     qkv = qkv.reshape(image_count, 2 * padded, 3 * HALF_D)
     mixed, lse = attend(qkv, key_fill)
     halved = mixed.reshape(image_count, 2, padded, HALF_D)
     mixed_oth = shift(halved, "core", 1)
+    g_own = pick(out_grad, after(g_got, mixed))
+    g_oth = shift(g_own, "core", 1)
     x2, h2 = middle(x_own, x_oth, halved, mixed_oth, my_out, other_out, out_bias, gain_two, shift_two)
 
     grad_a, grad_b, y_own, y_oth, dh2, g_bu = mlp(
         at, h2.reshape(tokens, D), g_own, g_oth, up_bias.reshape(shards * 2, half_ff), ff_a, ff_b
     )
-    share_ff = []
-    for grads, order in ((grad_a, ("x", "y")), (grad_b, ("y", "x"))):
-        total = reduce_plane(grads, *order)
-        share_ff.append(reduce_list([total[0], total[1]], "seq"))
-    share_ff = jnp.concatenate(share_ff, axis=1)
     result = y_own[:, :half] + shift(y_oth, "core", 1)[:, :half].astype(F32) + x2[:, 0, :half] + down_bias
-    activations = crossed(result.astype(BF)).astype(F32)
+    result = result.astype(BF)
 
     dh2 = dh2.reshape(image_count, 2, padded, D)
     dh2_oth = shift(dh2, "core", 1)
@@ -578,21 +589,28 @@
         spot = ((y + ky) % ny, (x + kx) % nx)
         oa[ky, kx] = lax.dynamic_slice(g_out, (*spot, h, 0, 0), (1, 1, 1, rows_out, D)).reshape(rows_out, D)
         ob[ky, kx] = lax.dynamic_slice(g_out, (*spot, 1 - h, 0, 0), (1, 1, 1, rows_out, D)).reshape(rows_out, D)
-    keep = crossed(reduce_plane(oa, "x", "y"))
-    give = crossed(reduce_plane(ob, "y", "x"))
-    share_out = (keep.astype(F32) + shift(give, "core", 1).astype(F32)).astype(BF)
-
+    result_got = crossing(after(result, dattn))
     dqkv, sums_qkv = attend_back(qkv, key_fill, mixed, dattn.reshape(mixed.shape), lse)
     ia, ib = grad_in(at, h1.reshape(tokens, D), dqkv.reshape(tokens, 3 * HALF_D), keys, rows_in)
-    ia = reduce_plane(ia, "x", "y")
-    ib = reduce_plane(ib, "y", "x")
-    ia, ib = reduce_list([ia[0], ia[1]], "seq"), reduce_list([ib[0], ib[1]], "seq")
+    dh_own, dh_oth = project_back(at, dqkv.reshape(image_count, 2, padded, 3 * HALF_D), in_a, in_b)
+    dh_got = shift(dh_oth, "core", 1)
+    activations = pick(result, after(result_got, dh_own)).astype(F32)
+    share_ff = []
+    for grads, order in ((grad_a, ("x", "y")), (grad_b, ("y", "x"))):
+        total = reduce_plane(grads, *order, dattn, dqkv)
+        share_ff.append(reduce_list([total[0], total[1]], "seq", dh_own))
+    share_ff = jnp.concatenate(share_ff, axis=1)
+    keep = crossed(reduce_plane(oa, "x", "y", dqkv, dh_own))
+    give = crossed(reduce_plane(ob, "y", "x", dqkv, dh_own))
+    share_out = (keep.astype(F32) + shift(give, "core", 1).astype(F32)).astype(BF)
+    ia = reduce_plane(ia, "x", "y", dh_own, dh_own)
+    ib = reduce_plane(ib, "y", "x", dh_own, dh_own)
+    ia, ib = reduce_list([ia[0], ia[1]], "seq", dh_own), reduce_list([ib[0], ib[1]], "seq", dh_own)
     ib = shift(ib, "core", 1)
     ia, ib = (t.reshape(rows_in, 3, 1, HALF_D) for t in (ia, ib))
     share_in = jnp.where(c == 0, jnp.concatenate([ia, ib], 2), jnp.concatenate([ib, ia], 2)).reshape(rows_in, 3 * D)
 
-    dh_own, dh_oth = project_back(at, dqkv.reshape(image_count, 2, padded, 3 * HALF_D), in_a, in_b)
-    input_grad, sums_one = input_back(x_own, dh_own, shift(dh_oth, "core", 1), dx2, gain_one)
+    input_grad, sums_one = input_back(x_own, dh_own, dh_got, dx2, gain_one)
     input_grad = crossed(input_grad).astype(F32)
 
     zero = jnp.zeros((D,), F32)

time: 735 us -> 678 us (0.922)
  Pallas kernels: 229 us -> 201 us
  waiting for transfers between devices: 248 us -> 224 us
  starting transfers between devices: 165 us -> 148 us
  local copies, waits for them, and re-layouts: 20.5 us -> 30.6 us
    pallas_call x1, Pallas kernels: 33.6 us -> 3 us  [gather_rows(): pl.pallas_call(functools.partial(gather_kernel, keys), in_specs=[SM] + [A...]
    ppermute x73, waiting for transfers between devices: 221 us -> 191 us  [shift(): return lax.ppermute(value, axis, [(i, (i + up) % n) for i in range(n)])]
    ppermute x73, starting transfers between devices: 134 us -> 112 us  [shift(): return lax.ppermute(value, axis, [(i, (i + up) % n) for i in range(n)])]
    unnamed x138 -> x184, local copies, waits for them, and re-layouts: 13.7 us -> 17.5 us
  transfers between devices with their start and end apart: 81 -> 81, of which waited for: 32 -> 31; matrix products, arithmetic and copies ran while one was open for 9% -> 10% of each run, Pallas kernels for 13% -> 19%
where the time goes in v2:
time: 678 us; the launch traced here: 673 us
  waiting for transfers between devices  224 us (33%)
  Pallas kernels  201 us (30%)
  starting transfers between devices  148 us (22%)
  other arithmetic  61 us (9%)
  local copies, waits for them, and re-layouts  30.6 us (5%)
  between operations  8.08 us (1%)
    ppermute x73, waiting for transfers between devices, shift(): return lax.ppermute(value, axis, [(i, (i + up) % n) for i in range(n)])  191 us
    ppermute x73, starting transfers between devices, shift(): return lax.ppermute(value, axis, [(i, (i + up) % n) for i in range(n)])  112 us
    pallas_call x1, Pallas kernels, mlp(): pl.pallas_call(functools.partial(mlp_kernel, keys, gtile=min(gtile, width...  73.8 us
    ppermute x8, starting transfers between devices, crossing(): return lax.ppermute(value, ('seq', 'core'), [(1, 2), (2, 1)])  36.3 us
    ppermute x8, waiting for transfers between devices, crossing(): return lax.ppermute(value, ('seq', 'core'), [(1, 2), (2, 1)])  33.2 us
    pallas_call x1, Pallas kernels, attend_back(): pl.pallas_call(functools.partial(attend_back_kernel, pairs=pairs, chunk=c...  30.5 us
    pallas_call x1, Pallas kernels, attend(): pl.pallas_call(attend_kernel, grid=(n, pairs), in_specs=[blk(0), blk(pair...  20.7 us
    unnamed x184, local copies, waits for them, and re-layouts  17.5 us
  transfers between devices with their start and end apart: 81, of which 31 were waited for; matrix products, arithmetic and copies ran while one was open for 10% of the time, Pallas kernels for 19%

profile of v2, /device:TPU:1, one launch (start us, length us, event | category | flops | bytes accessed | tf_op | source)
XLA Modules:
  0.0 672.7 jit_solution(8992663829546868990)
XLA Ops:
  0.7 5.6 collective-permute-start
  11.6 29.4 %collective-permute-done.1 = bf16[64,1536]{1,0:T(8,128)(2,1)S(1)} collective-permute-done((bf16[64,1536]{1,0:T(8,128)(2,1)S(1)}, bf16[64,1536]{1,0:T(8,128)(2,1)S(1)}, u32[]{:S(2)}, u32[]{:S(2)}) %collective-permute-start.1) | collective-permute-done | bytes 196640 | tf_op jit(solution)/shard_map/ppermute | solution.py:439
  42.3 2.9 collective-permute-done.6
  53.3 2.9 collective-permute-done.2.refs_2_
  57.7 20.7 %collective-permute-start.15 = (f32[3,584]{1,0:T(4,128)S(1)}, f32[3,584]{1,0:T(4,128)S(1)}, u32[]{:S(2)}, u32[]{:S(2)}) collective-permute-start(f32[3,584]{1,0:T(4,128)S(1)} %convert_element_type.310), channel_id=1, source_target_pairs={{0,2},{2,0},{1,3},{3,1},{4,6},{6,4},{5,7},{7,5},{8,10},{10,8},{9,1... | collective-permute-start | bytes 21032 | tf_op jit(solution)/shard_map/ppermute | solution.py:439
  88.5 5.0 collective-permute-start.17
  95.2 2.3 collective-permute-done.17
  99.3 4.0 collective-permute-start.22
  103.6 4.0 collective-permute-start.27
  112.7 14.7 %project.1 = (bf16[3,2,304,1024]{3,2,1,0:T(8,128)(2,1)}, bf16[3,2,304,1536]{3,2,1,0:T(8,128)(2,1)}) custom-call(s32[8]{0:T(128)S(1)} %stack.70.at_ref.refs_0_, bf16[3,292,1024]{2,1,0:T(8,128)(2,1)} %copy-done, bf16[3,292,1024]{2,1,0:T(8,128)(2,1)} %collective-permute-done.10.oth_ref, f32[1,1024]{1,0:T(1,128)S(1)} %bitcast.116, f32[1,1024]{1,0:T(1,128)S(1)} %bitcast.122, ...), custom_call_target="tpu_custom_call" | custom-call | flops 5737807872 | bytes 25165824 | tf_op jit(solution)/shard_map/project/pallas_call | solution.py:293
  127.7 20.7 %attend.1 = (bf16[3,608,512]{2,1,0:T(8,128)(2,1)}, f32[3,4,8,608]{3,2,1,0:T(8,128)S(1)}) custom-call(bf16[3,608,1536]{2,1,0:T(8,128)(2,1)} %bitcast.123, bf16[3,608,1536]{2,1,0:T(8,128)(2,1)} %bitcast.124, bf16[3,608,1536]{2,1,0:T(8,128)(2,1)} %bitcast.125, bf16[3,608,128]{2,1,0:T(8,128)(2,1)S(1)} %broadcast_in_dim.71.kb_ref), custom_call_target="tpu_custom_call" | custom-call | flops 4542431232 | bytes 8404992 | tf_op jit(solution)/shard_map/attend/pallas_call | solution.py:181
  149.4 1.9 collective-permute-start.33
  151.4 2.4 collective-permute-done.24.refs_6_
  154.0 3.6 collective-permute-done.23.refs_5_
  157.8 3.6 collective-permute-done.25.refs_7_
  162.1 3.0 gather_rows.1.wo_ref.w_ref
  165.1 3.7 collective-permute-start.26
  168.8 2.2 pad_maximum_fusion.refs_5_
  171.3 4.0 collective-permute-done.33
  177.7 3.8 collective-permute-done.27
  181.4 2.9 broadcast_select_fusion.refs_2_.go_ref
  184.4 7.3 %collective-permute-start.28 = (bf16[3,292,1024]{2,1,0:T(8,128)(2,1)}, bf16[3,292,1024]{2,1,0:T(8,128)(2,1)}, u32[]{:S(2)}, u32[]{:S(2)}) collective-permute-start(bf16[3,292,1024]{2,1,0:T(8,128)(2,1)} %broadcast_select_fusion.refs_2_.go_ref), channel_id=1, source_target_pairs={{0,2},{2,0},{1,3},{3,1},{4,6},{6,4},{5,7},{7,5},{8,10},{10,8},{9,1... | collective-permute-start | bytes 5382152 | tf_op jit(solution)/shard_map/ppermute | solution.py:439
  191.7 4.4 collective-permute-done.30.refs_6_
  201.9 9.7 %middle.1 = (f32[3,2,304,1024]{3,2,1,0:T(8,128)}, bf16[3,2,304,1024]{3,2,1,0:T(8,128)(2,1)}) custom-call(bf16[3,292,1024]{2,1,0:T(8,128)(2,1)S(1)} %copy-done.1, bf16[3,292,1024]{2,1,0:T(8,128)(2,1)} %collective-permute-done.10.oth_ref, bf16[3,2,304,512]{3,2,1,0:T(8,128)(2,1)} %bitcast.11.mo_ref.mix_ref, ...), custom_call_target="tpu_custom_call" | custom-call | flops 3825205248 | bytes 27262976 | tf_op jit(solution)/shard_map/middle/pallas_call | solution.py:330
  211.6 10.1 %collective-permute-done.31.refs_7_ = bf16[2,2,128,1024]{3,2,1,0:T(8,128)(2,1)} collective-permute-done((bf16[2,2,128,1024]{3,2,1,0:T(8,128)(2,1)}, bf16[2,2,128,1024]{3,2,1,0:T(8,128)(2,1)}, u32[]{:S(2)}, u32[]{:S(2)}) %collective-permute-start.31) | collective-permute-done | bytes 1048608 | tf_op jit(solution)/shard_map/ppermute | solution.py:439
  221.7 22.5 %collective-permute-done.32.refs_8_ = bf16[2,2,128,1024]{3,2,1,0:T(8,128)(2,1)} collective-permute-done((bf16[2,2,128,1024]{3,2,1,0:T(8,128)(2,1)}, bf16[2,2,128,1024]{3,2,1,0:T(8,128)(2,1)}, u32[]{:S(2)}, u32[]{:S(2)}) %collective-permute-start.32) | collective-permute-done | bytes 1048608 | tf_op jit(solution)/shard_map/ppermute | solution.py:439
  244.2 73.8 %feed_forward.1 = (bf16[2,2,128,1024]{3,2,1,0:T(8,128)(2,1)}, bf16[2,2,128,1024]{3,2,1,0:T(8,128)(2,1)}, bf16[2,2,128,1024]{3,2,1,0:T(8,128)(2,1)}, bf16[2,2,128...) custom-call(s32[8]{0:T(128)} %copy-done.12, ...), custom_call_target="tpu_custom_call" | custom-call | flops 45902462976 | bytes 41943040 | tf_op jit(solution)/shard_map/feed_forward/pallas_call | solution.py:139
  318.0 4.7 collective-permute-start.37
  325.4 6.4 collective-permute-done.78
  333.0 6.0 fusion.2
  339.0 15.7 %middle_back.1 = (f32[3,304,1024]{2,1,0:T(8,128)}, bf16[3,2,304,512]{3,2,1,0:T(8,128)(2,1)}, bf16[512,1024]{1,0:T(8,128)(2,1)}, f32[8,1024]{1,0:T(8,128)}) custom-call(f32[3,2,304,1024]{3,2,1,0:T(8,128)} %get-tuple-element.98.x2_ref, bf16[3,2,304,1024]{3,2,1,0:T(8,128)(2,1)} %bitcast.130, bf16[3,2,304,1024]{3,2,1,0:T(8,128)(2,1)} %collective-permute-done.37.db_ref, ...), custom_call_target="tpu_custom_call" | custom-call | flops 3825205248 | bytes 31457280 | tf_op jit(solution)/shard_map/middle_back/pallas_call | solution.py:364
  354.7 30.5 %attend_back.1 = (bf16[3,608,1536]{2,1,0:T(8,128)(2,1)}, f32[8,1536]{1,0:T(8,128)S(1)}) custom-call(bf16[3,608,1536]{2,1,0:T(8,128)(2,1)} %bitcast.126, bf16[3,608,1536]{2,1,0:T(8,128)(2,1)} %bitcast.127, bf16[3,608,1536]{2,1,0:T(8,128)(2,1)} %bitcast.128, bf16[3,608,128]{2,1,0:T(8,128)(2,1)S(1)} %broadcast_in_dim.71.kb_ref, ...), custom_call_target="tpu_custom_call" | custom-call | flops 11356078080 | bytes 14008320 | tf_op jit(solution)/shard_map/attend_back/pallas_call | solution.py:229
  385.2 15.3 %grad_in.1 = (bf16[2,64,1536]{2,1,0:T(8,128)(2,1)S(1)}, bf16[2,64,1536]{2,1,0:T(8,128)(2,1)S(1)}, bf16[2,64,1536]{2,1,0:T(8,128)(2,1)S(1)}, bf16[2,64,1536]{2,1,...) custom-call(s32[8]{0:T(128)S(1)} %copy-done.13, ...), custom_call_target="tpu_custom_call" | custom-call | flops 5737807872 | bytes 14680064 | tf_op jit(solution)/shard_map/grad_in/pallas_call | solution.py:383
  409.1 13.4 %project_back.1 = (f32[3,304,1024]{2,1,0:T(8,128)}, bf16[3,304,1024]{2,1,0:T(8,128)(2,1)}) custom-call(s32[8]{0:T(128)S(1)} %copy-done.13, bf16[3,2,304,1536]{3,2,1,0:T(8,128)(2,1)} %bitcast.152, bf16[2,64,1536]{2,1,0:T(8,128)(2,1)S(1)} %copy-done.8, bf16[2,64,1536]{2,1,0:T(8,128)(2,1)S(1)} %copy-done.17, bf16[2,64,1536]{2,1,0:T(8,128)(2,1)S(1)} %copy-done.23, ...), custom_call_target="tpu_custom_call" | custom-call | flops 5737807872 | bytes 18874368 | tf_op jit(solution)/shard_map/project_back/pallas_call | solution.py:404
  432.2 5.6 collective-permute-start.55
  438.9 4.5 collective-permute-start.68
  443.4 3.1 collective-permute-done.40
  446.6 6.5 collective-permute-start.79
  455.2 22.3 %collective-permute-done.43 = bf16[2,64,1536]{2,1,0:T(8,128)(2,1)S(1)} collective-permute-done((bf16[2,64,1536]{2,1,0:T(8,128)(2,1)S(1)}, bf16[2,64,1536]{2,1,0:T(8,128)(2,1)S(1)}, u32[]{:S(2)}, u32[]{:S(2)}) %collective-permute-start.43) | collective-permute-done | bytes 393248 | tf_op jit(solution)/shard_map/ppermute | solution.py:439
  478.7 6.5 collective-permute-done.39
  485.4 9.8 %collective-permute-done.45 = bf16[64,1536]{1,0:T(8,128)(2,1)S(1)} collective-permute-done((bf16[64,1536]{1,0:T(8,128)(2,1)S(1)}, bf16[64,1536]{1,0:T(8,128)(2,1)S(1)}, u32[]{:S(2)}, u32[]{:S(2)}) %collective-permute-start.45) | collective-permute-done | bytes 196640 | tf_op jit(solution)/shard_map/ppermute | solution.py:439
  495.9 7.2 %collective-permute-done.41 = bf16[64,1536]{1,0:T(8,128)(2,1)S(1)} collective-permute-done((bf16[64,1536]{1,0:T(8,128)(2,1)S(1)}, bf16[64,1536]{1,0:T(8,128)(2,1)S(1)}, u32[]{:S(2)}, u32[]{:S(2)}) %collective-permute-start.41) | collective-permute-done | bytes 196640 | tf_op jit(solution)/shard_map/ppermute | solution.py:439
  503.1 10.1 %collective-permute-start.46 = (bf16[64,1536]{1,0:T(8,128)(2,1)}, bf16[64,1536]{1,0:T(8,128)(2,1)}, u32[]{:S(2)}, u32[]{:S(2)}) collective-permute-start(bf16[64,1536]{1,0:T(8,128)(2,1)} %fusion.14), channel_id=1, source_target_pairs={{0,2},{2,0},{1,3},{3,1},{4,6},{6,4},{5,7},{7,5},{8,10},{10,8},{9,1... | collective-permute-start | bytes 589832 | tf_op jit(solution)/shard_map/ppermute | solution.py:439
  517.3 2.4 collective-permute-start.61
  522.1 2.1 collective-permute-start.51
  530.3 21.0 %collective-permute-done.65 = bf16[2,128,1024]{2,1,0:T(8,128)(2,1)} collective-permute-done((bf16[2,128,1024]{2,1,0:T(8,128)(2,1)}, bf16[2,128,1024]{2,1,0:T(8,128)(2,1)}, u32[]{:S(2)}, u32[]{:S(2)}) %collective-permute-start.65) | collective-permute-done | bytes 524320 | tf_op jit(solution)/shard_map/ppermute | solution.py:439
  551.8 10.8 %collective-permute-done.61 = bf16[2,128,1024]{2,1,0:T(8,128)(2,1)} collective-permute-done((bf16[2,128,1024]{2,1,0:T(8,128)(2,1)}, bf16[2,128,1024]{2,1,0:T(8,128)(2,1)}, u32[]{:S(2)}, u32[]{:S(2)}) %collective-permute-start.61) | collective-permute-done | bytes 524320 | tf_op jit(solution)/shard_map/ppermute | solution.py:439
  567.0 2.1 copy-done.4
  569.1 4.1 input_back.1
  577.5 4.8 collective-permute-done.69
  582.4 3.9 collective-permute-start.70
  590.4 2.3 collective-permute-done.71
  592.7 6.1 collective-permute-start.72
  602.0 1.9 fusion.3
  608.6 2.2 collective-permute-done.74
  616.1 3.3 collective-permute-start.77
  619.4 3.6 select_convert_fusion.1
  622.9 3.5 collective-permute-start.80
  628.5 2.2 fusion.33
  630.7 4.3 fusion.31
  635.1 2.5 fusion.29
  637.6 3.0 fusion.35
  640.6 27.2 %collective-permute-done.80 = bf16[3,292,1024]{2,1,0:T(8,128)(2,1)} collective-permute-done((bf16[3,292,1024]{2,1,0:T(8,128)(2,1)S(1)}, bf16[3,292,1024]{2,1,0:T(8,128)(2,1)}, u32[]{:S(2)}, u32[]{:S(2)}) %collective-permute-start.80) | collective-permute-done | bytes 1794080 | tf_op jit(solution)/shard_map/ppermute | solution.py:447
  667.8 3.6 select_convert_fusion
  (398 shorter events, 109.5 us)
Async XLA Ops:
  0.7 79.2 %collective-permute-start = (bf16[3,292,1024]{2,1,0:T(8,128)(2,1)}, bf16[3,292,1024]{2,1,0:T(8,128)(2,1)}, u32[]{:S(2)}, u32[]{:S(2)}) collective-permute-start(bf16[3,292,1024]{2,1,0:T(8,128)(2,1)} %param.19), channel_id=1, source_target_pairs={{2,16},{16,2},{3,17},{17,3},{6,20},{20,6},{7,21},{21,7},{10,24},{2... | collective-permute-start | bytes 5382152 | tf_op jit(solution)/shard_map/ppermute | solution.py:447
  8.8 32.2 %collective-permute-start.1 = (bf16[64,1536]{1,0:T(8,128)(2,1)S(1)}, bf16[64,1536]{1,0:T(8,128)(2,1)S(1)}, u32[]{:S(2)}, u32[]{:S(2)}) collective-permute-start(bf16[64,1536]{1,0:T(8,128)(2,1)S(1)} %bitcast.137), channel_id=1, source_target_pairs={{0,16},{16,0},{1,17},{17,1},{2,18},{18,2},{3,19},{19,3},{4,20},{20... | collective-permute-start | bytes 589832 | tf_op jit(solution)/shard_map/ppermute | solution.py:439
  10.2 35.0 %collective-permute-start.6 = (bf16[64,1536]{1,0:T(8,128)(2,1)S(1)}, bf16[64,1536]{1,0:T(8,128)(2,1)S(1)}, u32[]{:S(2)}, u32[]{:S(2)}) collective-permute-start(bf16[64,1536]{1,0:T(8,128)(2,1)S(1)} %collective-permute-done.5), channel_id=1, source_target_pairs={{0,16},{16,0},{1,17},{17,1},{2,18},{18,2},{3,19},{19,3},{4,20},{20... | collective-permute-start | bytes 589832 | tf_op jit(solution)/shard_map/ppermute | solution.py:439
  41.1 8.6 %collective-permute-start.3 = (bf16[2,64,1536]{2,1,0:T(8,128)(2,1)S(1)}, bf16[2,64,1536]{2,1,0:T(8,128)(2,1)S(1)}, u32[]{:S(2)}, u32[]{:S(2)}) collective-permute-start(bf16[2,64,1536]{2,1,0:T(8,128)(2,1)S(1)} %pad_maximum_fusion.5.refs_0_), channel_id=1, source_target_pairs={{0,4},{4,0},{1,5},{5,1},{2,6},{6,2},{3,7},{7,3},{8,12},{12,8},{9,1... | collective-permute-start | bytes 1179656 | tf_op jit(solution)/shard_map/ppermute | solution.py:439
  45.3 6.7 collective-permute-start.8
  48.2 8.0 %collective-permute-start.2 = (bf16[2,64,1536]{2,1,0:T(8,128)(2,1)S(1)}, bf16[2,64,1536]{2,1,0:T(8,128)(2,1)S(1)}, u32[]{:S(2)}, u32[]{:S(2)}) collective-permute-start(bf16[2,64,1536]{2,1,0:T(8,128)(2,1)S(1)} %pad_maximum_fusion.5.refs_0_), channel_id=1, source_target_pairs={{0,8},{8,0},{1,9},{9,1},{2,10},{10,2},{3,11},{11,3},{4,12},{12,4},... | collective-permute-start | bytes 1179656 | tf_op jit(solution)/shard_map/ppermute | solution.py:439
  48.4 8.5 %collective-permute-start.7 = (bf16[2,64,1536]{2,1,0:T(8,128)(2,1)S(1)}, bf16[2,64,1536]{2,1,0:T(8,128)(2,1)S(1)}, u32[]{:S(2)}, u32[]{:S(2)}) collective-permute-start(bf16[2,64,1536]{2,1,0:T(8,128)(2,1)S(1)} %pad_maximum_fusion.6.refs_4_), channel_id=1, source_target_pairs={{0,4},{4,0},{1,5},{5,1},{2,6},{6,2},{3,7},{7,3},{8,12},{12,8},{9,1... | collective-permute-start | bytes 1179656 | tf_op jit(solution)/shard_map/ppermute | solution.py:439
  49.7 28.7 %collective-permute-start.4 = (bf16[2,64,1536]{2,1,0:T(8,128)(2,1)S(1)}, bf16[2,64,1536]{2,1,0:T(8,128)(2,1)S(1)}, u32[]{:S(2)}, u32[]{:S(2)}) collective-permute-start(bf16[2,64,1536]{2,1,0:T(8,128)(2,1)S(1)} %collective-permute-done.3.refs_1_), channel_id=1, source_target_pairs={{0,8},{8,0},{1,9},{9,1},{2,10},{10,2},{3,11},{11,3},{4,12},{12,4},... | collective-permute-start | bytes 1179656 | tf_op jit(solution)/shard_map/ppermute | solution.py:439
  52.0 27.1 %collective-permute-start.9 = (bf16[2,64,1536]{2,1,0:T(8,128)(2,1)S(1)}, bf16[2,64,1536]{2,1,0:T(8,128)(2,1)S(1)}, u32[]{:S(2)}, u32[]{:S(2)}) collective-permute-start(bf16[2,64,1536]{2,1,0:T(8,128)(2,1)S(1)} %collective-permute-done.8.refs_6_), channel_id=1, source_target_pairs={{0,4},{4,0},{1,5},{5,1},{2,6},{6,2},{3,7},{7,3},{8,12},{12,8},{9,1... | collective-permute-start | bytes 1179656 | tf_op jit(solution)/shard_map/ppermute | solution.py:439
  56.9 27.5 %collective-permute-start.11 = (bf16[16,768]{1,0:T(8,128)(2,1)S(1)}, bf16[16,768]{1,0:T(8,128)(2,1)S(1)}, u32[]{:S(2)}, u32[]{:S(2)}) collective-permute-start(bf16[16,768]{1,0:T(8,128)(2,1)S(1)} %broadcast_select_fusion.7), channel_id=1, source_target_pairs={{0,16},{16,0},{1,17},{17,1},{2,18},{18,2},{3,19},{19,3},{4,20},{20... | collective-permute-start | bytes 73736 | tf_op jit(solution)/shard_map/ppermute | solution.py:439
  57.7 28.1 %collective-permute-start.15 = (f32[3,584]{1,0:T(4,128)S(1)}, f32[3,584]{1,0:T(4,128)S(1)}, u32[]{:S(2)}, u32[]{:S(2)}) collective-permute-start(f32[3,584]{1,0:T(4,128)S(1)} %convert_element_type.310), channel_id=1, source_target_pairs={{0,2},{2,0},{1,3},{3,1},{4,6},{6,4},{5,7},{7,5},{8,10},{10,8},{9,1... | collective-permute-start | bytes 21032 | tf_op jit(solution)/shard_map/ppermute | solution.py:439
  81.6 22.0 %collective-permute-start.10 = (bf16[3,292,1024]{2,1,0:T(8,128)(2,1)S(1)}, bf16[3,292,1024]{2,1,0:T(8,128)(2,1)}, u32[]{:S(2)}, u32[]{:S(2)}) collective-permute-start(bf16[3,292,1024]{2,1,0:T(8,128)(2,1)S(1)} %broadcast_select_fusion.1.own_ref.x_ref), channel_id=1, source_target_pairs={{0,2},{2,0},{1,3},{3,1},{4,6},{6,4},{5,7},{7,5},{8,10},{10,8},{9,1... | collective-permute-start | bytes 5382152 | tf_op jit(solution)/shard_map/ppermute | solution.py:439
  88.5 8.9 %collective-permute-start.17 = (bf16[64,1024]{1,0:T(8,128)(2,1)S(1)}, bf16[64,1024]{1,0:T(8,128)(2,1)S(1)}, u32[]{:S(2)}, u32[]{:S(2)}) collective-permute-start(bf16[64,1024]{1,0:T(8,128)(2,1)S(1)} %convert_element_type.313), channel_id=1, source_target_pairs={{2,16},{16,2},{3,17},{17,3},{6,20},{20,6},{7,21},{21,7},{10,24},{2... | collective-permute-start | bytes 393224 | tf_op jit(solution)/shard_map/ppermute | solution.py:447
  97.9 70.9 %collective-permute-start.29 = (bf16[2,128,1024]{2,1,0:T(8,128)(2,1)}, bf16[2,128,1024]{2,1,0:T(8,128)(2,1)}, u32[]{:S(2)}, u32[]{:S(2)}) collective-permute-start(bf16[2,128,1024]{2,1,0:T(8,128)(2,1)} %get-tuple-element.102), channel_id=1, source_target_pairs={{0,16},{16,0},{1,17},{17,1},{2,18},{18,2},{3,19},{19,3},{4,20},{20... | collective-permute-start | bytes 1572872 | tf_op jit(solution)/shard_map/ppermute | solution.py:439
  98.0 51.1 %collective-permute-start.19 = (bf16[64,1024]{1,0:T(8,128)(2,1)S(1)}, bf16[64,1024]{1,0:T(8,128)(2,1)S(1)}, u32[]{:S(2)}, u32[]{:S(2)}) collective-permute-start(bf16[64,1024]{1,0:T(8,128)(2,1)S(1)} %broadcast_select_fusion.6.refs_0_), channel_id=1, source_target_pairs={{0,8},{8,0},{1,9},{9,1},{2,10},{10,2},{3,11},{11,3},{4,12},{12,4},... | collective-permute-start | bytes 393224 | tf_op jit(solution)/shard_map/ppermute | solution.py:439
  99.3 49.7 %collective-permute-start.22 = (bf16[64,1024]{1,0:T(8,128)(2,1)S(1)}, bf16[64,1024]{1,0:T(8,128)(2,1)S(1)}, u32[]{:S(2)}, u32[]{:S(2)}) collective-permute-start(bf16[64,1024]{1,0:T(8,128)(2,1)S(1)} %collective-permute-done.21), channel_id=1, source_target_pairs={{2,16},{16,2},{3,17},{17,3},{6,20},{20,6},{7,21},{21,7},{10,24},{2... | collective-permute-start | bytes 393224 | tf_op jit(solution)/shard_map/ppermute | solution.py:447
  103.3 46.1 %collective-permute-start.20 = (bf16[64,1024]{1,0:T(8,128)(2,1)S(1)}, bf16[64,1024]{1,0:T(8,128)(2,1)S(1)}, u32[]{:S(2)}, u32[]{:S(2)}) collective-permute-start(bf16[64,1024]{1,0:T(8,128)(2,1)S(1)} %collective-permute-done.18.refs_1_), channel_id=1, source_target_pairs={{0,8},{8,0},{1,9},{9,1},{2,10},{10,2},{3,11},{11,3},{4,12},{12,4},... | collective-permute-start | bytes 393224 | tf_op jit(solution)/shard_map/ppermute | solution.py:439
  103.6 77.8 %collective-permute-start.27 = (bf16[3,292,1024]{2,1,0:T(8,128)(2,1)}, bf16[3,292,1024]{2,1,0:T(8,128)(2,1)}, u32[]{:S(2)}, u32[]{:S(2)}) collective-permute-start(bf16[3,292,1024]{2,1,0:T(8,128)(2,1)} %param.21), channel_id=1, source_target_pairs={{2,16},{16,2},{3,17},{17,3},{6,20},{20,6},{7,21},{21,7},{10,24},{2... | collective-permute-start | bytes 5382152 | tf_op jit(solution)/shard_map/ppermute | solution.py:447
  149.1 49.8 %collective-permute-start.16 = (bf16[3,2,304,512]{3,2,1,0:T(8,128)(2,1)}, bf16[3,2,304,512]{3,2,1,0:T(8,128)(2,1)}, u32[]{:S(2)}, u32[]{:S(2)}) collective-permute-start(bf16[3,2,304,512]{3,2,1,0:T(8,128)(2,1)} %bitcast.11.mo_ref.mix_ref), channel_id=1, source_target_pairs={{0,2},{2,0},{1,3},{3,1},{4,6},{6,4},{5,7},{7,5},{8,10},{10,8},{9,1... | collective-permute-start | bytes 5603336 | tf_op jit(solution)/shard_map/ppermute | solution.py:439
  149.4 25.9 %collective-permute-start.33 = (bf16[2,128,1024]{2,1,0:T(8,128)(2,1)S(1)}, bf16[2,128,1024]{2,1,0:T(8,128)(2,1)S(1)}, u32[]{:S(2)}, u32[]{:S(2)}) collective-permute-start(bf16[2,128,1024]{2,1,0:T(8,128)(2,1)S(1)} %copy-done.66), channel_id=1, source_target_pairs={{0,16},{16,0},{1,17},{17,1},{2,18},{18,2},{3,19},{19,3},{4,20},{20... | collective-permute-start | bytes 1572872 | tf_op jit(solution)/shard_map/ppermute | solution.py:439
  165.1 32.5 %collective-permute-start.26 = (bf16[512,1024]{1,0:T(8,128)(2,1)}, bf16[512,1024]{1,0:T(8,128)(2,1)S(1)}, u32[]{:S(2)}, u32[]{:S(2)}) collective-permute-start(bf16[512,1024]{1,0:T(8,128)(2,1)} %gather_rows.1.wo_ref.w_ref), channel_id=1, source_target_pairs={{0,2},{2,0},{1,3},{3,1},{4,6},{6,4},{5,7},{7,5},{8,10},{10,8},{9,1... | collective-permute-start | bytes 3145736 | tf_op jit(solution)/shard_map/ppermute | solution.py:439
  171.1 25.1 %collective-permute-start.30 = (bf16[2,2,128,1024]{3,2,1,0:T(8,128)(2,1)}, bf16[2,2,128,1024]{3,2,1,0:T(8,128)(2,1)}, u32[]{:S(2)}, u32[]{:S(2)}) collective-permute-start(bf16[2,2,128,1024]{3,2,1,0:T(8,128)(2,1)} %pad_maximum_fusion.refs_5_), channel_id=1, source_target_pairs={{0,4},{4,0},{1,5},{5,1},{2,6},{6,2},{3,7},{7,3},{8,12},{12,8},{9,1... | collective-permute-start | bytes 3145736 | tf_op jit(solution)/shard_map/ppermute | solution.py:439
  176.4 19.9 %collective-permute-start.35 = (bf16[2,2,128,1024]{3,2,1,0:T(8,128)(2,1)}, bf16[2,2,128,1024]{3,2,1,0:T(8,128)(2,1)}, u32[]{:S(2)}, u32[]{:S(2)}) collective-permute-start(bf16[2,2,128,1024]{3,2,1,0:T(8,128)(2,1)} %pad_maximum_fusion.1.refs_9_), channel_id=1, source_target_pairs={{0,8},{8,0},{1,9},{9,1},{2,10},{10,2},{3,11},{11,3},{4,12},{12,4},... | collective-permute-start | bytes 3145736 | tf_op jit(solution)/shard_map/ppermute | solution.py:439
  184.4 59.8 %collective-permute-start.28 = (bf16[3,292,1024]{2,1,0:T(8,128)(2,1)}, bf16[3,292,1024]{2,1,0:T(8,128)(2,1)}, u32[]{:S(2)}, u32[]{:S(2)}) collective-permute-start(bf16[3,292,1024]{2,1,0:T(8,128)(2,1)} %broadcast_select_fusion.refs_2_.go_ref), channel_id=1, source_target_pairs={{0,2},{2,0},{1,3},{3,1},{4,6},{6,4},{5,7},{7,5},{8,10},{10,8},{9,1... | collective-permute-start | bytes 5382152 | tf_op jit(solution)/shard_map/ppermute | solution.py:439
  196.1 25.6 %collective-permute-start.31 = (bf16[2,2,128,1024]{3,2,1,0:T(8,128)(2,1)}, bf16[2,2,128,1024]{3,2,1,0:T(8,128)(2,1)}, u32[]{:S(2)}, u32[]{:S(2)}) collective-permute-start(bf16[2,2,128,1024]{3,2,1,0:T(8,128)(2,1)} %pad_maximum_fusion.refs_5_), channel_id=1, source_target_pairs={{0,8},{8,0},{1,9},{9,1},{2,10},{10,2},{3,11},{11,3},{4,12},{12,4},... | collective-permute-start | bytes 3145736 | tf_op jit(solution)/shard_map/ppermute | solution.py:439
  196.4 25.3 %collective-permute-start.34 = (bf16[2,2,128,1024]{3,2,1,0:T(8,128)(2,1)}, bf16[2,2,128,1024]{3,2,1,0:T(8,128)(2,1)}, u32[]{:S(2)}, u32[]{:S(2)}) collective-permute-start(bf16[2,2,128,1024]{3,2,1,0:T(8,128)(2,1)} %pad_maximum_fusion.1.refs_9_), channel_id=1, source_target_pairs={{0,4},{4,0},{1,5},{5,1},{2,6},{6,2},{3,7},{7,3},{8,12},{12,8},{9,1... | collective-permute-start | bytes 3145736 | tf_op jit(solution)/shard_map/ppermute | solution.py:439
  198.5 45.6 %collective-permute-start.32 = (bf16[2,2,128,1024]{3,2,1,0:T(8,128)(2,1)}, bf16[2,2,128,1024]{3,2,1,0:T(8,128)(2,1)}, u32[]{:S(2)}, u32[]{:S(2)}) collective-permute-start(bf16[2,2,128,1024]{3,2,1,0:T(8,128)(2,1)} %collective-permute-done.30.refs_6_), channel_id=1, source_target_pairs={{0,8},{8,0},{1,9},{9,1},{2,10},{10,2},{3,11},{11,3},{4,12},{12,4},... | collective-permute-start | bytes 3145736 | tf_op jit(solution)/shard_map/ppermute | solution.py:439
  198.8 45.3 %collective-permute-start.36 = (bf16[2,2,128,1024]{3,2,1,0:T(8,128)(2,1)}, bf16[2,2,128,1024]{3,2,1,0:T(8,128)(2,1)}, u32[]{:S(2)}, u32[]{:S(2)}) collective-permute-start(bf16[2,2,128,1024]{3,2,1,0:T(8,128)(2,1)} %collective-permute-done.35.refs_11_), channel_id=1, source_target_pairs={{0,4},{4,0},{1,5},{5,1},{2,6},{6,2},{3,7},{7,3},{8,12},{12,8},{9,1... | collective-permute-start | bytes 3145736 | tf_op jit(solution)/shard_map/ppermute | solution.py:439
  318.0 21.1 %collective-permute-start.37 = (bf16[3,2,304,1024]{3,2,1,0:T(8,128)(2,1)}, bf16[3,2,304,1024]{3,2,1,0:T(8,128)(2,1)}, u32[]{:S(2)}, u32[]{:S(2)}) collective-permute-start(bf16[3,2,304,1024]{3,2,1,0:T(8,128)(2,1)} %bitcast.129), channel_id=1, source_target_pairs={{0,2},{2,0},{1,3},{3,1},{4,6},{6,4},{5,7},{7,5},{8,10},{10,8},{9,1... | collective-permute-start | bytes 11206664 | tf_op jit(solution)/shard_map/ppermute | solution.py:439
  322.6 9.1 %collective-permute-start.78 = (bf16[3,304,1024]{2,1,0:T(8,128)(2,1)}, bf16[3,304,1024]{2,1,0:T(8,128)(2,1)}, u32[]{:S(2)}, u32[]{:S(2)}) collective-permute-start(bf16[3,304,1024]{2,1,0:T(8,128)(2,1)} %get-tuple-element.159), channel_id=1, source_target_pairs={{0,2},{2,0},{1,3},{3,1},{4,6},{6,4},{5,7},{7,5},{8,10},{10,8},{9,1... | collective-permute-start | bytes 5603336 | tf_op jit(solution)/shard_map/ppermute | solution.py:439
  322.7 79.9 %collective-permute-start.62 = (bf16[2,2,128,1024]{3,2,1,0:T(8,128)(2,1)}, bf16[2,2,128,1024]{3,2,1,0:T(8,128)(2,1)S(1)}, u32[]{:S(2)}, u32[]{:S(2)}) collective-permute-start(bf16[2,2,128,1024]{3,2,1,0:T(8,128)(2,1)} %get-tuple-element.144), channel_id=1, source_target_pairs={{0,4},{4,0},{1,5},{5,1},{2,6},{6,2},{3,7},{7,3},{8,12},{12,8},{9,1... | collective-permute-start | bytes 3145736 | tf_op jit(solution)/shard_map/ppermute | solution.py:439
  323.9 78.9 %collective-permute-start.64 = (bf16[2,2,128,1024]{3,2,1,0:T(8,128)(2,1)}, bf16[2,2,128,1024]{3,2,1,0:T(8,128)(2,1)S(1)}, u32[]{:S(2)}, u32[]{:S(2)}) collective-permute-start(bf16[2,2,128,1024]{3,2,1,0:T(8,128)(2,1)} %get-tuple-element.148), channel_id=1, source_target_pairs={{0,4},{4,0},{1,5},{5,1},{2,6},{6,2},{3,7},{7,3},{8,12},{12,8},{9,1... | collective-permute-start | bytes 3145736 | tf_op jit(solution)/shard_map/ppermute | solution.py:439
  324.2 78.9 %collective-permute-start.58 = (bf16[2,2,128,1024]{3,2,1,0:T(8,128)(2,1)}, bf16[2,2,128,1024]{3,2,1,0:T(8,128)(2,1)S(1)}, u32[]{:S(2)}, u32[]{:S(2)}) collective-permute-start(bf16[2,2,128,1024]{3,2,1,0:T(8,128)(2,1)} %get-tuple-element.136), channel_id=1, source_target_pairs={{0,8},{8,0},{1,9},{9,1},{2,10},{10,2},{3,11},{11,3},{4,12},{12,4},... | collective-permute-start | bytes 3145736 | tf_op jit(solution)/shard_map/ppermute | solution.py:439
  331.8 72.5 %collective-permute-start.60 = (bf16[2,2,128,1024]{3,2,1,0:T(8,128)(2,1)}, bf16[2,2,128,1024]{3,2,1,0:T(8,128)(2,1)S(1)}, u32[]{:S(2)}, u32[]{:S(2)}) collective-permute-start(bf16[2,2,128,1024]{3,2,1,0:T(8,128)(2,1)} %get-tuple-element.140), channel_id=1, source_target_pairs={{0,8},{8,0},{1,9},{9,1},{2,10},{10,2},{3,11},{11,3},{4,12},{12,4},... | collective-permute-start | bytes 3145736 | tf_op jit(solution)/shard_map/ppermute | solution.py:439
  400.5 31.6 %collective-permute-start.42 = (bf16[2,64,1536]{2,1,0:T(8,128)(2,1)}, bf16[2,64,1536]{2,1,0:T(8,128)(2,1)}, u32[]{:S(2)}, u32[]{:S(2)}) collective-permute-start(bf16[2,64,1536]{2,1,0:T(8,128)(2,1)} %get-tuple-element.121), channel_id=1, source_target_pairs={{0,4},{4,0},{1,5},{5,1},{2,6},{6,2},{3,7},{7,3},{8,12},{12,8},{9,1... | collective-permute-start | bytes 1179656 | tf_op jit(solution)/shard_map/ppermute | solution.py:439
  402.6 21.0 %collective-permute-start.48 = (bf16[64,1024]{1,0:T(8,128)(2,1)}, bf16[64,1024]{1,0:T(8,128)(2,1)}, u32[]{:S(2)}, u32[]{:S(2)}) collective-permute-start(bf16[64,1024]{1,0:T(8,128)(2,1)} %get-tuple-element.192), channel_id=1, source_target_pairs={{0,8},{8,0},{1,9},{9,1},{2,10},{10,2},{3,11},{11,3},{4,12},{12,4},... | collective-permute-start | bytes 393224 | tf_op jit(solution)/shard_map/ppermute | solution.py:439
  402.8 20.8 %collective-permute-start.52 = (bf16[64,1024]{1,0:T(8,128)(2,1)}, bf16[64,1024]{1,0:T(8,128)(2,1)}, u32[]{:S(2)}, u32[]{:S(2)}) collective-permute-start(bf16[64,1024]{1,0:T(8,128)(2,1)} %get-tuple-element.191), channel_id=1, source_target_pairs={{0,4},{4,0},{1,5},{5,1},{2,6},{6,2},{3,7},{7,3},{8,12},{12,8},{9,1... | collective-permute-start | bytes 393224 | tf_op jit(solution)/shard_map/ppermute | solution.py:439
  403.1 23.9 %collective-permute-start.50 = (bf16[64,1024]{1,0:T(8,128)(2,1)}, bf16[64,1024]{1,0:T(8,128)(2,1)}, u32[]{:S(2)}, u32[]{:S(2)}) collective-permute-start(bf16[64,1024]{1,0:T(8,128)(2,1)} %get-tuple-element.189), channel_id=1, source_target_pairs={{0,8},{8,0},{1,9},{9,1},{2,10},{10,2},{3,11},{11,3},{4,12},{12,4},... | collective-permute-start | bytes 393224 | tf_op jit(solution)/shard_map/ppermute | solution.py:439
  404.3 23.9 %collective-permute-start.54 = (bf16[64,1024]{1,0:T(8,128)(2,1)S(1)}, bf16[64,1024]{1,0:T(8,128)(2,1)}, u32[]{:S(2)}, u32[]{:S(2)}) collective-permute-start(bf16[64,1024]{1,0:T(8,128)(2,1)S(1)} %get-tuple-element.190), channel_id=1, source_target_pairs={{0,4},{4,0},{1,5},{5,1},{2,6},{6,2},{3,7},{7,3},{8,12},{12,8},{9,1... | collective-permute-start | bytes 393224 | tf_op jit(solution)/shard_map/ppermute | solution.py:439
  427.0 11.9 %collective-permute-start.44 = (bf16[2,64,1536]{2,1,0:T(8,128)(2,1)}, bf16[2,64,1536]{2,1,0:T(8,128)(2,1)S(1)}, u32[]{:S(2)}, u32[]{:S(2)}) collective-permute-start(bf16[2,64,1536]{2,1,0:T(8,128)(2,1)} %copy-done.35), channel_id=1, source_target_pairs={{0,4},{4,0},{1,5},{5,1},{2,6},{6,2},{3,7},{7,3},{8,12},{12,8},{9,1... | collective-permute-start | bytes 1179656 | tf_op jit(solution)/shard_map/ppermute | solution.py:439
  428.2 10.7 %collective-permute-start.38 = (bf16[2,64,1536]{2,1,0:T(8,128)(2,1)}, bf16[2,64,1536]{2,1,0:T(8,128)(2,1)S(1)}, u32[]{:S(2)}, u32[]{:S(2)}) collective-permute-start(bf16[2,64,1536]{2,1,0:T(8,128)(2,1)} %copy-done.34), channel_id=1, source_target_pairs={{0,8},{8,0},{1,9},{9,1},{2,10},{10,2},{3,11},{11,3},{4,12},{12,4},... | collective-permute-start | bytes 1179656 | tf_op jit(solution)/shard_map/ppermute | solution.py:439
  429.5 17.1 %collective-permute-start.40 = (bf16[2,64,1536]{2,1,0:T(8,128)(2,1)}, bf16[2,64,1536]{2,1,0:T(8,128)(2,1)S(1)}, u32[]{:S(2)}, u32[]{:S(2)}) collective-permute-start(bf16[2,64,1536]{2,1,0:T(8,128)(2,1)} %copy-done.33), channel_id=1, source_target_pairs={{0,8},{8,0},{1,9},{9,1},{2,10},{10,2},{3,11},{11,3},{4,12},{12,4},... | collective-permute-start | bytes 1179656 | tf_op jit(solution)/shard_map/ppermute | solution.py:439
  429.7 83.5 %collective-permute-start.63 = (bf16[2,2,128,1024]{3,2,1,0:T(8,128)(2,1)}, bf16[2,2,128,1024]{3,2,1,0:T(8,128)(2,1)S(1)}, u32[]{:S(2)}, u32[]{:S(2)}) collective-permute-start(bf16[2,2,128,1024]{3,2,1,0:T(8,128)(2,1)} %add_convert_fusion.2), channel_id=1, source_target_pairs={{0,8},{8,0},{1,9},{9,1},{2,10},{10,2},{3,11},{11,3},{4,12},{12,4},... | collective-permute-start | bytes 3145736 | tf_op jit(solution)/shard_map/ppermute | solution.py:439
  432.2 20.9 %collective-permute-start.55 = (bf16[64,1024]{1,0:T(8,128)(2,1)S(1)}, bf16[64,1024]{1,0:T(8,128)(2,1)S(1)}, u32[]{:S(2)}, u32[]{:S(2)}) collective-permute-start(bf16[64,1024]{1,0:T(8,128)(2,1)S(1)} %get-tuple-element.188), channel_id=1, source_target_pairs={{2,16},{16,2},{3,17},{17,3},{6,20},{20,6},{7,21},{21,7},{10,24},{2... | collective-permute-start | bytes 393224 | tf_op jit(solution)/shard_map/ppermute | solution.py:447
  438.9 75.9 %collective-permute-start.59 = (bf16[2,2,128,1024]{3,2,1,0:T(8,128)(2,1)S(1)}, bf16[2,2,128,1024]{3,2,1,0:T(8,128)(2,1)S(1)}, u32[]{:S(2)}, u32[]{:S(2)}) collective-permute-start(bf16[2,2,128,1024]{3,2,1,0:T(8,128)(2,1)S(1)} %copy-done.53), channel_id=1, source_target_pairs={{0,4},{4,0},{1,5},{5,1},{2,6},{6,2},{3,7},{7,3},{8,12},{12,8},{9,1... | collective-permute-start | bytes 3145736 | tf_op jit(solution)/shard_map/ppermute | solution.py:439
  438.9 126.5 %collective-permute-start.68 = (bf16[3,304,1024]{2,1,0:T(8,128)(2,1)}, bf16[3,304,1024]{2,1,0:T(8,128)(2,1)}, u32[]{:S(2)}, u32[]{:S(2)}) collective-permute-start(bf16[3,304,1024]{2,1,0:T(8,128)(2,1)} %get-tuple-element.152), channel_id=1, source_target_pairs={{0,2},{2,0},{1,3},{3,1},{4,6},{6,4},{5,7},{7,5},{8,10},{10,8},{9,1... | collective-permute-start | bytes 5603336 | tf_op jit(solution)/shard_map/ppermute | solution.py:439
  446.6 167.8 %collective-permute-start.79 = (bf16[3,292,1024]{2,1,0:T(8,128)(2,1)}, bf16[3,292,1024]{2,1,0:T(8,128)(2,1)}, u32[]{:S(2)}, u32[]{:S(2)}) collective-permute-start(bf16[3,292,1024]{2,1,0:T(8,128)(2,1)} %fusion.2), channel_id=1, source_target_pairs={{2,16},{16,2},{3,17},{17,3},{6,20},{20,6},{7,21},{21,7},{10,24},{2... | collective-permute-start | bytes 5382152 | tf_op jit(solution)/shard_map/ppermute | solution.py:447
  453.1 24.4 %collective-permute-start.43 = (bf16[2,64,1536]{2,1,0:T(8,128)(2,1)S(1)}, bf16[2,64,1536]{2,1,0:T(8,128)(2,1)S(1)}, u32[]{:S(2)}, u32[]{:S(2)}) collective-permute-start(bf16[2,64,1536]{2,1,0:T(8,128)(2,1)S(1)} %add_convert_fusion.8), channel_id=1, source_target_pairs={{0,8},{8,0},{1,9},{9,1},{2,10},{10,2},{3,11},{11,3},{4,12},{12,4},... | collective-permute-start | bytes 1179656 | tf_op jit(solution)/shard_map/ppermute | solution.py:439
  477.4 7.8 %collective-permute-start.39 = (bf16[2,64,1536]{2,1,0:T(8,128)(2,1)S(1)}, bf16[2,64,1536]{2,1,0:T(8,128)(2,1)S(1)}, u32[]{:S(2)}, u32[]{:S(2)}) collective-permute-start(bf16[2,64,1536]{2,1,0:T(8,128)(2,1)S(1)} %add_convert_fusion.11), channel_id=1, source_target_pairs={{0,4},{4,0},{1,5},{5,1},{2,6},{6,2},{3,7},{7,3},{8,12},{12,8},{9,1... | collective-permute-start | bytes 1179656 | tf_op jit(solution)/shard_map/ppermute | solution.py:439
  485.2 10.0 %collective-permute-start.45 = (bf16[64,1536]{1,0:T(8,128)(2,1)S(1)}, bf16[64,1536]{1,0:T(8,128)(2,1)S(1)}, u32[]{:S(2)}, u32[]{:S(2)}) collective-permute-start(bf16[64,1536]{1,0:T(8,128)(2,1)S(1)} %slice_bitcast_fusion.10), channel_id=1, source_target_pairs={{0,16},{16,0},{1,17},{17,1},{2,18},{18,2},{3,19},{19,3},{4,20},{20... | collective-permute-start | bytes 589832 | tf_op jit(solution)/shard_map/ppermute | solution.py:439
  495.2 7.9 %collective-permute-start.41 = (bf16[64,1536]{1,0:T(8,128)(2,1)S(1)}, bf16[64,1536]{1,0:T(8,128)(2,1)S(1)}, u32[]{:S(2)}, u32[]{:S(2)}) collective-permute-start(bf16[64,1536]{1,0:T(8,128)(2,1)S(1)} %slice_bitcast_fusion.12), channel_id=1, source_target_pairs={{0,16},{16,0},{1,17},{17,1},{2,18},{18,2},{3,19},{19,3},{4,20},{20... | collective-permute-start | bytes 589832 | tf_op jit(solution)/shard_map/ppermute | solution.py:439
  503.1 19.0 %collective-permute-start.46 = (bf16[64,1536]{1,0:T(8,128)(2,1)}, bf16[64,1536]{1,0:T(8,128)(2,1)}, u32[]{:S(2)}, u32[]{:S(2)}) collective-permute-start(bf16[64,1536]{1,0:T(8,128)(2,1)} %fusion.14), channel_id=1, source_target_pairs={{0,2},{2,0},{1,3},{3,1},{4,6},{6,4},{5,7},{7,5},{8,10},{10,8},{9,1... | collective-permute-start | bytes 589832 | tf_op jit(solution)/shard_map/ppermute | solution.py:439
  514.8 36.6 %collective-permute-start.65 = (bf16[2,128,1024]{2,1,0:T(8,128)(2,1)}, bf16[2,128,1024]{2,1,0:T(8,128)(2,1)}, u32[]{:S(2)}, u32[]{:S(2)}) collective-permute-start(bf16[2,128,1024]{2,1,0:T(8,128)(2,1)} %slice_bitcast_fusion.2), channel_id=1, source_target_pairs={{0,16},{16,0},{1,17},{17,1},{2,18},{18,2},{3,19},{19,3},{4,20},{20... | collective-permute-start | bytes 1572872 | tf_op jit(solution)/shard_map/ppermute | solution.py:439
  517.3 45.3 %collective-permute-start.61 = (bf16[2,128,1024]{2,1,0:T(8,128)(2,1)}, bf16[2,128,1024]{2,1,0:T(8,128)(2,1)}, u32[]{:S(2)}, u32[]{:S(2)}) collective-permute-start(bf16[2,128,1024]{2,1,0:T(8,128)(2,1)} %slice_bitcast_fusion.4), channel_id=1, source_target_pairs={{0,16},{16,0},{1,17},{17,1},{2,18},{18,2},{3,19},{19,3},{4,20},{20... | collective-permute-start | bytes 1572872 | tf_op jit(solution)/shard_map/ppermute | solution.py:439
  522.1 52.5 %collective-permute-start.51 = (bf16[64,1024]{1,0:T(8,128)(2,1)S(1)}, bf16[64,1024]{1,0:T(8,128)(2,1)}, u32[]{:S(2)}, u32[]{:S(2)}) collective-permute-start(bf16[64,1024]{1,0:T(8,128)(2,1)S(1)} %get-tuple-element.187), channel_id=1, source_target_pairs={{2,16},{16,2},{3,17},{17,3},{6,20},{20,6},{7,21},{21,7},{10,24},{2... | collective-permute-start | bytes 393224 | tf_op jit(solution)/shard_map/ppermute | solution.py:447
  551.3 23.7 %collective-permute-start.56 = (bf16[64,1024]{1,0:T(8,128)(2,1)}, bf16[64,1024]{1,0:T(8,128)(2,1)}, u32[]{:S(2)}, u32[]{:S(2)}) collective-permute-start(bf16[64,1024]{1,0:T(8,128)(2,1)} %broadcast_select_fusion.4), channel_id=1, source_target_pairs={{0,2},{2,0},{1,3},{3,1},{4,6},{6,4},{5,7},{7,5},{8,10},{10,8},{9,1... | collective-permute-start | bytes 393224 | tf_op jit(solution)/shard_map/ppermute | solution.py:439
  562.6 36.2 %collective-permute-start.47 = (bf16[64,3072]{1,0:T(8,128)(2,1)S(1)}, bf16[64,3072]{1,0:T(8,128)(2,1)}, u32[]{:S(2)}, u32[]{:S(2)}) collective-permute-start(bf16[64,3072]{1,0:T(8,128)(2,1)S(1)} %select_n.204), channel_id=1, source_target_pairs={{0,1},{1,0},{2,3},{3,2},{4,5},{5,4},{6,7},{7,6},{8,9},{9,8},{10,11... | collective-permute-start | bytes 1179656 | tf_op jit(solution)/shard_map/ppermute | solution.py:439
  565.5 36.6 %collective-permute-start.66 = (bf16[256,1024]{1,0:T(8,128)(2,1)S(1)}, bf16[256,1024]{1,0:T(8,128)(2,1)}, u32[]{:S(2)}, u32[]{:S(2)}) collective-permute-start(bf16[256,1024]{1,0:T(8,128)(2,1)S(1)} %get-tuple-element.186), channel_id=1, source_target_pairs={{0,1},{1,0},{2,3},{3,2},{4,5},{5,4},{6,7},{7,6},{8,9},{9,8},{10,11... | collective-permute-start | bytes 1572872 | tf_op jit(solution)/shard_map/ppermute | solution.py:439
  574.7 7.7 %collective-permute-start.69 = (f32[16,768]{1,0:T(8,128)S(1)}, f32[16,768]{1,0:T(8,128)S(1)}, u32[]{:S(2)}, u32[]{:S(2)}) collective-permute-start(f32[16,768]{1,0:T(8,128)S(1)} %reshape.208), channel_id=1, source_target_pairs={{0,16},{16,0},{1,17},{17,1},{2,18},{18,2},{3,19},{19,3},{4,20},{20... | collective-permute-start | bytes 147464 | tf_op jit(solution)/shard_map/ppermute | solution.py:439
  576.0 13.7 %collective-permute-start.57 = (bf16[64,1024]{1,0:T(8,128)(2,1)S(1)}, bf16[64,1024]{1,0:T(8,128)(2,1)S(1)}, u32[]{:S(2)}, u32[]{:S(2)}) collective-permute-start(bf16[64,1024]{1,0:T(8,128)(2,1)S(1)} %add_convert_fusion.12), channel_id=1, source_target_pairs={{0,1},{1,0},{2,3},{3,2},{4,5},{5,4},{6,7},{7,6},{8,9},{9,8},{10,11... | collective-permute-start | bytes 393224 | tf_op jit(solution)/shard_map/ppermute | solution.py:439
  588.0 16.0 %collective-permute-start.67 = (bf16[256,1024]{1,0:T(8,128)(2,1)S(1)}, bf16[256,1024]{1,0:T(8,128)(2,1)S(1)}, u32[]{:S(2)}, u32[]{:S(2)}) collective-permute-start(bf16[256,1024]{1,0:T(8,128)(2,1)S(1)} %get-tuple-element.185), channel_id=1, source_target_pairs={{0,1},{1,0},{2,3},{3,2},{4,5},{5,4},{6,7},{7,6},{8,9},{9,8},{10,11... | collective-permute-start | bytes 1572872 | tf_op jit(solution)/shard_map/ppermute | solution.py:439
  592.7 9.2 %collective-permute-start.72 = (f32[16,768]{1,0:T(8,128)S(1)}, f32[16,768]{1,0:T(8,128)S(1)}, u32[]{:S(2)}, u32[]{:S(2)}) collective-permute-start(f32[16,768]{1,0:T(8,128)S(1)} %add.349), channel_id=1, source_target_pairs={{0,2},{2,0},{1,3},{3,1},{4,6},{6,4},{5,7},{7,5},{8,10},{10,8},{9,1... | collective-permute-start | bytes 147464 | tf_op jit(solution)/shard_map/ppermute | solution.py:439
  616.1 10.4 %collective-permute-start.77 = (f32[8,128]{1,0:T(8,128)S(1)}, f32[8,128]{1,0:T(8,128)S(1)}, u32[]{:S(2)}, u32[]{:S(2)}) collective-permute-start(f32[8,128]{1,0:T(8,128)S(1)} %add.356), channel_id=1, source_target_pairs={{0,2},{2,0},{1,3},{3,1},{4,6},{6,4},{5,7},{7,5},{8,10},{10,8},{9,1... | collective-permute-start | bytes 12296 | tf_op jit(solution)/shard_map/ppermute | solution.py:439
  622.9 44.8 %collective-permute-start.80 = (bf16[3,292,1024]{2,1,0:T(8,128)(2,1)S(1)}, bf16[3,292,1024]{2,1,0:T(8,128)(2,1)}, u32[]{:S(2)}, u32[]{:S(2)}) collective-permute-start(bf16[3,292,1024]{2,1,0:T(8,128)(2,1)S(1)} %copy-done.6), channel_id=1, source_target_pairs={{2,16},{16,2},{3,17},{17,3},{6,20},{20,6},{7,21},{21,7},{10,24},{2... | collective-permute-start | bytes 5382152 | tf_op jit(solution)/shard_map/ppermute | solution.py:447
  (104 other events, 1167.9 us)

commit v3 on v2

--- a/solution.py
+++ b/solution.py
@@ -433,6 +433,321 @@
         cost_estimate=pl.CostEstimate(flops=n*20*padded*feat,bytes_accessed=14<<20,transcendentals=0),
     )(x_own,dh_own,dh_oth,dx2,gain[None])
 
+MESH_ID = pl.DeviceIdType.MESH
+
+
+class Wires:
+    def __init__(self, send_sem, recv_sem):
+        self.send_sem, self.recv_sem, self.count, self.sent = send_sem, recv_sem, 0, []
+
+    def make(self, src, dst, to):
+        cp = pltpu.make_async_remote_copy(
+            src_ref=src, dst_ref=dst, send_sem=self.send_sem.at[self.count], recv_sem=self.recv_sem.at[self.count],
+            device_id=to, device_id_type=MESH_ID)
+        self.count += 1
+        return cp
+
+    def send(self, src, dst, to):
+        cp = self.make(src, dst, to)
+        cp.start()
+        self.sent.append(cp)
+        return cp
+
+    def finish(self):
+        for cp in self.sent:
+            cp.wait_send()
+
+
+def greet(peers, crossing_peer, apart):
+    barrier = pltpu.get_barrier_semaphore()
+    for peer in peers:
+        pl.semaphore_signal(barrier, inc=1, device_id=peer, device_id_type=MESH_ID)
+
+    @pl.when(apart)
+    def _():
+        pl.semaphore_signal(barrier, inc=1, device_id=crossing_peer, device_id_type=MESH_ID)
+
+    pl.semaphore_wait(barrier, len(peers) + jnp.where(apart, 1, 0))
+
+
+def add_all(first, *others):
+    total = first.astype(F32)
+    for other in others:
+        total = total + other.astype(F32)
+    return total
+
+
+def tail_kernel(keys, ny, nx, *refs):
+    nk = len(keys)
+    h1_ref, dqkv_ref, go_ref, x_ref, dx_ref, gain_ref, vec_ref = refs[:7]
+    wa, wb = refs[7:7 + nk], refs[7 + nk:7 + 2 * nk]
+    o = 7 + 2 * nk
+    fa, fb = refs[o:o + nx], refs[o + nx:o + nx + ny]
+    o += nx + ny
+    mine_ref, theirs_ref, so_ref, sf_ref, ig_ref, vout_ref, norm_ref = refs[o:o + 7]
+    (w, grad, ra1, ra2, rb1, rb2, sa, sb, oa1, oa2, ob1, ob2, ta, tb, osum, ocross, ocore, odp, ofin,
+     rfa, rfb, fsum, fpart, frecv, fdp, isum, ipart, irecv, idp, ifin,
+     buf, give, got, stage, vrecv, nrecv, nval, wsem, send_sem, recv_sem) = refs[o + 7:]
+    h, y, x, c, l = (lax.axis_index(a) for a in AXES)
+    images, half, feat = x_ref.shape
+    padded = dx_ref.shape[1]
+    rows = grad.shape[4]
+    apart = h != c
+    cross = {"seq": 1 - h, "core": 1 - c}
+    to_core, to_seq, to_dp = {"core": 1 - c}, {"seq": 1 - h}, {"dp": 1 - l}
+    to_x = [{"x": lax.rem(x + k, nx)} for k in range(nx)]
+    to_y = [{"y": lax.rem(y + k, ny)} for k in range(ny)]
+    yy = [lax.rem(y + k, ny) for k in range(ny)]
+    xx = [lax.rem(x + k, nx) for k in range(nx)]
+    zz = [h, 1 - h]
+    wires = Wires(send_sem, recv_sem)
+    loads = []
+    for ki, (ky, kx) in enumerate(keys):
+        for kz in range(2):
+            for core, src in ((c, wa), (1 - c, wb)):
+                row = (((zz[kz] * ny + yy[ky]) * nx + xx[kx]) * 2 + core) * rows
+                cp = pltpu.make_async_copy(src[ki].at[kz], w.at[pl.ds(pl.multiple_of(row, 16), rows)], wsem.at[len(loads)])
+                cp.start()
+                loads.append(cp)
+    greet([to_core, to_seq, to_dp] + to_x[1:] + to_y[1:], cross, apart)
+
+    ff_got = [wires.send(fa[k], rfa.at[k - 1], to_x[k]) for k in range(1, nx)]
+    ff_got += [wires.send(fb[k], rfb.at[k - 1], to_y[k]) for k in range(1, ny)]
+    oa_got = [[wires.send(go_ref.at[yy[ky], xx[kx], h], oa1.at[ky - 1, kx], to_y[ky]) for kx in range(nx)] for ky in range(1, ny)]
+    ob_got = [[wires.send(go_ref.at[yy[ky], xx[kx], 1 - h], ob1.at[kx - 1, ky], to_x[kx]) for ky in range(ny)] for kx in range(1, nx)]
+    width = nx * 2 * rows
+    ia_got, ib_got = [], []
+    for ky in range(ny - 1, -1, -1):
+        for kz in range(2):
+            col = pl.multiple_of((zz[kz] * ny + yy[ky]) * width, 128)
+            t = dot(h1_ref[:, pl.ds(col, width)], dqkv_ref[...], TN).astype(BF)
+            for q in range(nx):
+                for core in range(2):
+                    r = (q * 2 + core) * rows
+                    grad[zz[kz], yy[ky], q, core] = t[r:r + rows]
+        if ky > 0:
+            for kx in range(nx):
+                for kz in range(2):
+                    ia_got.append(wires.send(grad.at[zz[kz], yy[ky], xx[kx], c], ra1.at[ky - 1, kz, kx], to_y[ky]))
+    for kx in range(1, nx):
+        for ky in range(ny):
+            for kz in range(2):
+                ib_got.append(wires.send(grad.at[zz[kz], yy[ky], xx[kx], 1 - c], rb1.at[kx - 1, kz, ky], to_x[kx]))
+    for cp in loads:
+        cp.wait()
+    dh_got = []
+    for i in range(images):
+        r = (2 * i + 1) * padded
+        give[i] = dot(dqkv_ref[r:r + padded, :], w[...], NT).astype(BF)
+        dh_got.append(wires.send(give.at[i], got.at[i], to_core))
+    for cp in ff_got:
+        cp.wait_recv()
+    fsum[0] = add_all(fa[0][...], *(rfa[k] for k in range(nx - 1))).astype(BF)
+    fsum[1] = add_all(fb[0][...], *(rfb[k] for k in range(ny - 1))).astype(BF)
+    fd = wires.send(fsum.at[1 - l], fdp, to_dp)
+    for row in oa_got + ob_got:
+        for cp in row:
+            cp.wait_recv()
+    o_got = []
+    for kx in range(1, nx):
+        ta[kx - 1] = add_all(go_ref[y, xx[kx], h], *(oa1[k, kx] for k in range(ny - 1))).astype(BF)
+        o_got.append(wires.send(ta.at[kx - 1], oa2.at[kx - 1], to_x[kx]))
+    for ky in range(1, ny):
+        tb[ky - 1] = add_all(go_ref[yy[ky], x, 1 - h], *(ob1[k, ky] for k in range(nx - 1))).astype(BF)
+        o_got.append(wires.send(tb.at[ky - 1], ob2.at[ky - 1], to_y[ky]))
+
+    sum_gain, sum_shift = jnp.zeros((1, feat), F32), jnp.zeros((1, feat), F32)
+    crossing_copies = [wires.make(stage.at[i], ig_ref.at[i], cross) for i in range(images)]
+
+    def input_back(i, sum_gain, sum_shift):
+        r = 2 * i * padded
+        own = dot(dqkv_ref[r:r + padded, :], w[...], NT)
+        dh_got[i].wait_recv()
+        g = own + got[i].astype(F32)
+        dx, gg = norm_back(wide_rows(buf, x_ref[i]), gain_ref[...], g)
+        stage[i] = (dx + dx_ref[i]).astype(BF)[:half]
+
+        @pl.when(apart)
+        def _():
+            crossing_copies[i].start()
+
+        @pl.when(jnp.logical_not(apart))
+        def _():
+            ig_ref[i] = stage[i]
+
+        return sum_gain + jnp.sum(gg, axis=0, keepdims=True), sum_shift + jnp.sum(g, axis=0, keepdims=True)
+
+    sum_gain, sum_shift = input_back(0, sum_gain, sum_shift)
+    for cp in ia_got + ib_got:
+        cp.wait_recv()
+    i_got = []
+    for kz in range(2):
+        for kx in range(1, nx):
+            sa[kx - 1, kz] = add_all(grad[zz[kz], y, xx[kx], c], *(ra1[k, kz, kx] for k in range(ny - 1))).astype(BF)
+        for ky in range(1, ny):
+            sb[ky - 1, kz] = add_all(grad[zz[kz], yy[ky], x, 1 - c], *(rb1[k, kz, ky] for k in range(nx - 1))).astype(BF)
+    for kx in range(1, nx):
+        i_got.append(wires.send(sa.at[kx - 1], ra2.at[kx - 1], to_x[kx]))
+    for ky in range(1, ny):
+        i_got.append(wires.send(sb.at[ky - 1], rb2.at[ky - 1], to_y[ky]))
+    sum_gain, sum_shift = input_back(1, sum_gain, sum_shift)
+    fd.wait_recv()
+    fpart[...] = add_all(fsum[l], fdp[...]).astype(BF)
+    fs = wires.send(fpart.at[1], frecv, to_seq)
+    for i in range(2, images):
+        sum_gain, sum_shift = input_back(i, sum_gain, sum_shift)
+    vout_ref[...] = vec_ref[...]
+    for q in range(feat // 128):
+        vout_ref[q:q + 1, :] = sum_gain[:, q * 128:(q + 1) * 128]
+        vout_ref[feat // 128 + q:feat // 128 + q + 1, :] = sum_shift[:, q * 128:(q + 1) * 128]
+    rounds = [[to_core], to_x[1:], to_y[1:], [to_seq], [to_dp]]
+    slot = [0]
+
+    def start_round(value, landing, peers):
+        first = slot[0]
+        cps = [wires.send(value, landing.at[first + k], peer) for k, peer in enumerate(peers)]
+        slot[0] += len(peers)
+        return first, cps
+
+    def end_round(value_ref, landing, started):
+        first, cps = started
+        for cp in cps:
+            cp.wait_recv()
+        for cp in cps:
+            cp.wait_send()
+        wires.sent = [cp for cp in wires.sent if all(cp is not other for other in cps)]
+        value_ref[...] = add_all(value_ref[...], *(landing[first + k] for k in range(len(cps))))
+
+    vec_round = start_round(vout_ref, vrecv, rounds[0])
+    for cp in i_got:
+        cp.wait_recv()
+    for kz in range(2):
+        isum[0, kz] = add_all(grad[zz[kz], y, x, c], *(ra1[k, kz, 0] for k in range(ny - 1)), *(ra2[k, kz] for k in range(nx - 1))).astype(BF)
+        isum[1, kz] = add_all(grad[zz[kz], y, x, 1 - c], *(rb1[k, kz, 0] for k in range(nx - 1)), *(rb2[k, kz] for k in range(ny - 1))).astype(BF)
+    idd = wires.send(isum.at[1 - l], idp, to_dp)
+    for cp in o_got:
+        cp.wait_recv()
+    osum[0] = add_all(go_ref[y, x, h], *(oa1[k, 0] for k in range(ny - 1)), *(oa2[k] for k in range(nx - 1))).astype(BF)
+    osum[1] = add_all(go_ref[y, x, 1 - h], *(ob1[k, 0] for k in range(nx - 1)), *(ob2[k] for k in range(ny - 1))).astype(BF)
+    out_cross = wires.make(osum, ocross, cross)
+
+    @pl.when(apart)
+    def _():
+        out_cross.start()
+
+    @pl.when(jnp.logical_not(apart))
+    def _():
+        ocross[...] = osum[...]
+
+    end_round(vout_ref, vrecv, vec_round)
+    vec_round = start_round(vout_ref, vrecv, rounds[1])
+    idd.wait_recv()
+    ipart[...] = add_all(isum[l], idp[...]).astype(BF)
+    is_ = wires.send(ipart.at[1], irecv, to_seq)
+    end_round(vout_ref, vrecv, vec_round)
+    vec_round = start_round(vout_ref, vrecv, rounds[2])
+
+    @pl.when(apart)
+    def _():
+        out_cross.wait_recv()
+
+    oc = wires.send(ocross.at[1], ocore, to_core)
+    fs.wait_recv()
+    sf_ref[l] = add_all(fpart[0], frecv[...]).astype(BF)
+    ff_last = wires.send(sf_ref.at[l], sf_ref.at[l], to_dp)
+    end_round(vout_ref, vrecv, vec_round)
+    vec_round = start_round(vout_ref, vrecv, rounds[3])
+    oc.wait_recv()
+    ofin[...] = add_all(ocross[0], ocore[...]).astype(BF)
+    od = wires.send(ofin, odp, to_dp)
+    is_.wait_recv()
+    ifin[l] = add_all(ipart[0], irecv[...]).astype(BF)
+    in_last = wires.send(ifin.at[l], ifin.at[l], to_dp)
+    end_round(vout_ref, vrecv, vec_round)
+    vec_round = start_round(vout_ref, vrecv, rounds[4])
+    in_last.wait_recv()
+    ic = wires.send(ifin.at[1], theirs_ref, to_core)
+    mine_ref[...] = ifin[0]
+    od.wait_recv()
+    so_ref[...] = add_all(ofin[...], odp[...]).astype(BF)
+    end_round(vout_ref, vrecv, vec_round)
+    ff_last.wait_recv()
+
+    def squares(value):
+        value = value.astype(F32)
+        return jnp.sum(jnp.sum(value * value, axis=0, keepdims=True), axis=1, keepdims=True)
+
+    shard = ((h * ny + y) * nx + x) * 2 + c
+    v = vout_ref[...]
+    place = lax.broadcasted_iota(jnp.int32, v.shape, 0) * 128 + lax.broadcasted_iota(jnp.int32, v.shape, 1)
+    share = v.shape[0] * 128 // (4 * ny * nx)
+    v = jnp.where((place >= shard * share) & (place < (shard + 1) * share), v, 0.0)
+    total = squares(v) + squares(so_ref[...]) + squares(mine_ref[...])
+    for ab in range(2):
+        for ud in range(2):
+            total = total + squares(sf_ref[ab, ud])
+    ic.wait_recv()
+    total = total + squares(theirs_ref[...])
+    nval[...] = jnp.broadcast_to(total, nval.shape)
+    slot[0] = 0
+    for peers in rounds[:4]:
+        end_round(nval, nrecv, start_round(nval, nrecv, peers))
+    norm_ref[...] = jnp.sqrt(nval[...])
+
+    @pl.when(apart)
+    def _():
+        for cp in crossing_copies:
+            cp.wait_recv()
+        for cp in crossing_copies:
+            cp.wait_send()
+        out_cross.wait_send()
+
+    wires.finish()
+
+
+def tail_stage(h1, dqkv, g_out, x_own, dx2, gain, vec, wa, wb, fa, fb, ny, nx):
+    keys = sorted(wa)
+    nk = len(keys)
+    tokens, feat = h1.shape
+    width = dqkv.shape[1]
+    rows = wa[keys[0]].shape[1]
+    rows_o = g_out.shape[3]
+    images, half, _ = x_own.shape
+    padded = dx2.shape[1]
+    _, ud, hid, _ = fa[0].shape
+    ma, mb = max(ny - 1, 1), max(nx - 1, 1)
+    piece, out_piece, ff = (rows, width), (rows_o, feat), (ud, hid, feat)
+    peers = 4 + nx - 1 + ny - 1
+    many = 200 + 8 * nk * 4
+    V = lambda *s: pltpu.VMEM(s, BF)
+    scratch = [
+        V(feat, width), V(2, ny, nx, 2, *piece),
+        V(ny - 1, 2, nx, *piece), V(nx - 1, 2, *piece), V(nx - 1, 2, ny, *piece), V(ny - 1, 2, *piece),
+        V(nx - 1, 2, *piece), V(ny - 1, 2, *piece),
+        V(ny - 1, nx, *out_piece), V(nx - 1, *out_piece), V(nx - 1, ny, *out_piece), V(ny - 1, *out_piece),
+        V(nx - 1, *out_piece), V(ny - 1, *out_piece),
+        V(2, *out_piece), V(2, *out_piece), V(*out_piece), V(*out_piece), V(*out_piece),
+        V(nx - 1, 2, *ff), V(ny - 1, 2, *ff), V(2, 2, *ff), V(2, *ff), V(*ff), V(2, *ff),
+        V(2, 2, *piece), V(2, *piece), V(*piece), V(2, *piece), V(2, *piece),
+        pltpu.VMEM((padded, feat), F32), V(images, padded, feat), V(images, padded, feat), V(images, half, feat),
+        pltpu.VMEM((peers,) + vec.shape, F32), pltpu.VMEM((peers, 8, 128), F32), pltpu.VMEM((8, 128), F32),
+        pltpu.SemaphoreType.DMA((4 * nk,)), pltpu.SemaphoreType.DMA((many,)), pltpu.SemaphoreType.DMA((many,)),
+    ]
+    return pl.pallas_call(
+        functools.partial(tail_kernel, keys, ny, nx),
+        in_specs=[VM] * 7 + [ANY] * (2 * nk) + [VM] * (nx + ny),
+        out_specs=[VM] * 7,
+        out_shape=[
+            jax.ShapeDtypeStruct(piece, BF), jax.ShapeDtypeStruct(piece, BF), jax.ShapeDtypeStruct(out_piece, BF),
+            jax.ShapeDtypeStruct((2,) + ff, BF), jax.ShapeDtypeStruct(x_own.shape, BF),
+            jax.ShapeDtypeStruct(vec.shape, F32), jax.ShapeDtypeStruct((8, 128), F32),
+        ],
+        scratch_shapes=scratch,
+        name="tail_stage",
+        compiler_params=pltpu.CompilerParams(collective_id=1, has_side_effects=True, vmem_limit_bytes=62 << 20),
+        cost_estimate=pl.CostEstimate(flops=4 * tokens * feat * width, bytes_accessed=40 << 20, transcendentals=0),
+    )(h1, dqkv, g_out, x_own, dx2, gain[None], vec, *[wa[k] for k in keys], *[wb[k] for k in keys], *fa, *fb)
+
 
 def shift(value, axis, up):
     n = lax.axis_size(axis)
@@ -489,13 +804,13 @@
     return total
 
 
-def reduce_plane(pieces, first, second, dep_one, dep_two):
+def reduce_second(pieces, first, second, dep):
     n_first, n_second = lax.axis_size(first), lax.axis_size(second)
     part = []
     for i in range(n_first):
         row = [pieces[(j, i) if first == "x" else (i, j)] for j in range(n_second)]
-        part.append(reduce_list(row, second, dep_one))
-    return reduce_list(part, first, dep_two)
+        part.append(reduce_list(row, second, dep))
+    return part
 
 
 def adam_update(master, first_moment, second_moment, gradient, step_rate, bias_one, bias_two):
@@ -583,41 +898,15 @@
     dh2 = dh2.reshape(image_count, 2, padded, D)
     dh2_oth = shift(dh2, "core", 1)
     dx2, dattn, g_out, sums_two = middle_back(x2, dh2, dh2_oth, g_own, g_oth, halved, my_out, gain_two)
-    g_out = g_out.reshape(ny, nx, 2, rows_out, D)
-    oa, ob = {}, {}
-    for ky, kx in keys:
-        spot = ((y + ky) % ny, (x + kx) % nx)
-        oa[ky, kx] = lax.dynamic_slice(g_out, (*spot, h, 0, 0), (1, 1, 1, rows_out, D)).reshape(rows_out, D)
-        ob[ky, kx] = lax.dynamic_slice(g_out, (*spot, 1 - h, 0, 0), (1, 1, 1, rows_out, D)).reshape(rows_out, D)
     result_got = crossing(after(result, dattn))
     dqkv, sums_qkv = attend_back(qkv, key_fill, mixed, dattn.reshape(mixed.shape), lse)
-    ia, ib = grad_in(at, h1.reshape(tokens, D), dqkv.reshape(tokens, 3 * HALF_D), keys, rows_in)
-    dh_own, dh_oth = project_back(at, dqkv.reshape(image_count, 2, padded, 3 * HALF_D), in_a, in_b)
-    dh_got = shift(dh_oth, "core", 1)
-    activations = pick(result, after(result_got, dh_own)).astype(F32)
-    share_ff = []
-    for grads, order in ((grad_a, ("x", "y")), (grad_b, ("y", "x"))):
-        total = reduce_plane(grads, *order, dattn, dqkv)
-        share_ff.append(reduce_list([total[0], total[1]], "seq", dh_own))
-    share_ff = jnp.concatenate(share_ff, axis=1)
-    keep = crossed(reduce_plane(oa, "x", "y", dqkv, dh_own))
-    give = crossed(reduce_plane(ob, "y", "x", dqkv, dh_own))
-    share_out = (keep.astype(F32) + shift(give, "core", 1).astype(F32)).astype(BF)
-    ia = reduce_plane(ia, "x", "y", dh_own, dh_own)
-    ib = reduce_plane(ib, "y", "x", dh_own, dh_own)
-    ia, ib = reduce_list([ia[0], ia[1]], "seq", dh_own), reduce_list([ib[0], ib[1]], "seq", dh_own)
-    ib = shift(ib, "core", 1)
-    ia, ib = (t.reshape(rows_in, 3, 1, HALF_D) for t in (ia, ib))
-    share_in = jnp.where(c == 0, jnp.concatenate([ia, ib], 2), jnp.concatenate([ib, ia], 2)).reshape(rows_in, 3 * D)
-
-    input_grad, sums_one = input_back(x_own, dh_own, dh_got, dx2, gain_one)
-    input_grad = crossed(input_grad).astype(F32)
-
+    part_a = reduce_second(grad_a, "x", "y", dqkv)
+    part_b = reduce_second(grad_b, "y", "x", dqkv)
     zero = jnp.zeros((D,), F32)
-    grad_vec = jnp.concatenate(
+    vec = jnp.concatenate(
         [
-            sums_one[0],
-            sums_one[1],
+            zero,
+            zero,
             lax.dynamic_update_slice(zero, sums_qkv[0, :HALF_D], (c * HALF_D,)),
             lax.dynamic_update_slice(zero, sums_qkv[0, 2 * HALF_D :], (c * HALF_D,)),
             sums_two[2],
@@ -626,17 +915,32 @@
             sums_two[3],
             g_bu.reshape(-1),
         ]
-    ).reshape(shards, -1)
-    grad_vec = small_sum(grad_vec, AXES)
-    share_vec = lax.dynamic_slice(grad_vec, (shard, 0), (1, grad_vec.shape[1])).reshape(-1)
-
-    def over_dp(share):
-        return small_sum(share, ("dp",)).astype(F32)
-
-    shares = (over_dp(share_in), over_dp(share_out), over_dp(share_ff[0]), over_dp(share_ff[1]), share_vec)
-    square = sum(jnp.sum(s * s) for s in shares)
-    square = small_sum(jnp.full((8, 128), square), SHARD)[0, 0]
-    grad_norm = jnp.sqrt(square)
+    ).reshape(-1, 128)
+    in_mine, in_theirs, share_out, share_ff, input_grad, vec, norm = tail_stage(
+        h1.reshape(tokens, D),
+        dqkv.reshape(tokens, 3 * HALF_D),
+        g_out.reshape(ny, nx, 2, rows_out, D),
+        x_own,
+        dx2,
+        gain_one,
+        vec,
+        in_a,
+        in_b,
+        part_a,
+        part_b,
+        ny,
+        nx,
+    )
+    activations = pick(result, after(result_got, norm)).astype(F32)
+    input_grad = input_grad.astype(F32)
+    share_vec = lax.dynamic_slice(vec.reshape(shards, -1), (shard, 0), (1, vec.size // shards)).reshape(-1)
+    in_mine, in_theirs = (s.reshape(rows_in, 3, 1, HALF_D) for s in (in_mine, in_theirs))
+    share_in = jnp.where(
+        c == 0, jnp.concatenate([in_mine, in_theirs], 2), jnp.concatenate([in_theirs, in_mine], 2)
+    ).reshape(rows_in, 3 * D)
+    share_up, share_down = (share_ff[:, i].reshape(rows_ff, D) for i in range(2))
+    shares = tuple(s.astype(F32) for s in (share_in, share_out, share_up, share_down, share_vec))
+    grad_norm = norm[0, 0]
     threshold = 0.5 * math.sqrt(4 * D * D + 2 * D * FF + 12 * D)
     clip_factor = jnp.minimum(1.0, threshold / grad_norm)
     bias = 1.0 - jnp.power(F32(0.5), step_count.astype(F32))

time: 678 us -> 615 us (0.907)
  Pallas kernels: 201 us -> 326 us
  waiting for transfers between devices: 224 us -> 116 us
  starting transfers between devices: 148 us -> 88.5 us
  other arithmetic: 61 us -> 49.5 us
    pallas_call x3 -> x1, Pallas kernels: 32.8 us -> 158 us  [tail_stage(): pl.pallas_call(functools.partial(tail_kernel, keys, ny, nx), in_specs=[VM...]
    ppermute x73 -> x39, waiting for transfers between devices: 191 us -> 92.7 us  [shift(): return lax.ppermute(value, axis, [(i, (i + up) % n) for i in range(n)])]
    ppermute x73 -> x39, starting transfers between devices: 112 us -> 64.7 us  [shift(): return lax.ppermute(value, axis, [(i, (i + up) % n) for i in range(n)])]
    ppermute x8 -> x5, starting transfers between devices: 36.3 us -> 23.8 us  [crossing(): return lax.ppermute(value, ('seq', 'core'), [(1, 2), (2, 1)])]
    ppermute x8 -> x5, waiting for transfers between devices: 33.2 us -> 23.1 us  [crossing(): return lax.ppermute(value, ('seq', 'core'), [(1, 2), (2, 1)])]
    unnamed x184 -> x143, local copies, waits for them, and re-layouts: 17.5 us -> 15.1 us
  transfers between devices with their start and end apart: 81 -> 44, of which waited for: 31 -> 18; matrix products, arithmetic and copies ran while one was open for 10% -> 7% of each run, Pallas kernels for 19% -> 15%
where the time goes in v3:
time: 615 us; the launch traced here: 610 us
  Pallas kernels  326 us (53%)
  waiting for transfers between devices  116 us (19%)
  starting transfers between devices  88.5 us (14%)
  other arithmetic  49.5 us (8%)
  local copies, waits for them, and re-layouts  26.7 us (4%)
    pallas_call x1, Pallas kernels, tail_stage(): pl.pallas_call(functools.partial(tail_kernel, keys, ny, nx), in_specs=[VM...  158 us
    ppermute x39, waiting for transfers between devices, shift(): return lax.ppermute(value, axis, [(i, (i + up) % n) for i in range(n)])  92.7 us
    pallas_call x1, Pallas kernels, mlp(): pl.pallas_call(functools.partial(mlp_kernel, keys, gtile=min(gtile, width...  73.8 us
    ppermute x39, starting transfers between devices, shift(): return lax.ppermute(value, axis, [(i, (i + up) % n) for i in range(n)])  64.7 us
    pallas_call x1, Pallas kernels, attend_back(): pl.pallas_call(functools.partial(attend_back_kernel, pairs=pairs, chunk=c...  30.4 us
    ppermute x5, starting transfers between devices, crossing(): return lax.ppermute(value, ('seq', 'core'), [(1, 2), (2, 1)])  23.8 us
    ppermute x5, waiting for transfers between devices, crossing(): return lax.ppermute(value, ('seq', 'core'), [(1, 2), (2, 1)])  23.1 us
    pallas_call x1, Pallas kernels, attend(): pl.pallas_call(attend_kernel, grid=(n, pairs), in_specs=[blk(0), blk(pair...  20.2 us
  transfers between devices with their start and end apart: 44, of which 18 were waited for; matrix products, arithmetic and copies ran while one was open for 7% of the time, Pallas kernels for 15%

profile of v3, /device:TPU:1, one launch (start us, length us, event | category | flops | bytes accessed | tf_op | source)
XLA Modules:
  0.0 609.5 jit_solution(14789084320187738417)
XLA Ops:
  0.7 5.6 collective-permute-start
  10.2 1.4 collective-permute-start.6
  11.6 29.4 %collective-permute-done.1 = bf16[64,1536]{1,0:T(8,128)(2,1)S(1)} collective-permute-done((bf16[64,1536]{1,0:T(8,128)(2,1)S(1)}, bf16[64,1536]{1,0:T(8,128)(2,1)S(1)}, u32[]{:S(2)}, u32[]{:S(2)}) %collective-permute-start.1) | collective-permute-done | bytes 196640 | tf_op jit(solution)/shard_map/ppermute | solution.py:754
  41.1 1.3 collective-permute-start.3
  42.3 2.9 collective-permute-done.6
  45.3 1.3 collective-permute-start.8
  46.6 1.4 convert.12
  49.7 1.2 collective-permute-start.4
  53.3 2.9 collective-permute-done.2.refs_2_.refs_9_
  57.7 20.7 %collective-permute-start.15 = (f32[3,584]{1,0:T(4,128)S(1)}, f32[3,584]{1,0:T(4,128)S(1)}, u32[]{:S(2)}, u32[]{:S(2)}) collective-permute-start(f32[3,584]{1,0:T(4,128)S(1)} %convert_element_type.118), channel_id=1, source_target_pairs={{0,2},{2,0},{1,3},{3,1},{4,6},{6,4},{5,7},{7,5},{8,10},{10,8},{9,1... | collective-permute-start | bytes 21032 | tf_op jit(solution)/shard_map/ppermute | solution.py:754
  80.0 1.7 broadcast_select_fusion.1.own_ref.refs_3_
  81.7 1.2 collective-permute-start.10
  83.0 1.4 fusion.10
  84.6 1.2 collective-permute-start.12
  88.5 5.1 collective-permute-start.17
  95.2 2.2 collective-permute-done.17
  98.1 1.3 collective-permute-start.19
  99.4 4.0 collective-permute-start.22
  103.7 4.2 collective-permute-start.27
  113.0 14.7 %project.1 = (bf16[3,2,304,1024]{3,2,1,0:T(8,128)(2,1)}, bf16[3,2,304,1536]{3,2,1,0:T(8,128)(2,1)}) custom-call(s32[8]{0:T(128)S(1)} %stack.70.at_ref.refs_0_, bf16[3,292,1024]{2,1,0:T(8,128)(2,1)} %copy-done.3, bf16[3,292,1024]{2,1,0:T(8,128)(2,1)} %collective-permute-done.10.oth_ref, f32[1,1024]{1,0:T(1,128)S(1)} %bitcast.77, f32[1,1024]{1,0:T(1,128)S(1)} %bitcast.81, ...), custom_call_target="tpu_custom_call" | custom-call | flops 5737807872 | bytes 25165824 | tf_op jit(solution)/shard_map/project/pallas_call | solution.py:293
  128.0 20.2 %attend.1 = (bf16[3,608,512]{2,1,0:T(8,128)(2,1)S(1)}, f32[3,4,8,608]{3,2,1,0:T(8,128)S(1)}) custom-call(bf16[3,608,1536]{2,1,0:T(8,128)(2,1)} %bitcast.82, bf16[3,608,1536]{2,1,0:T(8,128)(2,1)} %bitcast.83, bf16[3,608,1536]{2,1,0:T(8,128)(2,1)} %bitcast.84, bf16[3,608,128]{2,1,0:T(8,128)(2,1)S(1)} %broadcast_in_dim.68.kb_ref), custom_call_target="tpu_custom_call" | custom-call | flops 4542431232 | bytes 8404992 | tf_op jit(solution)/shard_map/attend/pallas_call | solution.py:181
  149.3 1.9 collective-permute-start.33
  151.2 2.5 collective-permute-done.24.refs_6_
  153.9 3.6 collective-permute-done.23.refs_5_
  158.1 3.3 collective-permute-done.25.refs_7_
  161.4 3.0 gather_rows.1.wo_ref.w_ref
  164.4 3.7 collective-permute-start.26
  168.1 2.2 pad_maximum_fusion.refs_5_
  170.6 4.9 collective-permute-done.33
  175.5 2.1 pad_maximum_fusion.1.refs_9_
  177.6 1.2 collective-permute-start.35
  178.8 2.7 collective-permute-done.27
  181.5 2.9 broadcast_select_fusion.refs_2_.go_ref
  184.4 8.5 %collective-permute-start.28 = (bf16[3,292,1024]{2,1,0:T(8,128)(2,1)}, bf16[3,292,1024]{2,1,0:T(8,128)(2,1)}, u32[]{:S(2)}, u32[]{:S(2)}) collective-permute-start(bf16[3,292,1024]{2,1,0:T(8,128)(2,1)} %broadcast_select_fusion.refs_2_.go_ref), channel_id=1, source_target_pairs={{0,2},{2,0},{1,3},{3,1},{4,6},{6,4},{5,7},{7,5},{8,10},{10,8},{9,1... | collective-permute-start | bytes 5382152 | tf_op jit(solution)/shard_map/ppermute | solution.py:754
  192.9 2.5 collective-permute-done.30.refs_6_
  200.0 1.5 copy-done.4
  201.5 1.2 copy-done.11
  202.7 9.7 %middle.1 = (f32[3,2,304,1024]{3,2,1,0:T(8,128)}, bf16[3,2,304,1024]{3,2,1,0:T(8,128)(2,1)}) custom-call(bf16[3,292,1024]{2,1,0:T(8,128)(2,1)S(1)} %copy-done.4, bf16[3,292,1024]{2,1,0:T(8,128)(2,1)} %collective-permute-done.10.oth_ref, bf16[3,2,304,512]{3,2,1,0:T(8,128)(2,1)} %bitcast.73, bf16[3,2,304,512]{3,2,1,0:T(8,128)(2,1)} %collective-permute-done.16.mt_ref, ...), custom_call_target="tpu_custom_call" | custom-call | flops 3825205248 | bytes 27262976 | tf_op jit(solution)/shard_map/middle/pallas_call | solution.py:330
  212.4 8.6 %collective-permute-done.31.refs_7_ = bf16[2,2,128,1024]{3,2,1,0:T(8,128)(2,1)} collective-permute-done((bf16[2,2,128,1024]{3,2,1,0:T(8,128)(2,1)}, bf16[2,2,128,1024]{3,2,1,0:T(8,128)(2,1)}, u32[]{:S(2)}, u32[]{:S(2)}) %collective-permute-start.31) | collective-permute-done | bytes 1048608 | tf_op jit(solution)/shard_map/ppermute | solution.py:754
  221.0 22.5 %collective-permute-done.32.refs_8_ = bf16[2,2,128,1024]{3,2,1,0:T(8,128)(2,1)} collective-permute-done((bf16[2,2,128,1024]{3,2,1,0:T(8,128)(2,1)}, bf16[2,2,128,1024]{3,2,1,0:T(8,128)(2,1)}, u32[]{:S(2)}, u32[]{:S(2)}) %collective-permute-start.32) | collective-permute-done | bytes 1048608 | tf_op jit(solution)/shard_map/ppermute | solution.py:754
  243.5 73.8 %feed_forward.1 = (bf16[2,2,128,1024]{3,2,1,0:T(8,128)(2,1)}, bf16[2,2,128,1024]{3,2,1,0:T(8,128)(2,1)}, bf16[2,2,128,1024]{3,2,1,0:T(8,128)(2,1)}, bf16[2,2,128...) custom-call(s32[8]{0:T(128)} %copy-done.9, ...), custom_call_target="tpu_custom_call" | custom-call | flops 45902462976 | bytes 41943040 | tf_op jit(solution)/shard_map/feed_forward/pallas_call | solution.py:139
  317.3 6.6 %collective-permute-start.37 = (bf16[3,2,304,1024]{3,2,1,0:T(8,128)(2,1)}, bf16[3,2,304,1024]{3,2,1,0:T(8,128)(2,1)}, u32[]{:S(2)}, u32[]{:S(2)}) collective-permute-start(bf16[3,2,304,1024]{3,2,1,0:T(8,128)(2,1)} %bitcast.88), channel_id=1, source_target_pairs={{0,2},{2,0},{1,3},{3,1},{4,6},{6,4},{5,7},{7,5},{8,10},{10,8},{9,1... | collective-permute-start | bytes 11206664 | tf_op jit(solution)/shard_map/ppermute | solution.py:754
  324.7 1.3 collective-permute-start.38
  327.4 5.4 collective-permute-done.42
  334.0 5.4 fusion.2
  339.4 16.5 %middle_back.1 = (f32[3,304,1024]{2,1,0:T(8,128)}, bf16[3,2,304,512]{3,2,1,0:T(8,128)(2,1)}, bf16[512,1024]{1,0:T(8,128)(2,1)}, f32[8,1024]{1,0:T(8,128)}) custom-call(f32[3,2,304,1024]{3,2,1,0:T(8,128)} %get-tuple-element.75.x2_ref, bf16[3,2,304,1024]{3,2,1,0:T(8,128)(2,1)} %bitcast.89, bf16[3,2,304,1024]{3,2,1,0:T(8,128)(2,1)} %collective-permute-done.37.db_ref, ...), custom_call_target="tpu_custom_call" | custom-call | flops 3825205248 | bytes 31457280 | tf_op jit(solution)/shard_map/middle_back/pallas_call | solution.py:364
  356.0 30.4 %attend_back.1 = (bf16[3,608,1536]{2,1,0:T(8,128)(2,1)}, f32[8,1536]{1,0:T(8,128)S(1)}) custom-call(bf16[3,608,1536]{2,1,0:T(8,128)(2,1)} %bitcast.85, bf16[3,608,1536]{2,1,0:T(8,128)(2,1)} %bitcast.86, bf16[3,608,1536]{2,1,0:T(8,128)(2,1)} %bitcast.87, bf16[3,608,128]{2,1,0:T(8,128)(2,1)S(1)} %broadcast_in_dim.68.kb_ref, ...), custom_call_target="tpu_custom_call" | custom-call | flops 11356078080 | bytes 14008320 | tf_op jit(solution)/shard_map/attend_back/pallas_call | solution.py:229
  388.3 2.6 add_convert_fusion.3.refs_15_
  390.9 1.4 add_convert_fusion.2.refs_16_
  392.3 2.7 add_convert_fusion.1.refs_17_
  395.0 2.6 add_convert_fusion.refs_18_
  397.6 157.7 %tail_stage.1 = (bf16[64,1536]{1,0:T(8,128)(2,1)}, bf16[64,1536]{1,0:T(8,128)(2,1)}, bf16[64,1024]{1,0:T(8,128)(2,1)}, bf16[2,2,128,1024]{3,2,1,0:T(8,128)(2,1)}...) custom-call(bf16[1824,1024]{1,0:T(8,128)(2,1)} %bitcast.107, bf16[1824,1536]{1,0:T(8,128)(2,1)} %bitcast.106, ...), custom_call_target="tpu_custom_call" | custom-call | flops 11475615744 | bytes 41943040 | tf_op jit(solution)/shard_map/tail_stage/pallas_call | solution.py:736
  559.5 1.4 reshape.179
  560.9 4.9 collective-permute-start.43
  565.8 2.5 convert_multiply_fusion
  569.0 2.1 fusion.18
  571.9 1.5 copy.59
  573.4 2.7 mul.181
  576.1 3.9 convert_element_type.148
  580.0 2.5 fusion.16
  582.8 2.5 fusion.14
  585.7 2.0 fusion.20
  587.7 18.1 %collective-permute-done.43 = bf16[3,292,1024]{2,1,0:T(8,128)(2,1)} collective-permute-done((bf16[3,292,1024]{2,1,0:T(8,128)(2,1)S(1)}, bf16[3,292,1024]{2,1,0:T(8,128)(2,1)}, u32[]{:S(2)}, u32[]{:S(2)}) %collective-permute-start.43) | collective-permute-done | bytes 1794080 | tf_op jit(solution)/shard_map/ppermute | solution.py:762
  605.8 3.6 select_convert_fusion
  (251 shorter events, 38.6 us)
Async XLA Ops:
  0.7 79.3 %collective-permute-start = (bf16[3,292,1024]{2,1,0:T(8,128)(2,1)}, bf16[3,292,1024]{2,1,0:T(8,128)(2,1)}, u32[]{:S(2)}, u32[]{:S(2)}) collective-permute-start(bf16[3,292,1024]{2,1,0:T(8,128)(2,1)} %param.19), channel_id=1, source_target_pairs={{2,16},{16,2},{3,17},{17,3},{6,20},{20,6},{7,21},{21,7},{10,24},{2... | collective-permute-start | bytes 5382152 | tf_op jit(solution)/shard_map/ppermute | solution.py:762
  8.3 38.3 %copy-start.61 = (f32[768]{0:T(1024)S(1)}, f32[768]{0:T(1024)}, u32[]{:S(2)}) copy-start(f32[768]{0:T(1024)} %param.27) | copy-start | bytes 9220
  8.3 38.3 %copy-start.60 = (s32[3,584]{1,0:T(4,128)S(1)}, s32[3,584]{1,0:T(4,128)}, u32[]{:S(2)}) copy-start(s32[3,584]{1,0:T(4,128)} %param.20) | copy-start | bytes 21028
  8.7 39.4 %copy-start.26 = (f32[256,1024]{1,0:T(8,128)S(1)}, f32[256,1024]{1,0:T(8,128)}, u32[]{:S(2)}) copy-start(f32[256,1024]{1,0:T(8,128)} %param.25) | copy-start | bytes 3145732
  8.7 1.5 collective-permute-start.5
  8.8 32.2 %collective-permute-start.1 = (bf16[64,1536]{1,0:T(8,128)(2,1)S(1)}, bf16[64,1536]{1,0:T(8,128)(2,1)S(1)}, u32[]{:S(2)}, u32[]{:S(2)}) collective-permute-start(bf16[64,1536]{1,0:T(8,128)(2,1)S(1)} %bitcast.92), channel_id=1, source_target_pairs={{0,16},{16,0},{1,17},{17,1},{2,18},{18,2},{3,19},{19,3},{4,20},{20... | collective-permute-start | bytes 589832 | tf_op jit(solution)/shard_map/ppermute | solution.py:754
  10.2 35.0 %collective-permute-start.6 = (bf16[64,1536]{1,0:T(8,128)(2,1)S(1)}, bf16[64,1536]{1,0:T(8,128)(2,1)S(1)}, u32[]{:S(2)}, u32[]{:S(2)}) collective-permute-start(bf16[64,1536]{1,0:T(8,128)(2,1)S(1)} %collective-permute-done.5), channel_id=1, source_target_pairs={{0,16},{16,0},{1,17},{17,1},{2,18},{18,2},{3,19},{19,3},{4,20},{20... | collective-permute-start | bytes 589832 | tf_op jit(solution)/shard_map/ppermute | solution.py:754
  41.1 66.9 %copy-start.5 = (bf16[2,64,1536]{2,1,0:T(8,128)(2,1)}, bf16[2,64,1536]{2,1,0:T(8,128)(2,1)S(1)}, u32[]{:S(2)}) copy-start(bf16[2,64,1536]{2,1,0:T(8,128)(2,1)S(1)} %pad_maximum_fusion.4.refs_0_.refs_7_) | copy-start | bytes 1179652
  41.1 8.6 %collective-permute-start.3 = (bf16[2,64,1536]{2,1,0:T(8,128)(2,1)S(1)}, bf16[2,64,1536]{2,1,0:T(8,128)(2,1)S(1)}, u32[]{:S(2)}, u32[]{:S(2)}) collective-permute-start(bf16[2,64,1536]{2,1,0:T(8,128)(2,1)S(1)} %pad_maximum_fusion.4.refs_0_.refs_7_), channel_id=1, source_target_pairs={{0,4},{4,0},{1,5},{5,1},{2,6},{6,2},{3,7},{7,3},{8,12},{12,8},{9,1... | collective-permute-start | bytes 1179656 | tf_op jit(solution)/shard_map/ppermute | solution.py:754
  45.3 62.7 %copy-start.6 = (bf16[2,64,1536]{2,1,0:T(8,128)(2,1)}, bf16[2,64,1536]{2,1,0:T(8,128)(2,1)S(1)}, u32[]{:S(2)}) copy-start(bf16[2,64,1536]{2,1,0:T(8,128)(2,1)S(1)} %pad_maximum_fusion.5.refs_4_.refs_11_) | copy-start | bytes 1179652
  45.3 6.7 %collective-permute-start.8 = (bf16[2,64,1536]{2,1,0:T(8,128)(2,1)S(1)}, bf16[2,64,1536]{2,1,0:T(8,128)(2,1)S(1)}, u32[]{:S(2)}, u32[]{:S(2)}) collective-permute-start(bf16[2,64,1536]{2,1,0:T(8,128)(2,1)S(1)} %pad_maximum_fusion.5.refs_4_.refs_11_), channel_id=1, source_target_pairs={{0,8},{8,0},{1,9},{9,1},{2,10},{10,2},{3,11},{11,3},{4,12},{12,4},... | collective-permute-start | bytes 1179656 | tf_op jit(solution)/shard_map/ppermute | solution.py:754
  46.6 33.4 %copy-start.34 = (bf16[3,292,1024]{2,1,0:T(8,128)(2,1)S(1)}, bf16[3,292,1024]{2,1,0:T(8,128)(2,1)}, u32[]{:S(2)}) copy-start(bf16[3,292,1024]{2,1,0:T(8,128)(2,1)} %param.19) | copy-start | bytes 5382148
  48.2 8.0 %collective-permute-start.2 = (bf16[2,64,1536]{2,1,0:T(8,128)(2,1)S(1)}, bf16[2,64,1536]{2,1,0:T(8,128)(2,1)S(1)}, u32[]{:S(2)}, u32[]{:S(2)}) collective-permute-start(bf16[2,64,1536]{2,1,0:T(8,128)(2,1)S(1)} %pad_maximum_fusion.4.refs_0_.refs_7_), channel_id=1, source_target_pairs={{0,8},{8,0},{1,9},{9,1},{2,10},{10,2},{3,11},{11,3},{4,12},{12,4},... | collective-permute-start | bytes 1179656 | tf_op jit(solution)/shard_map/ppermute | solution.py:754
  48.4 8.5 %collective-permute-start.7 = (bf16[2,64,1536]{2,1,0:T(8,128)(2,1)S(1)}, bf16[2,64,1536]{2,1,0:T(8,128)(2,1)S(1)}, u32[]{:S(2)}, u32[]{:S(2)}) collective-permute-start(bf16[2,64,1536]{2,1,0:T(8,128)(2,1)S(1)} %pad_maximum_fusion.5.refs_4_.refs_11_), channel_id=1, source_target_pairs={{0,4},{4,0},{1,5},{5,1},{2,6},{6,2},{3,7},{7,3},{8,12},{12,8},{9,1... | collective-permute-start | bytes 1179656 | tf_op jit(solution)/shard_map/ppermute | solution.py:754
  49.7 58.3 %copy-start.12 = (bf16[2,64,1536]{2,1,0:T(8,128)(2,1)}, bf16[2,64,1536]{2,1,0:T(8,128)(2,1)S(1)}, u32[]{:S(2)}) copy-start(bf16[2,64,1536]{2,1,0:T(8,128)(2,1)S(1)} %collective-permute-done.3.refs_1_.refs_8_) | copy-start | bytes 1179652
  49.7 28.7 %collective-permute-start.4 = (bf16[2,64,1536]{2,1,0:T(8,128)(2,1)S(1)}, bf16[2,64,1536]{2,1,0:T(8,128)(2,1)S(1)}, u32[]{:S(2)}, u32[]{:S(2)}) collective-permute-start(bf16[2,64,1536]{2,1,0:T(8,128)(2,1)S(1)} %collective-permute-done.3.refs_1_.refs_8_), channel_id=1, source_target_pairs={{0,8},{8,0},{1,9},{9,1},{2,10},{10,2},{3,11},{11,3},{4,12},{12,4},... | collective-permute-start | bytes 1179656 | tf_op jit(solution)/shard_map/ppermute | solution.py:754
  52.0 27.2 %copy-start.13 = (bf16[2,64,1536]{2,1,0:T(8,128)(2,1)}, bf16[2,64,1536]{2,1,0:T(8,128)(2,1)S(1)}, u32[]{:S(2)}) copy-start(bf16[2,64,1536]{2,1,0:T(8,128)(2,1)S(1)} %collective-permute-done.8.refs_6_.refs_13_) | copy-start | bytes 1179652
  52.0 27.2 %collective-permute-start.9 = (bf16[2,64,1536]{2,1,0:T(8,128)(2,1)S(1)}, bf16[2,64,1536]{2,1,0:T(8,128)(2,1)S(1)}, u32[]{:S(2)}, u32[]{:S(2)}) collective-permute-start(bf16[2,64,1536]{2,1,0:T(8,128)(2,1)S(1)} %collective-permute-done.8.refs_6_.refs_13_), channel_id=1, source_target_pairs={{0,4},{4,0},{1,5},{5,1},{2,6},{6,2},{3,7},{7,3},{8,12},{12,8},{9,1... | collective-permute-start | bytes 1179656 | tf_op jit(solution)/shard_map/ppermute | solution.py:754
  56.9 27.5 %collective-permute-start.11 = (bf16[16,768]{1,0:T(8,128)(2,1)S(1)}, bf16[16,768]{1,0:T(8,128)(2,1)S(1)}, u32[]{:S(2)}, u32[]{:S(2)}) collective-permute-start(bf16[16,768]{1,0:T(8,128)(2,1)S(1)} %broadcast_select_fusion.6), channel_id=1, source_target_pairs={{0,16},{16,0},{1,17},{17,1},{2,18},{18,2},{3,19},{19,3},{4,20},{20... | collective-permute-start | bytes 73736 | tf_op jit(solution)/shard_map/ppermute | solution.py:754
  57.7 28.1 %collective-permute-start.15 = (f32[3,584]{1,0:T(4,128)S(1)}, f32[3,584]{1,0:T(4,128)S(1)}, u32[]{:S(2)}, u32[]{:S(2)}) collective-permute-start(f32[3,584]{1,0:T(4,128)S(1)} %convert_element_type.118), channel_id=1, source_target_pairs={{0,2},{2,0},{1,3},{3,1},{4,6},{6,4},{5,7},{7,5},{8,10},{10,8},{9,1... | collective-permute-start | bytes 21032 | tf_op jit(solution)/shard_map/ppermute | solution.py:754
  81.7 22.0 %collective-permute-start.10 = (bf16[3,292,1024]{2,1,0:T(8,128)(2,1)S(1)}, bf16[3,292,1024]{2,1,0:T(8,128)(2,1)}, u32[]{:S(2)}, u32[]{:S(2)}) collective-permute-start(bf16[3,292,1024]{2,1,0:T(8,128)(2,1)S(1)} %broadcast_select_fusion.1.own_ref.refs_3_), channel_id=1, source_target_pairs={{0,2},{2,0},{1,3},{3,1},{4,6},{6,4},{5,7},{7,5},{8,10},{10,8},{9,1... | collective-permute-start | bytes 5382152 | tf_op jit(solution)/shard_map/ppermute | solution.py:754
  84.5 43.2 %copy-start.9 = (s32[8]{0:T(128)}, s32[8]{0:T(128)S(1)}, u32[]{:S(2)}) copy-start(s32[8]{0:T(128)S(1)} %stack.70.at_ref.refs_0_) | copy-start | bytes 100
  84.6 2.7 collective-permute-start.12
  87.3 6.3 %collective-permute-start.13 = (bf16[16,768]{1,0:T(8,128)(2,1)S(1)}, bf16[16,768]{1,0:T(8,128)(2,1)S(1)}, u32[]{:S(2)}, u32[]{:S(2)}) collective-permute-start(bf16[16,768]{1,0:T(8,128)(2,1)S(1)} %fusion.26), channel_id=1, source_target_pairs={{0,4},{4,0},{1,5},{5,1},{2,6},{6,2},{3,7},{7,3},{8,12},{12,8},{9,1... | collective-permute-start | bytes 73736 | tf_op jit(solution)/shard_map/ppermute | solution.py:754
  88.5 8.9 %collective-permute-start.17 = (bf16[64,1024]{1,0:T(8,128)(2,1)S(1)}, bf16[64,1024]{1,0:T(8,128)(2,1)S(1)}, u32[]{:S(2)}, u32[]{:S(2)}) collective-permute-start(bf16[64,1024]{1,0:T(8,128)(2,1)S(1)} %convert_element_type.121), channel_id=1, source_target_pairs={{2,16},{16,2},{3,17},{17,3},{6,20},{20,6},{7,21},{21,7},{10,24},{2... | collective-permute-start | bytes 393224 | tf_op jit(solution)/shard_map/ppermute | solution.py:762
  93.7 1.3 collective-permute-start.14
  95.0 32.7 %copy-start.53 = (bf16[16,768]{1,0:T(8,128)(2,1)}, bf16[16,768]{1,0:T(8,128)(2,1)S(1)}, u32[]{:S(2)}) copy-start(bf16[16,768]{1,0:T(8,128)(2,1)S(1)} %add.133) | copy-start | bytes 73732
  95.0 4.4 collective-permute-start.21
  97.5 30.2 %copy-start.51 = (bf16[64,1024]{1,0:T(8,128)(2,1)}, bf16[64,1024]{1,0:T(8,128)(2,1)S(1)}, u32[]{:S(2)}) copy-start(bf16[64,1024]{1,0:T(8,128)(2,1)S(1)} %broadcast_select_fusion.5.refs_0_) | copy-start | bytes 393220
  97.5 5.9 collective-permute-start.18
  97.8 29.9 %copy-start.8 = (f32[1024]{0:T(1024)}, f32[1024]{0:T(1024)S(1)}, u32[]{:S(2)}) copy-start(f32[1024]{0:T(1024)S(1)} %get-tuple-element.158) | copy-start | bytes 12292
  97.8 102.2 %copy-start.7 = (f32[1024]{0:T(1024)}, f32[1024]{0:T(1024)S(1)}, u32[]{:S(2)}) copy-start(f32[1024]{0:T(1024)S(1)} %get-tuple-element.153) | copy-start | bytes 12292
  98.0 70.1 %collective-permute-start.29 = (bf16[2,128,1024]{2,1,0:T(8,128)(2,1)}, bf16[2,128,1024]{2,1,0:T(8,128)(2,1)}, u32[]{:S(2)}, u32[]{:S(2)}) collective-permute-start(bf16[2,128,1024]{2,1,0:T(8,128)(2,1)} %get-tuple-element.79), channel_id=1, source_target_pairs={{0,16},{16,0},{1,17},{17,1},{2,18},{18,2},{3,19},{19,3},{4,20},{20... | collective-permute-start | bytes 1572872 | tf_op jit(solution)/shard_map/ppermute | solution.py:754
  98.1 50.9 %collective-permute-start.19 = (bf16[64,1024]{1,0:T(8,128)(2,1)S(1)}, bf16[64,1024]{1,0:T(8,128)(2,1)S(1)}, u32[]{:S(2)}, u32[]{:S(2)}) collective-permute-start(bf16[64,1024]{1,0:T(8,128)(2,1)S(1)} %broadcast_select_fusion.5.refs_0_), channel_id=1, source_target_pairs={{0,8},{8,0},{1,9},{9,1},{2,10},{10,2},{3,11},{11,3},{4,12},{12,4},... | collective-permute-start | bytes 393224 | tf_op jit(solution)/shard_map/ppermute | solution.py:754
  99.4 49.5 %collective-permute-start.22 = (bf16[64,1024]{1,0:T(8,128)(2,1)S(1)}, bf16[64,1024]{1,0:T(8,128)(2,1)S(1)}, u32[]{:S(2)}, u32[]{:S(2)}) collective-permute-start(bf16[64,1024]{1,0:T(8,128)(2,1)S(1)} %collective-permute-done.21), channel_id=1, source_target_pairs={{2,16},{16,2},{3,17},{17,3},{6,20},{20,6},{7,21},{21,7},{10,24},{2... | collective-permute-start | bytes 393224 | tf_op jit(solution)/shard_map/ppermute | solution.py:762
  103.4 24.3 %copy-start.55 = (bf16[64,1024]{1,0:T(8,128)(2,1)}, bf16[64,1024]{1,0:T(8,128)(2,1)S(1)}, u32[]{:S(2)}) copy-start(bf16[64,1024]{1,0:T(8,128)(2,1)S(1)} %collective-permute-done.18.refs_1_) | copy-start | bytes 393220
  103.4 45.9 %collective-permute-start.20 = (bf16[64,1024]{1,0:T(8,128)(2,1)S(1)}, bf16[64,1024]{1,0:T(8,128)(2,1)S(1)}, u32[]{:S(2)}, u32[]{:S(2)}) collective-permute-start(bf16[64,1024]{1,0:T(8,128)(2,1)S(1)} %collective-permute-done.18.refs_1_), channel_id=1, source_target_pairs={{0,8},{8,0},{1,9},{9,1},{2,10},{10,2},{3,11},{11,3},{4,12},{12,4},... | collective-permute-start | bytes 393224 | tf_op jit(solution)/shard_map/ppermute | solution.py:754
  103.7 77.8 %collective-permute-start.27 = (bf16[3,292,1024]{2,1,0:T(8,128)(2,1)}, bf16[3,292,1024]{2,1,0:T(8,128)(2,1)}, u32[]{:S(2)}, u32[]{:S(2)}) collective-permute-start(bf16[3,292,1024]{2,1,0:T(8,128)(2,1)} %param.21), channel_id=1, source_target_pairs={{2,16},{16,2},{3,17},{17,3},{6,20},{20,6},{7,21},{21,7},{10,24},{2... | collective-permute-start | bytes 5382152 | tf_op jit(solution)/shard_map/ppermute | solution.py:762
  148.9 49.2 %collective-permute-start.16 = (bf16[3,2,304,512]{3,2,1,0:T(8,128)(2,1)S(1)}, bf16[3,2,304,512]{3,2,1,0:T(8,128)(2,1)}, u32[]{:S(2)}, u32[]{:S(2)}) collective-permute-start(bf16[3,2,304,512]{3,2,1,0:T(8,128)(2,1)S(1)} %bitcast.72), channel_id=1, source_target_pairs={{0,2},{2,0},{1,3},{3,1},{4,6},{6,4},{5,7},{7,5},{8,10},{10,8},{9,1... | collective-permute-start | bytes 5603336 | tf_op jit(solution)/shard_map/ppermute | solution.py:754
  149.0 4.6 collective-permute-start.24
  149.3 26.2 %copy-start.32 = (bf16[1,2,128,1024]{3,2,1,0:T(8,128)(2,1)S(1)}, bf16[1,2,128,1024]{3,2,1,0:T(8,128)(2,1)}, u32[]{:S(2)}) copy-start(bf16[1,2,128,1024]{3,2,1,0:T(8,128)(2,1)} %get-tuple-element.141) | copy-start | bytes 1572868
  149.3 26.2 %collective-permute-start.33 = (bf16[2,128,1024]{2,1,0:T(8,128)(2,1)}, bf16[2,128,1024]{2,1,0:T(8,128)(2,1)}, u32[]{:S(2)}, u32[]{:S(2)}) collective-permute-start(bf16[2,128,1024]{2,1,0:T(8,128)(2,1)} %get-tuple-element.82), channel_id=1, source_target_pairs={{0,16},{16,0},{1,17},{17,1},{2,18},{18,2},{3,19},{19,3},{4,20},{20... | collective-permute-start | bytes 1572872 | tf_op jit(solution)/shard_map/ppermute | solution.py:754
  153.7 3.8 collective-permute-start.23
  157.5 3.9 collective-permute-start.25
  164.4 32.5 %collective-permute-start.26 = (bf16[512,1024]{1,0:T(8,128)(2,1)}, bf16[512,1024]{1,0:T(8,128)(2,1)S(1)}, u32[]{:S(2)}, u32[]{:S(2)}) collective-permute-start(bf16[512,1024]{1,0:T(8,128)(2,1)} %gather_rows.1.wo_ref.w_ref), channel_id=1, source_target_pairs={{0,2},{2,0},{1,3},{3,1},{4,6},{6,4},{5,7},{7,5},{8,10},{10,8},{9,1... | collective-permute-start | bytes 3145736 | tf_op jit(solution)/shard_map/ppermute | solution.py:754
  170.4 25.1 %collective-permute-start.30 = (bf16[2,2,128,1024]{3,2,1,0:T(8,128)(2,1)}, bf16[2,2,128,1024]{3,2,1,0:T(8,128)(2,1)}, u32[]{:S(2)}, u32[]{:S(2)}) collective-permute-start(bf16[2,2,128,1024]{3,2,1,0:T(8,128)(2,1)} %pad_maximum_fusion.refs_5_), channel_id=1, source_target_pairs={{0,4},{4,0},{1,5},{5,1},{2,6},{6,2},{3,7},{7,3},{8,12},{12,8},{9,1... | collective-permute-start | bytes 3145736 | tf_op jit(solution)/shard_map/ppermute | solution.py:754
  177.6 22.4 %copy-start = (bf16[512,1024]{1,0:T(8,128)(2,1)S(1)}, bf16[512,1024]{1,0:T(8,128)(2,1)}, u32[]{:S(2)}) copy-start(bf16[512,1024]{1,0:T(8,128)(2,1)} %gather_rows.1.wo_ref.w_ref) | copy-start | bytes 3145732
  177.6 18.1 %collective-permute-start.35 = (bf16[2,2,128,1024]{3,2,1,0:T(8,128)(2,1)}, bf16[2,2,128,1024]{3,2,1,0:T(8,128)(2,1)}, u32[]{:S(2)}, u32[]{:S(2)}) collective-permute-start(bf16[2,2,128,1024]{3,2,1,0:T(8,128)(2,1)} %pad_maximum_fusion.1.refs_9_), channel_id=1, source_target_pairs={{0,8},{8,0},{1,9},{9,1},{2,10},{10,2},{3,11},{11,3},{4,12},{12,4},... | collective-permute-start | bytes 3145736 | tf_op jit(solution)/shard_map/ppermute | solution.py:754
  184.4 59.0 %collective-permute-start.28 = (bf16[3,292,1024]{2,1,0:T(8,128)(2,1)}, bf16[3,292,1024]{2,1,0:T(8,128)(2,1)}, u32[]{:S(2)}, u32[]{:S(2)}) collective-permute-start(bf16[3,292,1024]{2,1,0:T(8,128)(2,1)} %broadcast_select_fusion.refs_2_.go_ref), channel_id=1, source_target_pairs={{0,2},{2,0},{1,3},{3,1},{4,6},{6,4},{5,7},{7,5},{8,10},{10,8},{9,1... | collective-permute-start | bytes 5382152 | tf_op jit(solution)/shard_map/ppermute | solution.py:754
  195.4 25.6 %collective-permute-start.31 = (bf16[2,2,128,1024]{3,2,1,0:T(8,128)(2,1)}, bf16[2,2,128,1024]{3,2,1,0:T(8,128)(2,1)}, u32[]{:S(2)}, u32[]{:S(2)}) collective-permute-start(bf16[2,2,128,1024]{3,2,1,0:T(8,128)(2,1)} %pad_maximum_fusion.refs_5_), channel_id=1, source_target_pairs={{0,8},{8,0},{1,9},{9,1},{2,10},{10,2},{3,11},{11,3},{4,12},{12,4},... | collective-permute-start | bytes 3145736 | tf_op jit(solution)/shard_map/ppermute | solution.py:754
  195.7 25.3 %collective-permute-start.34 = (bf16[2,2,128,1024]{3,2,1,0:T(8,128)(2,1)}, bf16[2,2,128,1024]{3,2,1,0:T(8,128)(2,1)}, u32[]{:S(2)}, u32[]{:S(2)}) collective-permute-start(bf16[2,2,128,1024]{3,2,1,0:T(8,128)(2,1)} %pad_maximum_fusion.1.refs_9_), channel_id=1, source_target_pairs={{0,4},{4,0},{1,5},{5,1},{2,6},{6,2},{3,7},{7,3},{8,12},{12,8},{9,1... | collective-permute-start | bytes 3145736 | tf_op jit(solution)/shard_map/ppermute | solution.py:754
  197.8 45.6 %collective-permute-start.32 = (bf16[2,2,128,1024]{3,2,1,0:T(8,128)(2,1)}, bf16[2,2,128,1024]{3,2,1,0:T(8,128)(2,1)}, u32[]{:S(2)}, u32[]{:S(2)}) collective-permute-start(bf16[2,2,128,1024]{3,2,1,0:T(8,128)(2,1)} %collective-permute-done.30.refs_6_), channel_id=1, source_target_pairs={{0,8},{8,0},{1,9},{9,1},{2,10},{10,2},{3,11},{11,3},{4,12},{12,4},... | collective-permute-start | bytes 3145736 | tf_op jit(solution)/shard_map/ppermute | solution.py:754
  198.1 45.3 %collective-permute-start.36 = (bf16[2,2,128,1024]{3,2,1,0:T(8,128)(2,1)}, bf16[2,2,128,1024]{3,2,1,0:T(8,128)(2,1)}, u32[]{:S(2)}, u32[]{:S(2)}) collective-permute-start(bf16[2,2,128,1024]{3,2,1,0:T(8,128)(2,1)} %collective-permute-done.35.refs_11_), channel_id=1, source_target_pairs={{0,4},{4,0},{1,5},{5,1},{2,6},{6,2},{3,7},{7,3},{8,12},{12,8},{9,1... | collective-permute-start | bytes 3145736 | tf_op jit(solution)/shard_map/ppermute | solution.py:754
  317.3 22.1 %collective-permute-start.37 = (bf16[3,2,304,1024]{3,2,1,0:T(8,128)(2,1)}, bf16[3,2,304,1024]{3,2,1,0:T(8,128)(2,1)}, u32[]{:S(2)}, u32[]{:S(2)}) collective-permute-start(bf16[3,2,304,1024]{3,2,1,0:T(8,128)(2,1)} %bitcast.88), channel_id=1, source_target_pairs={{0,2},{2,0},{1,3},{3,1},{4,6},{6,4},{5,7},{7,5},{8,10},{10,8},{9,1... | collective-permute-start | bytes 11206664 | tf_op jit(solution)/shard_map/ppermute | solution.py:754
  323.9 8.9 %collective-permute-start.42 = (bf16[3,304,1024]{2,1,0:T(8,128)(2,1)}, bf16[3,304,1024]{2,1,0:T(8,128)(2,1)S(1)}, u32[]{:S(2)}, u32[]{:S(2)}) collective-permute-start(bf16[3,304,1024]{2,1,0:T(8,128)(2,1)} %get-tuple-element.113), channel_id=1, source_target_pairs={{0,2},{2,0},{1,3},{3,1},{4,6},{6,4},{5,7},{7,5},{8,10},{10,8},{9,1... | collective-permute-start | bytes 5603336 | tf_op jit(solution)/shard_map/ppermute | solution.py:754
  324.7 61.7 %collective-permute-start.38 = (bf16[2,2,128,1024]{3,2,1,0:T(8,128)(2,1)}, bf16[2,2,128,1024]{3,2,1,0:T(8,128)(2,1)S(1)}, u32[]{:S(2)}, u32[]{:S(2)}) collective-permute-start(bf16[2,2,128,1024]{3,2,1,0:T(8,128)(2,1)} %get-tuple-element.94), channel_id=1, source_target_pairs={{0,8},{8,0},{1,9},{9,1},{2,10},{10,2},{3,11},{11,3},{4,12},{12,4},... | collective-permute-start | bytes 3145736 | tf_op jit(solution)/shard_map/ppermute | solution.py:754
  326.0 60.5 %collective-permute-start.39 = (bf16[2,2,128,1024]{3,2,1,0:T(8,128)(2,1)}, bf16[2,2,128,1024]{3,2,1,0:T(8,128)(2,1)S(1)}, u32[]{:S(2)}, u32[]{:S(2)}) collective-permute-start(bf16[2,2,128,1024]{3,2,1,0:T(8,128)(2,1)} %get-tuple-element.97), channel_id=1, source_target_pairs={{0,8},{8,0},{1,9},{9,1},{2,10},{10,2},{3,11},{11,3},{4,12},{12,4},... | collective-permute-start | bytes 3145736 | tf_op jit(solution)/shard_map/ppermute | solution.py:754
  326.2 60.2 %collective-permute-start.40 = (bf16[2,2,128,1024]{3,2,1,0:T(8,128)(2,1)}, bf16[2,2,128,1024]{3,2,1,0:T(8,128)(2,1)}, u32[]{:S(2)}, u32[]{:S(2)}) collective-permute-start(bf16[2,2,128,1024]{3,2,1,0:T(8,128)(2,1)} %get-tuple-element.100), channel_id=1, source_target_pairs={{0,4},{4,0},{1,5},{5,1},{2,6},{6,2},{3,7},{7,3},{8,12},{12,8},{9,1... | collective-permute-start | bytes 3145736 | tf_op jit(solution)/shard_map/ppermute | solution.py:754
  332.8 55.0 %collective-permute-start.41 = (bf16[2,2,128,1024]{3,2,1,0:T(8,128)(2,1)}, bf16[2,2,128,1024]{3,2,1,0:T(8,128)(2,1)}, u32[]{:S(2)}, u32[]{:S(2)}) collective-permute-start(bf16[2,2,128,1024]{3,2,1,0:T(8,128)(2,1)} %get-tuple-element.103), channel_id=1, source_target_pairs={{0,4},{4,0},{1,5},{5,1},{2,6},{6,2},{3,7},{7,3},{8,12},{12,8},{9,1... | collective-permute-start | bytes 3145736 | tf_op jit(solution)/shard_map/ppermute | solution.py:754
  356.0 31.7 %copy-start.63 = (f32[8,1024]{1,0:T(8,128)S(1)}, f32[8,1024]{1,0:T(8,128)}, u32[]{:S(2)}) copy-start(f32[8,1024]{1,0:T(8,128)} %get-tuple-element.92) | copy-start | bytes 98308
  356.0 32.3 %copy-start.62 = (f32[32,128]{1,0:T(8,128)S(1)}, f32[32,128]{1,0:T(8,128)}, u32[]{:S(2)}) copy-start(f32[32,128]{1,0:T(8,128)} %get-tuple-element.93) | copy-start | bytes 49156
  356.0 32.3 %copy-start.43 = (bf16[2,2,128,1024]{3,2,1,0:T(8,128)(2,1)S(1)}, bf16[2,2,128,1024]{3,2,1,0:T(8,128)(2,1)}, u32[]{:S(2)}) copy-start(bf16[2,2,128,1024]{3,2,1,0:T(8,128)(2,1)} %get-tuple-element.96) | copy-start | bytes 3145732
  397.6 163.3 %copy-start.25 = (bf16[3,292,1024]{2,1,0:T(8,128)(2,1)S(1)}, bf16[3,292,1024]{2,1,0:T(8,128)(2,1)}, u32[]{:S(2)}) copy-start(bf16[3,292,1024]{2,1,0:T(8,128)(2,1)} %fusion.2) | copy-start | bytes 5382148
  560.9 44.9 %collective-permute-start.43 = (bf16[3,292,1024]{2,1,0:T(8,128)(2,1)S(1)}, bf16[3,292,1024]{2,1,0:T(8,128)(2,1)}, u32[]{:S(2)}, u32[]{:S(2)}) collective-permute-start(bf16[3,292,1024]{2,1,0:T(8,128)(2,1)S(1)} %copy-done.25), channel_id=1, source_target_pairs={{2,16},{16,2},{3,17},{17,3},{6,20},{20,6},{7,21},{21,7},{10,24},{2... | collective-permute-start | bytes 5382152 | tf_op jit(solution)/shard_map/ppermute | solution.py:762
  (47 other events, 235.1 us)

commit v4 on v3

--- a/solution.py
+++ b/solution.py
@@ -41,13 +41,14 @@
 def mlp_kernel(keys,*refs,gtile):
     nk=len(keys)
     at_ref,h2_ref,go_ref,gt_ref,bu_ref=refs[:5]
-    pa,pb=refs[5:5+nk],refs[5+nk:5+2*nk]
-    o=5+2*nk
+    own=refs[5:7]
+    pa,pb=refs[7:7+nk],refs[7+nk:7+2*nk]
+    o=7+2*nk
     ga,gb=refs[o:o+nk],refs[o+nk:o+2*nk]
     yown_ref,yoth_ref,dh_ref,gbu_ref=refs[o+2*nk:o+2*nk+4]
     w,dd,a_all,du_all,y_acc,dh_acc,g_out,wsem,gsem=refs[o+2*nk+4:]
     images,half,feat=go_ref.shape
-    hid=pa[0].shape[2]
+    hid=pa[0].shape[1]
     width=4*hid
     padded=h2_ref.shape[0]//(2*images)
     blocks=2*images
@@ -59,7 +60,8 @@
                 for kz in range(2):
                     for ud in range(2):
                         for ab,src in enumerate((pa[ki],pb[ki])):
-                            cp=pltpu.make_async_copy(src.at[kz,ud],w.at[slot,ud,pl.ds((kz*2+ab)*hid,hid)],wsem.at[slot,kz*4+ud*2+ab])
+                            src=own[ab].at[keys[ki][0],keys[ki][1]] if kz==0 else src
+                            cp=pltpu.make_async_copy(src.at[ud],w.at[slot,ud,pl.ds((kz*2+ab)*hid,hid)],wsem.at[slot,kz*4+ud*2+ab])
                             cp.start() if go else cp.wait()
     def save(i,go):
         for ki in range(nk):
@@ -129,15 +131,15 @@
     dh_ref[...]=dh_acc[...].astype(BF)
     save(nk-1,False)
 
-def mlp(at,h2,g_own,g_oth,bu_rows,fa,fb,gtile=256):
+def mlp(at,h2,g_own,g_oth,bu_rows,own_a,own_b,fa,fb,gtile=256):
     keys=sorted(fa); nk=len(keys)
     images,half,feat=g_own.shape
     tokens=h2.shape[0]; padded=tokens//(2*images)
-    _,_,hid,_=fa[keys[0]].shape
+    ud,hid,_=fa[keys[0]].shape
     width=4*hid
-    piece=jax.ShapeDtypeStruct(fa[keys[0]].shape,BF)
+    piece=jax.ShapeDtypeStruct((2,ud,hid,feat),BF)
     out=pl.pallas_call(functools.partial(mlp_kernel,keys,gtile=min(gtile,width)),
-        in_specs=[SM]+[VM]*4+[ANY]*(2*nk),
+        in_specs=[SM]+[VM]*4+[ANY]*(2+2*nk),
         out_specs=[ANY]*(2*nk)+[VM]*4,
         out_shape=[piece]*(2*nk)+[jax.ShapeDtypeStruct((images,padded,feat),F32),jax.ShapeDtypeStruct((images,padded,feat),BF),
             jax.ShapeDtypeStruct((tokens,feat),BF),jax.ShapeDtypeStruct(bu_rows.shape,F32)],
@@ -147,7 +149,7 @@
         name="feed_forward",
         compiler_params=pltpu.CompilerParams(vmem_limit_bytes=60<<20),
         cost_estimate=pl.CostEstimate(flops=nk*6*2*tokens*feat*width,bytes_accessed=40<<20,transcendentals=nk*tokens*width),
-    )(at,h2,g_own,g_oth,bu_rows,*[fa[k] for k in keys],*[fb[k] for k in keys])
+    )(at,h2,g_own,g_oth,bu_rows,own_a,own_b,*[fa[k] for k in keys],*[fb[k] for k in keys])
     return dict(zip(keys,out[:nk])),dict(zip(keys,out[nk:2*nk])),out[2*nk],out[2*nk+1],out[2*nk+2],out[2*nk+3]
 
 HD=64; HALF_D=512
@@ -477,17 +479,15 @@
     return total
 
 
-def tail_kernel(keys, ny, nx, *refs):
-    nk = len(keys)
-    h1_ref, dqkv_ref, go_ref, x_ref, dx_ref, gain_ref, vec_ref = refs[:7]
-    wa, wb = refs[7:7 + nk], refs[7 + nk:7 + 2 * nk]
-    o = 7 + 2 * nk
+def tail_kernel(ny, nx, *refs):
+    h1_ref, dqkv_ref, go_ref, x_ref, dx_ref, gain_ref, vec_ref, w = refs[:8]
+    o = 8
     fa, fb = refs[o:o + nx], refs[o + nx:o + nx + ny]
     o += nx + ny
     mine_ref, theirs_ref, so_ref, sf_ref, ig_ref, vout_ref, norm_ref = refs[o:o + 7]
-    (w, grad, ra1, ra2, rb1, rb2, sa, sb, oa1, oa2, ob1, ob2, ta, tb, osum, ocross, ocore, odp, ofin,
+    (grad, ra1, ra2, rb1, rb2, sa, sb, oa1, oa2, ob1, ob2, ta, tb, osum, ocross, ocore, odp, ofin,
      rfa, rfb, fsum, fpart, frecv, fdp, isum, ipart, irecv, idp, ifin,
-     buf, give, got, stage, vrecv, nrecv, nval, wsem, send_sem, recv_sem) = refs[o + 7:]
+     buf, give, got, stage, vrecv, nrecv, nval, send_sem, recv_sem) = refs[o + 7:]
     h, y, x, c, l = (lax.axis_index(a) for a in AXES)
     images, half, feat = x_ref.shape
     padded = dx_ref.shape[1]
@@ -501,14 +501,6 @@
     xx = [lax.rem(x + k, nx) for k in range(nx)]
     zz = [h, 1 - h]
     wires = Wires(send_sem, recv_sem)
-    loads = []
-    for ki, (ky, kx) in enumerate(keys):
-        for kz in range(2):
-            for core, src in ((c, wa), (1 - c, wb)):
-                row = (((zz[kz] * ny + yy[ky]) * nx + xx[kx]) * 2 + core) * rows
-                cp = pltpu.make_async_copy(src[ki].at[kz], w.at[pl.ds(pl.multiple_of(row, 16), rows)], wsem.at[len(loads)])
-                cp.start()
-                loads.append(cp)
     greet([to_core, to_seq, to_dp] + to_x[1:] + to_y[1:], cross, apart)
 
     ff_got = [wires.send(fa[k], rfa.at[k - 1], to_x[k]) for k in range(1, nx)]
@@ -533,8 +525,6 @@
         for ky in range(ny):
             for kz in range(2):
                 ib_got.append(wires.send(grad.at[zz[kz], yy[ky], xx[kx], 1 - c], rb1.at[kx - 1, kz, ky], to_x[kx]))
-    for cp in loads:
-        cp.wait()
     dh_got = []
     for i in range(images):
         r = (2 * i + 1) * padded
@@ -705,12 +695,10 @@
     wires.finish()
 
 
-def tail_stage(h1, dqkv, g_out, x_own, dx2, gain, vec, wa, wb, fa, fb, ny, nx):
-    keys = sorted(wa)
-    nk = len(keys)
+def tail_stage(h1, dqkv, g_out, x_own, dx2, gain, vec, w, fa, fb, ny, nx):
     tokens, feat = h1.shape
     width = dqkv.shape[1]
-    rows = wa[keys[0]].shape[1]
+    rows = feat // (4 * ny * nx)
     rows_o = g_out.shape[3]
     images, half, _ = x_own.shape
     padded = dx2.shape[1]
@@ -718,10 +706,10 @@
     ma, mb = max(ny - 1, 1), max(nx - 1, 1)
     piece, out_piece, ff = (rows, width), (rows_o, feat), (ud, hid, feat)
     peers = 4 + nx - 1 + ny - 1
-    many = 200 + 8 * nk * 4
+    many = 200 + 32 * ny * nx
     V = lambda *s: pltpu.VMEM(s, BF)
     scratch = [
-        V(feat, width), V(2, ny, nx, 2, *piece),
+        V(2, ny, nx, 2, *piece),
         V(ny - 1, 2, nx, *piece), V(nx - 1, 2, *piece), V(nx - 1, 2, ny, *piece), V(ny - 1, 2, *piece),
         V(nx - 1, 2, *piece), V(ny - 1, 2, *piece),
         V(ny - 1, nx, *out_piece), V(nx - 1, *out_piece), V(nx - 1, ny, *out_piece), V(ny - 1, *out_piece),
@@ -731,11 +719,11 @@
         V(2, 2, *piece), V(2, *piece), V(*piece), V(2, *piece), V(2, *piece),
         pltpu.VMEM((padded, feat), F32), V(images, padded, feat), V(images, padded, feat), V(images, half, feat),
         pltpu.VMEM((peers,) + vec.shape, F32), pltpu.VMEM((peers, 8, 128), F32), pltpu.VMEM((8, 128), F32),
-        pltpu.SemaphoreType.DMA((4 * nk,)), pltpu.SemaphoreType.DMA((many,)), pltpu.SemaphoreType.DMA((many,)),
+        pltpu.SemaphoreType.DMA((many,)), pltpu.SemaphoreType.DMA((many,)),
     ]
     return pl.pallas_call(
-        functools.partial(tail_kernel, keys, ny, nx),
-        in_specs=[VM] * 7 + [ANY] * (2 * nk) + [VM] * (nx + ny),
+        functools.partial(tail_kernel, ny, nx),
+        in_specs=[VM] * (8 + nx + ny),
         out_specs=[VM] * 7,
         out_shape=[
             jax.ShapeDtypeStruct(piece, BF), jax.ShapeDtypeStruct(piece, BF), jax.ShapeDtypeStruct(out_piece, BF),
@@ -746,7 +734,284 @@
         name="tail_stage",
         compiler_params=pltpu.CompilerParams(collective_id=1, has_side_effects=True, vmem_limit_bytes=62 << 20),
         cost_estimate=pl.CostEstimate(flops=4 * tokens * feat * width, bytes_accessed=40 << 20, transcendentals=0),
-    )(h1, dqkv, g_out, x_own, dx2, gain[None], vec, *[wa[k] for k in keys], *[wb[k] for k in keys], *fa, *fb)
+    )(h1, dqkv, g_out, x_own, dx2, gain[None], vec, w, *fa, *fb)
+
+def head_kernel(ny, nx, *refs):
+    (in_ref, out_ref, up_ref, down_ref, vec_ref, img_ref,
+     h1_ref, qkv_ref, xb, w, my_out, other_out, fa, fb, cast_ref, vfull,
+     theirs, o_own, o_core, tmp, buf, xsem, csem, send_sem, recv_sem) = refs
+    h, y, x, c, _ = (lax.axis_index(a) for a in AXES)
+    images, half, feat = img_ref.shape
+    rows = in_ref.shape[0]
+    width = w.shape[1]
+    part = width // 3
+    hid = up_ref.shape[0] // 2
+    apart = h != c
+    cross = {"seq": 1 - h, "core": 1 - c}
+    to_core, to_seq = {"core": 1 - c}, {"seq": 1 - h}
+    to_x = [{"x": lax.rem(x + nx - k, nx)} for k in range(nx)]
+    to_y = [{"y": lax.rem(y + ny - k, ny)} for k in range(ny)]
+    yy = [lax.rem(y + k, ny) for k in range(ny)]
+    xx = [lax.rem(x + k, nx) for k in range(nx)]
+    zz = [h, 1 - h]
+    wires = Wires(send_sem, recv_sem)
+    barrier = pltpu.get_barrier_semaphore()
+    peers = [to_core, to_seq] + to_x[1:] + to_y[1:]
+    for peer in peers:
+        pl.semaphore_signal(barrier, inc=1, device_id=peer, device_id_type=MESH_ID)
+
+    @pl.when(apart)
+    def _():
+        pl.semaphore_signal(barrier, inc=1, device_id=cross, device_id_type=MESH_ID)
+
+    local_images = pltpu.make_async_copy(img_ref, xb.at[0], xsem)
+
+    @pl.when(jnp.logical_not(apart))
+    def _():
+        local_images.start()
+
+    def slot(z, yi, xi, core):
+        return w.at[pl.ds(pl.multiple_of((((z * ny + yi) * nx + xi) * 2 + core) * rows, 16), rows)]
+
+    mine = slot(h, y, x, c)
+    for t in range(3):
+        mine[:, t * part:(t + 1) * part] = in_ref[:, pl.ds(pl.multiple_of(t * 2 * part + c * part, 128), part)].astype(BF)
+        theirs[:, t * part:(t + 1) * part] = in_ref[:, pl.ds(pl.multiple_of(t * 2 * part + (1 - c) * part, 128), part)].astype(BF)
+    vfull[h, y, x, c] = vec_ref[...].astype(BF).astype(F32)
+    o_own[...] = out_ref[...].astype(BF)
+    pl.semaphore_wait(barrier, len(peers) + jnp.where(apart, 1, 0))
+
+    def spread(piece_at, kz, first):
+        got = {}
+        for k in range(1, nx):
+            got[0, k] = wires.send(piece_at(kz, 0, 0), piece_at(kz, 0, 0, k, "x"), to_x[k])
+        for k in range(1, ny):
+            got[k, 0] = wires.send(piece_at(kz, 0, 0), piece_at(kz, 0, 0, k, "y"), to_y[k])
+        return got
+
+    def forward(piece_at, kz, first, got):
+        if first == "x":
+            for kx in range(1, nx):
+                got[0, kx].wait_recv()
+                for ky in range(1, ny):
+                    got[ky, kx] = wires.send(piece_at(kz, 0, kx), piece_at(kz, 0, kx, ky, "y"), to_y[ky])
+            for ky in range(1, ny):
+                got[ky, 0].wait_recv()
+        else:
+            for ky in range(1, ny):
+                got[ky, 0].wait_recv()
+                for kx in range(1, nx):
+                    got[ky, kx] = wires.send(piece_at(kz, ky, 0), piece_at(kz, ky, 0, kx, "x"), to_x[kx])
+            for kx in range(1, nx):
+                got[0, kx].wait_recv()
+
+    def settle(got):
+        for (ky, kx), cp in got.items():
+            if ky > 0 and kx > 0:
+                cp.wait_recv()
+
+    def in_a(kz, ky, kx, *_):
+        return slot(zz[kz], yy[ky], xx[kx], c)
+
+    def in_b(kz, ky, kx, *_):
+        return slot(zz[kz], yy[ky], xx[kx], 1 - c)
+
+    def out_a(kz, ky, kx, *_):
+        return my_out.at[yy[ky], xx[kx], h]
+
+    def out_b(kz, ky, kx, *_):
+        return my_out.at[yy[ky], xx[kx], 1 - h]
+
+    def by_offset(store, own):
+        def piece_at(kz, ky, kx, k=0, axis=""):
+            if k == 0 and ky == 0 and kx == 0:
+                return own
+            return store.at[ky + (k if axis == "y" else 0), kx + (k if axis == "x" else 0)]
+
+        return piece_at
+
+    ff_a, ff_b = by_offset(fa, tmp.at[0]), by_offset(fb, tmp.at[1])
+
+    b_got = wires.send(theirs, slot(h, y, x, c), to_core)
+    az = wires.send(mine, mine, to_seq)
+    a0 = spread(in_a, 0, "x")
+    vec_peers = [[to_core], to_x[1:], to_y[1:], [to_seq]]
+    vec_at = [vfull.at[h, y, x, c], vfull.at[h, y, x], vfull.at[h, y], vfull.at[h]]
+
+    def vec_send(r):
+        return [wires.send(vec_at[r], vec_at[r], peer) for peer in vec_peers[r]]
+
+    v = vec_send(0)
+    oc = wires.send(o_own, o_core, to_core)
+    xl = wires.make(img_ref, xb.at[1], to_core)
+
+    @pl.when(jnp.logical_not(apart))
+    def _():
+        xl.start()
+
+    b_got.wait_recv()
+    bz = wires.send(in_b(0, 0, 0), in_b(0, 0, 0), to_seq)
+    b0 = spread(in_b, 0, "y")
+    for cp in v:
+        cp.wait_recv()
+    v = vec_send(1)
+    for ab in range(2):
+        tmp[ab, 0] = up_ref[ab * hid:(ab + 1) * hid, :].astype(BF)
+        tmp[ab, 1] = down_ref[ab * hid:(ab + 1) * hid, :].astype(BF)
+    keep = [
+        pltpu.make_async_copy(tmp.at[0], fa.at[0, 0], csem.at[0]),
+        pltpu.make_async_copy(tmp.at[1], fb.at[0, 0], csem.at[1]),
+        pltpu.make_async_copy(tmp, cast_ref, csem.at[2]),
+    ]
+    for cp in keep:
+        cp.start()
+    for cp in v:
+        cp.wait_recv()
+    v = vec_send(2)
+    forward(in_a, 0, "x", a0)
+    forward(in_b, 0, "y", b0)
+    az.wait_recv()
+    a1 = spread(in_a, 1, "x")
+    bz.wait_recv()
+    b1 = spread(in_b, 1, "y")
+    for cp in v:
+        cp.wait_recv()
+    v = vec_send(3)
+    oc.wait_recv()
+    x_cross = [wires.make(img_ref.at[i], xb.at[0, i], cross) for i in range(images)]
+    o_cross = [wires.make(o_own, my_out.at[y, x, 1 - h], cross), wires.make(o_core, my_out.at[y, x, h], cross)]
+
+    @pl.when(apart)
+    def _():
+        x_cross[0].start()
+        for cp in o_cross:
+            cp.start()
+        for cp in x_cross[1:]:
+            cp.start()
+
+    @pl.when(jnp.logical_not(apart))
+    def _():
+        my_out[y, x, h] = o_own[...]
+        my_out[y, x, 1 - h] = o_core[...]
+        local_images.wait()
+
+    forward(in_a, 1, "x", a1)
+    forward(in_b, 1, "y", b1)
+    fa0 = spread(ff_a, 0, "x")
+    fb0 = spread(ff_b, 0, "y")
+    for got in (a0, b0, a1, b1):
+        settle(got)
+    for cp in v:
+        cp.wait_recv()
+
+    def row(start, count):
+        per = vec_ref.shape[1]
+        pieces, at = [], start
+        while at < start + count:
+            s, r = at // per, at % per
+            n = min(per - r, start + count - at)
+            xs = s // 2
+            pieces.append(vfull[xs // (nx * ny), xs // nx % ny, xs % nx, s % 2][:, r:r + n])
+            at += n
+        return pieces[0] if len(pieces) == 1 else jnp.concatenate(pieces, axis=1)
+
+    gain, shift_row = row(0, feat), row(feat, feat)
+    q_row, v_row = row(2 * feat, feat), row(3 * feat, feat)
+    q_row = jnp.where(c == 0, q_row[:, :part], q_row[:, part:])
+    v_row = jnp.where(c == 0, v_row[:, :part], v_row[:, part:])
+    bias = jnp.concatenate([q_row, jnp.zeros((1, part), F32), v_row], axis=1)
+
+    def project(i, s):
+        value = wide_rows(buf, xb[s, i])
+        normed = (norm_parts(value)[0] * gain + shift_row).astype(BF)
+        h1_ref[i, s] = normed
+        qkv_ref[i, s] = (dot(normed, w[...]) + bias).astype(BF)
+
+    near = jnp.where(apart, 1, 0)
+
+    @pl.when(apart)
+    def _():
+        xl.wait_recv()
+
+    def near_step(i, carry):
+        project(i, near)
+        return carry
+
+    lax.fori_loop(0, images, near_step, 0)
+
+    @pl.when(apart)
+    def _():
+        for cp in o_cross:
+            cp.wait_recv()
+
+    oa = spread(out_a, 0, "x")
+    ob = spread(out_b, 0, "y")
+    forward(ff_a, 0, "x", fa0)
+    forward(ff_b, 0, "y", fb0)
+    x_core = [wires.make(xb.at[0, i], xb.at[1, i], to_core) for i in range(images)]
+    for i in range(images):
+        @pl.when(apart)
+        def _():
+            x_cross[i].wait_recv()
+            x_core[i].start()
+
+        @pl.when(jnp.logical_not(apart))
+        def _():
+            x_core[i].wait_recv()
+
+        project(i, 1 - near)
+        if i == 0:
+            forward(out_a, 0, "x", oa)
+            forward(out_b, 0, "y", ob)
+        if i == 1 or images == 1:
+            settle(oa)
+            settle(ob)
+            other = wires.send(my_out, other_out, to_core)
+    other.wait_recv()
+    settle(fa0)
+    settle(fb0)
+
+    @pl.when(apart)
+    def _():
+        for cp in x_cross + o_cross + x_core:
+            cp.wait_send()
+
+    @pl.when(jnp.logical_not(apart))
+    def _():
+        xl.wait_send()
+
+    for cp in keep:
+        cp.wait()
+    wires.finish()
+
+
+def head_stage(in_w, out_w, up_w, down_w, vec, images, padded, ny, nx):
+    n, half, feat = images.shape
+    rows, rows_out, rows_ff = in_w.shape[0], out_w.shape[0], up_w.shape[0]
+    width = in_w.shape[1] // 2
+    hid = rows_ff // 2
+    many = 60 + 24 * ny * nx
+    S = jax.ShapeDtypeStruct
+    return pl.pallas_call(
+        functools.partial(head_kernel, ny, nx),
+        in_specs=[VM] * 5 + [ANY],
+        out_specs=[VM] * 6 + [ANY] * 3 + [VM],
+        out_shape=[
+            S((n, 2, padded, feat), BF), S((n, 2, padded, width), BF), S((2, n, half, feat), BF), S((feat, width), BF),
+            S((ny, nx, 2, rows_out, feat), BF), S((ny, nx, 2, rows_out, feat), BF),
+            S((ny, nx, 2, hid, feat), BF), S((ny, nx, 2, hid, feat), BF), S((2, 2, hid, feat), BF),
+            S((2, ny, nx, 2, 1, vec.shape[1]), F32),
+        ],
+        scratch_shapes=[
+            pltpu.VMEM((rows, width), BF), pltpu.VMEM((rows_out, feat), BF), pltpu.VMEM((rows_out, feat), BF),
+            pltpu.VMEM((2, 2, hid, feat), BF), pltpu.VMEM((padded, feat), F32),
+            pltpu.SemaphoreType.DMA(()), pltpu.SemaphoreType.DMA((3,)),
+            pltpu.SemaphoreType.DMA((many,)), pltpu.SemaphoreType.DMA((many,)),
+        ],
+        name="head_stage",
+        compiler_params=pltpu.CompilerParams(collective_id=2, has_side_effects=True, vmem_limit_bytes=60 << 20),
+        cost_estimate=pl.CostEstimate(flops=n * 4 * padded * feat * width, bytes_accessed=40 << 20, transcendentals=0),
+    )(in_w, out_w, up_w, down_w, vec, images)
 
 
 def shift(value, axis, up):
@@ -833,64 +1098,46 @@
     shard = ((h * ny + y) * nx + x) * 2 + c
     at = jnp.stack([h, y, x, c, jnp.int32(ny), jnp.int32(nx), jnp.int32(0), jnp.int32(0)]).astype(jnp.int32)
 
-    placed = jnp.where(
-        lax.broadcasted_iota(jnp.int32, (shards, 1), 0) == shard, vectors.astype(BF)[None, :], jnp.zeros((), BF)
+    h1, qkv, x_both, full_in, my_out, other_out, own_a, own_b, low_ff, full_vec = head_stage(
+        in_weights, out_weights, up_weights, down_weights, vectors[None], images, padded, ny, nx
     )
-    full_vec = small_sum(placed, SHARD).reshape(-1).astype(F32)
+    my_out, other_out = my_out.reshape(HALF_D, D), other_out.reshape(HALF_D, D)
+    x_own, x_oth = x_both[0], x_both[1]
+    rows_in, rows_out, rows_ff = in_weights.shape[0], out_weights.shape[0], up_weights.shape[0]
+    half_ff = rows_ff // 2
+    keys = [(ky, kx) for ky in range(ny) for kx in range(nx)]
+    full_vec = full_vec.reshape(-1)
     gain_one, shift_one, query_bias, value_bias, out_bias, gain_two, shift_two, down_bias = (
         full_vec[i * D : (i + 1) * D] for i in range(8)
     )
     up_bias = full_vec[8 * D :]
 
-    rows_in = in_weights.shape[0]
-    by_core = in_weights.astype(BF).reshape(rows_in, 3, 2, HALF_D)
-    mine = jnp.where(c == 0, by_core[:, :, 0], by_core[:, :, 1]).reshape(rows_in, 3 * HALF_D)
-    theirs = jnp.where(c == 0, by_core[:, :, 1], by_core[:, :, 0]).reshape(rows_in, 3 * HALF_D)
-    in_za = jnp.stack(gather_list(mine, "seq"))
-    in_zb = jnp.stack(gather_list(shift(theirs, "core", 1), "seq"))
-    in_a = gather_plane(in_za, "x", "y")
-    in_b = gather_plane(in_zb, "y", "x")
-    keys = sorted(in_a)
-
-    x_got = crossing(images)
-    x_own = pick(images, after(x_got, list(in_a.values()), list(in_b.values())))
-    x_oth = shift(x_own, "core", 1)
     mask = key_mask.astype(F32)
     mask = jnp.where(h == c, mask, shift(mask, "core", 1)).reshape(image_count, 2, half)
     mask = jnp.where(c == 0, mask, mask[:, ::-1])
     mask = jnp.pad(mask, ((0, 0), (0, 0), (0, padded - half))).reshape(image_count, 2 * padded)
     key_fill = jnp.broadcast_to(jnp.where(mask > 0, 0.0, NEG_FILL)[..., None], mask.shape + (128,)).astype(BF)
 
-    out_low = after(out_weights.astype(BF), in_za, in_zb)
-    rows_out = out_low.shape[0]
-    out_a = gather_plane(crossed(out_low), "x", "y")
-    out_b = gather_plane(crossed(shift(out_low, "core", 1)), "y", "x")
-    my_out = gather_rows(at, out_a, out_b)
-    other_out = shift(my_out, "core", 1)
-
-    rows_ff = up_weights.shape[0]
-    half_ff = rows_ff // 2
-    updown = [jnp.stack([up_weights[r].astype(BF), down_weights[r].astype(BF)]) for r in (slice(0, half_ff), slice(half_ff, rows_ff))]
-    ff_za, ff_zb = (jnp.stack([t, after(shift(after(t, in_za, in_zb), "seq", -1), x_own)]) for t in updown)
-    g_got = crossing(after(out_grad, x_got))
-
-    q_bias = lax.dynamic_slice(query_bias, (c * HALF_D,), (HALF_D,))
-    v_bias = lax.dynamic_slice(value_bias, (c * HALF_D,), (HALF_D,))
-    in_bias = jnp.concatenate([q_bias, jnp.zeros_like(q_bias), v_bias])
-    h1, qkv = project(at, x_own, x_oth, gain_one, shift_one, in_bias, in_a, in_b, padded)
+    ff_near = lax.ppermute(low_ff, ("seq", "dp"), [(1, 2), (2, 1)])
+    g_got = crossing(after(out_grad, ff_near))
+
     tokens = image_count * 2 * padded
-    ff_a = gather_plane(ff_za, "x", "y", qkv)
-    ff_b = gather_plane(ff_zb, "y", "x", qkv)
     qkv = qkv.reshape(image_count, 2 * padded, 3 * HALF_D)
     mixed, lse = attend(qkv, key_fill)
     halved = mixed.reshape(image_count, 2, padded, HALF_D)
     mixed_oth = shift(halved, "core", 1)
-    g_own = pick(out_grad, after(g_got, mixed))
+    ff_near = after(ff_near, mixed)
+    ff_far = lax.ppermute(ff_near, ("seq", "dp"), [(1, 0), (2, 3)])
+    x2, h2 = middle(x_own, x_oth, halved, mixed_oth, my_out, other_out, out_bias, gain_two, shift_two)
+
+    ff_far, h2 = lax.optimization_barrier((ff_far, h2))
+    ff_other = jnp.where(h != lax.axis_index("dp"), ff_near, ff_far)
+    ff_a = gather_plane(ff_other[0], "x", "y")
+    ff_b = gather_plane(ff_other[1], "y", "x")
+    g_own = pick(out_grad, after(g_got, h2))
     g_oth = shift(g_own, "core", 1)
-    x2, h2 = middle(x_own, x_oth, halved, mixed_oth, my_out, other_out, out_bias, gain_two, shift_two)
-
     grad_a, grad_b, y_own, y_oth, dh2, g_bu = mlp(
-        at, h2.reshape(tokens, D), g_own, g_oth, up_bias.reshape(shards * 2, half_ff), ff_a, ff_b
+        at, h2.reshape(tokens, D), g_own, g_oth, up_bias.reshape(shards * 2, half_ff), own_a, own_b, ff_a, ff_b
     )
     result = y_own[:, :half] + shift(y_oth, "core", 1)[:, :half].astype(F32) + x2[:, 0, :half] + down_bias
     result = result.astype(BF)
@@ -924,8 +1171,7 @@
         dx2,
         gain_one,
         vec,
-        in_a,
-        in_b,
+        full_in,
         part_a,
         part_b,
         ny,

time: 615 us -> 578 us (0.940)
  Pallas kernels: 326 us -> 399 us
  starting transfers between devices: 88.5 us -> 25.4 us
  waiting for transfers between devices: 116 us -> 91.3 us
  other arithmetic: 49.5 us -> 36.2 us
  local copies, waits for them, and re-layouts: 26.7 us -> 16.3 us
    pallas_call x3 -> x2, Pallas kernels: 175 us -> 247 us  [the longest x1 157 us: tail_stage(): pl.pallas_call(functools.partial(tail_kernel, ny, nx), in_specs=[VM] * (8...]
    ppermute x39 -> x15, waiting for transfers between devices: 92.7 us -> 36.2 us  [shift(): return lax.ppermute(value, axis, [(i, (i + up) % n) for i in range(n)])]
    ppermute x39 -> x15, starting transfers between devices: 64.7 us -> 11.4 us  [shift(): return lax.ppermute(value, axis, [(i, (i + up) % n) for i in range(n)])]
    ppermute x0 -> x2, waiting for transfers between devices: none -> 27.8 us  [the longest x1 27.7 us: on_device(): ff_far = lax.ppermute(ff_near, ('seq', 'dp'), [(1, 0), (2, 3)])]
    ppermute x5 -> x2, starting transfers between devices: 23.8 us -> 11.5 us  [crossing(): return lax.ppermute(value, ('seq', 'core'), [(1, 2), (2, 1)])]
    unnamed x143 -> x97, local copies, waits for them, and re-layouts: 15.1 us -> 4.92 us
    another operation x7 -> x0, other arithmetic: 7.3 us -> none  [the longest x3 5.73 us: on_device(): jnp.stack([t, after(shift(after(t, in_za, in_zb), 'seq', -1), x_own)])]
    ppermute x5 -> x2, waiting for transfers between devices: 23.1 us -> 27.3 us  [crossing(): return lax.ppermute(value, ('seq', 'core'), [(1, 2), (2, 1)])]
  transfers between devices with their start and end apart: 44 -> 19, of which waited for: 18 -> 8; matrix products, arithmetic and copies ran while one was open for 7% -> 4% of each run, Pallas kernels for 15% -> 29%
where the time goes in v4:
time: 578 us; the launch traced here: 571 us
  Pallas kernels  399 us (69%)
  waiting for transfers between devices  91.3 us (16%)
  other arithmetic  36.2 us (6%)
  starting transfers between devices  25.4 us (4%)
  local copies, waits for them, and re-layouts  16.3 us (3%)
    pallas_call x1, Pallas kernels, tail_stage(): pl.pallas_call(functools.partial(tail_kernel, ny, nx), in_specs=[VM] * (8...  157 us
    pallas_call x1, Pallas kernels, head_stage(): pl.pallas_call(functools.partial(head_kernel, ny, nx), in_specs=[VM] * 5...  90.6 us
    pallas_call x1, Pallas kernels, mlp(): pl.pallas_call(functools.partial(mlp_kernel, keys, gtile=min(gtile, width...  73.8 us
    ppermute x15, waiting for transfers between devices, shift(): return lax.ppermute(value, axis, [(i, (i + up) % n) for i in range(n)])  36.2 us
    pallas_call x1, Pallas kernels, attend_back(): pl.pallas_call(functools.partial(attend_back_kernel, pairs=pairs, chunk=c...  30.4 us
    ppermute x1, waiting for transfers between devices, on_device(): ff_far = lax.ppermute(ff_near, ('seq', 'dp'), [(1, 0), (2, 3)])  27.7 us
    ppermute x2, waiting for transfers between devices, crossing(): return lax.ppermute(value, ('seq', 'core'), [(1, 2), (2, 1)])  27.3 us
    pallas_call x1, Pallas kernels, attend(): pl.pallas_call(attend_kernel, grid=(n, pairs), in_specs=[blk(0), blk(pair...  20.3 us
  transfers between devices with their start and end apart: 19, of which 8 were waited for; matrix products, arithmetic and copies ran while one was open for 4% of the time, Pallas kernels for 29%

profile of v4, /device:TPU:1, one launch (start us, length us, event | category | flops | bytes accessed | tf_op | source)
XLA Modules:
  0.0 571.4 jit_solution(17119662058252804219)
XLA Ops:
  0.7 0.7 convert_element_type.91
  1.4 1.3 broadcast_in_dim.32.refs_4_
  2.7 90.6 %head_stage.1 = (bf16[3,2,304,1024]{3,2,1,0:T(8,128)(2,1)}, bf16[3,2,304,1536]{3,2,1,0:T(8,128)(2,1)}, bf16[2,3,292,1024]{3,2,1,0:T(8,128)(2,1)}, bf16[1024,1536...) custom-call(f32[64,3072]{1,0:T(8,128)} %refs_0_.1, ...), custom_call_target="tpu_custom_call" | custom-call | flops 5737807872 | bytes 41943040 | tf_op jit(solution)/shard_map/head_stage/pallas_call | solution.py:995
  93.3 0.7 collective-permute-start.2
  94.4 0.3 broadcast_in_dim.34.kb_ref
  94.8 20.3 %attend.1 = (bf16[3,608,512]{2,1,0:T(8,128)(2,1)S(1)}, f32[3,4,8,608]{3,2,1,0:T(8,128)S(1)}) custom-call(bf16[3,608,1536]{2,1,0:T(8,128)(2,1)} %bitcast.66, bf16[3,608,1536]{2,1,0:T(8,128)(2,1)} %bitcast.67, bf16[3,608,1536]{2,1,0:T(8,128)(2,1)} %bitcast.68, bf16[3,608,128]{2,1,0:T(8,128)(2,1)S(1)} %broadcast_in_dim.34.kb_ref), custom_call_target="tpu_custom_call" | custom-call | flops 4542431232 | bytes 8404992 | tf_op jit(solution)/shard_map/attend/pallas_call | solution.py:183
  115.2 0.7 copy-done.5
  115.8 1.8 collective-permute-start.1
  117.6 6.6 %collective-permute-start.4 = (bf16[3,292,1024]{2,1,0:T(8,128)(2,1)S(1)}, bf16[3,292,1024]{2,1,0:T(8,128)(2,1)}, u32[]{:S(2)}, u32[]{:S(2)}) collective-permute-start(bf16[3,292,1024]{2,1,0:T(8,128)(2,1)S(1)} %copy-done.12), channel_id=1, source_target_pairs={{2,16},{16,2},{3,17},{17,3},{6,20},{20,6},{7,21},{21,7},{10,24},{2... | collective-permute-start | bytes 5382152 | tf_op jit(solution)/shard_map/ppermute | solution.py:1027
  124.3 1.8 collective-permute-start.3
  126.0 0.6 fusion.19
  126.6 1.6 slice_bitcast_fusion.1
  128.3 1.3 copy-done.44
  129.5 10.2 %middle.1 = (f32[3,2,304,1024]{3,2,1,0:T(8,128)}, bf16[3,2,304,1024]{3,2,1,0:T(8,128)(2,1)}) custom-call(bf16[3,292,1024]{2,1,0:T(8,128)(2,1)S(1)} %get-tuple-element.144.own_ref.refs_3_, bf16[3,292,1024]{2,1,0:T(8,128)(2,1)} %get-tuple-element.143.oth_ref, bf16[3,2,304,512]{3,2,1,0:T(8,128)(2,1)} %bitcast.57, bf16[3,2,304,512]{3,2,1,0:T(8,128)(2,1)} %copy-done.44, ...), custom_call_target="tpu_custom_call" | custom-call | flops 3825205248 | bytes 27262976 | tf_op jit(solution)/shard_map/middle/pallas_call | solution.py:332
  139.7 27.7 %collective-permute-done.3 = bf16[2,2,128,1024]{3,2,1,0:T(8,128)(2,1)S(1)} collective-permute-done((bf16[2,2,128,1024]{3,2,1,0:T(8,128)(2,1)S(1)}, bf16[2,2,128,1024]{3,2,1,0:T(8,128)(2,1)S(1)}, u32[]{:S(2)}, u32[]{:S(2)}) %collective-permute-start.3) | collective-permute-done | bytes 1048608 | tf_op jit(solution)/shard_map/ppermute | solution.py:1130
  167.5 2.1 broadcast_select_fusion.refs_2_.go_ref
  169.7 1.9 broadcast_select_fusion.1
  171.7 0.3 collective-permute-start.6
  172.1 1.2 collective-permute-start.10
  173.3 0.3 collective-permute-start.7
  173.5 1.2 collective-permute-start.9
  174.7 10.8 %collective-permute-done.6.refs_8_ = bf16[2,128,1024]{2,1,0:T(8,128)(2,1)} collective-permute-done((bf16[2,128,1024]{2,1,0:T(8,128)(2,1)S(1)}, bf16[2,128,1024]{2,1,0:T(8,128)(2,1)}, u32[]{:S(2)}, u32[]{:S(2)}) %collective-permute-start.6) | collective-permute-done | bytes 524320 | tf_op jit(solution)/shard_map/ppermute | solution.py:1019
  185.6 0.2 collective-permute-start.8
  185.8 1.2 collective-permute-start.11
  187.0 0.6 slice.95.refs_4_
  187.7 0.6 stack.19.refs_0_
  188.3 8.5 %collective-permute-done.7.refs_9_ = bf16[2,128,1024]{2,1,0:T(8,128)(2,1)} collective-permute-done((bf16[2,128,1024]{2,1,0:T(8,128)(2,1)S(1)}, bf16[2,128,1024]{2,1,0:T(8,128)(2,1)}, u32[]{:S(2)}, u32[]{:S(2)}) %collective-permute-start.7) | collective-permute-done | bytes 524320 | tf_op jit(solution)/shard_map/ppermute | solution.py:1019
  196.8 11.2 %collective-permute-done.8.refs_10_ = bf16[2,128,1024]{2,1,0:T(8,128)(2,1)} collective-permute-done((bf16[2,128,1024]{2,1,0:T(8,128)(2,1)}, bf16[2,128,1024]{2,1,0:T(8,128)(2,1)}, u32[]{:S(2)}, u32[]{:S(2)}) %collective-permute-start.8) | collective-permute-done | bytes 524320 | tf_op jit(solution)/shard_map/ppermute | solution.py:1019
  208.1 73.8 %feed_forward.1 = (bf16[2,2,128,1024]{3,2,1,0:T(8,128)(2,1)}, bf16[2,2,128,1024]{3,2,1,0:T(8,128)(2,1)}, bf16[2,2,128,1024]{3,2,1,0:T(8,128)(2,1)}, bf16[2,2,128...) custom-call(s32[8]{0:T(128)} %stack.19.refs_0_, ...), custom_call_target="tpu_custom_call" | custom-call | flops 45902462976 | bytes 41943040 | tf_op jit(solution)/shard_map/feed_forward/pallas_call | solution.py:141
  281.8 1.0 collective-permute-start.12
  283.6 1.3 collective-permute-start.13
  284.9 0.3 collective-permute-start.14
  285.2 1.2 collective-permute-start.15
  286.4 5.6 collective-permute-done.17
  292.0 1.2 collective-permute-start.16
  293.2 4.8 fusion.2
  298.0 16.8 %middle_back.1 = (f32[3,304,1024]{2,1,0:T(8,128)}, bf16[3,2,304,512]{3,2,1,0:T(8,128)(2,1)}, bf16[512,1024]{1,0:T(8,128)(2,1)}, f32[8,1024]{1,0:T(8,128)}) custom-call(f32[3,2,304,1024]{3,2,1,0:T(8,128)} %get-tuple-element.80.x2_ref, bf16[3,2,304,1024]{3,2,1,0:T(8,128)(2,1)} %bitcast.73, bf16[3,2,304,1024]{3,2,1,0:T(8,128)(2,1)} %collective-permute-done.12.db_ref, ...), custom_call_target="tpu_custom_call" | custom-call | flops 3825205248 | bytes 31457280 | tf_op jit(solution)/shard_map/middle_back/pallas_call | solution.py:366
  314.9 30.4 %attend_back.1 = (bf16[3,608,1536]{2,1,0:T(8,128)(2,1)}, f32[8,1536]{1,0:T(8,128)S(1)}) custom-call(bf16[3,608,1536]{2,1,0:T(8,128)(2,1)} %bitcast.69, bf16[3,608,1536]{2,1,0:T(8,128)(2,1)} %bitcast.70, bf16[3,608,1536]{2,1,0:T(8,128)(2,1)} %bitcast.71, bf16[3,608,128]{2,1,0:T(8,128)(2,1)S(1)} %broadcast_in_dim.34.kb_ref, ...), custom_call_target="tpu_custom_call" | custom-call | flops 11356078080 | bytes 14008320 | tf_op jit(solution)/shard_map/attend_back/pallas_call | solution.py:231
  345.3 0.9 copy-done.22
  346.2 0.3 copy-done.23
  346.6 0.3 dynamic_update_slice.6
  346.9 0.2 dynamic_update_slice.7
  347.1 2.9 add_convert_fusion.3.refs_8_
  350.1 2.7 add_convert_fusion.2.refs_9_
  352.8 2.7 add_convert_fusion.1.refs_10_
  355.5 2.6 add_convert_fusion.refs_11_
  358.1 156.8 %tail_stage.1 = (bf16[64,1536]{1,0:T(8,128)(2,1)}, bf16[64,1536]{1,0:T(8,128)(2,1)}, bf16[64,1024]{1,0:T(8,128)(2,1)}, bf16[2,2,128,1024]{3,2,1,0:T(8,128)(2,1)}...) custom-call(bf16[1824,1024]{1,0:T(8,128)(2,1)} %bitcast.87, bf16[1824,1536]{1,0:T(8,128)(2,1)} %bitcast.86, ...), custom_call_target="tpu_custom_call" | custom-call | flops 11475615744 | bytes 41943040 | tf_op jit(solution)/shard_map/tail_stage/pallas_call | solution.py:724
  514.9 1.2 slice.85
  516.1 1.1 reshape.146
  517.2 1.1 reshape.145
  519.1 0.6 copy.51
  519.7 1.6 mul.176
  521.3 2.5 convert_multiply_fusion
  523.8 4.9 collective-permute-start.18
  528.8 3.9 convert_element_type.119
  532.8 1.1 fusion.15
  533.8 0.6 fusion.9
  534.5 1.9 fusion.17
  536.7 0.6 copy-done.15
  537.3 0.3 copy-done.16
  537.7 0.3 copy-done.17
  538.0 3.6 fusion.11
  541.6 27.3 %collective-permute-done.18 = bf16[3,292,1024]{2,1,0:T(8,128)(2,1)S(1)} collective-permute-done((bf16[3,292,1024]{2,1,0:T(8,128)(2,1)S(1)}, bf16[3,292,1024]{2,1,0:T(8,128)(2,1)S(1)}, u32[]{:S(2)}, u32[]{:S(2)}) %collective-permute-start.18) | collective-permute-done | bytes 1794080 | tf_op jit(solution)/shard_map/ppermute | solution.py:1027
  568.9 2.1 select_convert_fusion
  (125 shorter events, 1.4 us)
Async XLA Ops:
  1.4 92.7 %collective-permute-start = (f32[3,584]{1,0:T(4,128)S(1)}, f32[3,584]{1,0:T(4,128)S(1)}, u32[]{:S(2)}, u32[]{:S(2)}) collective-permute-start(f32[3,584]{1,0:T(4,128)S(1)} %convert_element_type.91), channel_id=1, source_target_pairs={{0,2},{2,0},{1,3},{3,1},{4,6},{6,4},{5,7},{7,5},{8,10},{10,8},{9,1... | collective-permute-start | bytes 21032 | tf_op jit(solution)/shard_map/ppermute | solution.py:1019
  2.7 91.4 %copy-start.36 = (s32[3,584]{1,0:T(4,128)S(1)}, s32[3,584]{1,0:T(4,128)}, u32[]{:S(2)}) copy-start(s32[3,584]{1,0:T(4,128)} %param.20) | copy-start | bytes 21028
  93.3 24.3 %collective-permute-start.2 = (bf16[2,2,128,1024]{3,2,1,0:T(8,128)(2,1)}, bf16[2,2,128,1024]{3,2,1,0:T(8,128)(2,1)S(1)}, u32[]{:S(2)}, u32[]{:S(2)}) collective-permute-start(bf16[2,2,128,1024]{3,2,1,0:T(8,128)(2,1)} %get-tuple-element.81), channel_id=1, source_target_pairs={{1,16},{16,1},{3,18},{18,3},{5,20},{20,5},{7,22},{22,7},{9,24},{24... | collective-permute-start | bytes 3145736 | tf_op jit(solution)/shard_map/ppermute | solution.py:1121
  94.8 22.9 %copy-start.12 = (bf16[3,292,1024]{2,1,0:T(8,128)(2,1)S(1)}, bf16[3,292,1024]{2,1,0:T(8,128)(2,1)}, u32[]{:S(2)}) copy-start(bf16[3,292,1024]{2,1,0:T(8,128)(2,1)} %param.21) | copy-start | bytes 5382148
  94.8 31.3 %copy-start.37 = (f32[2,2,2,2,1,768]{5,4,3,2,1,0:T(1,128)S(1)}, f32[2,2,2,2,1,768]{5,4,3,2,1,0:T(1,128)}, u32[]{:S(2)}) copy-start(f32[2,2,2,2,1,768]{5,4,3,2,1,0:T(1,128)} %get-tuple-element.79) | copy-start | bytes 147460
  94.8 31.9 %copy-start.10 = (bf16[2,3,292,1024]{3,2,1,0:T(8,128)(2,1)S(1)}, bf16[2,3,292,1024]{3,2,1,0:T(8,128)(2,1)}, u32[]{:S(2)}) copy-start(bf16[2,3,292,1024]{3,2,1,0:T(8,128)(2,1)} %get-tuple-element.76) | copy-start | bytes 10764292
  115.1 0.7 copy-start.5
  115.8 12.4 %copy-start = (bf16[3,608,512]{2,1,0:T(8,128)(2,1)}, bf16[3,608,512]{2,1,0:T(8,128)(2,1)S(1)}, u32[]{:S(2)}) copy-start(bf16[3,608,512]{2,1,0:T(8,128)(2,1)S(1)} %get-tuple-element.75.o_ref) | copy-start | bytes 5603332
  115.8 12.4 %collective-permute-start.1 = (bf16[3,2,304,512]{3,2,1,0:T(8,128)(2,1)S(1)}, bf16[3,2,304,512]{3,2,1,0:T(8,128)(2,1)S(1)}, u32[]{:S(2)}, u32[]{:S(2)}) collective-permute-start(bf16[3,2,304,512]{3,2,1,0:T(8,128)(2,1)S(1)} %bitcast.56), channel_id=1, source_target_pairs={{0,2},{2,0},{1,3},{3,1},{4,6},{6,4},{5,7},{7,5},{8,10},{10,8},{9,1... | collective-permute-start | bytes 5603336 | tf_op jit(solution)/shard_map/ppermute | solution.py:1019
  117.6 49.8 %collective-permute-start.4 = (bf16[3,292,1024]{2,1,0:T(8,128)(2,1)S(1)}, bf16[3,292,1024]{2,1,0:T(8,128)(2,1)}, u32[]{:S(2)}, u32[]{:S(2)}) collective-permute-start(bf16[3,292,1024]{2,1,0:T(8,128)(2,1)S(1)} %copy-done.12), channel_id=1, source_target_pairs={{2,16},{16,2},{3,17},{17,3},{6,20},{20,6},{7,21},{21,7},{10,24},{2... | collective-permute-start | bytes 5382152 | tf_op jit(solution)/shard_map/ppermute | solution.py:1027
  124.3 43.2 %collective-permute-start.3 = (bf16[2,2,128,1024]{3,2,1,0:T(8,128)(2,1)S(1)}, bf16[2,2,128,1024]{3,2,1,0:T(8,128)(2,1)S(1)}, u32[]{:S(2)}, u32[]{:S(2)}) collective-permute-start(bf16[2,2,128,1024]{3,2,1,0:T(8,128)(2,1)S(1)} %collective-permute-done.2), channel_id=1, source_target_pairs={{1,0},{16,17},{3,2},{18,19},{5,4},{20,21},{7,6},{22,23},{9,8},{24,... | collective-permute-start | bytes 3145736 | tf_op jit(solution)/shard_map/ppermute | solution.py:1130
  126.6 2.9 copy-start.4
  126.6 2.9 copy-start.3
  126.6 2.9 copy-start.7
  128.3 11.4 %copy-start.2 = (bf16[3,292,1024]{2,1,0:T(8,128)(2,1)}, bf16[3,292,1024]{2,1,0:T(8,128)(2,1)S(1)}, u32[]{:S(2)}) copy-start(bf16[3,292,1024]{2,1,0:T(8,128)(2,1)S(1)} %get-tuple-element.144.own_ref.refs_3_) | copy-start | bytes 5382148
  128.3 1.3 copy-start.44
  129.5 37.9 %copy-start.13 = (bf16[3,292,1024]{2,1,0:T(8,128)(2,1)S(1)}, bf16[3,292,1024]{2,1,0:T(8,128)(2,1)}, u32[]{:S(2)}) copy-start(bf16[3,292,1024]{2,1,0:T(8,128)(2,1)} %param.21) | copy-start | bytes 5382148
  167.5 2.1 copy-start.25
  169.6 2.1 copy-start.8
  169.6 38.4 %collective-permute-start.5 = (bf16[3,292,1024]{2,1,0:T(8,128)(2,1)S(1)}, bf16[3,292,1024]{2,1,0:T(8,128)(2,1)}, u32[]{:S(2)}, u32[]{:S(2)}) collective-permute-start(bf16[3,292,1024]{2,1,0:T(8,128)(2,1)S(1)} %broadcast_select_fusion.refs_2_.go_ref), channel_id=1, source_target_pairs={{0,2},{2,0},{1,3},{3,1},{4,6},{6,4},{5,7},{7,5},{8,10},{10,8},{9,1... | collective-permute-start | bytes 5382152 | tf_op jit(solution)/shard_map/ppermute | solution.py:1019
  171.7 36.3 %copy-start.29 = (bf16[2,128,1024]{2,1,0:T(8,128)(2,1)}, bf16[2,128,1024]{2,1,0:T(8,128)(2,1)S(1)}, u32[]{:S(2)}) copy-start(bf16[2,128,1024]{2,1,0:T(8,128)(2,1)S(1)} %get-tuple-element.147.refs_11_) | copy-start | bytes 1572868
  171.7 36.3 %copy-start.30 = (bf16[2,128,1024]{2,1,0:T(8,128)(2,1)}, bf16[2,128,1024]{2,1,0:T(8,128)(2,1)S(1)}, u32[]{:S(2)}) copy-start(bf16[2,128,1024]{2,1,0:T(8,128)(2,1)S(1)} %get-tuple-element.148.refs_7_) | copy-start | bytes 1572868
  171.7 13.8 %collective-permute-start.6 = (bf16[2,128,1024]{2,1,0:T(8,128)(2,1)S(1)}, bf16[2,128,1024]{2,1,0:T(8,128)(2,1)}, u32[]{:S(2)}, u32[]{:S(2)}) collective-permute-start(bf16[2,128,1024]{2,1,0:T(8,128)(2,1)S(1)} %get-tuple-element.148.refs_7_), channel_id=1, source_target_pairs={{0,4},{4,0},{1,5},{5,1},{2,6},{6,2},{3,7},{7,3},{8,12},{12,8},{9,1... | collective-permute-start | bytes 1572872 | tf_op jit(solution)/shard_map/ppermute | solution.py:1019
  172.1 13.8 %collective-permute-start.10 = (bf16[2,128,1024]{2,1,0:T(8,128)(2,1)S(1)}, bf16[2,128,1024]{2,1,0:T(8,128)(2,1)}, u32[]{:S(2)}, u32[]{:S(2)}) collective-permute-start(bf16[2,128,1024]{2,1,0:T(8,128)(2,1)S(1)} %get-tuple-element.147.refs_11_), channel_id=1, source_target_pairs={{0,8},{8,0},{1,9},{9,1},{2,10},{10,2},{3,11},{11,3},{4,12},{12,4},... | collective-permute-start | bytes 1572872 | tf_op jit(solution)/shard_map/ppermute | solution.py:1019
  173.3 23.5 %collective-permute-start.7 = (bf16[2,128,1024]{2,1,0:T(8,128)(2,1)S(1)}, bf16[2,128,1024]{2,1,0:T(8,128)(2,1)}, u32[]{:S(2)}, u32[]{:S(2)}) collective-permute-start(bf16[2,128,1024]{2,1,0:T(8,128)(2,1)S(1)} %get-tuple-element.148.refs_7_), channel_id=1, source_target_pairs={{0,8},{8,0},{1,9},{9,1},{2,10},{10,2},{3,11},{11,3},{4,12},{12,4},... | collective-permute-start | bytes 1572872 | tf_op jit(solution)/shard_map/ppermute | solution.py:1019
  173.5 23.3 %collective-permute-start.9 = (bf16[2,128,1024]{2,1,0:T(8,128)(2,1)S(1)}, bf16[2,128,1024]{2,1,0:T(8,128)(2,1)}, u32[]{:S(2)}, u32[]{:S(2)}) collective-permute-start(bf16[2,128,1024]{2,1,0:T(8,128)(2,1)S(1)} %get-tuple-element.147.refs_11_), channel_id=1, source_target_pairs={{0,4},{4,0},{1,5},{5,1},{2,6},{6,2},{3,7},{7,3},{8,12},{12,8},{9,1... | collective-permute-start | bytes 1572872 | tf_op jit(solution)/shard_map/ppermute | solution.py:1019
  185.6 22.4 %collective-permute-start.8 = (bf16[2,128,1024]{2,1,0:T(8,128)(2,1)}, bf16[2,128,1024]{2,1,0:T(8,128)(2,1)}, u32[]{:S(2)}, u32[]{:S(2)}) collective-permute-start(bf16[2,128,1024]{2,1,0:T(8,128)(2,1)} %collective-permute-done.6.refs_8_), channel_id=1, source_target_pairs={{0,8},{8,0},{1,9},{9,1},{2,10},{10,2},{3,11},{11,3},{4,12},{12,4},... | collective-permute-start | bytes 1572872 | tf_op jit(solution)/shard_map/ppermute | solution.py:1019
  185.8 22.2 %collective-permute-start.11 = (bf16[2,128,1024]{2,1,0:T(8,128)(2,1)}, bf16[2,128,1024]{2,1,0:T(8,128)(2,1)}, u32[]{:S(2)}, u32[]{:S(2)}) collective-permute-start(bf16[2,128,1024]{2,1,0:T(8,128)(2,1)} %collective-permute-done.10.refs_13_), channel_id=1, source_target_pairs={{0,4},{4,0},{1,5},{5,1},{2,6},{6,2},{3,7},{7,3},{8,12},{12,8},{9,1... | collective-permute-start | bytes 1572872 | tf_op jit(solution)/shard_map/ppermute | solution.py:1019
  281.8 16.2 %collective-permute-start.12 = (bf16[3,2,304,1024]{3,2,1,0:T(8,128)(2,1)}, bf16[3,2,304,1024]{3,2,1,0:T(8,128)(2,1)}, u32[]{:S(2)}, u32[]{:S(2)}) collective-permute-start(bf16[3,2,304,1024]{3,2,1,0:T(8,128)(2,1)} %bitcast.72), channel_id=1, source_target_pairs={{0,2},{2,0},{1,3},{3,1},{4,6},{6,4},{5,7},{7,5},{8,10},{10,8},{9,1... | collective-permute-start | bytes 11206664 | tf_op jit(solution)/shard_map/ppermute | solution.py:1019
  282.8 9.1 %collective-permute-start.17 = (bf16[3,304,1024]{2,1,0:T(8,128)(2,1)}, bf16[3,304,1024]{2,1,0:T(8,128)(2,1)}, u32[]{:S(2)}, u32[]{:S(2)}) collective-permute-start(bf16[3,304,1024]{2,1,0:T(8,128)(2,1)} %get-tuple-element.119), channel_id=1, source_target_pairs={{0,2},{2,0},{1,3},{3,1},{4,6},{6,4},{5,7},{7,5},{8,10},{10,8},{9,1... | collective-permute-start | bytes 5603336 | tf_op jit(solution)/shard_map/ppermute | solution.py:1019
  283.6 61.6 %collective-permute-start.13 = (bf16[2,2,128,1024]{3,2,1,0:T(8,128)(2,1)}, bf16[2,2,128,1024]{3,2,1,0:T(8,128)(2,1)S(1)}, u32[]{:S(2)}, u32[]{:S(2)}) collective-permute-start(bf16[2,2,128,1024]{3,2,1,0:T(8,128)(2,1)} %get-tuple-element.100), channel_id=1, source_target_pairs={{0,8},{8,0},{1,9},{9,1},{2,10},{10,2},{3,11},{11,3},{4,12},{12,4},... | collective-permute-start | bytes 3145736 | tf_op jit(solution)/shard_map/ppermute | solution.py:1019
  284.9 60.3 %collective-permute-start.14 = (bf16[2,2,128,1024]{3,2,1,0:T(8,128)(2,1)}, bf16[2,2,128,1024]{3,2,1,0:T(8,128)(2,1)S(1)}, u32[]{:S(2)}, u32[]{:S(2)}) collective-permute-start(bf16[2,2,128,1024]{3,2,1,0:T(8,128)(2,1)} %get-tuple-element.103), channel_id=1, source_target_pairs={{0,8},{8,0},{1,9},{9,1},{2,10},{10,2},{3,11},{11,3},{4,12},{12,4},... | collective-permute-start | bytes 3145736 | tf_op jit(solution)/shard_map/ppermute | solution.py:1019
  285.2 60.1 %collective-permute-start.15 = (bf16[2,2,128,1024]{3,2,1,0:T(8,128)(2,1)}, bf16[2,2,128,1024]{3,2,1,0:T(8,128)(2,1)}, u32[]{:S(2)}, u32[]{:S(2)}) collective-permute-start(bf16[2,2,128,1024]{3,2,1,0:T(8,128)(2,1)} %get-tuple-element.106), channel_id=1, source_target_pairs={{0,4},{4,0},{1,5},{5,1},{2,6},{6,2},{3,7},{7,3},{8,12},{12,8},{9,1... | collective-permute-start | bytes 3145736 | tf_op jit(solution)/shard_map/ppermute | solution.py:1019
  292.0 54.6 %collective-permute-start.16 = (bf16[2,2,128,1024]{3,2,1,0:T(8,128)(2,1)}, bf16[2,2,128,1024]{3,2,1,0:T(8,128)(2,1)}, u32[]{:S(2)}, u32[]{:S(2)}) collective-permute-start(bf16[2,2,128,1024]{3,2,1,0:T(8,128)(2,1)} %get-tuple-element.109), channel_id=1, source_target_pairs={{0,4},{4,0},{1,5},{5,1},{2,6},{6,2},{3,7},{7,3},{8,12},{12,8},{9,1... | collective-permute-start | bytes 3145736 | tf_op jit(solution)/shard_map/ppermute | solution.py:1019
  297.9 16.9 %copy-start.1 = (bf16[3,608,512]{2,1,0:T(8,128)(2,1)S(1)}, bf16[3,608,512]{2,1,0:T(8,128)(2,1)}, u32[]{:S(2)}) copy-start(bf16[3,608,512]{2,1,0:T(8,128)(2,1)} %copy-done) | copy-start | bytes 5603332
  298.0 16.9 %copy-start.6 = (f32[3,4,8,608]{3,2,1,0:T(8,128)S(1)}, f32[3,4,8,608]{3,2,1,0:T(8,128)}, u32[]{:S(2)}) copy-start(f32[3,4,8,608]{3,2,1,0:T(8,128)} %copy-done.5) | copy-start | bytes 700420
  314.8 31.7 %copy-start.40 = (f32[8,1024]{1,0:T(8,128)S(1)}, f32[8,1024]{1,0:T(8,128)}, u32[]{:S(2)}) copy-start(f32[8,1024]{1,0:T(8,128)} %get-tuple-element.97) | copy-start | bytes 98308
  314.9 32.2 %copy-start.39 = (f32[32,128]{1,0:T(8,128)S(1)}, f32[32,128]{1,0:T(8,128)}, u32[]{:S(2)}) copy-start(f32[32,128]{1,0:T(8,128)} %get-tuple-element.98) | copy-start | bytes 49156
  345.2 1.0 copy-start.22
  345.2 1.3 copy-start.23
  346.6 3.5 copy-start.24
  347.1 5.6 copy-start.43
  350.1 2.7 copy-start.21
  352.8 2.7 copy-start.20
  519.7 4.0 copy-start.35
  523.8 45.1 %collective-permute-start.18 = (bf16[3,292,1024]{2,1,0:T(8,128)(2,1)S(1)}, bf16[3,292,1024]{2,1,0:T(8,128)(2,1)S(1)}, u32[]{:S(2)}, u32[]{:S(2)}) collective-permute-start(bf16[3,292,1024]{2,1,0:T(8,128)(2,1)S(1)} %fusion.2), channel_id=1, source_target_pairs={{2,16},{16,2},{3,17},{17,3},{6,20},{20,6},{7,21},{21,7},{10,24},{2... | collective-permute-start | bytes 5382152 | tf_op jit(solution)/shard_map/ppermute | solution.py:1027
  528.7 4.0 copy-start.31
  528.7 4.0 copy-start.32
  528.7 4.0 copy-start.33
  528.7 4.0 copy-start.34
  528.7 5.1 copy-start.38
  528.7 5.1 copy-start.41
  528.7 5.1 copy-start.42
  528.7 5.7 copy-start.26
  528.8 5.7 copy-start.27
  528.8 5.7 copy-start.28
  528.8 7.7 %copy-start.19 = (f32[256,1024]{1,0:T(8,128)S(1)}, f32[256,1024]{1,0:T(8,128)}, u32[]{:S(2)}) copy-start(f32[256,1024]{1,0:T(8,128)} %param.30) | copy-start | bytes 3145732
  532.7 1.8 copy-start.11
  532.7 3.7 copy-start.18
  534.5 2.0 copy-start.9
  534.5 2.2 copy-start.14
  534.5 2.8 copy-start.15
  534.5 3.1 copy-start.16
  534.5 3.4 copy-start.17

commit v5 on v4

--- a/solution.py
+++ b/solution.py
@@ -20,6 +20,95 @@
 AXES = ("seq", "y", "x", "core", "dp")
 SHARD = ("seq", "y", "x", "core")
 
+BF = jnp.bfloat16
+F32 = jnp.float32
+MESH_ID = pl.DeviceIdType.MESH
+
+
+class Wires:
+    def __init__(self, send_sem, recv_sem):
+        self.send_sem, self.recv_sem, self.count, self.sent = send_sem, recv_sem, 0, []
+
+    def make(self, src, dst, to):
+        cp = pltpu.make_async_remote_copy(
+            src_ref=src, dst_ref=dst, send_sem=self.send_sem.at[self.count], recv_sem=self.recv_sem.at[self.count],
+            device_id=to, device_id_type=MESH_ID)
+        self.count += 1
+        return cp
+
+    def send(self, src, dst, to):
+        cp = self.make(src, dst, to)
+        cp.start()
+        self.sent.append(cp)
+        return cp
+
+    def finish(self):
+        for cp in self.sent:
+            cp.wait_send()
+
+
+def greet(peers, crossing_peer, apart):
+    barrier = pltpu.get_barrier_semaphore()
+    for peer in peers:
+        pl.semaphore_signal(barrier, inc=1, device_id=peer, device_id_type=MESH_ID)
+
+    @pl.when(apart)
+    def _():
+        pl.semaphore_signal(barrier, inc=1, device_id=crossing_peer, device_id_type=MESH_ID)
+
+    pl.semaphore_wait(barrier, len(peers) + jnp.where(apart, 1, 0))
+
+
+def add_all(first, *others):
+    total = first.astype(F32)
+    for other in others:
+        total = total + other.astype(F32)
+    return total
+
+
+def plane_moves(wires, to_x, to_y):
+    nx, ny = len(to_x), len(to_y)
+
+    def spread(piece_at, kz, first):
+        got = {}
+        for k in range(1, nx):
+            got[0, k] = wires.send(piece_at(kz, 0, 0), piece_at(kz, 0, 0, k, "x"), to_x[k])
+        for k in range(1, ny):
+            got[k, 0] = wires.send(piece_at(kz, 0, 0), piece_at(kz, 0, 0, k, "y"), to_y[k])
+        return got
+
+    def forward(piece_at, kz, first, got):
+        if first == "x":
+            for kx in range(1, nx):
+                got[0, kx].wait_recv()
+                for ky in range(1, ny):
+                    got[ky, kx] = wires.send(piece_at(kz, 0, kx), piece_at(kz, 0, kx, ky, "y"), to_y[ky])
+            for ky in range(1, ny):
+                got[ky, 0].wait_recv()
+        else:
+            for ky in range(1, ny):
+                got[ky, 0].wait_recv()
+                for kx in range(1, nx):
+                    got[ky, kx] = wires.send(piece_at(kz, ky, 0), piece_at(kz, ky, 0, kx, "x"), to_x[kx])
+            for kx in range(1, nx):
+                got[0, kx].wait_recv()
+
+    def settle(got):
+        for (ky, kx), cp in got.items():
+            if ky > 0 and kx > 0:
+                cp.wait_recv()
+
+    return spread, forward, settle
+
+
+def by_offset(store, own):
+    def piece_at(kz, ky, kx, k=0, axis=""):
+        if k == 0 and ky == 0 and kx == 0:
+            return own
+        return store.at[ky + (k if axis == "y" else 0), kx + (k if axis == "x" else 0)]
+
+    return piece_at
+
 BF=jnp.bfloat16; F32=jnp.float32
 def dot(a, b, dims=(((1,), (0,)), ((), ()))):
     return lax.dot_general(a, b, dims, preferred_element_type=F32)
@@ -38,17 +127,29 @@
     slope=half+(0.5*u)*(1.0-t*t)*(c0+(3*c0*0.044715)*sq)
     return value,slope
 
-def mlp_kernel(keys,*refs,gtile):
+def mlp_kernel(keys,ny,nx,*refs,gtile):
     nk=len(keys)
-    at_ref,h2_ref,go_ref,gt_ref,bu_ref=refs[:5]
-    own=refs[5:7]
-    pa,pb=refs[7:7+nk],refs[7+nk:7+2*nk]
-    o=7+2*nk
+    h2_ref,go_ref,gt_ref,bu_ref=refs[:4]
+    planes=(refs[4:6],refs[6:8])
+    o=8
     ga,gb=refs[o:o+nk],refs[o+nk:o+2*nk]
-    yown_ref,yoth_ref,dh_ref,gbu_ref=refs[o+2*nk:o+2*nk+4]
-    w,dd,a_all,du_all,y_acc,dh_acc,g_out,wsem,gsem=refs[o+2*nk+4:]
+    yown_ref,yoth_ref,dh_ref,gbu_ref,ra_ref,rb_ref=refs[o+2*nk:o+2*nk+6]
+    w,dd,a_all,du_all,y_acc,dh_acc,g_out,wsem,gsem,send_sem,recv_sem=refs[o+2*nk+6:]
+    h,y,x,c,_=(lax.axis_index(a) for a in AXES)
+    to_x=[{"x":lax.rem(x+k,nx)} for k in range(nx)]
+    to_y=[{"y":lax.rem(y+k,ny)} for k in range(ny)]
+    wires=Wires(send_sem,recv_sem)
+    moves=[]
+    for ki,(ky,kx) in enumerate(keys):
+        cps=[]
+        if ky>0: cps.append(wires.make(ga[ki],ra_ref.at[ky-1,kx],to_y[ky]))
+        if kx>0: cps.append(wires.make(gb[ki],rb_ref.at[kx-1,ky],to_x[kx]))
+        moves.append(cps)
+    barrier=pltpu.get_barrier_semaphore()
+    for peer in to_x[1:]+to_y[1:]:
+        pl.semaphore_signal(barrier,inc=1,device_id=peer,device_id_type=MESH_ID)
     images,half,feat=go_ref.shape
-    hid=pa[0].shape[1]
+    hid=planes[0][0].shape[3]
     width=4*hid
     padded=h2_ref.shape[0]//(2*images)
     blocks=2*images
@@ -59,9 +160,8 @@
             def _():
                 for kz in range(2):
                     for ud in range(2):
-                        for ab,src in enumerate((pa[ki],pb[ki])):
-                            src=own[ab].at[keys[ki][0],keys[ki][1]] if kz==0 else src
-                            cp=pltpu.make_async_copy(src.at[ud],w.at[slot,ud,pl.ds((kz*2+ab)*hid,hid)],wsem.at[slot,kz*4+ud*2+ab])
+                        for ab in range(2):
+                            cp=pltpu.make_async_copy(planes[kz][ab].at[keys[ki][0],keys[ki][1],ud],w.at[slot,ud,pl.ds((kz*2+ab)*hid,hid)],wsem.at[slot,kz*4+ud*2+ab])
                             cp.start() if go else cp.wait()
     def save(i,go):
         for ki in range(nk):
@@ -80,8 +180,16 @@
             tail=padded-16
             dd[r+tail:r+padded,:]=jnp.zeros((16,feat),BF)
             dd[r:r+half,:]=src[i]
+    pl.semaphore_wait(barrier,nx+ny-2)
     def step(i,_):
         slot=lax.rem(i,2)
+        @pl.when(i>0)
+        def _(): save(i-1,False)
+        for ki,cps in enumerate(moves):
+            if cps:
+                @pl.when(i==ki+1)
+                def _():
+                    for cp in cps: cp.start()
         load(i,slot,False)
         @pl.when(i+1<nk)
         def _(): load(i+1,1-slot,True)
@@ -90,8 +198,7 @@
             for ab in range(2):
                 row=jnp.int32(0)
                 for ki,(ky,kx) in enumerate(keys):
-                    z=lax.rem(at_ref[0]+kz,2); y=lax.rem(at_ref[1]+ky,at_ref[4]); x=lax.rem(at_ref[2]+kx,at_ref[5])
-                    here=(((z*at_ref[4]+y)*at_ref[5]+x)*2+at_ref[3])*2+ab
+                    here=(((lax.rem(h+kz,2)*ny+lax.rem(y+ky,ny))*nx+lax.rem(x+kx,nx))*2+c)*2+ab
                     row=jnp.where(i==ki,here,row)
                 rows.append(row)
         bias=jnp.concatenate([bu_ref[pl.ds(r,1),:] for r in rows],axis=1)
@@ -116,8 +223,6 @@
         sums=lax.fori_loop(0,blocks,tokens,jnp.zeros((1,width),F32))
         for q,row in enumerate(rows):
             gbu_ref[pl.ds(row,1),:]=sums[:,q*hid:(q+1)*hid]
-        @pl.when(i>0)
-        def _(): save(i-1,False)
         for t in range(0,width,gtile):
             g_out[1,t:t+gtile,:]=dot(a_all[:,t:t+gtile],dd[...],TN).astype(BF)
             g_out[0,t:t+gtile,:]=dot(du_all[:,t:t+gtile],h2_ref[...],TN).astype(BF)
@@ -130,32 +235,37 @@
         yoth_ref[i]=y_acc[r+padded:r+2*padded,:].astype(BF)
     dh_ref[...]=dh_acc[...].astype(BF)
     save(nk-1,False)
-
-def mlp(at,h2,g_own,g_oth,bu_rows,own_a,own_b,fa,fb,gtile=256):
-    keys=sorted(fa); nk=len(keys)
+    for cps in moves:
+        for cp in cps:
+            cp.wait_recv()
+            cp.wait_send()
+
+def mlp(ny,nx,h2,g_own,g_oth,bu_rows,own_a,own_b,oth_a,oth_b,gtile=256):
+    keys=sorted(((ky,kx) for ky in range(ny) for kx in range(nx)),reverse=True); nk=len(keys)
     images,half,feat=g_own.shape
     tokens=h2.shape[0]; padded=tokens//(2*images)
-    ud,hid,_=fa[keys[0]].shape
+    ud,hid=own_a.shape[2:4]
     width=4*hid
     piece=jax.ShapeDtypeStruct((2,ud,hid,feat),BF)
-    out=pl.pallas_call(functools.partial(mlp_kernel,keys,gtile=min(gtile,width)),
-        in_specs=[SM]+[VM]*4+[ANY]*(2+2*nk),
-        out_specs=[ANY]*(2*nk)+[VM]*4,
+    out=pl.pallas_call(functools.partial(mlp_kernel,keys,ny,nx,gtile=min(gtile,width)),
+        in_specs=[VM]*4+[ANY]*4,
+        out_specs=[ANY]*(2*nk)+[VM]*4+[ANY]*2,
         out_shape=[piece]*(2*nk)+[jax.ShapeDtypeStruct((images,padded,feat),F32),jax.ShapeDtypeStruct((images,padded,feat),BF),
-            jax.ShapeDtypeStruct((tokens,feat),BF),jax.ShapeDtypeStruct(bu_rows.shape,F32)],
+            jax.ShapeDtypeStruct((tokens,feat),BF),jax.ShapeDtypeStruct(bu_rows.shape,F32),
+            jax.ShapeDtypeStruct((ny-1,nx,2,ud,hid,feat),BF),jax.ShapeDtypeStruct((nx-1,ny,2,ud,hid,feat),BF)],
         scratch_shapes=[pltpu.VMEM((2,2,width,feat),BF),pltpu.VMEM((tokens,feat),BF),pltpu.VMEM((tokens,width),BF),pltpu.VMEM((tokens,width),BF),
             pltpu.VMEM((tokens,feat),F32),pltpu.VMEM((tokens,feat),F32),pltpu.VMEM((2,width,feat),BF),
-            pltpu.SemaphoreType.DMA((2,8)),pltpu.SemaphoreType.DMA((8,))],
+            pltpu.SemaphoreType.DMA((2,8)),pltpu.SemaphoreType.DMA((8,)),pltpu.SemaphoreType.DMA((2*nk,)),pltpu.SemaphoreType.DMA((2*nk,))],
         name="feed_forward",
-        compiler_params=pltpu.CompilerParams(vmem_limit_bytes=60<<20),
+        compiler_params=pltpu.CompilerParams(collective_id=3,has_side_effects=True,vmem_limit_bytes=60<<20),
         cost_estimate=pl.CostEstimate(flops=nk*6*2*tokens*feat*width,bytes_accessed=40<<20,transcendentals=nk*tokens*width),
-    )(at,h2,g_own,g_oth,bu_rows,own_a,own_b,*[fa[k] for k in keys],*[fb[k] for k in keys])
-    return dict(zip(keys,out[:nk])),dict(zip(keys,out[nk:2*nk])),out[2*nk],out[2*nk+1],out[2*nk+2],out[2*nk+3]
+    )(h2,g_own,g_oth,bu_rows,own_a,own_b,oth_a,oth_b)
+    return dict(zip(keys,out[:nk])),dict(zip(keys,out[nk:2*nk])),out[2*nk:]
 
 HD=64; HALF_D=512
 
-def head_operands(q_ref,k_ref,kb_ref,scale):
-    q=q_ref[0].astype(F32)*scale; k=k_ref[0].astype(F32); kb=kb_ref[0].astype(F32)
+def head_operands(q,k,kb,scale):
+    q=q.astype(F32)*scale; k=k.astype(F32); kb=kb.astype(F32)
     lane=lax.broadcasted_iota(jnp.int32,q.shape,1)
     low=lane<HD
     one=jnp.where((lane==0)|(lane==HD),1.0,0.0)
@@ -163,10 +273,10 @@
     ks=[jnp.where(low,k,kb).astype(BF),jnp.where(low,kb,k).astype(BF)]
     return q,k,low,qs,ks
 
-def attend_kernel(q_ref,k_ref,v_ref,kb_ref,o_ref,lse_ref):
-    q,k,low,qs,ks=head_operands(q_ref,k_ref,kb_ref,HD**-0.5)
-    vt=v_ref[0].astype(F32).T.astype(BF)
-    outs=[]
+def attend_pair(q,k,v,kb):
+    q,k,low,qs,ks=head_operands(q,k,kb,HD**-0.5)
+    vt=v.astype(F32).T.astype(BF)
+    outs=[]; sums=[]
     for j in range(2):
         s=dot(ks[j],qs[j],NT)
         m=jnp.max(s,axis=0,keepdims=True)
@@ -174,27 +284,27 @@
         l=jnp.sum(e,axis=0,keepdims=True)
         o=dot(vt[j*HD:(j+1)*HD],e.astype(BF))
         outs.append(o*(1.0/l))
-        lse_ref[0,0,j:j+1,:]=m+jnp.log(l)
-    o_ref[0]=jnp.concatenate(outs,axis=0).T.astype(BF)
-
-def attend(qkv,kbias):
-    n,rows,w=qkv.shape; pairs=w//3//128
-    blk=lambda off: pl.BlockSpec((1,rows,128),lambda i,p: (i,0,off+p))
-    return pl.pallas_call(attend_kernel,grid=(n,pairs),
-        in_specs=[blk(0),blk(pairs),blk(2*pairs),pl.BlockSpec((1,rows,128),lambda i,p:(i,0,0))],
-        out_specs=[blk(0),pl.BlockSpec((1,1,8,rows),lambda i,p:(i,p,0,0))],
-        out_shape=[jax.ShapeDtypeStruct((n,rows,w//3),BF),jax.ShapeDtypeStruct((n,pairs,8,rows),F32)],
-        name="attend",
-        compiler_params=pltpu.CompilerParams(vmem_limit_bytes=50<<20),
-        cost_estimate=pl.CostEstimate(flops=n*pairs*8*rows*rows*128,bytes_accessed=n*rows*w*3,transcendentals=n*pairs*2*rows*rows),
-    )(qkv,qkv,qkv,kbias)
-
-def attend_back_kernel(q_ref,k_ref,v_ref,kb_ref,o_ref,g_ref,lse_ref,out_ref,sum_ref,*,pairs,chunk):
+        sums.append(m+jnp.log(l))
+    return jnp.concatenate(outs,axis=0).T.astype(BF),sums
+
+def attend_back_kernel(q_ref,k_ref,v_ref,kb_ref,o_ref,g_ref,lse_ref,keep_ref,give_ref,out_ref,sum_ref,part_ref,land,send_sem,recv_sem,*,pairs,chunk):
     p=pl.program_id(1)
+    to_dp={"dp":1-lax.axis_index("dp")}
+    cp=pltpu.make_async_remote_copy(src_ref=give_ref,dst_ref=land,send_sem=send_sem,recv_sem=recv_sem,device_id=to_dp,device_id_type=MESH_ID)
+    @pl.when((pl.program_id(0)==0)&(p==0))
+    def _():
+        barrier=pltpu.get_barrier_semaphore()
+        pl.semaphore_signal(barrier,inc=1,device_id=to_dp,device_id_type=MESH_ID)
+        pl.semaphore_wait(barrier,1)
+        cp.start()
+    @pl.when((pl.program_id(0)==pl.num_programs(0)-1)&(p==pairs-1))
+    def _():
+        cp.wait()
+        part_ref[...]=add_all(keep_ref[...],land[...]).astype(BF)
     @pl.when((pl.program_id(0)==0)&(p==0))
     def _(): sum_ref[...]=jnp.zeros_like(sum_ref)
     scale=HD**-0.5
-    q,k,low,qs,ks=head_operands(q_ref,k_ref,kb_ref,scale)
+    q,k,low,qs,ks=head_operands(q_ref[0],k_ref[0],kb_ref[0],scale)
     qb=q.astype(BF)
     kt=k.T.astype(BF)
     g=g_ref[0]; gf=g.astype(F32)
@@ -224,18 +334,19 @@
         out_ref[0,:,at]=part
         sum_ref[0:1,at]+=jnp.sum(part.astype(F32),axis=0,keepdims=True)
 
-def attend_back(qkv,kbias,mixed,grad,lse,chunk=None):
+def attend_back(qkv,kbias,mixed,grad,lse,keep,give,chunk=None):
     n,rows,w=qkv.shape; pairs=w//3//128
     chunk=chunk or rows
     blk=lambda off: pl.BlockSpec((1,rows,128),lambda i,p: (i,0,off+p))
     return pl.pallas_call(functools.partial(attend_back_kernel,pairs=pairs,chunk=chunk),grid=(n,pairs),
-        in_specs=[blk(0),blk(pairs),blk(2*pairs),pl.BlockSpec((1,rows,128),lambda i,p:(i,0,0)),blk(0),blk(0),pl.BlockSpec((1,1,8,rows),lambda i,p:(i,p,0,0))],
-        out_specs=[pl.BlockSpec((1,rows,w),lambda i,p:(i,0,0)),pl.BlockSpec((8,w),lambda i,p:(0,0))],
-        out_shape=[jax.ShapeDtypeStruct((n,rows,w),BF),jax.ShapeDtypeStruct((8,w),F32)],
+        in_specs=[blk(0),blk(pairs),blk(2*pairs),pl.BlockSpec((1,rows,128),lambda i,p:(i,0,0)),blk(0),blk(0),pl.BlockSpec((1,1,8,rows),lambda i,p:(i,p,0,0)),VM,VM],
+        out_specs=[pl.BlockSpec((1,rows,w),lambda i,p:(i,0,0)),pl.BlockSpec((8,w),lambda i,p:(0,0)),VM],
+        out_shape=[jax.ShapeDtypeStruct((n,rows,w),BF),jax.ShapeDtypeStruct((8,w),F32),jax.ShapeDtypeStruct(keep.shape,BF)],
+        scratch_shapes=[pltpu.VMEM(keep.shape,BF),pltpu.SemaphoreType.DMA(()),pltpu.SemaphoreType.DMA(())],
         name="attend_back",
-        compiler_params=pltpu.CompilerParams(vmem_limit_bytes=50<<20),
+        compiler_params=pltpu.CompilerParams(collective_id=4,has_side_effects=True,vmem_limit_bytes=50<<20),
         cost_estimate=pl.CostEstimate(flops=n*pairs*20*rows*rows*128,bytes_accessed=n*rows*w*5,transcendentals=n*pairs*2*rows*rows),
-    )(qkv,qkv,qkv,kbias,mixed,grad,lse)
+    )(qkv,qkv,qkv,kbias,mixed,grad,lse,keep,give)
 
 NORM_EPS=1e-6
 def norm_parts(values):
@@ -255,86 +366,6 @@
     buf[total-16:,:]=jnp.zeros((16,buf.shape[1]),F32)
     buf[0:n,:]=block.astype(F32)
     return buf[...]
-
-def place(at_ref,keys,ka,size,pieces,buf,sem,gather):
-    def both(go):
-        n=0
-        for ki,(ky,kx) in enumerate(keys):
-            y=lax.rem(at_ref[1]+ky,at_ref[4]); x=lax.rem(at_ref[2]+kx,at_ref[5])
-            for ab in range(2):
-                for kz in range(ka):
-                    z=lax.rem(at_ref[0]+kz,2) if ka==2 else 0
-                    core=at_ref[3] if ab==0 else 1-at_ref[3]
-                    if ka==1: core=at_ref[0] if ab==0 else 1-at_ref[0]
-                    row=(((z*at_ref[4]+y)*at_ref[5]+x)*2+core)*size
-                    inner=buf.at[pl.ds(pl.multiple_of(row,16),size)]
-                    piece=pieces[ab*len(keys)+ki]
-                    piece=piece.at[kz] if ka==2 else piece
-                    cp=pltpu.make_async_copy(piece,inner,sem.at[n]) if gather else pltpu.make_async_copy(inner,piece,sem.at[n])
-                    cp.start() if go else cp.wait()
-                    n+=1
-    both(True); both(False)
-
-def project_kernel(keys,at_ref,own_ref,oth_ref,gain_ref,shift_ref,bias_ref,*refs):
-    nk=len(keys)
-    pieces=refs[:2*nk]; h_ref,qkv_ref,w,buf,sem=refs[2*nk:]
-    @pl.when(pl.program_id(0)==0)
-    def _(): place(at_ref,keys,2,pieces[0].shape[1],pieces,w,sem,True)
-    for s,src in enumerate((own_ref,oth_ref)):
-        v=wide_rows(buf.at[s],src[0])
-        h=(norm_parts(v)[0]*gain_ref[...]+shift_ref[...]).astype(BF)
-        h_ref[0,s]=h
-        qkv_ref[0,s]=(dot(h,w[...])+bias_ref[...]).astype(BF)
-
-def project(at,x_own,x_oth,gain,shift,bias,wa,wb,padded):
-    keys=sorted(wa); nk=len(keys)
-    n,half,feat=x_own.shape
-    width=wa[keys[0]].shape[-1]
-    tok=pl.BlockSpec((1,half,feat),lambda i:(i,0,0))
-    row=lambda w: pl.BlockSpec((1,w),lambda i:(0,0))
-    return pl.pallas_call(functools.partial(project_kernel,keys),grid=(n,),
-        in_specs=[SM,tok,tok,row(feat),row(feat),row(width)]+[ANY]*(2*nk),
-        out_specs=[pl.BlockSpec((1,2,padded,feat),lambda i:(i,0,0,0)),pl.BlockSpec((1,2,padded,width),lambda i:(i,0,0,0))],
-        out_shape=[jax.ShapeDtypeStruct((n,2,padded,feat),BF),jax.ShapeDtypeStruct((n,2,padded,width),BF)],
-        scratch_shapes=[pltpu.VMEM((feat,width),BF),pltpu.VMEM((2,padded,feat),F32),pltpu.SemaphoreType.DMA((4*nk,))],
-        name="project",
-        compiler_params=pltpu.CompilerParams(vmem_limit_bytes=50<<20),
-        cost_estimate=pl.CostEstimate(flops=n*4*padded*feat*width,bytes_accessed=24<<20,transcendentals=0),
-    )(at,x_own,x_oth,gain[None],shift[None],bias[None],*[wa[k] for k in keys],*[wb[k] for k in keys])
-
-def gather_kernel(keys,at_ref,*refs):
-    nk=len(keys)
-    place(at_ref,keys,1,refs[0].shape[0],refs[:2*nk],refs[2*nk],refs[2*nk+1],True)
-
-def gather_rows(at,pa,pb):
-    keys=sorted(pa); nk=len(keys)
-    rows,feat=pa[keys[0]].shape
-    return pl.pallas_call(functools.partial(gather_kernel,keys),in_specs=[SM]+[ANY]*(2*nk),out_specs=VM,
-        out_shape=jax.ShapeDtypeStruct((2*nk*rows,feat),BF),scratch_shapes=[pltpu.SemaphoreType.DMA((2*nk,))],name="gather_rows",
-    )(at,*[pa[k] for k in keys],*[pb[k] for k in keys])
-
-def middle_kernel(own_ref,oth_ref,mo_ref,mt_ref,wo_ref,wt_ref,bias_ref,gain_ref,shift_ref,x2_ref,h2_ref,buf):
-    for s,src in enumerate((own_ref,oth_ref)):
-        v=wide_rows(buf.at[s],src[0])
-        v=v+(dot(mo_ref[0,s],wo_ref[...])+dot(mt_ref[0,1-s],wt_ref[...]))+bias_ref[...]
-        x2_ref[0,s]=v
-        h2_ref[0,s]=(norm_parts(v)[0]*gain_ref[...]+shift_ref[...]).astype(BF)
-
-def middle(x_own,x_oth,mixed,mixed_oth,w_own,w_oth,bias,gain,shift):
-    n,half,feat=x_own.shape
-    _,_,padded,width=mixed.shape
-    tok=pl.BlockSpec((1,half,feat),lambda i:(i,0,0))
-    mix=pl.BlockSpec((1,2,padded,width),lambda i:(i,0,0,0))
-    swp=pl.BlockSpec((1,2,padded,width),lambda i:(i,0,0,0))
-    full=pl.BlockSpec((width,feat),lambda i:(0,0))
-    row=pl.BlockSpec((1,feat),lambda i:(0,0))
-    out=pl.BlockSpec((1,2,padded,feat),lambda i:(i,0,0,0))
-    return pl.pallas_call(middle_kernel,grid=(n,),in_specs=[tok,tok,mix,swp,full,full,row,row,row],out_specs=[out,out],
-        out_shape=[jax.ShapeDtypeStruct((n,2,padded,feat),F32),jax.ShapeDtypeStruct((n,2,padded,feat),BF)],
-        scratch_shapes=[pltpu.VMEM((2,padded,feat),F32)],name="middle",
-        compiler_params=pltpu.CompilerParams(vmem_limit_bytes=50<<20),
-        cost_estimate=pl.CostEstimate(flops=n*8*padded*feat*width,bytes_accessed=26<<20,transcendentals=0),
-    )(x_own,x_oth,mixed,mixed_oth,w_own,w_oth,bias[None],gain[None],shift[None])
 
 def middle_back_kernel(x2_ref,da_ref,db_ref,go_ref,gt_ref,mix_ref,w_ref,gain_ref,dx_ref,dat_ref,gw_ref,sum_ref,buf,acc):
     i=pl.program_id(0)
@@ -372,121 +403,14 @@
         cost_estimate=pl.CostEstimate(flops=n*8*padded*feat*width,bytes_accessed=30<<20,transcendentals=0),
     )(x2,dh_own,dh_oth,g_own,g_oth,mixed,w_own,gain[None])
 
-def grad_in_kernel(keys,tile,at_ref,h_ref,d_ref,*refs):
-    nk=len(keys)
-    pieces=refs[:2*nk]; buf,sem=refs[2*nk:]
-    for t in range(0,h_ref.shape[1],tile):
-        buf[t:t+tile,:]=dot(h_ref[:,t:t+tile],d_ref[...],TN).astype(BF)
-    place(at_ref,keys,2,pieces[0].shape[1],pieces,buf,sem,False)
-
-def grad_in(at,h1,dqkv,keys,rows):
-    tokens,feat=h1.shape; width=dqkv.shape[1]
-    nk=len(keys)
-    out=pl.pallas_call(functools.partial(grad_in_kernel,keys,256),in_specs=[SM,VM,VM],out_specs=[ANY]*(2*nk),
-        out_shape=[jax.ShapeDtypeStruct((2,rows,width),BF)]*(2*nk),
-        scratch_shapes=[pltpu.VMEM((feat,width),BF),pltpu.SemaphoreType.DMA((4*nk,))],name="grad_in",
-        compiler_params=pltpu.CompilerParams(vmem_limit_bytes=50<<20),
-        cost_estimate=pl.CostEstimate(flops=2*tokens*feat*width,bytes_accessed=14<<20,transcendentals=0),
-    )(at,h1,dqkv)
-    return dict(zip(keys,out[:nk])),dict(zip(keys,out[nk:]))
-
-def project_back_kernel(keys,at_ref,d_ref,*refs):
-    nk=len(keys)
-    pieces=refs[:2*nk]; own_ref,oth_ref,w,sem=refs[2*nk:]
-    @pl.when(pl.program_id(0)==0)
-    def _(): place(at_ref,keys,2,pieces[0].shape[1],pieces,w,sem,True)
-    own_ref[0]=dot(d_ref[0,0],w[...],NT)
-    oth_ref[0]=dot(d_ref[0,1],w[...],NT).astype(BF)
-
-def project_back(at,dqkv,wa,wb):
-    keys=sorted(wa); nk=len(keys)
-    n,_,padded,width=dqkv.shape
-    feat=wa[keys[0]].shape[1]*4*nk
-    out=pl.BlockSpec((1,padded,feat),lambda i:(i,0,0))
-    return pl.pallas_call(functools.partial(project_back_kernel,keys),grid=(n,),
-        in_specs=[SM,pl.BlockSpec((1,2,padded,width),lambda i:(i,0,0,0))]+[ANY]*(2*nk),out_specs=[out,out],
-        out_shape=[jax.ShapeDtypeStruct((n,padded,feat),F32),jax.ShapeDtypeStruct((n,padded,feat),BF)],
-        scratch_shapes=[pltpu.VMEM((feat,width),BF),pltpu.SemaphoreType.DMA((4*nk,))],name="project_back",
-        compiler_params=pltpu.CompilerParams(vmem_limit_bytes=50<<20),
-        cost_estimate=pl.CostEstimate(flops=n*4*padded*feat*width,bytes_accessed=18<<20,transcendentals=0),
-    )(at,dqkv,*[wa[k] for k in keys],*[wb[k] for k in keys])
-
-def input_back_kernel(x_ref,da_ref,db_ref,dx_ref,gain_ref,out_ref,sum_ref,buf):
-    @pl.when(pl.program_id(0)==0)
-    def _(): sum_ref[...]=jnp.zeros_like(sum_ref)
-    half=x_ref.shape[1]
-    v=wide_rows(buf,x_ref[0])
-    grad=da_ref[0]+db_ref[0].astype(F32)
-    dx,gg=norm_back(v,gain_ref[...],grad)
-    out_ref[0]=(dx+dx_ref[0]).astype(BF)[:half]
-    sum_ref[0:1,:]+=jnp.sum(gg,axis=0,keepdims=True)
-    sum_ref[1:2,:]+=jnp.sum(grad,axis=0,keepdims=True)
-
-def input_back(x_own,dh_own,dh_oth,dx2,gain):
-    n,half,feat=x_own.shape
-    padded=dx2.shape[1]
-    tok=pl.BlockSpec((1,half,feat),lambda i:(i,0,0))
-    big=pl.BlockSpec((1,padded,feat),lambda i:(i,0,0))
-    return pl.pallas_call(input_back_kernel,grid=(n,),in_specs=[tok,big,big,big,pl.BlockSpec((1,feat),lambda i:(0,0))],
-        out_specs=[tok,pl.BlockSpec((8,feat),lambda i:(0,0))],
-        out_shape=[jax.ShapeDtypeStruct(x_own.shape,BF),jax.ShapeDtypeStruct((8,feat),F32)],
-        scratch_shapes=[pltpu.VMEM((padded,feat),F32)],name="input_back",
-        compiler_params=pltpu.CompilerParams(vmem_limit_bytes=40<<20),
-        cost_estimate=pl.CostEstimate(flops=n*20*padded*feat,bytes_accessed=14<<20,transcendentals=0),
-    )(x_own,dh_own,dh_oth,dx2,gain[None])
-
-MESH_ID = pl.DeviceIdType.MESH
-
-
-class Wires:
-    def __init__(self, send_sem, recv_sem):
-        self.send_sem, self.recv_sem, self.count, self.sent = send_sem, recv_sem, 0, []
-
-    def make(self, src, dst, to):
-        cp = pltpu.make_async_remote_copy(
-            src_ref=src, dst_ref=dst, send_sem=self.send_sem.at[self.count], recv_sem=self.recv_sem.at[self.count],
-            device_id=to, device_id_type=MESH_ID)
-        self.count += 1
-        return cp
-
-    def send(self, src, dst, to):
-        cp = self.make(src, dst, to)
-        cp.start()
-        self.sent.append(cp)
-        return cp
-
-    def finish(self):
-        for cp in self.sent:
-            cp.wait_send()
-
-
-def greet(peers, crossing_peer, apart):
-    barrier = pltpu.get_barrier_semaphore()
-    for peer in peers:
-        pl.semaphore_signal(barrier, inc=1, device_id=peer, device_id_type=MESH_ID)
-
-    @pl.when(apart)
-    def _():
-        pl.semaphore_signal(barrier, inc=1, device_id=crossing_peer, device_id_type=MESH_ID)
-
-    pl.semaphore_wait(barrier, len(peers) + jnp.where(apart, 1, 0))
-
-
-def add_all(first, *others):
-    total = first.astype(F32)
-    for other in others:
-        total = total + other.astype(F32)
-    return total
-
 
 def tail_kernel(ny, nx, *refs):
     h1_ref, dqkv_ref, go_ref, x_ref, dx_ref, gain_ref, vec_ref, w = refs[:8]
-    o = 8
-    fa, fb = refs[o:o + nx], refs[o + nx:o + nx + ny]
-    o += nx + ny
+    fpart = refs[8]
+    o = 9
     mine_ref, theirs_ref, so_ref, sf_ref, ig_ref, vout_ref, norm_ref = refs[o:o + 7]
     (grad, ra1, ra2, rb1, rb2, sa, sb, oa1, oa2, ob1, ob2, ta, tb, osum, ocross, ocore, odp, ofin,
-     rfa, rfb, fsum, fpart, frecv, fdp, isum, ipart, irecv, idp, ifin,
+     frecv, isum, ipart, irecv, idp, ifin,
      buf, give, got, stage, vrecv, nrecv, nval, send_sem, recv_sem) = refs[o + 7:]
     h, y, x, c, l = (lax.axis_index(a) for a in AXES)
     images, half, feat = x_ref.shape
@@ -503,8 +427,7 @@
     wires = Wires(send_sem, recv_sem)
     greet([to_core, to_seq, to_dp] + to_x[1:] + to_y[1:], cross, apart)
 
-    ff_got = [wires.send(fa[k], rfa.at[k - 1], to_x[k]) for k in range(1, nx)]
-    ff_got += [wires.send(fb[k], rfb.at[k - 1], to_y[k]) for k in range(1, ny)]
+    fs = wires.send(fpart.at[1], frecv, to_seq)
     oa_got = [[wires.send(go_ref.at[yy[ky], xx[kx], h], oa1.at[ky - 1, kx], to_y[ky]) for kx in range(nx)] for ky in range(1, ny)]
     ob_got = [[wires.send(go_ref.at[yy[ky], xx[kx], 1 - h], ob1.at[kx - 1, ky], to_x[kx]) for ky in range(ny)] for kx in range(1, nx)]
     width = nx * 2 * rows
@@ -517,24 +440,16 @@
                 for core in range(2):
                     r = (q * 2 + core) * rows
                     grad[zz[kz], yy[ky], q, core] = t[r:r + rows]
-        if ky > 0:
             for kx in range(nx):
-                for kz in range(2):
+                if ky > 0:
                     ia_got.append(wires.send(grad.at[zz[kz], yy[ky], xx[kx], c], ra1.at[ky - 1, kz, kx], to_y[ky]))
-    for kx in range(1, nx):
-        for ky in range(ny):
-            for kz in range(2):
-                ib_got.append(wires.send(grad.at[zz[kz], yy[ky], xx[kx], 1 - c], rb1.at[kx - 1, kz, ky], to_x[kx]))
+                if kx > 0:
+                    ib_got.append(wires.send(grad.at[zz[kz], yy[ky], xx[kx], 1 - c], rb1.at[kx - 1, kz, ky], to_x[kx]))
     dh_got = []
     for i in range(images):
         r = (2 * i + 1) * padded
         give[i] = dot(dqkv_ref[r:r + padded, :], w[...], NT).astype(BF)
         dh_got.append(wires.send(give.at[i], got.at[i], to_core))
-    for cp in ff_got:
-        cp.wait_recv()
-    fsum[0] = add_all(fa[0][...], *(rfa[k] for k in range(nx - 1))).astype(BF)
-    fsum[1] = add_all(fb[0][...], *(rfb[k] for k in range(ny - 1))).astype(BF)
-    fd = wires.send(fsum.at[1 - l], fdp, to_dp)
     for row in oa_got + ob_got:
         for cp in row:
             cp.wait_recv()
@@ -567,7 +482,8 @@
 
         return sum_gain + jnp.sum(gg, axis=0, keepdims=True), sum_shift + jnp.sum(g, axis=0, keepdims=True)
 
-    sum_gain, sum_shift = input_back(0, sum_gain, sum_shift)
+    for i in range(min(2, images)):
+        sum_gain, sum_shift = input_back(i, sum_gain, sum_shift)
     for cp in ia_got + ib_got:
         cp.wait_recv()
     i_got = []
@@ -580,10 +496,6 @@
         i_got.append(wires.send(sa.at[kx - 1], ra2.at[kx - 1], to_x[kx]))
     for ky in range(1, ny):
         i_got.append(wires.send(sb.at[ky - 1], rb2.at[ky - 1], to_y[ky]))
-    sum_gain, sum_shift = input_back(1, sum_gain, sum_shift)
-    fd.wait_recv()
-    fpart[...] = add_all(fsum[l], fdp[...]).astype(BF)
-    fs = wires.send(fpart.at[1], frecv, to_seq)
     for i in range(2, images):
         sum_gain, sum_shift = input_back(i, sum_gain, sum_shift)
     vout_ref[...] = vec_ref[...]
@@ -695,14 +607,14 @@
     wires.finish()
 
 
-def tail_stage(h1, dqkv, g_out, x_own, dx2, gain, vec, w, fa, fb, ny, nx):
+def tail_stage(h1, dqkv, g_out, x_own, dx2, gain, vec, w, fpart, ny, nx):
     tokens, feat = h1.shape
     width = dqkv.shape[1]
     rows = feat // (4 * ny * nx)
     rows_o = g_out.shape[3]
     images, half, _ = x_own.shape
     padded = dx2.shape[1]
-    _, ud, hid, _ = fa[0].shape
+    _, ud, hid, _ = fpart.shape
     ma, mb = max(ny - 1, 1), max(nx - 1, 1)
     piece, out_piece, ff = (rows, width), (rows_o, feat), (ud, hid, feat)
     peers = 4 + nx - 1 + ny - 1
@@ -715,7 +627,7 @@
         V(ny - 1, nx, *out_piece), V(nx - 1, *out_piece), V(nx - 1, ny, *out_piece), V(ny - 1, *out_piece),
         V(nx - 1, *out_piece), V(ny - 1, *out_piece),
         V(2, *out_piece), V(2, *out_piece), V(*out_piece), V(*out_piece), V(*out_piece),
-        V(nx - 1, 2, *ff), V(ny - 1, 2, *ff), V(2, 2, *ff), V(2, *ff), V(*ff), V(2, *ff),
+        V(*ff),
         V(2, 2, *piece), V(2, *piece), V(*piece), V(2, *piece), V(2, *piece),
         pltpu.VMEM((padded, feat), F32), V(images, padded, feat), V(images, padded, feat), V(images, half, feat),
         pltpu.VMEM((peers,) + vec.shape, F32), pltpu.VMEM((peers, 8, 128), F32), pltpu.VMEM((8, 128), F32),
@@ -723,7 +635,7 @@
     ]
     return pl.pallas_call(
         functools.partial(tail_kernel, ny, nx),
-        in_specs=[VM] * (8 + nx + ny),
+        in_specs=[VM] * 9,
         out_specs=[VM] * 7,
         out_shape=[
             jax.ShapeDtypeStruct(piece, BF), jax.ShapeDtypeStruct(piece, BF), jax.ShapeDtypeStruct(out_piece, BF),
@@ -734,13 +646,13 @@
         name="tail_stage",
         compiler_params=pltpu.CompilerParams(collective_id=1, has_side_effects=True, vmem_limit_bytes=62 << 20),
         cost_estimate=pl.CostEstimate(flops=4 * tokens * feat * width, bytes_accessed=40 << 20, transcendentals=0),
-    )(h1, dqkv, g_out, x_own, dx2, gain[None], vec, w, *fa, *fb)
+    )(h1, dqkv, g_out, x_own, dx2, gain[None], vec, w, fpart)
 
 def head_kernel(ny, nx, *refs):
     (in_ref, out_ref, up_ref, down_ref, vec_ref, img_ref,
      h1_ref, qkv_ref, xb, w, my_out, other_out, fa, fb, cast_ref, vfull,
      theirs, o_own, o_core, tmp, buf, xsem, csem, send_sem, recv_sem) = refs
-    h, y, x, c, _ = (lax.axis_index(a) for a in AXES)
+    h, y, x, c, l = (lax.axis_index(a) for a in AXES)
     images, half, feat = img_ref.shape
     rows = in_ref.shape[0]
     width = w.shape[1]
@@ -748,7 +660,8 @@
     hid = up_ref.shape[0] // 2
     apart = h != c
     cross = {"seq": 1 - h, "core": 1 - c}
-    to_core, to_seq = {"core": 1 - c}, {"seq": 1 - h}
+    to_core, to_seq, to_dp = {"core": 1 - c}, {"seq": 1 - h}, {"dp": 1 - l}
+    inner, to_near = l != h, {"seq": 1 - h, "dp": 1 - l}
     to_x = [{"x": lax.rem(x + nx - k, nx)} for k in range(nx)]
     to_y = [{"y": lax.rem(y + ny - k, ny)} for k in range(ny)]
     yy = [lax.rem(y + k, ny) for k in range(ny)]
@@ -756,13 +669,17 @@
     zz = [h, 1 - h]
     wires = Wires(send_sem, recv_sem)
     barrier = pltpu.get_barrier_semaphore()
-    peers = [to_core, to_seq] + to_x[1:] + to_y[1:]
+    peers = [to_core, to_seq, to_dp] + to_x[1:] + to_y[1:]
     for peer in peers:
         pl.semaphore_signal(barrier, inc=1, device_id=peer, device_id_type=MESH_ID)
 
     @pl.when(apart)
     def _():
         pl.semaphore_signal(barrier, inc=1, device_id=cross, device_id_type=MESH_ID)
+
+    @pl.when(inner)
+    def _():
+        pl.semaphore_signal(barrier, inc=1, device_id=to_near, device_id_type=MESH_ID)
 
     local_images = pltpu.make_async_copy(img_ref, xb.at[0], xsem)
 
@@ -779,36 +696,9 @@
         theirs[:, t * part:(t + 1) * part] = in_ref[:, pl.ds(pl.multiple_of(t * 2 * part + (1 - c) * part, 128), part)].astype(BF)
     vfull[h, y, x, c] = vec_ref[...].astype(BF).astype(F32)
     o_own[...] = out_ref[...].astype(BF)
-    pl.semaphore_wait(barrier, len(peers) + jnp.where(apart, 1, 0))
-
-    def spread(piece_at, kz, first):
-        got = {}
-        for k in range(1, nx):
-            got[0, k] = wires.send(piece_at(kz, 0, 0), piece_at(kz, 0, 0, k, "x"), to_x[k])
-        for k in range(1, ny):
-            got[k, 0] = wires.send(piece_at(kz, 0, 0), piece_at(kz, 0, 0, k, "y"), to_y[k])
-        return got
-
-    def forward(piece_at, kz, first, got):
-        if first == "x":
-            for kx in range(1, nx):
-                got[0, kx].wait_recv()
-                for ky in range(1, ny):
-                    got[ky, kx] = wires.send(piece_at(kz, 0, kx), piece_at(kz, 0, kx, ky, "y"), to_y[ky])
-            for ky in range(1, ny):
-                got[ky, 0].wait_recv()
-        else:
-            for ky in range(1, ny):
-                got[ky, 0].wait_recv()
-                for kx in range(1, nx):
-                    got[ky, kx] = wires.send(piece_at(kz, ky, 0), piece_at(kz, ky, 0, kx, "x"), to_x[kx])
-            for kx in range(1, nx):
-                got[0, kx].wait_recv()
-
-    def settle(got):
-        for (ky, kx), cp in got.items():
-            if ky > 0 and kx > 0:
-                cp.wait_recv()
+    pl.semaphore_wait(barrier, len(peers) + jnp.where(apart, 1, 0) + jnp.where(inner, 1, 0))
+
+    spread, forward, settle = plane_moves(wires, to_x, to_y)
 
     def in_a(kz, ky, kx, *_):
         return slot(zz[kz], yy[ky], xx[kx], c)
@@ -822,18 +712,19 @@
     def out_b(kz, ky, kx, *_):
         return my_out.at[yy[ky], xx[kx], 1 - h]
 
-    def by_offset(store, own):
-        def piece_at(kz, ky, kx, k=0, axis=""):
-            if k == 0 and ky == 0 and kx == 0:
-                return own
-            return store.at[ky + (k if axis == "y" else 0), kx + (k if axis == "x" else 0)]
-
-        return piece_at
-
     ff_a, ff_b = by_offset(fa, tmp.at[0]), by_offset(fb, tmp.at[1])
 
     b_got = wires.send(theirs, slot(h, y, x, c), to_core)
-    az = wires.send(mine, mine, to_seq)
+    def across(core):
+        own, other = slot(h, y, x, core), slot(1 - h, y, x, core)
+        return wires.make(own, own, to_near), wires.make(other, other, to_dp)
+
+    az, bz = across(c), across(1 - c)
+
+    @pl.when(inner)
+    def _():
+        az[0].start()
+
     a0 = spread(in_a, 0, "x")
     vec_peers = [[to_core], to_x[1:], to_y[1:], [to_seq]]
     vec_at = [vfull.at[h, y, x, c], vfull.at[h, y, x], vfull.at[h, y], vfull.at[h]]
@@ -850,7 +741,11 @@
         xl.start()
 
     b_got.wait_recv()
-    bz = wires.send(in_b(0, 0, 0), in_b(0, 0, 0), to_seq)
+
+    @pl.when(inner)
+    def _():
+        bz[0].start()
+
     b0 = spread(in_b, 0, "y")
     for cp in v:
         cp.wait_recv()
@@ -870,23 +765,39 @@
     v = vec_send(2)
     forward(in_a, 0, "x", a0)
     forward(in_b, 0, "y", b0)
-    az.wait_recv()
+    oc.wait_recv()
+    x_cross = [wires.make(img_ref.at[i], xb.at[0, i], cross) for i in range(images)]
+
+    @pl.when(jnp.logical_and(apart, jnp.logical_not(inner)))
+    def _():
+        x_cross[0].start()
+
+    def arrive(pair):
+        @pl.when(inner)
+        def _():
+            pair[0].wait_recv()
+            pair[1].start()
+
+        @pl.when(jnp.logical_not(inner))
+        def _():
+            pair[1].wait_recv()
+
+    arrive(az)
     a1 = spread(in_a, 1, "x")
-    bz.wait_recv()
+    arrive(bz)
     b1 = spread(in_b, 1, "y")
     for cp in v:
         cp.wait_recv()
     v = vec_send(3)
-    oc.wait_recv()
-    x_cross = [wires.make(img_ref.at[i], xb.at[0, i], cross) for i in range(images)]
     o_cross = [wires.make(o_own, my_out.at[y, x, 1 - h], cross), wires.make(o_core, my_out.at[y, x, h], cross)]
 
+    @pl.when(jnp.logical_and(apart, inner))
+    def _():
+        x_cross[0].start()
+
     @pl.when(apart)
     def _():
-        x_cross[0].start()
-        for cp in o_cross:
-            cp.start()
-        for cp in x_cross[1:]:
+        for cp in x_cross[1:] + o_cross:
             cp.start()
 
     @pl.when(jnp.logical_not(apart))
@@ -979,6 +890,11 @@
     @pl.when(jnp.logical_not(apart))
     def _():
         xl.wait_send()
+
+    @pl.when(inner)
+    def _():
+        for cp in az + bz:
+            cp.wait_send()
 
     for cp in keep:
         cp.wait()
@@ -1014,6 +930,169 @@
     )(in_w, out_w, up_w, down_w, vec, images)
 
 
+def mid_kernel(ny, nx, *refs):
+    (qkv_ref, kf_ref, xb, wo_ref, wt_ref, vec_ref, cast_ref, grad_ref,
+     mix_ref, lse_ref, x2_ref, h2_ref, g_ref, fa, fb,
+     mix_oth, near_land, buf, csem, send_sem, recv_sem) = refs
+    h, y, x, c, l = (lax.axis_index(a) for a in AXES)
+    images, rows, width = mix_ref.shape
+    padded = rows // 2
+    pairs = width // 128
+    apart, inner = h != c, l != h
+    cross, to_near = {"seq": 1 - h, "core": 1 - c}, {"seq": 1 - h, "dp": 1 - l}
+    to_core, to_dp = {"core": 1 - c}, {"dp": 1 - l}
+    to_x = [{"x": lax.rem(x + nx - k, nx)} for k in range(nx)]
+    to_y = [{"y": lax.rem(y + ny - k, ny)} for k in range(ny)]
+    wires = Wires(send_sem, recv_sem)
+    spread, forward, settle = plane_moves(wires, to_x, to_y)
+    barrier = pltpu.get_barrier_semaphore()
+    peers = [to_core, to_dp] + to_x[1:] + to_y[1:]
+    for peer in peers:
+        pl.semaphore_signal(barrier, inc=1, device_id=peer, device_id_type=MESH_ID)
+
+    @pl.when(apart)
+    def _():
+        pl.semaphore_signal(barrier, inc=1, device_id=cross, device_id_type=MESH_ID)
+
+    @pl.when(inner)
+    def _():
+        pl.semaphore_signal(barrier, inc=1, device_id=to_near, device_id_type=MESH_ID)
+
+    pl.semaphore_wait(barrier, len(peers) + jnp.where(apart, 1, 0) + jnp.where(inner, 1, 0))
+    near_ff = [wires.make(cast_ref.at[ab], near_land.at[ab], to_near) for ab in range(2)]
+    far_ff = [wires.make(near_land.at[ab], near_land.at[ab], to_dp) for ab in range(2)]
+    local_grad = pltpu.make_async_copy(grad_ref, g_ref.at[0], csem.at[0])
+    grad_core = wires.make(grad_ref, g_ref.at[1], to_core)
+    g_cross = [wires.make(grad_ref.at[i], g_ref.at[0, i], cross) for i in range(images)]
+    g_core = [wires.make(g_ref.at[0, i], g_ref.at[1, i], to_core) for i in range(images)]
+
+    @pl.when(inner)
+    def _():
+        for cp in near_ff:
+            cp.start()
+
+    @pl.when(jnp.logical_not(apart))
+    def _():
+        local_grad.start()
+        grad_core.start()
+
+    @pl.when(apart)
+    def _():
+        g_cross[0].start()
+
+    mix_got = []
+    for i in range(images):
+        def pair(p, carry):
+            at = [pl.ds(pl.multiple_of((t * pairs + p) * 128, 128), 128) for t in range(3)]
+            mixed, sums = attend_pair(qkv_ref[i, :, at[0]], qkv_ref[i, :, at[1]], qkv_ref[i, :, at[2]], kf_ref[i])
+            mix_ref[i, :, at[0]] = mixed
+            for j in range(2):
+                lse_ref[i, p, j:j + 1, :] = sums[j]
+            return carry
+
+        lax.fori_loop(0, pairs, pair, 0)
+        mix_got.append(wires.send(mix_ref.at[i], mix_oth.at[i], to_core))
+        if i + 1 < images:
+            @pl.when(apart)
+            def _():
+                g_cross[i + 1].start()
+
+    gots = []
+
+    def arrive(ab):
+        @pl.when(inner)
+        def _():
+            near_ff[ab].wait_recv()
+            far_ff[ab].start()
+
+        @pl.when(jnp.logical_not(inner))
+        def _():
+            far_ff[ab].wait_recv()
+
+    ff = [by_offset(fa, near_land.at[0]), by_offset(fb, near_land.at[1])]
+    order = ("x", "y")
+
+    def middle(i):
+        mix_got[i].wait_recv()
+        for s in range(2):
+            own = slice(s * padded, (s + 1) * padded)
+            oth = slice((1 - s) * padded, (2 - s) * padded)
+            v = wide_rows(buf, xb[s, i])
+            v = v + (dot(mix_ref[i, own, :], wo_ref[...]) + dot(mix_oth[i, oth, :], wt_ref[...])) + vec_ref[0:1, :]
+            x2_ref[i, s] = v
+            h2_ref[i, s] = (norm_parts(v)[0] * vec_ref[1:2, :] + vec_ref[2:3, :]).astype(BF)
+
+    middle(0)
+    arrive(0)
+    gots.append(spread(ff[0], 1, "x"))
+    for i in range(1, images):
+        middle(i)
+    arrive(1)
+    gots.append(spread(ff[1], 1, "y"))
+    keep = [pltpu.make_async_copy(near_land.at[ab], (fa, fb)[ab].at[0, 0], csem.at[1 + ab]) for ab in range(2)]
+    for cp in keep:
+        cp.start()
+    for ab in range(2):
+        forward(ff[ab], 1, order[ab], gots[ab])
+    for i in range(images):
+        @pl.when(apart)
+        def _():
+            g_cross[i].wait_recv()
+            g_core[i].start()
+
+        @pl.when(jnp.logical_not(apart))
+        def _():
+            g_core[i].wait_recv()
+
+    @pl.when(apart)
+    def _():
+        grad_core.wait_recv()
+        for cp in g_cross + g_core:
+            cp.wait_send()
+
+    @pl.when(jnp.logical_not(apart))
+    def _():
+        local_grad.wait()
+        grad_core.wait_send()
+
+    @pl.when(inner)
+    def _():
+        for cp in near_ff + far_ff:
+            cp.wait_send()
+
+    for got in gots:
+        settle(got)
+    for cp in keep:
+        cp.wait()
+    wires.finish()
+
+
+def mid_stage(qkv, key_fill, x_both, w_own, w_oth, vec, low_ff, out_grad, ny, nx):
+    n, rows, w3 = qkv.shape
+    width, feat = w_own.shape
+    half = out_grad.shape[1]
+    _, ud, hid, _ = low_ff.shape
+    many = 40 + 4 * ny * nx
+    S = jax.ShapeDtypeStruct
+    return pl.pallas_call(
+        functools.partial(mid_kernel, ny, nx),
+        in_specs=[VM] * 6 + [ANY] * 2,
+        out_specs=[VM] * 5 + [ANY] * 2,
+        out_shape=[
+            S((n, rows, width), BF), S((n, width // 128, 8, rows), F32), S((n, 2, rows // 2, feat), F32),
+            S((n, 2, rows // 2, feat), BF), S((2, n, half, feat), BF),
+            S((ny, nx, ud, hid, feat), BF), S((ny, nx, ud, hid, feat), BF),
+        ],
+        scratch_shapes=[
+            pltpu.VMEM((n, rows, width), BF), pltpu.VMEM((2, ud, hid, feat), BF), pltpu.VMEM((rows // 2, feat), F32),
+            pltpu.SemaphoreType.DMA((3,)), pltpu.SemaphoreType.DMA((many,)), pltpu.SemaphoreType.DMA((many,)),
+        ],
+        name="mid_stage",
+        compiler_params=pltpu.CompilerParams(collective_id=5, has_side_effects=True, vmem_limit_bytes=60 << 20),
+        cost_estimate=pl.CostEstimate(flops=n * 4 * rows * rows * w3, bytes_accessed=50 << 20, transcendentals=n * 8 * rows * rows),
+    )(qkv, key_fill, x_both, w_own, w_oth, vec, low_ff, out_grad)
+
+
 def shift(value, axis, up):
     n = lax.axis_size(axis)
     return lax.ppermute(value, axis, [(i, (i + up) % n) for i in range(n)])
@@ -1033,49 +1112,6 @@
 
 def crossed(value):
     return pick(value, crossing(value))
-
-
-def small_sum(value, axes):
-    for axis in axes:
-        n = lax.axis_size(axis)
-        moved, total = value, value
-        for _ in range(n - 1):
-            moved = shift(moved, axis, 1)
-            total = total + moved
-        value = total
-    return value
-
-
-def gather_list(piece, axis):
-    out = [piece]
-    for _ in range(lax.axis_size(axis) - 1):
-        out.append(shift(out[-1], axis, -1))
-    return out
-
-
-def gather_plane(piece, first, second, dep=()):
-    out = {}
-    for i, one in enumerate(gather_list(piece, first)):
-        one = after(one, dep) if i else one
-        for j, two in enumerate(gather_list(one, second)):
-            out[(j, i) if first == "x" else (i, j)] = two
-    return out
-
-
-def reduce_list(pieces, axis, dep):
-    total = pieces[-1]
-    for piece in pieces[-2::-1]:
-        total = (after(shift(total, axis, 1), dep).astype(F32) + piece.astype(F32)).astype(BF)
-    return total
-
-
-def reduce_second(pieces, first, second, dep):
-    n_first, n_second = lax.axis_size(first), lax.axis_size(second)
-    part = []
-    for i in range(n_first):
-        row = [pieces[(j, i) if first == "x" else (i, j)] for j in range(n_second)]
-        part.append(reduce_list(row, second, dep))
-    return part
 
 
 def adam_update(master, first_moment, second_moment, gradient, step_rate, bias_one, bias_two):
@@ -1096,13 +1132,12 @@
     ny, nx = lax.axis_size("y"), lax.axis_size("x")
     shards = 4 * ny * nx
     shard = ((h * ny + y) * nx + x) * 2 + c
-    at = jnp.stack([h, y, x, c, jnp.int32(ny), jnp.int32(nx), jnp.int32(0), jnp.int32(0)]).astype(jnp.int32)
 
     h1, qkv, x_both, full_in, my_out, other_out, own_a, own_b, low_ff, full_vec = head_stage(
         in_weights, out_weights, up_weights, down_weights, vectors[None], images, padded, ny, nx
     )
     my_out, other_out = my_out.reshape(HALF_D, D), other_out.reshape(HALF_D, D)
-    x_own, x_oth = x_both[0], x_both[1]
+    x_own = x_both[0]
     rows_in, rows_out, rows_ff = in_weights.shape[0], out_weights.shape[0], up_weights.shape[0]
     half_ff = rows_ff // 2
     keys = [(ky, kx) for ky in range(ny) for kx in range(nx)]
@@ -1118,37 +1153,43 @@
     mask = jnp.pad(mask, ((0, 0), (0, 0), (0, padded - half))).reshape(image_count, 2 * padded)
     key_fill = jnp.broadcast_to(jnp.where(mask > 0, 0.0, NEG_FILL)[..., None], mask.shape + (128,)).astype(BF)
 
-    ff_near = lax.ppermute(low_ff, ("seq", "dp"), [(1, 2), (2, 1)])
-    g_got = crossing(after(out_grad, ff_near))
-
     tokens = image_count * 2 * padded
     qkv = qkv.reshape(image_count, 2 * padded, 3 * HALF_D)
-    mixed, lse = attend(qkv, key_fill)
+    mid_vec = jnp.pad(jnp.stack([out_bias, gain_two, shift_two]), ((0, 5), (0, 0)))
+    mixed, lse, x2, h2, g_both, oth_a, oth_b = mid_stage(
+        qkv, key_fill, x_both, my_out, other_out, mid_vec, low_ff, out_grad, ny, nx
+    )
+    g_own, g_oth = g_both[0], g_both[1]
     halved = mixed.reshape(image_count, 2, padded, HALF_D)
-    mixed_oth = shift(halved, "core", 1)
-    ff_near = after(ff_near, mixed)
-    ff_far = lax.ppermute(ff_near, ("seq", "dp"), [(1, 0), (2, 3)])
-    x2, h2 = middle(x_own, x_oth, halved, mixed_oth, my_out, other_out, out_bias, gain_two, shift_two)
-
-    ff_far, h2 = lax.optimization_barrier((ff_far, h2))
-    ff_other = jnp.where(h != lax.axis_index("dp"), ff_near, ff_far)
-    ff_a = gather_plane(ff_other[0], "x", "y")
-    ff_b = gather_plane(ff_other[1], "y", "x")
-    g_own = pick(out_grad, after(g_got, h2))
-    g_oth = shift(g_own, "core", 1)
-    grad_a, grad_b, y_own, y_oth, dh2, g_bu = mlp(
-        at, h2.reshape(tokens, D), g_own, g_oth, up_bias.reshape(shards * 2, half_ff), own_a, own_b, ff_a, ff_b
+
+    grad_a, grad_b, (y_own, y_oth, dh2, g_bu, first_a, first_b) = mlp(
+        ny, nx, h2.reshape(tokens, D), g_own, g_oth, up_bias.reshape(shards * 2, half_ff), own_a, own_b, oth_a, oth_b
     )
     result = y_own[:, :half] + shift(y_oth, "core", 1)[:, :half].astype(F32) + x2[:, 0, :half] + down_bias
     result = result.astype(BF)
+    result_got = crossing(result)
+
+    def second_stage(grads, firsts, swap):
+        sums = []
+        for k in range(firsts.shape[1]):
+            sums.append(add_all(grads[(k, 0) if swap else (0, k)], *firsts[:, k]).astype(BF))
+        return sums
+
+    sums_a, sums_b = second_stage(grad_a, first_a, False), second_stage(grad_b, first_b, True)
+    got_a = [lax.ppermute(s, "x", [(i, (i + k) % nx) for i in range(nx)]) for k, s in enumerate(sums_a) if k]
+    got_b = [lax.ppermute(s, "y", [(i, (i + k) % ny) for i in range(ny)]) for k, s in enumerate(sums_b) if k]
 
     dh2 = dh2.reshape(image_count, 2, padded, D)
     dh2_oth = shift(dh2, "core", 1)
     dx2, dattn, g_out, sums_two = middle_back(x2, dh2, dh2_oth, g_own, g_oth, halved, my_out, gain_two)
-    result_got = crossing(after(result, dattn))
-    dqkv, sums_qkv = attend_back(qkv, key_fill, mixed, dattn.reshape(mixed.shape), lse)
-    part_a = reduce_second(grad_a, "x", "y", dqkv)
-    part_b = reduce_second(grad_b, "y", "x", dqkv)
+    got_a, got_b = after(got_a, dattn), after(got_b, dattn)
+    plane_a, plane_b = add_all(sums_a[0], *got_a).astype(BF), add_all(sums_b[0], *got_b).astype(BF)
+    l = lax.axis_index("dp")
+    half_keep, half_give = jnp.where(l == 0, plane_a, plane_b), jnp.where(l == 0, plane_b, plane_a)
+    dqkv, sums_qkv, part_ff = attend_back(
+        qkv, key_fill, mixed, dattn.reshape(mixed.shape), lse, half_keep, half_give
+    )
+
     zero = jnp.zeros((D,), F32)
     vec = jnp.concatenate(
         [
@@ -1172,8 +1213,7 @@
         gain_one,
         vec,
         full_in,
-        part_a,
-        part_b,
+        part_ff,
         ny,
         nx,
     )

time: 578 us -> 547 us (0.946)
  waiting for transfers between devices: 91.3 us -> 0.02 us
  Pallas kernels: 399 us -> 483 us
  starting transfers between devices: 25.4 us -> 4.89 us
  other arithmetic: 36.2 us -> 29 us
    pallas_call x4 -> x3, Pallas kernels: 261 us -> 328 us  [the longest x1 129 us: tail_stage(): pl.pallas_call(functools.partial(tail_kernel, ny, nx), in_specs=[VM] * 9,...]
    ppermute x15 -> x3, waiting for transfers between devices: 36.2 us -> 0.01 us  [shift(): return lax.ppermute(value, axis, [(i, (i + up) % n) for i in range(n)])]
    ppermute x2, waiting for transfers between devices: 27.8 us -> 0.01 us  [the longest x1 0.01 us: on_device(): lax.ppermute(s, 'y', [(i, (i + k) % ny) for i in range(ny)])]
    ppermute x2 -> x1, waiting for transfers between devices: 27.3 us -> 0.01 us  [crossing(): return lax.ppermute(value, ('seq', 'core'), [(1, 2), (2, 1)])]
    pallas_call x1, Pallas kernels: 30.4 us -> 44.4 us  [attend_back(): pl.pallas_call(functools.partial(attend_back_kernel, pairs=pairs, chunk=c...]
    ppermute x15 -> x3, starting transfers between devices: 11.4 us -> 1.44 us  [shift(): return lax.ppermute(value, axis, [(i, (i + up) % n) for i in range(n)])]
    ppermute x2 -> x1, starting transfers between devices: 11.5 us -> 1.92 us  [crossing(): return lax.ppermute(value, ('seq', 'core'), [(1, 2), (2, 1)])]
    convert_element_type x4 -> x2, other arithmetic: 10.9 us -> 4.32 us  [second_stage(): add_all(grads[(k, 0) if swap else (0, k)], *firsts[:, k]).astype(BF)]
  transfers between devices with their start and end apart: 19 -> 6, of which waited for: 8 -> 0; matrix products, arithmetic and copies ran while one was open for 4% -> 4% of each run, Pallas kernels for 29% -> 53%
where the time goes in v5:
time: 547 us; the launch traced here: 540 us
  Pallas kernels  483 us (88%)
  other arithmetic  29 us (5%)
  local copies, waits for them, and re-layouts  20.2 us (4%)
    pallas_call x1, Pallas kernels, tail_stage(): pl.pallas_call(functools.partial(tail_kernel, ny, nx), in_specs=[VM] * 9,...  129 us
    pallas_call x1, Pallas kernels, mid_stage(): pl.pallas_call(functools.partial(mid_kernel, ny, nx), in_specs=[VM] * 6 +...  114 us
    pallas_call x1, Pallas kernels, head_stage(): pl.pallas_call(functools.partial(head_kernel, ny, nx), in_specs=[VM] * 5...  94.4 us
    pallas_call x1, Pallas kernels, mlp(): pl.pallas_call(functools.partial(mlp_kernel, keys, ny, nx, gtile=min(gtil...  85.4 us
    pallas_call x1, Pallas kernels, attend_back(): pl.pallas_call(functools.partial(attend_back_kernel, pairs=pairs, chunk=c...  44.4 us
    pallas_call x1, Pallas kernels, middle_back(): pl.pallas_call(middle_back_kernel, grid=(n,), in_specs=[big, big, big, to...  16.2 us
  transfers between devices with their start and end apart: 6, of which 0 were waited for; matrix products, arithmetic and copies ran while one was open for 4% of the time, Pallas kernels for 53%

profile of v5, /device:TPU:1, one launch (start us, length us, event | category | flops | bytes accessed | tf_op | source)
XLA Modules:
  0.0 540.3 jit_solution(10708640463000753503)
XLA Ops:
  0.7 0.7 convert_element_type.123
  1.4 0.1 collective-permute-start
  1.4 1.3 broadcast_in_dim.23.refs_4_
  2.7 94.4 %head_stage.1 = (bf16[3,2,304,1024]{3,2,1,0:T(8,128)(2,1)}, bf16[3,2,304,1536]{3,2,1,0:T(8,128)(2,1)}, bf16[2,3,292,1024]{3,2,1,0:T(8,128)(2,1)}, bf16[1024,1536...) custom-call(f32[64,3072]{1,0:T(8,128)} %refs_0_.1, ...), custom_call_target="tpu_custom_call" | custom-call | flops 5737807872 | bytes 41943040 | tf_op jit(solution)/shard_map/head_stage/pallas_call | solution.py:911
  97.1 1.3 fusion.23
  98.4 0.6 select_maximum_fusion.refs_5_
  99.0 1.3 slice.107.refs_3_
  100.4 0.1 reshape.141
  100.5 0.1 rev.3
  100.6 0.1 convert_element_type.125
  100.7 1.1 broadcast_in_dim.25.refs_1_.kb_ref
  101.8 113.5 %mid_stage.1 = (bf16[3,608,512]{2,1,0:T(8,128)(2,1)}, f32[3,4,8,608]{3,2,1,0:T(8,128)}, f32[3,2,304,1024]{3,2,1,0:T(8,128)}, bf16[3,2,304,1024]{3,2,1,0:T(8,128)...) custom-call(bf16[3,608,1536]{2,1,0:T(8,128)(2,1)} %bitcast.91, ...), custom_call_target="tpu_custom_call" | custom-call | flops 6813646848 | bytes 52428800 | tf_op jit(solution)/shard_map/mid_stage/pallas_call | solution.py:1077
  215.3 4.2 slice_bitcast_fusion.2
  219.5 85.4 %feed_forward.1 = (bf16[2,2,128,1024]{3,2,1,0:T(8,128)(2,1)}, bf16[2,2,128,1024]{3,2,1,0:T(8,128)(2,1)}, bf16[2,2,128,1024]{3,2,1,0:T(8,128)(2,1)}, bf16[2,2,128...) custom-call(bf16[1824,1024]{1,0:T(8,128)(2,1)} %bitcast.97, ...), custom_call_target="tpu_custom_call" | custom-call | flops 45902462976 | bytes 41943040 | tf_op jit(solution)/shard_map/feed_forward/pallas_call | solution.py:250
  305.0 1.3 collective-permute-start.1
  306.3 0.1 collective-permute-start.4
  306.4 2.9 fusion.3
  309.3 0.4 collective-permute-start.3
  309.7 1.4 fusion.5
  311.1 1.1 collective-permute-start.2
  312.2 2.9 slice_bitcast_fusion.1.refs_3_
  315.9 0.0 copy-start.7
  315.9 1.2 copy-done.7
  317.1 4.8 fusion.2
  321.9 1.9 collective-permute-start.5
  323.9 16.2 %middle_back.1 = (f32[3,304,1024]{2,1,0:T(8,128)}, bf16[3,2,304,512]{3,2,1,0:T(8,128)(2,1)}, bf16[512,1024]{1,0:T(8,128)(2,1)}, f32[8,1024]{1,0:T(8,128)}) custom-call(f32[3,2,304,1024]{3,2,1,0:T(8,128)} %get-tuple-element.75.x2_ref, bf16[3,2,304,1024]{3,2,1,0:T(8,128)(2,1)} %bitcast.71, bf16[3,2,304,1024]{3,2,1,0:T(8,128)(2,1)} %collective-permute-done.1.db_ref, ...), custom_call_target="tpu_custom_call" | custom-call | flops 3825205248 | bytes 31457280 | tf_op jit(solution)/shard_map/middle_back/pallas_call | solution.py:397
  340.2 0.0 copy-start
  340.2 3.8 broadcast_select_fusion
  344.0 0.0 copy-start.29
  344.0 44.4 %attend_back.1 = (bf16[3,608,1536]{2,1,0:T(8,128)(2,1)}, f32[8,1536]{1,0:T(8,128)S(1)}, bf16[2,2,128,1024]{3,2,1,0:T(8,128)(2,1)S(1)}) custom-call(bf16[3,608,1536]{2,1,0:T(8,128)(2,1)} %bitcast.92, bf16[3,608,1536]{2,1,0:T(8,128)(2,1)} %bitcast.93, bf16[3,608,1536]{2,1,0:T(8,128)(2,1)} %bitcast.94, bf16[3,608,128]{2,1,0:T(8,128)(2,1)S(1)} %copy-done, ...), custom_call_target="tpu_custom_call" | custom-call | flops 11356078080 | bytes 14008320 | tf_op jit(solution)/shard_map/attend_back/pallas_call | solution.py:341
  388.5 0.0 copy-start.1
  388.5 1.0 copy-done.1
  389.5 0.3 dynamic_update_slice.7
  389.7 0.2 dynamic_update_slice.6
  390.0 0.0 copy-start.32
  390.0 0.6 copy-done.32
  390.6 129.2 %tail_stage.1 = (bf16[64,1536]{1,0:T(8,128)(2,1)}, bf16[64,1536]{1,0:T(8,128)(2,1)}, bf16[64,1024]{1,0:T(8,128)(2,1)}, bf16[2,2,128,1024]{3,2,1,0:T(8,128)(2,1)}...) custom-call(bf16[1824,1024]{1,0:T(8,128)(2,1)} %bitcast.96, bf16[1824,1536]{1,0:T(8,128)(2,1)} %bitcast.95, ...), custom_call_target="tpu_custom_call" | custom-call | flops 11475615744 | bytes 41943040 | tf_op jit(solution)/shard_map/tail_stage/pallas_call | solution.py:636
  519.9 1.2 slice.97
  521.8 3.6 select_convert_fusion
  525.4 0.1 reshape.153
  525.6 0.1 reshape.154
  525.8 0.1 convert_multiply_fusion.2
  525.9 0.6 copy.51
  526.6 0.7 mul.176
  527.2 1.5 convert_multiply_fusion
  528.7 0.0 copy-start.27
  528.8 0.0 copy-start.30
  528.8 0.0 copy-start.31
  528.8 0.0 copy-start.18
  528.8 0.0 copy-start.19
  528.8 0.0 copy-start.20
  528.8 0.0 copy-start.16
  528.8 2.2 convert_element_type.161
  531.1 0.6 fusion.13
  531.8 0.0 copy-start.13
  531.8 1.1 fusion.19
  532.9 0.0 copy-start.9
  532.9 0.0 copy-start.10
  532.9 1.9 fusion.21
  534.9 0.3 copy-done.9
  535.2 0.6 copy-done.10
  535.8 0.3 copy-done.11
  536.1 0.3 copy-done.12
  536.4 3.6 fusion.15
  (69 shorter events, 0.3 us)
Async XLA Ops:
  1.4 99.0 %collective-permute-start = (f32[3,584]{1,0:T(4,128)S(1)}, f32[3,584]{1,0:T(4,128)S(1)}, u32[]{:S(2)}, u32[]{:S(2)}) collective-permute-start(f32[3,584]{1,0:T(4,128)S(1)} %convert_element_type.123), channel_id=1, source_target_pairs={{0,2},{2,0},{1,3},{3,1},{4,6},{6,4},{5,7},{7,5},{8,10},{10,8},{9,1... | collective-permute-start | bytes 21032 | tf_op jit(solution)/shard_map/ppermute | solution.py:1098
  2.7 97.7 %copy-start.25 = (s32[3,584]{1,0:T(4,128)S(1)}, s32[3,584]{1,0:T(4,128)}, u32[]{:S(2)}) copy-start(s32[3,584]{1,0:T(4,128)} %param.20) | copy-start | bytes 21028
  98.4 116.9 %copy-start.26 = (f32[1024]{0:T(1024)}, f32[1024]{0:T(1024)S(1)}, u32[]{:S(2)}) copy-start(f32[1024]{0:T(1024)S(1)} %get-tuple-element.140) | copy-start | bytes 12292
  305.0 4.7 copy-start.3
  305.0 4.7 copy-start.14
  305.0 18.8 %collective-permute-start.1 = (bf16[3,2,304,1024]{3,2,1,0:T(8,128)(2,1)}, bf16[3,2,304,1024]{3,2,1,0:T(8,128)(2,1)}, u32[]{:S(2)}, u32[]{:S(2)}) collective-permute-start(bf16[3,2,304,1024]{3,2,1,0:T(8,128)(2,1)} %bitcast.70), channel_id=1, source_target_pairs={{0,2},{2,0},{1,3},{3,1},{4,6},{6,4},{5,7},{7,5},{8,10},{10,8},{9,1... | collective-permute-start | bytes 11206664 | tf_op jit(solution)/shard_map/ppermute | solution.py:1098
  306.3 9.5 %collective-permute-start.4 = (bf16[3,304,1024]{2,1,0:T(8,128)(2,1)}, bf16[3,304,1024]{2,1,0:T(8,128)(2,1)S(1)}, u32[]{:S(2)}, u32[]{:S(2)}) collective-permute-start(bf16[3,304,1024]{2,1,0:T(8,128)(2,1)} %get-tuple-element.108), channel_id=1, source_target_pairs={{0,2},{2,0},{1,3},{3,1},{4,6},{6,4},{5,7},{7,5},{8,10},{10,8},{9,1... | collective-permute-start | bytes 5603336 | tf_op jit(solution)/shard_map/ppermute | solution.py:1098
  309.3 30.8 %collective-permute-start.3 = (bf16[2,2,128,1024]{3,2,1,0:T(8,128)(2,1)}, bf16[2,2,128,1024]{3,2,1,0:T(8,128)(2,1)}, u32[]{:S(2)}, u32[]{:S(2)}) collective-permute-start(bf16[2,2,128,1024]{3,2,1,0:T(8,128)(2,1)} %fusion.3), channel_id=1, source_target_pairs={{0,8},{8,0},{1,9},{9,1},{2,10},{10,2},{3,11},{11,3},{4,12},{12,4},... | collective-permute-start | bytes 3145736 | tf_op jit(solution)/shard_map/ppermute | solution.py:1180
  311.1 29.0 %collective-permute-start.2 = (bf16[2,2,128,1024]{3,2,1,0:T(8,128)(2,1)}, bf16[2,2,128,1024]{3,2,1,0:T(8,128)(2,1)}, u32[]{:S(2)}, u32[]{:S(2)}) collective-permute-start(bf16[2,2,128,1024]{3,2,1,0:T(8,128)(2,1)} %fusion.5), channel_id=1, source_target_pairs={{0,4},{4,0},{1,5},{5,1},{2,6},{6,2},{3,7},{7,3},{8,12},{12,8},{9,1... | collective-permute-start | bytes 3145736 | tf_op jit(solution)/shard_map/ppermute | solution.py:1179
  315.9 1.2 copy-start.7
  321.9 199.9 %collective-permute-start.5 = (bf16[3,292,1024]{2,1,0:T(8,128)(2,1)S(1)}, bf16[3,292,1024]{2,1,0:T(8,128)(2,1)}, u32[]{:S(2)}, u32[]{:S(2)}) collective-permute-start(bf16[3,292,1024]{2,1,0:T(8,128)(2,1)S(1)} %fusion.2), channel_id=1, source_target_pairs={{2,16},{16,2},{3,17},{17,3},{6,20},{20,6},{7,21},{21,7},{10,24},{2... | collective-permute-start | bytes 5382152 | tf_op jit(solution)/shard_map/ppermute | solution.py:1106
  323.9 16.3 %copy-start.4 = (bf16[1,2,2,2,128,1024]{5,4,3,2,1,0:T(8,128)(2,1)S(1)}, bf16[1,2,2,2,128,1024]{5,4,3,2,1,0:T(8,128)(2,1)}, u32[]{:S(2)}) copy-start(bf16[1,2,2,2,128,1024]{5,4,3,2,1,0:T(8,128)(2,1)} %get-tuple-element.86) | copy-start | bytes 6291460
  323.9 16.3 %copy-start.5 = (bf16[1,2,2,2,128,1024]{5,4,3,2,1,0:T(8,128)(2,1)S(1)}, bf16[1,2,2,2,128,1024]{5,4,3,2,1,0:T(8,128)(2,1)}, u32[]{:S(2)}) copy-start(bf16[1,2,2,2,128,1024]{5,4,3,2,1,0:T(8,128)(2,1)} %get-tuple-element.90) | copy-start | bytes 6291460
  340.2 3.8 copy-start
  340.2 3.8 copy-start.2
  344.0 45.5 %copy-start.29 = (f32[8,1024]{1,0:T(8,128)S(1)}, f32[8,1024]{1,0:T(8,128)}, u32[]{:S(2)}) copy-start(f32[8,1024]{1,0:T(8,128)} %get-tuple-element.97) | copy-start | bytes 98308
  344.0 46.0 %copy-start.28 = (f32[32,128]{1,0:T(8,128)S(1)}, f32[32,128]{1,0:T(8,128)}, u32[]{:S(2)}) copy-start(f32[32,128]{1,0:T(8,128)} %get-tuple-element.98) | copy-start | bytes 49156
  388.5 1.0 copy-start.1
  390.0 0.6 copy-start.32
  521.7 3.7 copy-start.24
  521.7 3.7 copy-start.22
  521.8 3.9 copy-start.21
  526.5 2.2 copy-start.6
  528.7 2.4 copy-start.27
  528.8 2.4 copy-start.30
  528.8 2.4 copy-start.31
  528.8 3.0 copy-start.18
  528.8 3.0 copy-start.19
  528.8 3.0 copy-start.20
  528.8 3.0 copy-start.23
  528.8 4.0 copy-start.16
  528.8 4.0 copy-start.17
  531.1 1.8 copy-start.15
  531.8 3.1 copy-start.13
  532.9 2.0 copy-start.8
  532.9 2.3 copy-start.9
  532.9 2.9 copy-start.10
  532.9 3.2 copy-start.11
  532.9 3.5 copy-start.12

commit v6 on v5

--- a/solution.py
+++ b/solution.py
@@ -127,11 +127,12 @@
     slope=half+(0.5*u)*(1.0-t*t)*(c0+(3*c0*0.044715)*sq)
     return value,slope
 
-def mlp_kernel(keys,ny,nx,*refs,gtile):
+def mlp_kernel(keys,keys_b,ny,nx,*refs,gtile):
     nk=len(keys)
-    h2_ref,go_ref,gt_ref,bu_ref=refs[:4]
-    planes=(refs[4:6],refs[6:8])
-    o=8
+    h2_ref,g_ref,bu_ref=refs[:3]
+    planes=(refs[3:5],refs[5:7])
+    o=7
+    order=(keys,keys_b)
     ga,gb=refs[o:o+nk],refs[o+nk:o+2*nk]
     yown_ref,yoth_ref,dh_ref,gbu_ref,ra_ref,rb_ref=refs[o+2*nk:o+2*nk+6]
     w,dd,a_all,du_all,y_acc,dh_acc,g_out,wsem,gsem,send_sem,recv_sem=refs[o+2*nk+6:]
@@ -140,15 +141,16 @@
     to_y=[{"y":lax.rem(y+k,ny)} for k in range(ny)]
     wires=Wires(send_sem,recv_sem)
     moves=[]
-    for ki,(ky,kx) in enumerate(keys):
+    for ki,((ky,_),(_,kx)) in enumerate(zip(keys,keys_b)):
         cps=[]
-        if ky>0: cps.append(wires.make(ga[ki],ra_ref.at[ky-1,kx],to_y[ky]))
+        if ky>0: cps.append(wires.make(ga[ki],ra_ref.at[ky-1,keys[ki][1]],to_y[ky]))
+        ky=keys_b[ki][0]
         if kx>0: cps.append(wires.make(gb[ki],rb_ref.at[kx-1,ky],to_x[kx]))
         moves.append(cps)
     barrier=pltpu.get_barrier_semaphore()
     for peer in to_x[1:]+to_y[1:]:
         pl.semaphore_signal(barrier,inc=1,device_id=peer,device_id_type=MESH_ID)
-    images,half,feat=go_ref.shape
+    _,images,half,feat=g_ref.shape
     hid=planes[0][0].shape[3]
     width=4*hid
     padded=h2_ref.shape[0]//(2*images)
@@ -161,7 +163,7 @@
                 for kz in range(2):
                     for ud in range(2):
                         for ab in range(2):
-                            cp=pltpu.make_async_copy(planes[kz][ab].at[keys[ki][0],keys[ki][1],ud],w.at[slot,ud,pl.ds((kz*2+ab)*hid,hid)],wsem.at[slot,kz*4+ud*2+ab])
+                            cp=pltpu.make_async_copy(planes[kz][ab].at[order[ab][ki][0],order[ab][ki][1],ud],w.at[slot,ud,pl.ds((kz*2+ab)*hid,hid)],wsem.at[slot,kz*4+ud*2+ab])
                             cp.start() if go else cp.wait()
     def save(i,go):
         for ki in range(nk):
@@ -175,11 +177,11 @@
     load(0,0,True)
     gbu_ref[...]=jnp.zeros_like(gbu_ref)
     for i in range(images):
-        for s,src in enumerate((go_ref,gt_ref)):
+        for s in range(2):
             r=(2*i+s)*padded
             tail=padded-16
             dd[r+tail:r+padded,:]=jnp.zeros((16,feat),BF)
-            dd[r:r+half,:]=src[i]
+            dd[r:r+half,:]=g_ref[s,i]
     pl.semaphore_wait(barrier,nx+ny-2)
     def step(i,_):
         slot=lax.rem(i,2)
@@ -197,7 +199,7 @@
         for kz in range(2):
             for ab in range(2):
                 row=jnp.int32(0)
-                for ki,(ky,kx) in enumerate(keys):
+                for ki,(ky,kx) in enumerate(order[ab]):
                     here=(((lax.rem(h+kz,2)*ny+lax.rem(y+ky,ny))*nx+lax.rem(x+kx,nx))*2+c)*2+ab
                     row=jnp.where(i==ki,here,row)
                 rows.append(row)
@@ -240,15 +242,16 @@
             cp.wait_recv()
             cp.wait_send()
 
-def mlp(ny,nx,h2,g_own,g_oth,bu_rows,own_a,own_b,oth_a,oth_b,gtile=256):
+def mlp(ny,nx,h2,g_both,bu_rows,own_a,own_b,oth_a,oth_b,gtile=256):
     keys=sorted(((ky,kx) for ky in range(ny) for kx in range(nx)),reverse=True); nk=len(keys)
-    images,half,feat=g_own.shape
+    _,images,half,feat=g_both.shape
+    keys_b=sorted(keys,key=lambda k:(k[1],k[0]),reverse=True)
     tokens=h2.shape[0]; padded=tokens//(2*images)
     ud,hid=own_a.shape[2:4]
     width=4*hid
     piece=jax.ShapeDtypeStruct((2,ud,hid,feat),BF)
-    out=pl.pallas_call(functools.partial(mlp_kernel,keys,ny,nx,gtile=min(gtile,width)),
-        in_specs=[VM]*4+[ANY]*4,
+    out=pl.pallas_call(functools.partial(mlp_kernel,keys,keys_b,ny,nx,gtile=min(gtile,width)),
+        in_specs=[VM]*3+[ANY]*4,
         out_specs=[ANY]*(2*nk)+[VM]*4+[ANY]*2,
         out_shape=[piece]*(2*nk)+[jax.ShapeDtypeStruct((images,padded,feat),F32),jax.ShapeDtypeStruct((images,padded,feat),BF),
             jax.ShapeDtypeStruct((tokens,feat),BF),jax.ShapeDtypeStruct(bu_rows.shape,F32),
@@ -259,8 +262,8 @@
         name="feed_forward",
         compiler_params=pltpu.CompilerParams(collective_id=3,has_side_effects=True,vmem_limit_bytes=60<<20),
         cost_estimate=pl.CostEstimate(flops=nk*6*2*tokens*feat*width,bytes_accessed=40<<20,transcendentals=nk*tokens*width),
-    )(h2,g_own,g_oth,bu_rows,own_a,own_b,oth_a,oth_b)
-    return dict(zip(keys,out[:nk])),dict(zip(keys,out[nk:2*nk])),out[2*nk:]
+    )(h2,g_both,bu_rows,own_a,own_b,oth_a,oth_b)
+    return dict(zip(keys,out[:nk])),dict(zip(keys_b,out[nk:2*nk])),out[2*nk:]
 
 HD=64; HALF_D=512
 
@@ -287,20 +290,8 @@
         sums.append(m+jnp.log(l))
     return jnp.concatenate(outs,axis=0).T.astype(BF),sums
 
-def attend_back_kernel(q_ref,k_ref,v_ref,kb_ref,o_ref,g_ref,lse_ref,keep_ref,give_ref,out_ref,sum_ref,part_ref,land,send_sem,recv_sem,*,pairs,chunk):
+def attend_back_kernel(q_ref,k_ref,v_ref,kb_ref,o_ref,g_ref,lse_ref,out_ref,sum_ref,*,pairs,chunk):
     p=pl.program_id(1)
-    to_dp={"dp":1-lax.axis_index("dp")}
-    cp=pltpu.make_async_remote_copy(src_ref=give_ref,dst_ref=land,send_sem=send_sem,recv_sem=recv_sem,device_id=to_dp,device_id_type=MESH_ID)
-    @pl.when((pl.program_id(0)==0)&(p==0))
-    def _():
-        barrier=pltpu.get_barrier_semaphore()
-        pl.semaphore_signal(barrier,inc=1,device_id=to_dp,device_id_type=MESH_ID)
-        pl.semaphore_wait(barrier,1)
-        cp.start()
-    @pl.when((pl.program_id(0)==pl.num_programs(0)-1)&(p==pairs-1))
-    def _():
-        cp.wait()
-        part_ref[...]=add_all(keep_ref[...],land[...]).astype(BF)
     @pl.when((pl.program_id(0)==0)&(p==0))
     def _(): sum_ref[...]=jnp.zeros_like(sum_ref)
     scale=HD**-0.5
@@ -334,19 +325,18 @@
         out_ref[0,:,at]=part
         sum_ref[0:1,at]+=jnp.sum(part.astype(F32),axis=0,keepdims=True)
 
-def attend_back(qkv,kbias,mixed,grad,lse,keep,give,chunk=None):
+def attend_back(qkv,kbias,mixed,grad,lse,chunk=None):
     n,rows,w=qkv.shape; pairs=w//3//128
     chunk=chunk or rows
     blk=lambda off: pl.BlockSpec((1,rows,128),lambda i,p: (i,0,off+p))
     return pl.pallas_call(functools.partial(attend_back_kernel,pairs=pairs,chunk=chunk),grid=(n,pairs),
-        in_specs=[blk(0),blk(pairs),blk(2*pairs),pl.BlockSpec((1,rows,128),lambda i,p:(i,0,0)),blk(0),blk(0),pl.BlockSpec((1,1,8,rows),lambda i,p:(i,p,0,0)),VM,VM],
-        out_specs=[pl.BlockSpec((1,rows,w),lambda i,p:(i,0,0)),pl.BlockSpec((8,w),lambda i,p:(0,0)),VM],
-        out_shape=[jax.ShapeDtypeStruct((n,rows,w),BF),jax.ShapeDtypeStruct((8,w),F32),jax.ShapeDtypeStruct(keep.shape,BF)],
-        scratch_shapes=[pltpu.VMEM(keep.shape,BF),pltpu.SemaphoreType.DMA(()),pltpu.SemaphoreType.DMA(())],
+        in_specs=[blk(0),blk(pairs),blk(2*pairs),pl.BlockSpec((1,rows,128),lambda i,p:(i,0,0)),blk(0),blk(0),pl.BlockSpec((1,1,8,rows),lambda i,p:(i,p,0,0))],
+        out_specs=[pl.BlockSpec((1,rows,w),lambda i,p:(i,0,0)),pl.BlockSpec((8,w),lambda i,p:(0,0))],
+        out_shape=[jax.ShapeDtypeStruct((n,rows,w),BF),jax.ShapeDtypeStruct((8,w),F32)],
         name="attend_back",
-        compiler_params=pltpu.CompilerParams(collective_id=4,has_side_effects=True,vmem_limit_bytes=50<<20),
+        compiler_params=pltpu.CompilerParams(vmem_limit_bytes=50<<20),
         cost_estimate=pl.CostEstimate(flops=n*pairs*20*rows*rows*128,bytes_accessed=n*rows*w*5,transcendentals=n*pairs*2*rows*rows),
-    )(qkv,qkv,qkv,kbias,mixed,grad,lse,keep,give)
+    )(qkv,qkv,qkv,kbias,mixed,grad,lse)
 
 NORM_EPS=1e-6
 def norm_parts(values):
@@ -373,7 +363,7 @@
     def _():
         acc[...]=jnp.zeros_like(acc); sum_ref[...]=jnp.zeros_like(sum_ref)
     for s,src in enumerate((go_ref,gt_ref)):
-        dd=wide_rows(buf.at[s],src[0])
+        dd=wide_rows(buf.at[s],src[0,0])
         grad=da_ref[0,s].astype(F32)+db_ref[0,1-s].astype(F32)
         dx,gg=norm_back(x2_ref[0,s],gain_ref[...],grad)
         dx=dx+dd
@@ -387,33 +377,33 @@
     @pl.when(i==pl.num_programs(0)-1)
     def _(): gw_ref[...]=acc[...].astype(BF)
 
-def middle_back(x2,dh_own,dh_oth,g_own,g_oth,mixed,w_own,gain):
-    n,half,feat=g_own.shape
+def middle_back(x2,dh_own,dh_oth,g_both,mixed,w_own,gain):
+    _,n,half,feat=g_both.shape
     _,_,padded,width=mixed.shape
-    tok=pl.BlockSpec((1,half,feat),lambda i:(i,0,0))
+    tok=lambda s: pl.BlockSpec((1,1,half,feat),lambda i:(s,i,0,0))
     mix=pl.BlockSpec((1,2,padded,width),lambda i:(i,0,0,0))
     big=pl.BlockSpec((1,2,padded,feat),lambda i:(i,0,0,0))
     full=pl.BlockSpec((width,feat),lambda i:(0,0))
     return pl.pallas_call(middle_back_kernel,grid=(n,),
-        in_specs=[big,big,big,tok,tok,mix,full,pl.BlockSpec((1,feat),lambda i:(0,0))],
+        in_specs=[big,big,big,tok(0),tok(1),mix,full,pl.BlockSpec((1,feat),lambda i:(0,0))],
         out_specs=[pl.BlockSpec((1,padded,feat),lambda i:(i,0,0)),mix,full,pl.BlockSpec((8,feat),lambda i:(0,0))],
         out_shape=[jax.ShapeDtypeStruct((n,padded,feat),F32),jax.ShapeDtypeStruct(mixed.shape,BF),jax.ShapeDtypeStruct((width,feat),BF),jax.ShapeDtypeStruct((8,feat),F32)],
         scratch_shapes=[pltpu.VMEM((2,padded,feat),F32),pltpu.VMEM((width,feat),F32)],name="middle_back",
         compiler_params=pltpu.CompilerParams(vmem_limit_bytes=56<<20),
         cost_estimate=pl.CostEstimate(flops=n*8*padded*feat*width,bytes_accessed=30<<20,transcendentals=0),
-    )(x2,dh_own,dh_oth,g_own,g_oth,mixed,w_own,gain[None])
+    )(x2,dh_own,dh_oth,g_both,g_both,mixed,w_own,gain[None])
 
 
 def tail_kernel(ny, nx, *refs):
     h1_ref, dqkv_ref, go_ref, x_ref, dx_ref, gain_ref, vec_ref, w = refs[:8]
-    fpart = refs[8]
-    o = 9
+    keep_ref, pass_ref = refs[8:10]
+    o = 10
     mine_ref, theirs_ref, so_ref, sf_ref, ig_ref, vout_ref, norm_ref = refs[o:o + 7]
     (grad, ra1, ra2, rb1, rb2, sa, sb, oa1, oa2, ob1, ob2, ta, tb, osum, ocross, ocore, odp, ofin,
-     frecv, isum, ipart, irecv, idp, ifin,
+     fpart, fdp, frecv, isum, ipart, irecv, idp, ifin,
      buf, give, got, stage, vrecv, nrecv, nval, send_sem, recv_sem) = refs[o + 7:]
     h, y, x, c, l = (lax.axis_index(a) for a in AXES)
-    images, half, feat = x_ref.shape
+    _, images, half, feat = x_ref.shape
     padded = dx_ref.shape[1]
     rows = grad.shape[4]
     apart = h != c
@@ -427,7 +417,7 @@
     wires = Wires(send_sem, recv_sem)
     greet([to_core, to_seq, to_dp] + to_x[1:] + to_y[1:], cross, apart)
 
-    fs = wires.send(fpart.at[1], frecv, to_seq)
+    fd = wires.send(pass_ref, fdp, to_dp)
     oa_got = [[wires.send(go_ref.at[yy[ky], xx[kx], h], oa1.at[ky - 1, kx], to_y[ky]) for kx in range(nx)] for ky in range(1, ny)]
     ob_got = [[wires.send(go_ref.at[yy[ky], xx[kx], 1 - h], ob1.at[kx - 1, ky], to_x[kx]) for ky in range(ny)] for kx in range(1, nx)]
     width = nx * 2 * rows
@@ -450,6 +440,32 @@
         r = (2 * i + 1) * padded
         give[i] = dot(dqkv_ref[r:r + padded, :], w[...], NT).astype(BF)
         dh_got.append(wires.send(give.at[i], got.at[i], to_core))
+    sum_gain, sum_shift = jnp.zeros((1, feat), F32), jnp.zeros((1, feat), F32)
+    crossing_copies = [wires.make(stage.at[i], ig_ref.at[i], cross) for i in range(images)]
+
+    def input_back(i, sum_gain, sum_shift):
+        r = 2 * i * padded
+        own = dot(dqkv_ref[r:r + padded, :], w[...], NT)
+        dh_got[i].wait_recv()
+        g = own + got[i].astype(F32)
+        dx, gg = norm_back(wide_rows(buf, x_ref[0, i]), gain_ref[...], g)
+        stage[i] = (dx + dx_ref[i]).astype(BF)[:half]
+
+        @pl.when(apart)
+        def _():
+            crossing_copies[i].start()
+
+        @pl.when(jnp.logical_not(apart))
+        def _():
+            ig_ref[i] = stage[i]
+
+        return sum_gain + jnp.sum(gg, axis=0, keepdims=True), sum_shift + jnp.sum(g, axis=0, keepdims=True)
+
+    for i in range(images):
+        sum_gain, sum_shift = input_back(i, sum_gain, sum_shift)
+    fd.wait_recv()
+    fpart[...] = add_all(keep_ref[...], fdp[...]).astype(BF)
+    fs = wires.send(fpart.at[1], frecv, to_seq)
     for row in oa_got + ob_got:
         for cp in row:
             cp.wait_recv()
@@ -461,29 +477,6 @@
         tb[ky - 1] = add_all(go_ref[yy[ky], x, 1 - h], *(ob1[k, ky] for k in range(nx - 1))).astype(BF)
         o_got.append(wires.send(tb.at[ky - 1], ob2.at[ky - 1], to_y[ky]))
 
-    sum_gain, sum_shift = jnp.zeros((1, feat), F32), jnp.zeros((1, feat), F32)
-    crossing_copies = [wires.make(stage.at[i], ig_ref.at[i], cross) for i in range(images)]
-
-    def input_back(i, sum_gain, sum_shift):
-        r = 2 * i * padded
-        own = dot(dqkv_ref[r:r + padded, :], w[...], NT)
-        dh_got[i].wait_recv()
-        g = own + got[i].astype(F32)
-        dx, gg = norm_back(wide_rows(buf, x_ref[i]), gain_ref[...], g)
-        stage[i] = (dx + dx_ref[i]).astype(BF)[:half]
-
-        @pl.when(apart)
-        def _():
-            crossing_copies[i].start()
-
-        @pl.when(jnp.logical_not(apart))
-        def _():
-            ig_ref[i] = stage[i]
-
-        return sum_gain + jnp.sum(gg, axis=0, keepdims=True), sum_shift + jnp.sum(g, axis=0, keepdims=True)
-
-    for i in range(min(2, images)):
-        sum_gain, sum_shift = input_back(i, sum_gain, sum_shift)
     for cp in ia_got + ib_got:
         cp.wait_recv()
     i_got = []
@@ -496,8 +489,6 @@
         i_got.append(wires.send(sa.at[kx - 1], ra2.at[kx - 1], to_x[kx]))
     for ky in range(1, ny):
         i_got.append(wires.send(sb.at[ky - 1], rb2.at[ky - 1], to_y[ky]))
-    for i in range(2, images):
-        sum_gain, sum_shift = input_back(i, sum_gain, sum_shift)
     vout_ref[...] = vec_ref[...]
     for q in range(feat // 128):
         vout_ref[q:q + 1, :] = sum_gain[:, q * 128:(q + 1) * 128]
@@ -607,14 +598,14 @@
     wires.finish()
 
 
-def tail_stage(h1, dqkv, g_out, x_own, dx2, gain, vec, w, fpart, ny, nx):
+def tail_stage(h1, dqkv, g_out, x_own, dx2, gain, vec, w, keep, give, ny, nx):
     tokens, feat = h1.shape
     width = dqkv.shape[1]
     rows = feat // (4 * ny * nx)
     rows_o = g_out.shape[3]
-    images, half, _ = x_own.shape
+    _, images, half, _ = x_own.shape
     padded = dx2.shape[1]
-    _, ud, hid, _ = fpart.shape
+    _, ud, hid, _ = keep.shape
     ma, mb = max(ny - 1, 1), max(nx - 1, 1)
     piece, out_piece, ff = (rows, width), (rows_o, feat), (ud, hid, feat)
     peers = 4 + nx - 1 + ny - 1
@@ -627,7 +618,7 @@
         V(ny - 1, nx, *out_piece), V(nx - 1, *out_piece), V(nx - 1, ny, *out_piece), V(ny - 1, *out_piece),
         V(nx - 1, *out_piece), V(ny - 1, *out_piece),
         V(2, *out_piece), V(2, *out_piece), V(*out_piece), V(*out_piece), V(*out_piece),
-        V(*ff),
+        V(2, *ff), V(2, *ff), V(*ff),
         V(2, 2, *piece), V(2, *piece), V(*piece), V(2, *piece), V(2, *piece),
         pltpu.VMEM((padded, feat), F32), V(images, padded, feat), V(images, padded, feat), V(images, half, feat),
         pltpu.VMEM((peers,) + vec.shape, F32), pltpu.VMEM((peers, 8, 128), F32), pltpu.VMEM((8, 128), F32),
@@ -635,18 +626,18 @@
     ]
     return pl.pallas_call(
         functools.partial(tail_kernel, ny, nx),
-        in_specs=[VM] * 9,
+        in_specs=[VM] * 10,
         out_specs=[VM] * 7,
         out_shape=[
             jax.ShapeDtypeStruct(piece, BF), jax.ShapeDtypeStruct(piece, BF), jax.ShapeDtypeStruct(out_piece, BF),
-            jax.ShapeDtypeStruct((2,) + ff, BF), jax.ShapeDtypeStruct(x_own.shape, BF),
+            jax.ShapeDtypeStruct((2,) + ff, BF), jax.ShapeDtypeStruct(x_own.shape[1:], BF),
             jax.ShapeDtypeStruct(vec.shape, F32), jax.ShapeDtypeStruct((8, 128), F32),
         ],
         scratch_shapes=scratch,
         name="tail_stage",
         compiler_params=pltpu.CompilerParams(collective_id=1, has_side_effects=True, vmem_limit_bytes=62 << 20),
         cost_estimate=pl.CostEstimate(flops=4 * tokens * feat * width, bytes_accessed=40 << 20, transcendentals=0),
-    )(h1, dqkv, g_out, x_own, dx2, gain[None], vec, w, fpart)
+    )(h1, dqkv, g_out, x_own, dx2, gain[None], vec, w, keep, give)
 
 def head_kernel(ny, nx, *refs):
     (in_ref, out_ref, up_ref, down_ref, vec_ref, img_ref,
@@ -767,6 +758,12 @@
     forward(in_b, 0, "y", b0)
     oc.wait_recv()
     x_cross = [wires.make(img_ref.at[i], xb.at[0, i], cross) for i in range(images)]
+    o_cross = [wires.make(o_own, my_out.at[y, x, 1 - h], cross), wires.make(o_core, my_out.at[y, x, h], cross)]
+
+    @pl.when(apart)
+    def _():
+        for cp in o_cross:
+            cp.start()
 
     @pl.when(jnp.logical_and(apart, jnp.logical_not(inner)))
     def _():
@@ -789,7 +786,6 @@
     for cp in v:
         cp.wait_recv()
     v = vec_send(3)
-    o_cross = [wires.make(o_own, my_out.at[y, x, 1 - h], cross), wires.make(o_core, my_out.at[y, x, h], cross)]
 
     @pl.when(jnp.logical_and(apart, inner))
     def _():
@@ -797,7 +793,7 @@
 
     @pl.when(apart)
     def _():
-        for cp in x_cross[1:] + o_cross:
+        for cp in x_cross[1:]:
             cp.start()
 
     @pl.when(jnp.logical_not(apart))
@@ -806,8 +802,17 @@
         my_out[y, x, 1 - h] = o_core[...]
         local_images.wait()
 
+    @pl.when(apart)
+    def _():
+        for cp in o_cross:
+            cp.wait_recv()
+
+    oa = spread(out_a, 0, "x")
+    ob = spread(out_b, 0, "y")
     forward(in_a, 1, "x", a1)
     forward(in_b, 1, "y", b1)
+    forward(out_a, 0, "x", oa)
+    forward(out_b, 0, "y", ob)
     fa0 = spread(ff_a, 0, "x")
     fb0 = spread(ff_b, 0, "y")
     for got in (a0, b0, a1, b1):
@@ -850,13 +855,6 @@
 
     lax.fori_loop(0, images, near_step, 0)
 
-    @pl.when(apart)
-    def _():
-        for cp in o_cross:
-            cp.wait_recv()
-
-    oa = spread(out_a, 0, "x")
-    ob = spread(out_b, 0, "y")
     forward(ff_a, 0, "x", fa0)
     forward(ff_b, 0, "y", fb0)
     x_core = [wires.make(xb.at[0, i], xb.at[1, i], to_core) for i in range(images)]
@@ -872,9 +870,6 @@
 
         project(i, 1 - near)
         if i == 0:
-            forward(out_a, 0, "x", oa)
-            forward(out_b, 0, "y", ob)
-        if i == 1 or images == 1:
             settle(oa)
             settle(ob)
             other = wires.send(my_out, other_out, to_core)
@@ -968,17 +963,23 @@
 
     @pl.when(inner)
     def _():
-        for cp in near_ff:
-            cp.start()
+        near_ff[0].start()
 
     @pl.when(jnp.logical_not(apart))
     def _():
         local_grad.start()
         grad_core.start()
 
-    @pl.when(apart)
-    def _():
-        g_cross[0].start()
+    def relay(ab):
+        @pl.when(inner)
+        def _():
+            near_ff[ab].wait_recv()
+            far_ff[ab].start()
+
+    def arrive(ab):
+        @pl.when(jnp.logical_not(inner))
+        def _():
+            far_ff[ab].wait_recv()
 
     mix_got = []
     for i in range(images):
@@ -992,22 +993,21 @@
 
         lax.fori_loop(0, pairs, pair, 0)
         mix_got.append(wires.send(mix_ref.at[i], mix_oth.at[i], to_core))
-        if i + 1 < images:
+        if i == 0:
+            @pl.when(inner)
+            def _():
+                near_ff[1].start()
+
+        if i == max(images - 2, 0):
+            relay(0)
+        if i == images - 1:
+            relay(1)
             @pl.when(apart)
             def _():
-                g_cross[i + 1].start()
+                for cp in g_cross:
+                    cp.start()
 
     gots = []
-
-    def arrive(ab):
-        @pl.when(inner)
-        def _():
-            near_ff[ab].wait_recv()
-            far_ff[ab].start()
-
-        @pl.when(jnp.logical_not(inner))
-        def _():
-            far_ff[ab].wait_recv()
 
     ff = [by_offset(fa, near_land.at[0]), by_offset(fb, near_land.at[1])]
     order = ("x", "y")
@@ -1137,7 +1137,6 @@
         in_weights, out_weights, up_weights, down_weights, vectors[None], images, padded, ny, nx
     )
     my_out, other_out = my_out.reshape(HALF_D, D), other_out.reshape(HALF_D, D)
-    x_own = x_both[0]
     rows_in, rows_out, rows_ff = in_weights.shape[0], out_weights.shape[0], up_weights.shape[0]
     half_ff = rows_ff // 2
     keys = [(ky, kx) for ky in range(ny) for kx in range(nx)]
@@ -1159,11 +1158,10 @@
     mixed, lse, x2, h2, g_both, oth_a, oth_b = mid_stage(
         qkv, key_fill, x_both, my_out, other_out, mid_vec, low_ff, out_grad, ny, nx
     )
-    g_own, g_oth = g_both[0], g_both[1]
     halved = mixed.reshape(image_count, 2, padded, HALF_D)
 
     grad_a, grad_b, (y_own, y_oth, dh2, g_bu, first_a, first_b) = mlp(
-        ny, nx, h2.reshape(tokens, D), g_own, g_oth, up_bias.reshape(shards * 2, half_ff), own_a, own_b, oth_a, oth_b
+        ny, nx, h2.reshape(tokens, D), g_both, up_bias.reshape(shards * 2, half_ff), own_a, own_b, oth_a, oth_b
     )
     result = y_own[:, :half] + shift(y_oth, "core", 1)[:, :half].astype(F32) + x2[:, 0, :half] + down_bias
     result = result.astype(BF)
@@ -1181,14 +1179,12 @@
 
     dh2 = dh2.reshape(image_count, 2, padded, D)
     dh2_oth = shift(dh2, "core", 1)
-    dx2, dattn, g_out, sums_two = middle_back(x2, dh2, dh2_oth, g_own, g_oth, halved, my_out, gain_two)
-    got_a, got_b = after(got_a, dattn), after(got_b, dattn)
+    dx2, dattn, g_out, sums_two = middle_back(x2, dh2, dh2_oth, g_both, halved, my_out, gain_two)
+    dqkv, sums_qkv = attend_back(qkv, key_fill, mixed, dattn.reshape(mixed.shape), lse)
+    got_a, got_b = after(got_a, dqkv), after(got_b, dqkv)
     plane_a, plane_b = add_all(sums_a[0], *got_a).astype(BF), add_all(sums_b[0], *got_b).astype(BF)
     l = lax.axis_index("dp")
     half_keep, half_give = jnp.where(l == 0, plane_a, plane_b), jnp.where(l == 0, plane_b, plane_a)
-    dqkv, sums_qkv, part_ff = attend_back(
-        qkv, key_fill, mixed, dattn.reshape(mixed.shape), lse, half_keep, half_give
-    )
 
     zero = jnp.zeros((D,), F32)
     vec = jnp.concatenate(
@@ -1208,12 +1204,13 @@
         h1.reshape(tokens, D),
         dqkv.reshape(tokens, 3 * HALF_D),
         g_out.reshape(ny, nx, 2, rows_out, D),
-        x_own,
+        x_both,
         dx2,
         gain_one,
         vec,
         full_in,
-        part_ff,
+        half_keep,
+        half_give,
         ny,
         nx,
     )

time: 547 us -> 522 us (0.954)
  Pallas kernels: 483 us -> 460 us
  local copies, waits for them, and re-layouts: 20.2 us -> 12.3 us
    pallas_call x1, Pallas kernels: 44.4 us -> 30.4 us  [attend_back(): pl.pallas_call(functools.partial(attend_back_kernel, pairs=pairs, chunk=c...]
    pallas_call x1, Pallas kernels: 114 us -> 105 us  [mid_stage(): pl.pallas_call(functools.partial(mid_kernel, ny, nx), in_specs=[VM] * 6 +...]
    squeeze x2 -> x0, local copies, waits for them, and re-layouts: 7.13 us -> none  [the longest x1 4.23 us: on_device(): g_own, g_oth = (g_both[0], g_both[1])]
  transfers between devices with their start and end apart: 6 -> 6, of which waited for: 0 -> 1; matrix products, arithmetic and copies ran while one was open for 4% -> 4% of each run, Pallas kernels for 53% -> 54%
where the time goes in v6:
time: 522 us; the launch traced here: 515 us
  Pallas kernels  460 us (88%)
  other arithmetic  31.2 us (6%)
  local copies, waits for them, and re-layouts  12.3 us (2%)
  starting transfers between devices  7.44 us (1%)
    pallas_call x1, Pallas kernels, tail_stage(): pl.pallas_call(functools.partial(tail_kernel, ny, nx), in_specs=[VM] * 10...  139 us
    pallas_call x1, Pallas kernels, mid_stage(): pl.pallas_call(functools.partial(mid_kernel, ny, nx), in_specs=[VM] * 6 +...  105 us
    pallas_call x1, Pallas kernels, head_stage(): pl.pallas_call(functools.partial(head_kernel, ny, nx), in_specs=[VM] * 5...  91.1 us
    pallas_call x1, Pallas kernels, mlp(): pl.pallas_call(functools.partial(mlp_kernel, keys, keys_b, ny, nx, gtile=...  77.7 us
    pallas_call x1, Pallas kernels, attend_back(): pl.pallas_call(functools.partial(attend_back_kernel, pairs=pairs, chunk=c...  30.4 us
    pallas_call x1, Pallas kernels, middle_back(): pl.pallas_call(middle_back_kernel, grid=(n,), in_specs=[big, big, big, to...  16.8 us
  transfers between devices with their start and end apart: 6, of which 1 were waited for; matrix products, arithmetic and copies ran while one was open for 4% of the time, Pallas kernels for 54%

profile of v6, /device:TPU:1, one launch (start us, length us, event | category | flops | bytes accessed | tf_op | source)
XLA Modules:
  0.0 515.5 jit_solution(16013405036257997575)
XLA Ops:
  0.7 0.7 convert_element_type.123
  1.4 0.1 collective-permute-start
  1.4 1.3 broadcast_in_dim.23.refs_4_
  2.7 91.1 %head_stage.1 = (bf16[3,2,304,1024]{3,2,1,0:T(8,128)(2,1)}, bf16[3,2,304,1536]{3,2,1,0:T(8,128)(2,1)}, bf16[2,3,292,1024]{3,2,1,0:T(8,128)(2,1)}, bf16[1024,1536...) custom-call(f32[64,3072]{1,0:T(8,128)} %refs_0_.1, ...), custom_call_target="tpu_custom_call" | custom-call | flops 5737807872 | bytes 41943040 | tf_op jit(solution)/shard_map/head_stage/pallas_call | solution.py:906
  93.8 1.3 fusion.23
  95.1 0.6 select_maximum_fusion.refs_5_
  95.8 1.3 slice.95.refs_2_
  97.1 0.0 collective-permute-done
  97.1 0.1 reshape.141
  97.2 0.1 rev.3
  97.4 0.1 convert_element_type.125
  97.4 1.1 broadcast_in_dim.25.refs_1_.kb_ref
  98.5 105.1 %mid_stage.1 = (bf16[3,608,512]{2,1,0:T(8,128)(2,1)}, f32[3,4,8,608]{3,2,1,0:T(8,128)}, f32[3,2,304,1024]{3,2,1,0:T(8,128)}, bf16[3,2,304,1024]{3,2,1,0:T(8,128)...) custom-call(bf16[3,608,1536]{2,1,0:T(8,128)(2,1)} %bitcast.85, ...), custom_call_target="tpu_custom_call" | custom-call | flops 6813646848 | bytes 52428800 | tf_op jit(solution)/shard_map/mid_stage/pallas_call | solution.py:1077
  203.6 77.7 %feed_forward.1 = (bf16[2,2,128,1024]{3,2,1,0:T(8,128)(2,1)}, bf16[2,2,128,1024]{3,2,1,0:T(8,128)(2,1)}, bf16[2,2,128,1024]{3,2,1,0:T(8,128)(2,1)}, bf16[2,2,128...) custom-call(bf16[1824,1024]{1,0:T(8,128)(2,1)} %bitcast.91, ...), custom_call_target="tpu_custom_call" | custom-call | flops 45902462976 | bytes 41943040 | tf_op jit(solution)/shard_map/feed_forward/pallas_call | solution.py:253
  281.4 3.9 collective-permute-start.1
  285.3 0.1 collective-permute-start.4
  286.1 3.1 fusion.3
  289.2 0.9 collective-permute-start.3
  290.0 2.6 fusion.5
  292.6 0.6 collective-permute-start.2
  293.2 1.2 collective-permute-done.4
  294.4 3.7 fusion.2
  298.2 1.9 collective-permute-start.5
  300.1 0.0 copy-start.1
  300.1 16.8 %middle_back.1 = (f32[3,304,1024]{2,1,0:T(8,128)}, bf16[3,2,304,512]{3,2,1,0:T(8,128)(2,1)}, bf16[512,1024]{1,0:T(8,128)(2,1)}, f32[8,1024]{1,0:T(8,128)}) custom-call(f32[3,2,304,1024]{3,2,1,0:T(8,128)} %get-tuple-element.74.x2_ref, bf16[3,2,304,1024]{3,2,1,0:T(8,128)(2,1)} %bitcast.66, bf16[3,2,304,1024]{3,2,1,0:T(8,128)(2,1)} %collective-permute-done.1.db_ref, ...), custom_call_target="tpu_custom_call" | custom-call | flops 3825205248 | bytes 31457280 | tf_op jit(solution)/shard_map/middle_back/pallas_call | solution.py:387
  317.0 0.0 copy-start.27
  317.0 30.4 %attend_back.1 = (bf16[3,608,1536]{2,1,0:T(8,128)(2,1)}, f32[8,1536]{1,0:T(8,128)S(1)}) custom-call(bf16[3,608,1536]{2,1,0:T(8,128)(2,1)} %bitcast.86, bf16[3,608,1536]{2,1,0:T(8,128)(2,1)} %bitcast.87, bf16[3,608,1536]{2,1,0:T(8,128)(2,1)} %bitcast.88, bf16[3,608,128]{2,1,0:T(8,128)(2,1)S(1)} %copy-done.1, bf16[3,608,512]{2,1,0:T(8,128)(2,1)S(1)} %copy-done, ...), custom_call_target="tpu_custom_call" | custom-call | flops 11356078080 | bytes 14008320 | tf_op jit(solution)/shard_map/attend_back/pallas_call | solution.py:332
  347.4 0.3 dynamic_update_slice.6
  347.6 0.2 dynamic_update_slice.7
  348.0 0.0 copy-start.30
  348.0 5.3 %broadcast_select_fusion = (bf16[2,2,128,1024]{3,2,1,0:T(8,128)(2,1)}, bf16[2,2,128,1024]{3,2,1,0:T(8,128)(2,1)}) fusion(pred[]{:T(512)S(6)} %eq.14, bf16[2,2,128,1024]{3,2,1,0:T(8,128)(2,1)} %collective-permute-done.2, bf16[1,2,2,2,128,1024]{5,4,3,2,1,0:T(8,128)(2,1)} %get-tuple-element.92, bf16[2,2,128,1024]{3,2,1,0:T(8,128)(2,1)S(1)} %copy-done.11, ...), kind=kLoop, calls=%fused_computation.27 | loop fusion | flops 9437184 | bytes 8388609 | tf_op jit(solution)/shard_map/jit(_where)/select_n | solution.py:1187
  353.3 139.3 %tail_stage.1 = (bf16[64,1536]{1,0:T(8,128)(2,1)}, bf16[64,1536]{1,0:T(8,128)(2,1)}, bf16[64,1024]{1,0:T(8,128)(2,1)}, bf16[2,2,128,1024]{3,2,1,0:T(8,128)(2,1)}...) custom-call(bf16[1824,1024]{1,0:T(8,128)(2,1)} %bitcast.90, bf16[1824,1536]{1,0:T(8,128)(2,1)} %bitcast.89, ...), custom_call_target="tpu_custom_call" | custom-call | flops 11475615744 | bytes 41943040 | tf_op jit(solution)/shard_map/tail_stage/pallas_call | solution.py:627
  492.6 1.2 slice.85
  493.8 3.6 select_convert_fusion
  498.2 0.1 reshape.153
  498.4 0.1 reshape.154
  498.6 0.0 copy-done.12
  498.6 0.3 convert_multiply_fusion
  498.9 0.1 convert_multiply_fusion.2
  499.0 1.5 copy.51
  500.5 1.8 mul.176
  502.3 0.0 copy-start.25
  502.3 0.0 copy-start.28
  502.3 0.0 copy-start.29
  502.4 0.0 copy-start.16
  502.4 0.0 copy-start.17
  502.4 0.0 copy-start.18
  502.4 0.0 copy-start.14
  502.4 0.0 copy-start.15
  502.4 3.9 convert_element_type.161
  506.4 0.6 fusion.13
  507.0 0.0 copy-start.10
  507.0 1.1 fusion.19
  508.1 0.0 copy-start.5
  508.1 0.0 copy-start.6
  508.1 0.0 copy-start.7
  508.1 0.0 copy-start.8
  508.1 0.0 copy-start.9
  508.2 1.9 fusion.21
  510.1 0.3 copy-done.6
  510.4 0.6 copy-done.7
  511.0 0.3 copy-done.8
  511.3 0.3 copy-done.9
  511.6 3.6 fusion.15
  (63 shorter events, 0.3 us)
Async XLA Ops:
  1.4 95.7 %collective-permute-start = (f32[3,584]{1,0:T(4,128)S(1)}, f32[3,584]{1,0:T(4,128)S(1)}, u32[]{:S(2)}, u32[]{:S(2)}) collective-permute-start(f32[3,584]{1,0:T(4,128)S(1)} %convert_element_type.123), channel_id=1, source_target_pairs={{0,2},{2,0},{1,3},{3,1},{4,6},{6,4},{5,7},{7,5},{8,10},{10,8},{9,1... | collective-permute-start | bytes 21032 | tf_op jit(solution)/shard_map/ppermute | solution.py:1098
  2.7 94.4 %copy-start.23 = (s32[3,584]{1,0:T(4,128)S(1)}, s32[3,584]{1,0:T(4,128)}, u32[]{:S(2)}) copy-start(s32[3,584]{1,0:T(4,128)} %param.20) | copy-start | bytes 21028
  95.1 108.5 %copy-start.24 = (f32[1024]{0:T(1024)}, f32[1024]{0:T(1024)S(1)}, u32[]{:S(2)}) copy-start(f32[1024]{0:T(1024)S(1)} %get-tuple-element.136) | copy-start | bytes 12292
  281.4 8.7 %copy-start.4 = (bf16[1,2,2,2,128,1024]{5,4,3,2,1,0:T(8,128)(2,1)S(1)}, bf16[1,2,2,2,128,1024]{5,4,3,2,1,0:T(8,128)(2,1)}, u32[]{:S(2)}) copy-start(bf16[1,2,2,2,128,1024]{5,4,3,2,1,0:T(8,128)(2,1)} %get-tuple-element.92) | copy-start | bytes 6291460
  281.4 18.7 %collective-permute-start.1 = (bf16[3,2,304,1024]{3,2,1,0:T(8,128)(2,1)}, bf16[3,2,304,1024]{3,2,1,0:T(8,128)(2,1)}, u32[]{:S(2)}, u32[]{:S(2)}) collective-permute-start(bf16[3,2,304,1024]{3,2,1,0:T(8,128)(2,1)} %bitcast.65), channel_id=1, source_target_pairs={{0,2},{2,0},{1,3},{3,1},{4,6},{6,4},{5,7},{7,5},{8,10},{10,8},{9,1... | collective-permute-start | bytes 11206664 | tf_op jit(solution)/shard_map/ppermute | solution.py:1098
  285.3 9.1 %collective-permute-start.4 = (bf16[3,304,1024]{2,1,0:T(8,128)(2,1)}, bf16[3,304,1024]{2,1,0:T(8,128)(2,1)}, u32[]{:S(2)}, u32[]{:S(2)}) collective-permute-start(bf16[3,304,1024]{2,1,0:T(8,128)(2,1)} %get-tuple-element.106), channel_id=1, source_target_pairs={{0,2},{2,0},{1,3},{3,1},{4,6},{6,4},{5,7},{7,5},{8,10},{10,8},{9,1... | collective-permute-start | bytes 5603336 | tf_op jit(solution)/shard_map/ppermute | solution.py:1098
  286.1 8.4 %copy-start.3 = (f32[3,304,1024]{2,1,0:T(8,128)S(1)}, f32[3,304,1024]{2,1,0:T(8,128)}, u32[]{:S(2)}) copy-start(f32[3,304,1024]{2,1,0:T(8,128)} %get-tuple-element.105) | copy-start | bytes 11206660
  289.2 58.8 %collective-permute-start.3 = (bf16[2,2,128,1024]{3,2,1,0:T(8,128)(2,1)}, bf16[2,2,128,1024]{3,2,1,0:T(8,128)(2,1)}, u32[]{:S(2)}, u32[]{:S(2)}) collective-permute-start(bf16[2,2,128,1024]{3,2,1,0:T(8,128)(2,1)} %fusion.3), channel_id=1, source_target_pairs={{0,8},{8,0},{1,9},{9,1},{2,10},{10,2},{3,11},{11,3},{4,12},{12,4},... | collective-permute-start | bytes 3145736 | tf_op jit(solution)/shard_map/ppermute | solution.py:1178
  292.6 55.3 %collective-permute-start.2 = (bf16[2,2,128,1024]{3,2,1,0:T(8,128)(2,1)}, bf16[2,2,128,1024]{3,2,1,0:T(8,128)(2,1)}, u32[]{:S(2)}, u32[]{:S(2)}) collective-permute-start(bf16[2,2,128,1024]{3,2,1,0:T(8,128)(2,1)} %fusion.5), channel_id=1, source_target_pairs={{0,4},{4,0},{1,5},{5,1},{2,6},{6,2},{3,7},{7,3},{8,12},{12,8},{9,1... | collective-permute-start | bytes 3145736 | tf_op jit(solution)/shard_map/ppermute | solution.py:1177
  298.2 195.6 %collective-permute-start.5 = (bf16[3,292,1024]{2,1,0:T(8,128)(2,1)S(1)}, bf16[3,292,1024]{2,1,0:T(8,128)(2,1)}, u32[]{:S(2)}, u32[]{:S(2)}) collective-permute-start(bf16[3,292,1024]{2,1,0:T(8,128)(2,1)S(1)} %fusion.2), channel_id=1, source_target_pairs={{2,16},{16,2},{3,17},{17,3},{6,20},{20,6},{7,21},{21,7},{10,24},{2... | collective-permute-start | bytes 5382152 | tf_op jit(solution)/shard_map/ppermute | solution.py:1106
  300.1 16.9 %copy-start = (bf16[3,608,512]{2,1,0:T(8,128)(2,1)S(1)}, bf16[3,608,512]{2,1,0:T(8,128)(2,1)}, u32[]{:S(2)}) copy-start(bf16[3,608,512]{2,1,0:T(8,128)(2,1)} %get-tuple-element.73.o_ref) | copy-start | bytes 5603332
  300.1 16.9 %copy-start.1 = (bf16[3,608,128]{2,1,0:T(8,128)(2,1)S(1)}, bf16[3,608,128]{2,1,0:T(8,128)(2,1)}, u32[]{:S(2)}) copy-start(bf16[3,608,128]{2,1,0:T(8,128)(2,1)} %broadcast_in_dim.25.refs_1_.kb_ref) | copy-start | bytes 1400836
  300.1 16.8 %copy-start.2 = (f32[3,4,8,608]{3,2,1,0:T(8,128)S(1)}, f32[3,4,8,608]{3,2,1,0:T(8,128)}, u32[]{:S(2)}) copy-start(f32[3,4,8,608]{3,2,1,0:T(8,128)} %get-tuple-element.83.lse_ref) | copy-start | bytes 700420
  317.0 30.9 %copy-start.27 = (f32[8,1024]{1,0:T(8,128)S(1)}, f32[8,1024]{1,0:T(8,128)}, u32[]{:S(2)}) copy-start(f32[8,1024]{1,0:T(8,128)} %get-tuple-element.88) | copy-start | bytes 98308
  317.0 31.0 %copy-start.26 = (f32[32,128]{1,0:T(8,128)S(1)}, f32[32,128]{1,0:T(8,128)}, u32[]{:S(2)}) copy-start(f32[32,128]{1,0:T(8,128)} %get-tuple-element.89) | copy-start | bytes 49156
  317.0 31.0 %copy-start.11 = (bf16[2,2,128,1024]{3,2,1,0:T(8,128)(2,1)S(1)}, bf16[2,2,128,1024]{3,2,1,0:T(8,128)(2,1)}, u32[]{:S(2)}) copy-start(bf16[2,2,128,1024]{3,2,1,0:T(8,128)(2,1)} %get-tuple-element.91) | copy-start | bytes 3145732
  348.0 5.4 %copy-start.30 = (f32[12288]{0:T(1024)}, f32[12288]{0:T(1024)S(1)}, u32[]{:S(2)}) copy-start(f32[12288]{0:T(1024)S(1)} %bitcast_dynamic-update-slice_fusion) | copy-start | bytes 147460
  493.8 3.6 copy-start.22
  493.8 4.4 copy-start.20
  493.8 4.6 copy-start.19
  497.4 1.2 copy-start.12
  502.3 4.0 copy-start.25
  502.3 4.0 copy-start.28
  502.3 4.0 copy-start.29
  502.4 4.6 copy-start.16
  502.4 4.6 copy-start.17
  502.4 4.6 copy-start.18
  502.4 4.6 copy-start.21
  502.4 5.7 %copy-start.14 = (f32[64,3072]{1,0:T(8,128)S(1)}, f32[64,3072]{1,0:T(8,128)}, u32[]{:S(2)}) copy-start(f32[64,3072]{1,0:T(8,128)} %param.33) | copy-start | bytes 2359300
  502.4 5.7 %copy-start.15 = (f32[64,3072]{1,0:T(8,128)S(1)}, f32[64,3072]{1,0:T(8,128)}, u32[]{:S(2)}) copy-start(f32[64,3072]{1,0:T(8,128)} %param.28) | copy-start | bytes 2359300
  506.3 1.8 copy-start.13
  507.0 3.1 copy-start.10
  508.1 2.0 copy-start.5
  508.1 2.3 copy-start.6
  508.1 2.9 copy-start.7
  508.1 3.2 copy-start.8
  508.1 3.5 copy-start.9

commit v7 on v6

--- a/solution.py
+++ b/solution.py
@@ -641,7 +641,7 @@
 
 def head_kernel(ny, nx, *refs):
     (in_ref, out_ref, up_ref, down_ref, vec_ref, img_ref,
-     h1_ref, qkv_ref, xb, w, my_out, other_out, fa, fb, cast_ref, vfull,
+     h1_ref, qkv_ref, xb, w, my_out, other_out, fa, fb, near_ref, vfull,
      theirs, o_own, o_core, tmp, buf, xsem, csem, send_sem, recv_sem) = refs
     h, y, x, c, l = (lax.axis_index(a) for a in AXES)
     images, half, feat = img_ref.shape
@@ -747,7 +747,6 @@
     keep = [
         pltpu.make_async_copy(tmp.at[0], fa.at[0, 0], csem.at[0]),
         pltpu.make_async_copy(tmp.at[1], fb.at[0, 0], csem.at[1]),
-        pltpu.make_async_copy(tmp, cast_ref, csem.at[2]),
     ]
     for cp in keep:
         cp.start()
@@ -857,6 +856,7 @@
 
     forward(ff_a, 0, "x", fa0)
     forward(ff_b, 0, "y", fb0)
+    near_ff = [wires.make(tmp.at[ab], near_ref.at[ab], to_near) for ab in range(2)]
     x_core = [wires.make(xb.at[0, i], xb.at[1, i], to_core) for i in range(images)]
     for i in range(images):
         @pl.when(apart)
@@ -867,6 +867,12 @@
         @pl.when(jnp.logical_not(apart))
         def _():
             x_core[i].wait_recv()
+
+        if i == images - 1:
+            @pl.when(inner)
+            def _():
+                for cp in near_ff:
+                    cp.start()
 
         project(i, 1 - near)
         if i == 0:
@@ -888,7 +894,9 @@
 
     @pl.when(inner)
     def _():
-        for cp in az + bz:
+        for cp in near_ff:
+            cp.wait_recv()
+        for cp in (*az, *bz, *near_ff):
             cp.wait_send()
 
     for cp in keep:
@@ -926,15 +934,15 @@
 
 
 def mid_kernel(ny, nx, *refs):
-    (qkv_ref, kf_ref, xb, wo_ref, wt_ref, vec_ref, cast_ref, grad_ref,
+    (qkv_ref, kf_ref, xb, wo_ref, wt_ref, vec_ref, near_ref, grad_ref,
      mix_ref, lse_ref, x2_ref, h2_ref, g_ref, fa, fb,
-     mix_oth, near_land, buf, csem, send_sem, recv_sem) = refs
+     mix_oth, land, buf, csem, send_sem, recv_sem) = refs
     h, y, x, c, l = (lax.axis_index(a) for a in AXES)
     images, rows, width = mix_ref.shape
     padded = rows // 2
     pairs = width // 128
     apart, inner = h != c, l != h
-    cross, to_near = {"seq": 1 - h, "core": 1 - c}, {"seq": 1 - h, "dp": 1 - l}
+    cross = {"seq": 1 - h, "core": 1 - c}
     to_core, to_dp = {"core": 1 - c}, {"dp": 1 - l}
     to_x = [{"x": lax.rem(x + nx - k, nx)} for k in range(nx)]
     to_y = [{"y": lax.rem(y + ny - k, ny)} for k in range(ny)]
@@ -949,13 +957,9 @@
     def _():
         pl.semaphore_signal(barrier, inc=1, device_id=cross, device_id_type=MESH_ID)
 
-    @pl.when(inner)
-    def _():
-        pl.semaphore_signal(barrier, inc=1, device_id=to_near, device_id_type=MESH_ID)
-
-    pl.semaphore_wait(barrier, len(peers) + jnp.where(apart, 1, 0) + jnp.where(inner, 1, 0))
-    near_ff = [wires.make(cast_ref.at[ab], near_land.at[ab], to_near) for ab in range(2)]
-    far_ff = [wires.make(near_land.at[ab], near_land.at[ab], to_dp) for ab in range(2)]
+    pl.semaphore_wait(barrier, len(peers) + jnp.where(apart, 1, 0))
+    here_ff = [pltpu.make_async_copy(near_ref.at[ab], land.at[ab], csem.at[3 + ab]) for ab in range(2)]
+    far_ff = [wires.make(near_ref.at[ab], land.at[ab], to_dp) for ab in range(2)]
     local_grad = pltpu.make_async_copy(grad_ref, g_ref.at[0], csem.at[0])
     grad_core = wires.make(grad_ref, g_ref.at[1], to_core)
     g_cross = [wires.make(grad_ref.at[i], g_ref.at[0, i], cross) for i in range(images)]
@@ -963,23 +967,33 @@
 
     @pl.when(inner)
     def _():
-        near_ff[0].start()
+        for cp in far_ff + here_ff:
+            cp.start()
 
     @pl.when(jnp.logical_not(apart))
     def _():
         local_grad.start()
         grad_core.start()
 
-    def relay(ab):
+    def arrive(ab):
         @pl.when(inner)
         def _():
-            near_ff[ab].wait_recv()
-            far_ff[ab].start()
-
-    def arrive(ab):
+            here_ff[ab].wait()
+
         @pl.when(jnp.logical_not(inner))
         def _():
             far_ff[ab].wait_recv()
+
+        return spread(ff[ab], 1, order[ab])
+
+    ff = [by_offset(fa, land.at[0]), by_offset(fb, land.at[1])]
+    order = ("x", "y")
+    gots = []
+
+    @pl.when(apart)
+    def _():
+        for cp in g_cross:
+            cp.start()
 
     mix_got = []
     for i in range(images):
@@ -993,24 +1007,10 @@
 
         lax.fori_loop(0, pairs, pair, 0)
         mix_got.append(wires.send(mix_ref.at[i], mix_oth.at[i], to_core))
-        if i == 0:
-            @pl.when(inner)
-            def _():
-                near_ff[1].start()
-
         if i == max(images - 2, 0):
-            relay(0)
+            gots.append(arrive(0))
         if i == images - 1:
-            relay(1)
-            @pl.when(apart)
-            def _():
-                for cp in g_cross:
-                    cp.start()
-
-    gots = []
-
-    ff = [by_offset(fa, near_land.at[0]), by_offset(fb, near_land.at[1])]
-    order = ("x", "y")
+            gots.append(arrive(1))
 
     def middle(i):
         mix_got[i].wait_recv()
@@ -1022,18 +1022,14 @@
             x2_ref[i, s] = v
             h2_ref[i, s] = (norm_parts(v)[0] * vec_ref[1:2, :] + vec_ref[2:3, :]).astype(BF)
 
-    middle(0)
-    arrive(0)
-    gots.append(spread(ff[0], 1, "x"))
-    for i in range(1, images):
+    for i in range(images):
         middle(i)
-    arrive(1)
-    gots.append(spread(ff[1], 1, "y"))
-    keep = [pltpu.make_async_copy(near_land.at[ab], (fa, fb)[ab].at[0, 0], csem.at[1 + ab]) for ab in range(2)]
+        if i == 0:
+            forward(ff[0], 1, order[0], gots[0])
+    keep = [pltpu.make_async_copy(land.at[ab], (fa, fb)[ab].at[0, 0], csem.at[1 + ab]) for ab in range(2)]
     for cp in keep:
         cp.start()
-    for ab in range(2):
-        forward(ff[ab], 1, order[ab], gots[ab])
+    forward(ff[1], 1, order[1], gots[1])
     for i in range(images):
         @pl.when(apart)
         def _():
@@ -1057,7 +1053,7 @@
 
     @pl.when(inner)
     def _():
-        for cp in near_ff + far_ff:
+        for cp in far_ff:
             cp.wait_send()
 
     for got in gots:
@@ -1085,7 +1081,7 @@
         ],
         scratch_shapes=[
             pltpu.VMEM((n, rows, width), BF), pltpu.VMEM((2, ud, hid, feat), BF), pltpu.VMEM((rows // 2, feat), F32),
-            pltpu.SemaphoreType.DMA((3,)), pltpu.SemaphoreType.DMA((many,)), pltpu.SemaphoreType.DMA((many,)),
+            pltpu.SemaphoreType.DMA((5,)), pltpu.SemaphoreType.DMA((many,)), pltpu.SemaphoreType.DMA((many,)),
         ],
         name="mid_stage",
         compiler_params=pltpu.CompilerParams(collective_id=5, has_side_effects=True, vmem_limit_bytes=60 << 20),

time: 522 us -> 503 us (0.964)
  Pallas kernels: 460 us -> 442 us
    pallas_call x1, Pallas kernels: 105 us -> 93.1 us  [mid_stage(): pl.pallas_call(functools.partial(mid_kernel, ny, nx), in_specs=[VM] * 6 +...]
    pallas_call x1, Pallas kernels: 139 us -> 133 us  [tail_stage(): pl.pallas_call(functools.partial(tail_kernel, ny, nx), in_specs=[VM] * 10...]
  transfers between devices with their start and end apart: 6 -> 6, of which waited for: 1 -> 1; matrix products, arithmetic and copies ran while one was open for 4% -> 4% of each run, Pallas kernels for 54% -> 55%
where the time goes in v7:
time: 503 us; the launch traced here: 495 us
  Pallas kernels  442 us (88%)
  other arithmetic  31.2 us (6%)
  local copies, waits for them, and re-layouts  12.3 us (2%)
  starting transfers between devices  5.92 us (1%)
    pallas_call x1, Pallas kernels, tail_stage(): pl.pallas_call(functools.partial(tail_kernel, ny, nx), in_specs=[VM] * 10...  133 us
    pallas_call x1, Pallas kernels, mid_stage(): pl.pallas_call(functools.partial(mid_kernel, ny, nx), in_specs=[VM] * 6 +...  93.1 us
    pallas_call x1, Pallas kernels, head_stage(): pl.pallas_call(functools.partial(head_kernel, ny, nx), in_specs=[VM] * 5...  91.1 us
    pallas_call x1, Pallas kernels, mlp(): pl.pallas_call(functools.partial(mlp_kernel, keys, keys_b, ny, nx, gtile=...  77.8 us
    pallas_call x1, Pallas kernels, attend_back(): pl.pallas_call(functools.partial(attend_back_kernel, pairs=pairs, chunk=c...  30.4 us
    pallas_call x1, Pallas kernels, middle_back(): pl.pallas_call(middle_back_kernel, grid=(n,), in_specs=[big, big, big, to...  16.8 us
  transfers between devices with their start and end apart: 6, of which 1 were waited for; matrix products, arithmetic and copies ran while one was open for 4% of the time, Pallas kernels for 55%

profile of v7, /device:TPU:1, one launch (start us, length us, event | category | flops | bytes accessed | tf_op | source)
XLA Modules:
  0.0 495.4 jit_solution(15732243099251765320)
XLA Ops:
  0.7 0.7 convert_element_type.123
  1.4 0.1 collective-permute-start
  1.4 1.3 broadcast_in_dim.23.refs_4_
  2.7 91.1 %head_stage.1 = (bf16[3,2,304,1024]{3,2,1,0:T(8,128)(2,1)}, bf16[3,2,304,1536]{3,2,1,0:T(8,128)(2,1)}, bf16[2,3,292,1024]{3,2,1,0:T(8,128)(2,1)}, bf16[1024,1536...) custom-call(f32[64,3072]{1,0:T(8,128)} %refs_0_.1, ...), custom_call_target="tpu_custom_call" | custom-call | flops 5737807872 | bytes 41943040 | tf_op jit(solution)/shard_map/head_stage/pallas_call | solution.py:914
  93.8 1.3 fusion.23
  95.1 0.6 select_maximum_fusion.refs_5_
  95.8 1.3 slice.95.refs_2_
  97.1 0.0 collective-permute-done
  97.1 0.1 reshape.141
  97.2 0.1 rev.3
  97.4 0.1 convert_element_type.125
  97.4 1.1 broadcast_in_dim.25.refs_1_.kb_ref
  98.5 93.1 %mid_stage.1 = (bf16[3,608,512]{2,1,0:T(8,128)(2,1)}, f32[3,4,8,608]{3,2,1,0:T(8,128)}, f32[3,2,304,1024]{3,2,1,0:T(8,128)}, bf16[3,2,304,1024]{3,2,1,0:T(8,128)...) custom-call(bf16[3,608,1536]{2,1,0:T(8,128)(2,1)} %bitcast.85, ...), custom_call_target="tpu_custom_call" | custom-call | flops 6813646848 | bytes 52428800 | tf_op jit(solution)/shard_map/mid_stage/pallas_call | solution.py:1073
  191.7 77.8 %feed_forward.1 = (bf16[2,2,128,1024]{3,2,1,0:T(8,128)(2,1)}, bf16[2,2,128,1024]{3,2,1,0:T(8,128)(2,1)}, bf16[2,2,128,1024]{3,2,1,0:T(8,128)(2,1)}, bf16[2,2,128...) custom-call(bf16[1824,1024]{1,0:T(8,128)(2,1)} %bitcast.91, ...), custom_call_target="tpu_custom_call" | custom-call | flops 45902462976 | bytes 41943040 | tf_op jit(solution)/shard_map/feed_forward/pallas_call | solution.py:253
  269.5 2.4 collective-permute-start.1
  271.9 0.1 collective-permute-start.4
  272.7 3.1 fusion.3
  275.8 0.9 collective-permute-start.3
  276.7 2.6 fusion.5
  279.3 0.6 collective-permute-start.2
  279.9 1.2 collective-permute-done.4
  281.1 3.7 fusion.2
  284.8 1.9 collective-permute-start.5
  286.8 0.0 copy-start.1
  286.8 16.8 %middle_back.1 = (f32[3,304,1024]{2,1,0:T(8,128)}, bf16[3,2,304,512]{3,2,1,0:T(8,128)(2,1)}, bf16[512,1024]{1,0:T(8,128)(2,1)}, f32[8,1024]{1,0:T(8,128)}) custom-call(f32[3,2,304,1024]{3,2,1,0:T(8,128)} %get-tuple-element.74.x2_ref, bf16[3,2,304,1024]{3,2,1,0:T(8,128)(2,1)} %bitcast.66, bf16[3,2,304,1024]{3,2,1,0:T(8,128)(2,1)} %collective-permute-done.1.db_ref, ...), custom_call_target="tpu_custom_call" | custom-call | flops 3825205248 | bytes 31457280 | tf_op jit(solution)/shard_map/middle_back/pallas_call | solution.py:387
  303.6 0.0 copy-start.27
  303.7 30.4 %attend_back.1 = (bf16[3,608,1536]{2,1,0:T(8,128)(2,1)}, f32[8,1536]{1,0:T(8,128)S(1)}) custom-call(bf16[3,608,1536]{2,1,0:T(8,128)(2,1)} %bitcast.86, bf16[3,608,1536]{2,1,0:T(8,128)(2,1)} %bitcast.87, bf16[3,608,1536]{2,1,0:T(8,128)(2,1)} %bitcast.88, bf16[3,608,128]{2,1,0:T(8,128)(2,1)S(1)} %copy-done.1, bf16[3,608,512]{2,1,0:T(8,128)(2,1)S(1)} %copy-done, ...), custom_call_target="tpu_custom_call" | custom-call | flops 11356078080 | bytes 14008320 | tf_op jit(solution)/shard_map/attend_back/pallas_call | solution.py:332
  334.1 0.3 dynamic_update_slice.6
  334.3 0.2 dynamic_update_slice.7
  334.6 0.0 copy-start.30
  334.7 5.3 %broadcast_select_fusion = (bf16[2,2,128,1024]{3,2,1,0:T(8,128)(2,1)}, bf16[2,2,128,1024]{3,2,1,0:T(8,128)(2,1)}) fusion(pred[]{:T(512)S(6)} %eq.14, bf16[2,2,128,1024]{3,2,1,0:T(8,128)(2,1)} %collective-permute-done.2, bf16[1,2,2,2,128,1024]{5,4,3,2,1,0:T(8,128)(2,1)} %get-tuple-element.92, bf16[2,2,128,1024]{3,2,1,0:T(8,128)(2,1)S(1)} %copy-done.11, ...), kind=kLoop, calls=%fused_computation.27 | loop fusion | flops 9437184 | bytes 8388609 | tf_op jit(solution)/shard_map/jit(_where)/select_n | solution.py:1183
  340.0 132.5 %tail_stage.1 = (bf16[64,1536]{1,0:T(8,128)(2,1)}, bf16[64,1536]{1,0:T(8,128)(2,1)}, bf16[64,1024]{1,0:T(8,128)(2,1)}, bf16[2,2,128,1024]{3,2,1,0:T(8,128)(2,1)}...) custom-call(bf16[1824,1024]{1,0:T(8,128)(2,1)} %bitcast.90, bf16[1824,1536]{1,0:T(8,128)(2,1)} %bitcast.89, ...), custom_call_target="tpu_custom_call" | custom-call | flops 11475615744 | bytes 41943040 | tf_op jit(solution)/shard_map/tail_stage/pallas_call | solution.py:627
  472.5 1.2 slice.85
  473.7 3.6 select_convert_fusion
  478.2 0.1 reshape.153
  478.4 0.1 reshape.154
  478.6 0.0 copy-done.12
  478.6 0.3 convert_multiply_fusion
  478.9 0.1 convert_multiply_fusion.2
  479.0 1.5 copy.51
  480.5 1.8 mul.176
  482.3 0.0 copy-start.25
  482.3 0.0 copy-start.28
  482.3 0.0 copy-start.29
  482.3 0.0 copy-start.16
  482.3 0.0 copy-start.17
  482.3 0.0 copy-start.18
  482.3 0.0 copy-start.14
  482.4 0.0 copy-start.15
  482.4 3.9 convert_element_type.161
  486.3 0.6 fusion.13
  487.0 0.0 copy-start.10
  487.0 1.1 fusion.19
  488.0 0.0 copy-start.5
  488.1 0.0 copy-start.6
  488.1 0.0 copy-start.7
  488.1 0.0 copy-start.8
  488.1 0.0 copy-start.9
  488.1 1.9 fusion.21
  490.0 0.3 copy-done.6
  490.3 0.6 copy-done.7
  491.0 0.3 copy-done.8
  491.3 0.3 copy-done.9
  491.6 3.6 fusion.15
  (63 shorter events, 0.3 us)
Async XLA Ops:
  1.4 95.7 %collective-permute-start = (f32[3,584]{1,0:T(4,128)S(1)}, f32[3,584]{1,0:T(4,128)S(1)}, u32[]{:S(2)}, u32[]{:S(2)}) collective-permute-start(f32[3,584]{1,0:T(4,128)S(1)} %convert_element_type.123), channel_id=1, source_target_pairs={{0,2},{2,0},{1,3},{3,1},{4,6},{6,4},{5,7},{7,5},{8,10},{10,8},{9,1... | collective-permute-start | bytes 21032 | tf_op jit(solution)/shard_map/ppermute | solution.py:1094
  2.7 94.4 %copy-start.23 = (s32[3,584]{1,0:T(4,128)S(1)}, s32[3,584]{1,0:T(4,128)}, u32[]{:S(2)}) copy-start(s32[3,584]{1,0:T(4,128)} %param.20) | copy-start | bytes 21028
  95.1 96.5 %copy-start.24 = (f32[1024]{0:T(1024)}, f32[1024]{0:T(1024)S(1)}, u32[]{:S(2)}) copy-start(f32[1024]{0:T(1024)S(1)} %get-tuple-element.136) | copy-start | bytes 12292
  269.5 7.2 %copy-start.4 = (bf16[1,2,2,2,128,1024]{5,4,3,2,1,0:T(8,128)(2,1)S(1)}, bf16[1,2,2,2,128,1024]{5,4,3,2,1,0:T(8,128)(2,1)}, u32[]{:S(2)}) copy-start(bf16[1,2,2,2,128,1024]{5,4,3,2,1,0:T(8,128)(2,1)} %get-tuple-element.92) | copy-start | bytes 6291460
  269.5 17.2 %collective-permute-start.1 = (bf16[3,2,304,1024]{3,2,1,0:T(8,128)(2,1)}, bf16[3,2,304,1024]{3,2,1,0:T(8,128)(2,1)}, u32[]{:S(2)}, u32[]{:S(2)}) collective-permute-start(bf16[3,2,304,1024]{3,2,1,0:T(8,128)(2,1)} %bitcast.65), channel_id=1, source_target_pairs={{0,2},{2,0},{1,3},{3,1},{4,6},{6,4},{5,7},{7,5},{8,10},{10,8},{9,1... | collective-permute-start | bytes 11206664 | tf_op jit(solution)/shard_map/ppermute | solution.py:1094
  271.9 9.1 %collective-permute-start.4 = (bf16[3,304,1024]{2,1,0:T(8,128)(2,1)}, bf16[3,304,1024]{2,1,0:T(8,128)(2,1)}, u32[]{:S(2)}, u32[]{:S(2)}) collective-permute-start(bf16[3,304,1024]{2,1,0:T(8,128)(2,1)} %get-tuple-element.106), channel_id=1, source_target_pairs={{0,2},{2,0},{1,3},{3,1},{4,6},{6,4},{5,7},{7,5},{8,10},{10,8},{9,1... | collective-permute-start | bytes 5603336 | tf_op jit(solution)/shard_map/ppermute | solution.py:1094
  272.7 8.4 %copy-start.3 = (f32[3,304,1024]{2,1,0:T(8,128)S(1)}, f32[3,304,1024]{2,1,0:T(8,128)}, u32[]{:S(2)}) copy-start(f32[3,304,1024]{2,1,0:T(8,128)} %get-tuple-element.105) | copy-start | bytes 11206660
  275.8 58.8 %collective-permute-start.3 = (bf16[2,2,128,1024]{3,2,1,0:T(8,128)(2,1)}, bf16[2,2,128,1024]{3,2,1,0:T(8,128)(2,1)}, u32[]{:S(2)}, u32[]{:S(2)}) collective-permute-start(bf16[2,2,128,1024]{3,2,1,0:T(8,128)(2,1)} %fusion.3), channel_id=1, source_target_pairs={{0,8},{8,0},{1,9},{9,1},{2,10},{10,2},{3,11},{11,3},{4,12},{12,4},... | collective-permute-start | bytes 3145736 | tf_op jit(solution)/shard_map/ppermute | solution.py:1174
  279.3 55.3 %collective-permute-start.2 = (bf16[2,2,128,1024]{3,2,1,0:T(8,128)(2,1)}, bf16[2,2,128,1024]{3,2,1,0:T(8,128)(2,1)}, u32[]{:S(2)}, u32[]{:S(2)}) collective-permute-start(bf16[2,2,128,1024]{3,2,1,0:T(8,128)(2,1)} %fusion.5), channel_id=1, source_target_pairs={{0,4},{4,0},{1,5},{5,1},{2,6},{6,2},{3,7},{7,3},{8,12},{12,8},{9,1... | collective-permute-start | bytes 3145736 | tf_op jit(solution)/shard_map/ppermute | solution.py:1173
  284.8 188.9 %collective-permute-start.5 = (bf16[3,292,1024]{2,1,0:T(8,128)(2,1)S(1)}, bf16[3,292,1024]{2,1,0:T(8,128)(2,1)}, u32[]{:S(2)}, u32[]{:S(2)}) collective-permute-start(bf16[3,292,1024]{2,1,0:T(8,128)(2,1)S(1)} %fusion.2), channel_id=1, source_target_pairs={{2,16},{16,2},{3,17},{17,3},{6,20},{20,6},{7,21},{21,7},{10,24},{2... | collective-permute-start | bytes 5382152 | tf_op jit(solution)/shard_map/ppermute | solution.py:1102
  286.7 16.9 %copy-start = (bf16[3,608,512]{2,1,0:T(8,128)(2,1)S(1)}, bf16[3,608,512]{2,1,0:T(8,128)(2,1)}, u32[]{:S(2)}) copy-start(bf16[3,608,512]{2,1,0:T(8,128)(2,1)} %get-tuple-element.73.o_ref) | copy-start | bytes 5603332
  286.8 16.9 %copy-start.1 = (bf16[3,608,128]{2,1,0:T(8,128)(2,1)S(1)}, bf16[3,608,128]{2,1,0:T(8,128)(2,1)}, u32[]{:S(2)}) copy-start(bf16[3,608,128]{2,1,0:T(8,128)(2,1)} %broadcast_in_dim.25.refs_1_.kb_ref) | copy-start | bytes 1400836
  286.8 16.9 %copy-start.2 = (f32[3,4,8,608]{3,2,1,0:T(8,128)S(1)}, f32[3,4,8,608]{3,2,1,0:T(8,128)}, u32[]{:S(2)}) copy-start(f32[3,4,8,608]{3,2,1,0:T(8,128)} %get-tuple-element.83.lse_ref) | copy-start | bytes 700420
  303.6 30.9 %copy-start.27 = (f32[8,1024]{1,0:T(8,128)S(1)}, f32[8,1024]{1,0:T(8,128)}, u32[]{:S(2)}) copy-start(f32[8,1024]{1,0:T(8,128)} %get-tuple-element.88) | copy-start | bytes 98308
  303.7 31.0 %copy-start.26 = (f32[32,128]{1,0:T(8,128)S(1)}, f32[32,128]{1,0:T(8,128)}, u32[]{:S(2)}) copy-start(f32[32,128]{1,0:T(8,128)} %get-tuple-element.89) | copy-start | bytes 49156
  303.7 31.0 %copy-start.11 = (bf16[2,2,128,1024]{3,2,1,0:T(8,128)(2,1)S(1)}, bf16[2,2,128,1024]{3,2,1,0:T(8,128)(2,1)}, u32[]{:S(2)}) copy-start(bf16[2,2,128,1024]{3,2,1,0:T(8,128)(2,1)} %get-tuple-element.91) | copy-start | bytes 3145732
  334.6 5.4 %copy-start.30 = (f32[12288]{0:T(1024)}, f32[12288]{0:T(1024)S(1)}, u32[]{:S(2)}) copy-start(f32[12288]{0:T(1024)S(1)} %bitcast_dynamic-update-slice_fusion) | copy-start | bytes 147460
  473.7 3.6 copy-start.22
  473.7 4.4 copy-start.20
  473.7 4.6 copy-start.19
  477.4 1.2 copy-start.12
  482.3 4.0 copy-start.25
  482.3 4.0 copy-start.28
  482.3 4.0 copy-start.29
  482.3 4.6 copy-start.16
  482.3 4.6 copy-start.17
  482.3 4.6 copy-start.18
  482.3 4.6 copy-start.21
  482.3 5.7 %copy-start.14 = (f32[64,3072]{1,0:T(8,128)S(1)}, f32[64,3072]{1,0:T(8,128)}, u32[]{:S(2)}) copy-start(f32[64,3072]{1,0:T(8,128)} %param.33) | copy-start | bytes 2359300
  482.4 5.7 %copy-start.15 = (f32[64,3072]{1,0:T(8,128)S(1)}, f32[64,3072]{1,0:T(8,128)}, u32[]{:S(2)}) copy-start(f32[64,3072]{1,0:T(8,128)} %param.28) | copy-start | bytes 2359300
  486.3 1.8 copy-start.13
  487.0 3.1 copy-start.10
  488.0 2.0 copy-start.5
  488.1 2.3 copy-start.6
  488.1 2.9 copy-start.7
  488.1 3.2 copy-start.8
  488.1 3.5 copy-start.9

commit v8 on v7

--- a/solution.py
+++ b/solution.py
@@ -451,9 +451,10 @@
         dx, gg = norm_back(wide_rows(buf, x_ref[0, i]), gain_ref[...], g)
         stage[i] = (dx + dx_ref[i]).astype(BF)[:half]
 
-        @pl.when(apart)
-        def _():
-            crossing_copies[i].start()
+        if i == 0:
+            @pl.when(apart)
+            def _():
+                crossing_copies[i].start()
 
         @pl.when(jnp.logical_not(apart))
         def _():
@@ -537,6 +538,12 @@
     idd.wait_recv()
     ipart[...] = add_all(isum[l], idp[...]).astype(BF)
     is_ = wires.send(ipart.at[1], irecv, to_seq)
+
+    @pl.when(apart)
+    def _():
+        for cp in crossing_copies[1:]:
+            cp.start()
+
     end_round(vout_ref, vrecv, vec_round)
     vec_round = start_round(vout_ref, vrecv, rounds[2])
 

time: 503 us -> 493 us (0.980)
  Pallas kernels: 442 us -> 433 us
    pallas_call x1, Pallas kernels: 133 us -> 123 us  [tail_stage(): pl.pallas_call(functools.partial(tail_kernel, ny, nx), in_specs=[VM] * 10...]
  transfers between devices with their start and end apart: 6 -> 6, of which waited for: 1 -> 1; matrix products, arithmetic and copies ran while one was open for 4% -> 4% of each run, Pallas kernels for 55% -> 54%
where the time goes in v8:
time: 493 us; the launch traced here: 486 us
  Pallas kernels  433 us (88%)
  other arithmetic  31.2 us (6%)
  local copies, waits for them, and re-layouts  12.3 us (2%)
  starting transfers between devices  5.92 us (1%)
    pallas_call x1, Pallas kernels, tail_stage(): pl.pallas_call(functools.partial(tail_kernel, ny, nx), in_specs=[VM] * 10...  123 us
    pallas_call x1, Pallas kernels, mid_stage(): pl.pallas_call(functools.partial(mid_kernel, ny, nx), in_specs=[VM] * 6 +...  93.1 us
    pallas_call x1, Pallas kernels, head_stage(): pl.pallas_call(functools.partial(head_kernel, ny, nx), in_specs=[VM] * 5...  91.1 us
    pallas_call x1, Pallas kernels, mlp(): pl.pallas_call(functools.partial(mlp_kernel, keys, keys_b, ny, nx, gtile=...  77.8 us
    pallas_call x1, Pallas kernels, attend_back(): pl.pallas_call(functools.partial(attend_back_kernel, pairs=pairs, chunk=c...  30.4 us
    pallas_call x1, Pallas kernels, middle_back(): pl.pallas_call(middle_back_kernel, grid=(n,), in_specs=[big, big, big, to...  16.8 us
  transfers between devices with their start and end apart: 6, of which 1 were waited for; matrix products, arithmetic and copies ran while one was open for 4% of the time, Pallas kernels for 54%

profile of v8, /device:TPU:1, one launch (start us, length us, event | category | flops | bytes accessed | tf_op | source)
XLA Modules:
  0.0 486.3 jit_solution(17647813847114664736)
XLA Ops:
  0.7 0.7 convert_element_type.123
  1.4 0.1 collective-permute-start
  1.4 1.3 broadcast_in_dim.23.refs_4_
  2.7 91.1 %head_stage.1 = (bf16[3,2,304,1024]{3,2,1,0:T(8,128)(2,1)}, bf16[3,2,304,1536]{3,2,1,0:T(8,128)(2,1)}, bf16[2,3,292,1024]{3,2,1,0:T(8,128)(2,1)}, bf16[1024,1536...) custom-call(f32[64,3072]{1,0:T(8,128)} %refs_0_.1, ...), custom_call_target="tpu_custom_call" | custom-call | flops 5737807872 | bytes 41943040 | tf_op jit(solution)/shard_map/head_stage/pallas_call | solution.py:921
  93.8 1.3 fusion.23
  95.1 0.6 select_maximum_fusion.refs_5_
  95.8 1.3 slice.95.refs_2_
  97.1 0.0 collective-permute-done
  97.1 0.1 reshape.141
  97.2 0.1 rev.3
  97.4 0.1 convert_element_type.125
  97.4 1.1 broadcast_in_dim.25.refs_1_.kb_ref
  98.5 93.1 %mid_stage.1 = (bf16[3,608,512]{2,1,0:T(8,128)(2,1)}, f32[3,4,8,608]{3,2,1,0:T(8,128)}, f32[3,2,304,1024]{3,2,1,0:T(8,128)}, bf16[3,2,304,1024]{3,2,1,0:T(8,128)...) custom-call(bf16[3,608,1536]{2,1,0:T(8,128)(2,1)} %bitcast.85, ...), custom_call_target="tpu_custom_call" | custom-call | flops 6813646848 | bytes 52428800 | tf_op jit(solution)/shard_map/mid_stage/pallas_call | solution.py:1080
  191.7 77.8 %feed_forward.1 = (bf16[2,2,128,1024]{3,2,1,0:T(8,128)(2,1)}, bf16[2,2,128,1024]{3,2,1,0:T(8,128)(2,1)}, bf16[2,2,128,1024]{3,2,1,0:T(8,128)(2,1)}, bf16[2,2,128...) custom-call(bf16[1824,1024]{1,0:T(8,128)(2,1)} %bitcast.91, ...), custom_call_target="tpu_custom_call" | custom-call | flops 45902462976 | bytes 41943040 | tf_op jit(solution)/shard_map/feed_forward/pallas_call | solution.py:253
  269.5 2.4 collective-permute-start.1
  271.9 0.1 collective-permute-start.4
  272.7 3.1 fusion.3
  275.8 0.9 collective-permute-start.3
  276.7 2.6 fusion.5
  279.3 0.6 collective-permute-start.2
  279.9 1.2 collective-permute-done.4
  281.1 3.7 fusion.2
  284.8 1.9 collective-permute-start.5
  286.8 0.0 copy-start.1
  286.8 16.8 %middle_back.1 = (f32[3,304,1024]{2,1,0:T(8,128)}, bf16[3,2,304,512]{3,2,1,0:T(8,128)(2,1)}, bf16[512,1024]{1,0:T(8,128)(2,1)}, f32[8,1024]{1,0:T(8,128)}) custom-call(f32[3,2,304,1024]{3,2,1,0:T(8,128)} %get-tuple-element.74.x2_ref, bf16[3,2,304,1024]{3,2,1,0:T(8,128)(2,1)} %bitcast.66, bf16[3,2,304,1024]{3,2,1,0:T(8,128)(2,1)} %collective-permute-done.1.db_ref, ...), custom_call_target="tpu_custom_call" | custom-call | flops 3825205248 | bytes 31457280 | tf_op jit(solution)/shard_map/middle_back/pallas_call | solution.py:387
  303.6 0.0 copy-start.27
  303.7 30.4 %attend_back.1 = (bf16[3,608,1536]{2,1,0:T(8,128)(2,1)}, f32[8,1536]{1,0:T(8,128)S(1)}) custom-call(bf16[3,608,1536]{2,1,0:T(8,128)(2,1)} %bitcast.86, bf16[3,608,1536]{2,1,0:T(8,128)(2,1)} %bitcast.87, bf16[3,608,1536]{2,1,0:T(8,128)(2,1)} %bitcast.88, bf16[3,608,128]{2,1,0:T(8,128)(2,1)S(1)} %copy-done.1, bf16[3,608,512]{2,1,0:T(8,128)(2,1)S(1)} %copy-done, ...), custom_call_target="tpu_custom_call" | custom-call | flops 11356078080 | bytes 14008320 | tf_op jit(solution)/shard_map/attend_back/pallas_call | solution.py:332
  334.1 0.3 dynamic_update_slice.6
  334.3 0.2 dynamic_update_slice.7
  334.6 0.0 copy-start.30
  334.7 5.3 %broadcast_select_fusion = (bf16[2,2,128,1024]{3,2,1,0:T(8,128)(2,1)}, bf16[2,2,128,1024]{3,2,1,0:T(8,128)(2,1)}) fusion(pred[]{:T(512)S(6)} %eq.14, bf16[2,2,128,1024]{3,2,1,0:T(8,128)(2,1)} %collective-permute-done.2, bf16[1,2,2,2,128,1024]{5,4,3,2,1,0:T(8,128)(2,1)} %get-tuple-element.92, bf16[2,2,128,1024]{3,2,1,0:T(8,128)(2,1)S(1)} %copy-done.11, ...), kind=kLoop, calls=%fused_computation.27 | loop fusion | flops 9437184 | bytes 8388609 | tf_op jit(solution)/shard_map/jit(_where)/select_n | solution.py:1190
  340.0 123.4 %tail_stage.1 = (bf16[64,1536]{1,0:T(8,128)(2,1)}, bf16[64,1536]{1,0:T(8,128)(2,1)}, bf16[64,1024]{1,0:T(8,128)(2,1)}, bf16[2,2,128,1024]{3,2,1,0:T(8,128)(2,1)}...) custom-call(bf16[1824,1024]{1,0:T(8,128)(2,1)} %bitcast.90, bf16[1824,1536]{1,0:T(8,128)(2,1)} %bitcast.89, ...), custom_call_target="tpu_custom_call" | custom-call | flops 11475615744 | bytes 41943040 | tf_op jit(solution)/shard_map/tail_stage/pallas_call | solution.py:634
  463.4 1.2 slice.85
  464.6 3.6 select_convert_fusion
  469.0 0.1 reshape.153
  469.2 0.1 reshape.154
  469.4 0.0 copy-done.12
  469.5 0.3 convert_multiply_fusion
  469.7 0.1 convert_multiply_fusion.2
  469.8 1.5 copy.51
  471.3 1.8 mul.176
  473.1 0.0 copy-start.25
  473.2 0.0 copy-start.28
  473.2 0.0 copy-start.29
  473.2 0.0 copy-start.16
  473.2 0.0 copy-start.17
  473.2 0.0 copy-start.18
  473.2 0.0 copy-start.14
  473.2 0.0 copy-start.15
  473.2 3.9 convert_element_type.161
  477.2 0.6 fusion.13
  477.8 0.0 copy-start.10
  477.8 1.1 fusion.19
  478.9 0.0 copy-start.5
  478.9 0.0 copy-start.6
  478.9 0.0 copy-start.7
  479.0 0.0 copy-start.8
  479.0 0.0 copy-start.9
  479.0 1.9 fusion.21
  480.9 0.3 copy-done.6
  481.2 0.6 copy-done.7
  481.8 0.3 copy-done.8
  482.2 0.3 copy-done.9
  482.5 3.6 fusion.15
  (63 shorter events, 0.3 us)
Async XLA Ops:
  1.4 95.7 %collective-permute-start = (f32[3,584]{1,0:T(4,128)S(1)}, f32[3,584]{1,0:T(4,128)S(1)}, u32[]{:S(2)}, u32[]{:S(2)}) collective-permute-start(f32[3,584]{1,0:T(4,128)S(1)} %convert_element_type.123), channel_id=1, source_target_pairs={{0,2},{2,0},{1,3},{3,1},{4,6},{6,4},{5,7},{7,5},{8,10},{10,8},{9,1... | collective-permute-start | bytes 21032 | tf_op jit(solution)/shard_map/ppermute | solution.py:1101
  2.7 94.4 %copy-start.23 = (s32[3,584]{1,0:T(4,128)S(1)}, s32[3,584]{1,0:T(4,128)}, u32[]{:S(2)}) copy-start(s32[3,584]{1,0:T(4,128)} %param.20) | copy-start | bytes 21028
  95.1 96.5 %copy-start.24 = (f32[1024]{0:T(1024)}, f32[1024]{0:T(1024)S(1)}, u32[]{:S(2)}) copy-start(f32[1024]{0:T(1024)S(1)} %get-tuple-element.136) | copy-start | bytes 12292
  269.5 7.2 %copy-start.4 = (bf16[1,2,2,2,128,1024]{5,4,3,2,1,0:T(8,128)(2,1)S(1)}, bf16[1,2,2,2,128,1024]{5,4,3,2,1,0:T(8,128)(2,1)}, u32[]{:S(2)}) copy-start(bf16[1,2,2,2,128,1024]{5,4,3,2,1,0:T(8,128)(2,1)} %get-tuple-element.92) | copy-start | bytes 6291460
  269.5 17.2 %collective-permute-start.1 = (bf16[3,2,304,1024]{3,2,1,0:T(8,128)(2,1)}, bf16[3,2,304,1024]{3,2,1,0:T(8,128)(2,1)}, u32[]{:S(2)}, u32[]{:S(2)}) collective-permute-start(bf16[3,2,304,1024]{3,2,1,0:T(8,128)(2,1)} %bitcast.65), channel_id=1, source_target_pairs={{0,2},{2,0},{1,3},{3,1},{4,6},{6,4},{5,7},{7,5},{8,10},{10,8},{9,1... | collective-permute-start | bytes 11206664 | tf_op jit(solution)/shard_map/ppermute | solution.py:1101
  271.9 9.1 %collective-permute-start.4 = (bf16[3,304,1024]{2,1,0:T(8,128)(2,1)}, bf16[3,304,1024]{2,1,0:T(8,128)(2,1)}, u32[]{:S(2)}, u32[]{:S(2)}) collective-permute-start(bf16[3,304,1024]{2,1,0:T(8,128)(2,1)} %get-tuple-element.106), channel_id=1, source_target_pairs={{0,2},{2,0},{1,3},{3,1},{4,6},{6,4},{5,7},{7,5},{8,10},{10,8},{9,1... | collective-permute-start | bytes 5603336 | tf_op jit(solution)/shard_map/ppermute | solution.py:1101
  272.7 8.4 %copy-start.3 = (f32[3,304,1024]{2,1,0:T(8,128)S(1)}, f32[3,304,1024]{2,1,0:T(8,128)}, u32[]{:S(2)}) copy-start(f32[3,304,1024]{2,1,0:T(8,128)} %get-tuple-element.105) | copy-start | bytes 11206660
  275.8 58.8 %collective-permute-start.3 = (bf16[2,2,128,1024]{3,2,1,0:T(8,128)(2,1)}, bf16[2,2,128,1024]{3,2,1,0:T(8,128)(2,1)}, u32[]{:S(2)}, u32[]{:S(2)}) collective-permute-start(bf16[2,2,128,1024]{3,2,1,0:T(8,128)(2,1)} %fusion.3), channel_id=1, source_target_pairs={{0,8},{8,0},{1,9},{9,1},{2,10},{10,2},{3,11},{11,3},{4,12},{12,4},... | collective-permute-start | bytes 3145736 | tf_op jit(solution)/shard_map/ppermute | solution.py:1181
  279.3 55.3 %collective-permute-start.2 = (bf16[2,2,128,1024]{3,2,1,0:T(8,128)(2,1)}, bf16[2,2,128,1024]{3,2,1,0:T(8,128)(2,1)}, u32[]{:S(2)}, u32[]{:S(2)}) collective-permute-start(bf16[2,2,128,1024]{3,2,1,0:T(8,128)(2,1)} %fusion.5), channel_id=1, source_target_pairs={{0,4},{4,0},{1,5},{5,1},{2,6},{6,2},{3,7},{7,3},{8,12},{12,8},{9,1... | collective-permute-start | bytes 3145736 | tf_op jit(solution)/shard_map/ppermute | solution.py:1180
  284.8 179.8 %collective-permute-start.5 = (bf16[3,292,1024]{2,1,0:T(8,128)(2,1)S(1)}, bf16[3,292,1024]{2,1,0:T(8,128)(2,1)}, u32[]{:S(2)}, u32[]{:S(2)}) collective-permute-start(bf16[3,292,1024]{2,1,0:T(8,128)(2,1)S(1)} %fusion.2), channel_id=1, source_target_pairs={{2,16},{16,2},{3,17},{17,3},{6,20},{20,6},{7,21},{21,7},{10,24},{2... | collective-permute-start | bytes 5382152 | tf_op jit(solution)/shard_map/ppermute | solution.py:1109
  286.7 16.9 %copy-start = (bf16[3,608,512]{2,1,0:T(8,128)(2,1)S(1)}, bf16[3,608,512]{2,1,0:T(8,128)(2,1)}, u32[]{:S(2)}) copy-start(bf16[3,608,512]{2,1,0:T(8,128)(2,1)} %get-tuple-element.73.o_ref) | copy-start | bytes 5603332
  286.8 16.9 %copy-start.1 = (bf16[3,608,128]{2,1,0:T(8,128)(2,1)S(1)}, bf16[3,608,128]{2,1,0:T(8,128)(2,1)}, u32[]{:S(2)}) copy-start(bf16[3,608,128]{2,1,0:T(8,128)(2,1)} %broadcast_in_dim.25.refs_1_.kb_ref) | copy-start | bytes 1400836
  286.8 16.9 %copy-start.2 = (f32[3,4,8,608]{3,2,1,0:T(8,128)S(1)}, f32[3,4,8,608]{3,2,1,0:T(8,128)}, u32[]{:S(2)}) copy-start(f32[3,4,8,608]{3,2,1,0:T(8,128)} %get-tuple-element.83.lse_ref) | copy-start | bytes 700420
  303.6 30.9 %copy-start.27 = (f32[8,1024]{1,0:T(8,128)S(1)}, f32[8,1024]{1,0:T(8,128)}, u32[]{:S(2)}) copy-start(f32[8,1024]{1,0:T(8,128)} %get-tuple-element.88) | copy-start | bytes 98308
  303.7 31.0 %copy-start.26 = (f32[32,128]{1,0:T(8,128)S(1)}, f32[32,128]{1,0:T(8,128)}, u32[]{:S(2)}) copy-start(f32[32,128]{1,0:T(8,128)} %get-tuple-element.89) | copy-start | bytes 49156
  303.7 31.0 %copy-start.11 = (bf16[2,2,128,1024]{3,2,1,0:T(8,128)(2,1)S(1)}, bf16[2,2,128,1024]{3,2,1,0:T(8,128)(2,1)}, u32[]{:S(2)}) copy-start(bf16[2,2,128,1024]{3,2,1,0:T(8,128)(2,1)} %get-tuple-element.91) | copy-start | bytes 3145732
  334.6 5.4 %copy-start.30 = (f32[12288]{0:T(1024)}, f32[12288]{0:T(1024)S(1)}, u32[]{:S(2)}) copy-start(f32[12288]{0:T(1024)S(1)} %bitcast_dynamic-update-slice_fusion) | copy-start | bytes 147460
  464.6 3.6 copy-start.22
  464.6 4.4 copy-start.20
  464.6 4.6 copy-start.19
  468.2 1.2 copy-start.12
  473.1 4.0 copy-start.25
  473.2 4.0 copy-start.28
  473.2 4.0 copy-start.29
  473.2 4.6 copy-start.16
  473.2 4.6 copy-start.17
  473.2 4.6 copy-start.18
  473.2 4.6 copy-start.21
  473.2 5.7 %copy-start.14 = (f32[64,3072]{1,0:T(8,128)S(1)}, f32[64,3072]{1,0:T(8,128)}, u32[]{:S(2)}) copy-start(f32[64,3072]{1,0:T(8,128)} %param.33) | copy-start | bytes 2359300
  473.2 5.7 %copy-start.15 = (f32[64,3072]{1,0:T(8,128)S(1)}, f32[64,3072]{1,0:T(8,128)}, u32[]{:S(2)}) copy-start(f32[64,3072]{1,0:T(8,128)} %param.28) | copy-start | bytes 2359300
  477.1 1.8 copy-start.13
  477.8 3.1 copy-start.10
  478.9 2.0 copy-start.5
  478.9 2.3 copy-start.6
  478.9 2.9 copy-start.7
  479.0 3.2 copy-start.8
  479.0 3.5 copy-start.9

commit v9 on v8

--- a/solution.py
+++ b/solution.py
@@ -875,11 +875,15 @@
         def _():
             x_core[i].wait_recv()
 
+        if i == max(images - 2, 0):
+            @pl.when(inner)
+            def _():
+                near_ff[0].start()
+
         if i == images - 1:
             @pl.when(inner)
             def _():
-                for cp in near_ff:
-                    cp.start()
+                near_ff[1].start()
 
         project(i, 1 - near)
         if i == 0:

time: 493 us -> 492 us (level)
  no operation moved by 1% of the time
where the time goes in v9:
time: 492 us; the launch traced here: 485 us
  Pallas kernels  431 us (88%)
  other arithmetic  31.2 us (6%)
  local copies, waits for them, and re-layouts  12.3 us (2%)
  starting transfers between devices  5.92 us (1%)
    pallas_call x1, Pallas kernels, tail_stage(): pl.pallas_call(functools.partial(tail_kernel, ny, nx), in_specs=[VM] * 10...  123 us
    pallas_call x1, Pallas kernels, mid_stage(): pl.pallas_call(functools.partial(mid_kernel, ny, nx), in_specs=[VM] * 6 +...  91.7 us
    pallas_call x1, Pallas kernels, head_stage(): pl.pallas_call(functools.partial(head_kernel, ny, nx), in_specs=[VM] * 5...  91.1 us
    pallas_call x1, Pallas kernels, mlp(): pl.pallas_call(functools.partial(mlp_kernel, keys, keys_b, ny, nx, gtile=...  77.9 us
    pallas_call x1, Pallas kernels, attend_back(): pl.pallas_call(functools.partial(attend_back_kernel, pairs=pairs, chunk=c...  30.4 us
    pallas_call x1, Pallas kernels, middle_back(): pl.pallas_call(middle_back_kernel, grid=(n,), in_specs=[big, big, big, to...  16.8 us
  transfers between devices with their start and end apart: 6, of which 1 were waited for; matrix products, arithmetic and copies ran while one was open for 4% of the time, Pallas kernels for 54%

profile of v9, /device:TPU:1, one launch (start us, length us, event | category | flops | bytes accessed | tf_op | source)
XLA Modules:
  0.0 484.9 jit_solution(11144261126701679638)
XLA Ops:
  0.7 0.7 convert_element_type.123
  1.4 0.1 collective-permute-start
  1.4 1.3 broadcast_in_dim.23.refs_4_
  2.7 91.1 %head_stage.1 = (bf16[3,2,304,1024]{3,2,1,0:T(8,128)(2,1)}, bf16[3,2,304,1536]{3,2,1,0:T(8,128)(2,1)}, bf16[2,3,292,1024]{3,2,1,0:T(8,128)(2,1)}, bf16[1024,1536...) custom-call(f32[64,3072]{1,0:T(8,128)} %refs_0_.1, ...), custom_call_target="tpu_custom_call" | custom-call | flops 5737807872 | bytes 41943040 | tf_op jit(solution)/shard_map/head_stage/pallas_call | solution.py:925
  93.8 1.3 fusion.23
  95.1 0.6 select_maximum_fusion.refs_5_
  95.8 1.3 slice.95.refs_2_
  97.1 0.0 collective-permute-done
  97.1 0.1 reshape.141
  97.2 0.1 rev.3
  97.4 0.1 convert_element_type.125
  97.4 1.1 broadcast_in_dim.25.refs_1_.kb_ref
  98.5 91.7 %mid_stage.1 = (bf16[3,608,512]{2,1,0:T(8,128)(2,1)}, f32[3,4,8,608]{3,2,1,0:T(8,128)}, f32[3,2,304,1024]{3,2,1,0:T(8,128)}, bf16[3,2,304,1024]{3,2,1,0:T(8,128)...) custom-call(bf16[3,608,1536]{2,1,0:T(8,128)(2,1)} %bitcast.85, ...), custom_call_target="tpu_custom_call" | custom-call | flops 6813646848 | bytes 52428800 | tf_op jit(solution)/shard_map/mid_stage/pallas_call | solution.py:1084
  190.3 77.9 %feed_forward.1 = (bf16[2,2,128,1024]{3,2,1,0:T(8,128)(2,1)}, bf16[2,2,128,1024]{3,2,1,0:T(8,128)(2,1)}, bf16[2,2,128,1024]{3,2,1,0:T(8,128)(2,1)}, bf16[2,2,128...) custom-call(bf16[1824,1024]{1,0:T(8,128)(2,1)} %bitcast.91, ...), custom_call_target="tpu_custom_call" | custom-call | flops 45902462976 | bytes 41943040 | tf_op jit(solution)/shard_map/feed_forward/pallas_call | solution.py:253
  268.1 2.4 collective-permute-start.1
  270.5 0.1 collective-permute-start.4
  271.3 3.1 fusion.3
  274.4 0.9 collective-permute-start.3
  275.3 2.6 fusion.5
  277.9 0.6 collective-permute-start.2
  278.5 1.2 collective-permute-done.4
  279.7 3.7 fusion.2
  283.4 1.9 collective-permute-start.5
  285.3 0.0 copy-start.1
  285.4 16.8 %middle_back.1 = (f32[3,304,1024]{2,1,0:T(8,128)}, bf16[3,2,304,512]{3,2,1,0:T(8,128)(2,1)}, bf16[512,1024]{1,0:T(8,128)(2,1)}, f32[8,1024]{1,0:T(8,128)}) custom-call(f32[3,2,304,1024]{3,2,1,0:T(8,128)} %get-tuple-element.74.x2_ref, bf16[3,2,304,1024]{3,2,1,0:T(8,128)(2,1)} %bitcast.66, bf16[3,2,304,1024]{3,2,1,0:T(8,128)(2,1)} %collective-permute-done.1.db_ref, ...), custom_call_target="tpu_custom_call" | custom-call | flops 3825205248 | bytes 31457280 | tf_op jit(solution)/shard_map/middle_back/pallas_call | solution.py:387
  302.2 0.0 copy-start.27
  302.3 30.4 %attend_back.1 = (bf16[3,608,1536]{2,1,0:T(8,128)(2,1)}, f32[8,1536]{1,0:T(8,128)S(1)}) custom-call(bf16[3,608,1536]{2,1,0:T(8,128)(2,1)} %bitcast.86, bf16[3,608,1536]{2,1,0:T(8,128)(2,1)} %bitcast.87, bf16[3,608,1536]{2,1,0:T(8,128)(2,1)} %bitcast.88, bf16[3,608,128]{2,1,0:T(8,128)(2,1)S(1)} %copy-done.1, bf16[3,608,512]{2,1,0:T(8,128)(2,1)S(1)} %copy-done, ...), custom_call_target="tpu_custom_call" | custom-call | flops 11356078080 | bytes 14008320 | tf_op jit(solution)/shard_map/attend_back/pallas_call | solution.py:332
  332.7 0.3 dynamic_update_slice.6
  332.9 0.2 dynamic_update_slice.7
  333.2 0.0 copy-start.30
  333.3 5.3 %broadcast_select_fusion = (bf16[2,2,128,1024]{3,2,1,0:T(8,128)(2,1)}, bf16[2,2,128,1024]{3,2,1,0:T(8,128)(2,1)}) fusion(pred[]{:T(512)S(6)} %eq.14, bf16[2,2,128,1024]{3,2,1,0:T(8,128)(2,1)} %collective-permute-done.2, bf16[1,2,2,2,128,1024]{5,4,3,2,1,0:T(8,128)(2,1)} %get-tuple-element.92, bf16[2,2,128,1024]{3,2,1,0:T(8,128)(2,1)S(1)} %copy-done.11, ...), kind=kLoop, calls=%fused_computation.27 | loop fusion | flops 9437184 | bytes 8388609 | tf_op jit(solution)/shard_map/jit(_where)/select_n | solution.py:1194
  338.6 123.4 %tail_stage.1 = (bf16[64,1536]{1,0:T(8,128)(2,1)}, bf16[64,1536]{1,0:T(8,128)(2,1)}, bf16[64,1024]{1,0:T(8,128)(2,1)}, bf16[2,2,128,1024]{3,2,1,0:T(8,128)(2,1)}...) custom-call(bf16[1824,1024]{1,0:T(8,128)(2,1)} %bitcast.90, bf16[1824,1536]{1,0:T(8,128)(2,1)} %bitcast.89, ...), custom_call_target="tpu_custom_call" | custom-call | flops 11475615744 | bytes 41943040 | tf_op jit(solution)/shard_map/tail_stage/pallas_call | solution.py:634
  462.0 1.2 slice.85
  463.2 3.6 select_convert_fusion
  467.6 0.1 reshape.153
  467.8 0.1 reshape.154
  468.0 0.0 copy-done.12
  468.1 0.3 convert_multiply_fusion
  468.3 0.1 convert_multiply_fusion.2
  468.4 1.5 copy.51
  469.9 1.8 mul.176
  471.7 0.0 copy-start.25
  471.7 0.0 copy-start.28
  471.8 0.0 copy-start.29
  471.8 0.0 copy-start.16
  471.8 0.0 copy-start.17
  471.8 0.0 copy-start.18
  471.8 0.0 copy-start.14
  471.8 0.0 copy-start.15
  471.8 3.9 convert_element_type.161
  475.8 0.6 fusion.13
  476.4 0.0 copy-start.10
  476.4 1.1 fusion.19
  477.5 0.0 copy-start.5
  477.5 0.0 copy-start.6
  477.5 0.0 copy-start.7
  477.5 0.0 copy-start.8
  477.6 0.0 copy-start.9
  477.6 1.9 fusion.21
  479.5 0.3 copy-done.6
  479.8 0.6 copy-done.7
  480.4 0.3 copy-done.8
  480.8 0.3 copy-done.9
  481.1 3.6 fusion.15
  (63 shorter events, 0.3 us)
Async XLA Ops:
  1.4 95.7 %collective-permute-start = (f32[3,584]{1,0:T(4,128)S(1)}, f32[3,584]{1,0:T(4,128)S(1)}, u32[]{:S(2)}, u32[]{:S(2)}) collective-permute-start(f32[3,584]{1,0:T(4,128)S(1)} %convert_element_type.123), channel_id=1, source_target_pairs={{0,2},{2,0},{1,3},{3,1},{4,6},{6,4},{5,7},{7,5},{8,10},{10,8},{9,1... | collective-permute-start | bytes 21032 | tf_op jit(solution)/shard_map/ppermute | solution.py:1105
  2.7 94.4 %copy-start.23 = (s32[3,584]{1,0:T(4,128)S(1)}, s32[3,584]{1,0:T(4,128)}, u32[]{:S(2)}) copy-start(s32[3,584]{1,0:T(4,128)} %param.20) | copy-start | bytes 21028
  95.1 95.1 %copy-start.24 = (f32[1024]{0:T(1024)}, f32[1024]{0:T(1024)S(1)}, u32[]{:S(2)}) copy-start(f32[1024]{0:T(1024)S(1)} %get-tuple-element.136) | copy-start | bytes 12292
  268.1 7.2 %copy-start.4 = (bf16[1,2,2,2,128,1024]{5,4,3,2,1,0:T(8,128)(2,1)S(1)}, bf16[1,2,2,2,128,1024]{5,4,3,2,1,0:T(8,128)(2,1)}, u32[]{:S(2)}) copy-start(bf16[1,2,2,2,128,1024]{5,4,3,2,1,0:T(8,128)(2,1)} %get-tuple-element.92) | copy-start | bytes 6291460
  268.1 17.2 %collective-permute-start.1 = (bf16[3,2,304,1024]{3,2,1,0:T(8,128)(2,1)}, bf16[3,2,304,1024]{3,2,1,0:T(8,128)(2,1)}, u32[]{:S(2)}, u32[]{:S(2)}) collective-permute-start(bf16[3,2,304,1024]{3,2,1,0:T(8,128)(2,1)} %bitcast.65), channel_id=1, source_target_pairs={{0,2},{2,0},{1,3},{3,1},{4,6},{6,4},{5,7},{7,5},{8,10},{10,8},{9,1... | collective-permute-start | bytes 11206664 | tf_op jit(solution)/shard_map/ppermute | solution.py:1105
  270.5 9.1 %collective-permute-start.4 = (bf16[3,304,1024]{2,1,0:T(8,128)(2,1)}, bf16[3,304,1024]{2,1,0:T(8,128)(2,1)}, u32[]{:S(2)}, u32[]{:S(2)}) collective-permute-start(bf16[3,304,1024]{2,1,0:T(8,128)(2,1)} %get-tuple-element.106), channel_id=1, source_target_pairs={{0,2},{2,0},{1,3},{3,1},{4,6},{6,4},{5,7},{7,5},{8,10},{10,8},{9,1... | collective-permute-start | bytes 5603336 | tf_op jit(solution)/shard_map/ppermute | solution.py:1105
  271.3 8.4 %copy-start.3 = (f32[3,304,1024]{2,1,0:T(8,128)S(1)}, f32[3,304,1024]{2,1,0:T(8,128)}, u32[]{:S(2)}) copy-start(f32[3,304,1024]{2,1,0:T(8,128)} %get-tuple-element.105) | copy-start | bytes 11206660
  274.4 58.8 %collective-permute-start.3 = (bf16[2,2,128,1024]{3,2,1,0:T(8,128)(2,1)}, bf16[2,2,128,1024]{3,2,1,0:T(8,128)(2,1)}, u32[]{:S(2)}, u32[]{:S(2)}) collective-permute-start(bf16[2,2,128,1024]{3,2,1,0:T(8,128)(2,1)} %fusion.3), channel_id=1, source_target_pairs={{0,8},{8,0},{1,9},{9,1},{2,10},{10,2},{3,11},{11,3},{4,12},{12,4},... | collective-permute-start | bytes 3145736 | tf_op jit(solution)/shard_map/ppermute | solution.py:1185
  277.9 55.3 %collective-permute-start.2 = (bf16[2,2,128,1024]{3,2,1,0:T(8,128)(2,1)}, bf16[2,2,128,1024]{3,2,1,0:T(8,128)(2,1)}, u32[]{:S(2)}, u32[]{:S(2)}) collective-permute-start(bf16[2,2,128,1024]{3,2,1,0:T(8,128)(2,1)} %fusion.5), channel_id=1, source_target_pairs={{0,4},{4,0},{1,5},{5,1},{2,6},{6,2},{3,7},{7,3},{8,12},{12,8},{9,1... | collective-permute-start | bytes 3145736 | tf_op jit(solution)/shard_map/ppermute | solution.py:1184
  283.4 179.8 %collective-permute-start.5 = (bf16[3,292,1024]{2,1,0:T(8,128)(2,1)S(1)}, bf16[3,292,1024]{2,1,0:T(8,128)(2,1)}, u32[]{:S(2)}, u32[]{:S(2)}) collective-permute-start(bf16[3,292,1024]{2,1,0:T(8,128)(2,1)S(1)} %fusion.2), channel_id=1, source_target_pairs={{2,16},{16,2},{3,17},{17,3},{6,20},{20,6},{7,21},{21,7},{10,24},{2... | collective-permute-start | bytes 5382152 | tf_op jit(solution)/shard_map/ppermute | solution.py:1113
  285.3 16.9 %copy-start = (bf16[3,608,512]{2,1,0:T(8,128)(2,1)S(1)}, bf16[3,608,512]{2,1,0:T(8,128)(2,1)}, u32[]{:S(2)}) copy-start(bf16[3,608,512]{2,1,0:T(8,128)(2,1)} %get-tuple-element.73.o_ref) | copy-start | bytes 5603332
  285.3 16.9 %copy-start.1 = (bf16[3,608,128]{2,1,0:T(8,128)(2,1)S(1)}, bf16[3,608,128]{2,1,0:T(8,128)(2,1)}, u32[]{:S(2)}) copy-start(bf16[3,608,128]{2,1,0:T(8,128)(2,1)} %broadcast_in_dim.25.refs_1_.kb_ref) | copy-start | bytes 1400836
  285.4 16.9 %copy-start.2 = (f32[3,4,8,608]{3,2,1,0:T(8,128)S(1)}, f32[3,4,8,608]{3,2,1,0:T(8,128)}, u32[]{:S(2)}) copy-start(f32[3,4,8,608]{3,2,1,0:T(8,128)} %get-tuple-element.83.lse_ref) | copy-start | bytes 700420
  302.2 30.9 %copy-start.27 = (f32[8,1024]{1,0:T(8,128)S(1)}, f32[8,1024]{1,0:T(8,128)}, u32[]{:S(2)}) copy-start(f32[8,1024]{1,0:T(8,128)} %get-tuple-element.88) | copy-start | bytes 98308
  302.2 31.0 %copy-start.26 = (f32[32,128]{1,0:T(8,128)S(1)}, f32[32,128]{1,0:T(8,128)}, u32[]{:S(2)}) copy-start(f32[32,128]{1,0:T(8,128)} %get-tuple-element.89) | copy-start | bytes 49156
  302.3 31.0 %copy-start.11 = (bf16[2,2,128,1024]{3,2,1,0:T(8,128)(2,1)S(1)}, bf16[2,2,128,1024]{3,2,1,0:T(8,128)(2,1)}, u32[]{:S(2)}) copy-start(bf16[2,2,128,1024]{3,2,1,0:T(8,128)(2,1)} %get-tuple-element.91) | copy-start | bytes 3145732
  333.2 5.4 %copy-start.30 = (f32[12288]{0:T(1024)}, f32[12288]{0:T(1024)S(1)}, u32[]{:S(2)}) copy-start(f32[12288]{0:T(1024)S(1)} %bitcast_dynamic-update-slice_fusion) | copy-start | bytes 147460
  463.2 3.6 copy-start.22
  463.2 4.4 copy-start.20
  463.2 4.6 copy-start.19
  466.8 1.2 copy-start.12
  471.7 4.0 copy-start.25
  471.7 4.0 copy-start.28
  471.8 4.0 copy-start.29
  471.8 4.6 copy-start.16
  471.8 4.6 copy-start.17
  471.8 4.6 copy-start.18
  471.8 4.6 copy-start.21
  471.8 5.7 %copy-start.14 = (f32[64,3072]{1,0:T(8,128)S(1)}, f32[64,3072]{1,0:T(8,128)}, u32[]{:S(2)}) copy-start(f32[64,3072]{1,0:T(8,128)} %param.33) | copy-start | bytes 2359300
  471.8 5.7 %copy-start.15 = (f32[64,3072]{1,0:T(8,128)S(1)}, f32[64,3072]{1,0:T(8,128)}, u32[]{:S(2)}) copy-start(f32[64,3072]{1,0:T(8,128)} %param.28) | copy-start | bytes 2359300
  475.7 1.8 copy-start.13
  476.4 3.1 copy-start.10
  477.5 2.0 copy-start.5
  477.5 2.3 copy-start.6
  477.5 2.9 copy-start.7
  477.5 3.2 copy-start.8
  477.6 3.5 copy-start.9
